TPU v7x, 256 devices: a whole 4x4x8 slice. The times are simulated.
256 devices in a mesh: tm: 16 (over z, core), height: 4 (over x), chan: 4 (over y).
Axes of the slice: x: 4, y: 4, z: 8, core: 2. Of those that a mesh axis runs over, the one named last changes fastest.
Arguments:
- frames: bfloat16 [32, 16, 256, 128], P('tm', 'height', 'chan'), may hold values from -6 to 6
- grad_out: bfloat16 [32, 16, 256, 128], P('tm', 'height', 'chan'), may hold values from -6 to 6
- weight_one: bfloat16 [256, 3, 3, 3, 256], P('chan'), may hold values from -0.078125 to 0.078125
- weight_two: bfloat16 [256, 3, 3, 3, 256], P('chan'), may hold values from -0.078125 to 0.078125
Outputs:
- grad_frames: bfloat16 [32, 16, 256, 128], P('tm', 'height', 'chan')
- grad_one: float32 [256, 3, 3, 3, 256], P('chan')
- grad_two: float32 [256, 3, 3, 3, 256], P('chan')
All inputs are finite; a program needn't handle non-finite values.
Results may differ from a plain program's by a relative error of at most 0.015.
Values may be sent and summed in bfloat16 or wider, within the bound.
No kernel may reach another device: no remote copies, remote signals or barrier semaphores. Data moves between devices by JAX's collectives and lax.ppermute only.
A program may use at most 128 MiB of HBM per device.

v0:
```python
import jax
import jax.numpy as jnp
from jax import lax
from jax.sharding import PartitionSpec as P


def passed_along(block, axis, distance):
    devices = range(lax.axis_size(axis))
    route = [(i - distance, i) for i in devices if i - distance in devices]
    return lax.ppermute(block, axis, route)


def extended(cells, sides, width):
    for axis, dim in sides:
        count = lax.axis_size(axis)
        ends = count - 1
        head = lax.slice_in_dim(cells, 0, width, axis=dim)
        tail = lax.slice_in_dim(cells, cells.shape[dim] - width, cells.shape[dim], axis=dim)
        cells = jnp.concatenate(
            [
                lax.ppermute(tail, axis, [(i, (i + 1) % count) for i in range(ends)]),
                cells,
                lax.ppermute(head, axis, [((i + 1) % count, i) for i in range(ends)]),
            ],
            axis=dim,
        )
    return cells


def product(form, left, right):
    return jnp.einsum(form, left, right, preferred_element_type=jnp.float32)


def shift_cols(block, offset):
    if offset == 0:
        return block
    edge = jnp.zeros(block.shape[:3] + (1,), block.dtype)
    if offset > 0:
        return jnp.concatenate([block[..., 1:], edge], 3)
    return jnp.concatenate([edge, block[..., :-1]], 3)


def forward_taps(padded, weight):
    frame_count = padded.shape[0] - 2
    row_count = padded.shape[1] - 2
    col_count = padded.shape[3]
    summed = jnp.zeros((frame_count, row_count, weight.shape[0], col_count), jnp.float32)
    for col_tap in range(3):
        partial_sum = jnp.zeros((frame_count, row_count, weight.shape[0], col_count), jnp.float32)
        for time_tap in range(3):
            for row_tap in range(3):
                window = padded[time_tap : time_tap + frame_count, row_tap : row_tap + row_count]
                partial_sum = partial_sum + product(
                    "frcw,oc->frow", window, weight[:, time_tap, row_tap, col_tap, :]
                )
        summed = summed + shift_cols(partial_sum, col_tap - 1)
    return summed


def backward_taps(padded, weight):
    frame_count = padded.shape[0] - 2
    row_count = padded.shape[1] - 2
    col_count = padded.shape[3]
    summed = jnp.zeros((frame_count, row_count, weight.shape[4], col_count), jnp.float32)
    for col_tap in range(3):
        partial_sum = jnp.zeros((frame_count, row_count, weight.shape[4], col_count), jnp.float32)
        for time_tap in range(3):
            for row_tap in range(3):
                window = padded[
                    2 - time_tap : 2 - time_tap + frame_count, 2 - row_tap : 2 - row_tap + row_count
                ]
                partial_sum = partial_sum + product(
                    "frow,oc->frcw", window, weight[:, time_tap, row_tap, col_tap, :]
                )
        summed = summed + shift_cols(partial_sum, 1 - col_tap)
    return summed


def forward_filter(padded, gradient):
    frame_count, row_count, out_width, col_count = gradient.shape
    moved = [shift_cols(gradient, 1 - col_tap) for col_tap in range(3)]
    pieces = []
    for time_tap in range(3):
        for row_tap in range(3):
            window = padded[time_tap : time_tap + frame_count, row_tap : row_tap + row_count]
            for col_tap in range(3):
                pieces.append(product("frcw,frow->oc", window, moved[col_tap]))
    return jnp.stack(pieces, 1).reshape(out_width, 3, 3, 3, padded.shape[2])


def backward_filter(source, padded):
    frame_count, row_count, in_width, col_count = source.shape
    moved = [shift_cols(padded, 1 - col_tap) for col_tap in range(3)]
    pieces = []
    for time_tap in range(3):
        for row_tap in range(3):
            for col_tap in range(3):
                window = moved[col_tap][
                    2 - time_tap : 2 - time_tap + frame_count, 2 - row_tap : 2 - row_tap + row_count
                ]
                pieces.append(product("frcw,frow->oc", source, window))
    return jnp.stack(pieces, 1).reshape(padded.shape[2], 3, 3, 3, in_width)


def on_device(frames, grad_out, weight_one, weight_two):
    earlier = passed_along(frames, "tm", 1)
    frames_time = jnp.concatenate([earlier, frames], 0)
    frames_rows = extended(frames_time, (("height", 1),), 1)
    frames_panel = lax.all_gather(frames_rows, "chan", axis=2, tiled=True)
    pre = forward_taps(frames_panel, weight_one)
    act = jax.nn.silu(pre).astype(jnp.bfloat16)
    later = passed_along(grad_out, "tm", -1)
    grads_time = jnp.concatenate([grad_out, later], 0)
    grads_padded = extended(grads_time, (("height", 1),), 1)
    act_full = lax.all_gather(act, "chan", axis=2, tiled=True)
    part_two = backward_filter(act_full, grads_padded)
    sigmoid_pre = jax.nn.sigmoid(pre)
    grad_act = lax.psum_scatter(
        backward_taps(grads_padded, weight_two), "chan", scatter_dimension=2, tiled=True
    )
    grad_pre = (grad_act * sigmoid_pre * (1.0 + pre * (1.0 - sigmoid_pre))).astype(jnp.bfloat16)
    pre_later = passed_along(grad_pre, "tm", -1)
    pre_time = jnp.concatenate([grad_pre, pre_later], 0)
    pre_padded = extended(pre_time, (("height", 1),), 1)
    grad_frames = lax.psum_scatter(
        backward_taps(pre_padded, weight_one).astype(jnp.bfloat16),
        "chan",
        scatter_dimension=2,
        tiled=True,
    )
    part_one = forward_filter(frames_panel, grad_pre)
    grad_one, grad_two = lax.psum((part_one, part_two), ("tm", "height"))
    return (grad_frames, grad_one, grad_two)


def solution(mesh):
    in_specs = (
        P("tm", "height", "chan", None),
        P("tm", "height", "chan", None),
        P("chan", None, None, None, None),
        P("chan", None, None, None, None),
    )
    out_specs = (
        P("tm", "height", "chan", None),
        P("chan", None, None, None, None),
        P("chan", None, None, None, None),
    )
    return jax.shard_map(
        on_device, mesh=mesh, in_specs=in_specs, out_specs=out_specs, check_vma=False
    )
```

profile of v0, /device:TPU:1, one launch (start us, length us, event | category | flops | bytes accessed | tf_op | source)
XLA Modules:
  0.0 437.2 jit_solution(17015021139338158347)
XLA Ops:
  7.2 5.3 %collective-permute-start = (bf16[2,4,64,128]{3,2,1,0:T(8,128)(2,1)}, bf16[2,4,64,128]{3,2,1,0:T(8,128)(2,1)S(1)}, u32[]{:S(2)}, u32[]{:S(2)}) collective-permute-start(bf16[2,4,64,128]{3,2,1,0:T(8,128)(2,1)} %param.5), channel_id=1, source_target_pairs={{16,0},{32,16},{48,32},{64,48},{80,64},{96,80},{112,96},{128,112},... | collective-permute-start | bytes 393224 | tf_op jit(solution)/shard_map/ppermute | solution.py:10
  12.5 1.3 convolution_bitcast_fusion.21
  13.8 1.3 convolution_bitcast_fusion.25
  15.1 0.3 convolution_bitcast_fusion.23
  16.5 2.8 collective-permute-start.2
  19.3 1.3 collective-permute-start.1
  20.6 0.3 convolution_bitcast_fusion.26
  21.0 0.3 convolution_bitcast_fusion.22
  21.3 0.3 convolution_bitcast_fusion.24
  22.0 0.3 convolution_bitcast_fusion.5
  22.4 0.3 convolution_bitcast_fusion
  22.7 0.3 convolution_bitcast_fusion.14
  23.0 1.3 collective-permute-done.1
  26.3 1.1 fusion.1
  27.4 1.1 fusion.10
  28.5 1.2 slice_add_fusion
  29.7 1.1 convolution_bitcast_fusion.11
  30.8 1.1 convolution_bitcast_fusion.12
  31.9 1.1 convolution_bitcast_fusion.8
  33.0 1.1 convolution_bitcast_fusion.9
  34.0 1.1 convolution_bitcast_fusion.7
  35.1 1.6 fusion.36
  36.7 1.3 copy.128
  38.1 3.6 collective-permute-start.3
  41.7 1.9 collective-permute-done.3
  43.7 3.1 collective-permute-start.4
  46.9 1.3 collective-permute-start.5
  48.2 3.7 collective-permute-done.5
  51.9 0.8 pad_maximum_fusion
  52.9 0.6 dynamic-slice
  54.4 35.9 %all-reduce.17.cloned.1.call-done = f32[2,4,256,128]{3,1,0,2:T(4,128)} async-done(((f32[2,4,256,128]{3,1,0,2:T(4,128)}), f32[2,4,256,128]{3,1,0,2:T(4,128)}) %all-reduce.17.cloned.1.call-update) | async-done | bytes 1048592
  90.4 1.7 constant_dynamic-slice_fusion.1
  92.0 32.3 %all-gather.2.cloned.1.call-done = bf16[4,6,256,128]{3,2,1,0:T(8,128)(2,1)} async-done(((bf16[4,6,64,128]{3,2,1,0:T(8,128)(2,1)}), bf16[4,6,256,128]{3,2,1,0:T(8,128)(2,1)}) %all-gather.2.cloned.1.call-update) | async-done | bytes 1572880 | tf_op jit(solution)/shard_map/all_gather | solution.py:109
  124.3 1.4 fusion.148
  125.7 1.3 convolution_add_fusion.13
  127.1 1.0 convolution_add_fusion.12
  128.0 1.0 convolution_add_fusion.11
  134.7 2.6 collective-permute-start.6
  137.6 0.3 fusion.190
  138.4 11.6 %all_gather.7 = bf16[2,4,256,128]{3,1,0,2:T(4,128)(2,1)S(1)} all-gather(bf16[2,4,64,128]{3,1,0,2:T(4,128)(2,1)S(1)} %copy.131), channel_id=1, replica_groups=mesh['tm'=16,'height'=4,'chan'=4] {'chan'}, dimensions={2}, use_global_device_ids=true | all-gather | bytes 655360 | tf_op jit(solution)/shard_map/all_gather | solution.py:115
  164.6 3.1 collective-permute-start.8
  167.7 1.5 collective-permute-start.7
  171.6 0.3 fusion.244
  171.9 0.8 collective-permute-done.7
  173.4 0.6 fusion.33
  174.4 0.3 fusion.204
  175.1 0.3 fusion.196
  175.7 0.3 fusion.228
  176.4 0.3 fusion.220
  176.7 0.3 fusion.217
  177.1 0.6 fusion.17
  177.6 0.3 fusion.11
  178.0 0.6 fusion.26
  178.5 0.4 fusion.37
  178.9 1.1 copy.130
  180.1 0.9 fusion.72
  181.0 0.9 fusion.71
  181.9 0.9 fusion.70
  182.9 45.5 %all-reduce.19.cloned.1.call-done = bf16[2,4,256,128]{3,1,0,2:T(4,128)(2,1)} async-done(((bf16[2,4,256,128]{3,1,0,2:T(4,128)(2,1)}), bf16[2,4,256,128]{3,1,0,2:T(4,128)(2,1)}) %all-reduce.19.cloned.1.call-update) | async-done | bytes 524304
  228.3 0.9 constant_dynamic-slice_fusion
  229.3 0.7 copy.159
  230.0 196.4 %all-reduce.21.cloned.1.call-done = (f32[64,3,3,3,256]{4,0,3,2,1:T(8,128)}, f32[64,3,3,3,256]{4,0,3,2,1:T(8,128)}) async-done(((f32[64,3,3,3,256]{4,0,3,2,1:T(8,128)}, f32[64,3,3,3,256]{4,0,3,2,1:T(8,128)}), (f32[64,3,3,3,256]{4,0,3,2,1:T(8,128)}, f32[64,3,3,3,256]{4,0,3,2,1:T(8,128)})) %all-reduce.21.cloned.1.call-update) | async-done | bytes 3538960 | tf_op jit(solution)/shard_map/psum | solution.py:132
  426.4 3.0 copy.391
  429.4 1.2 copy.392
  (145 shorter events, 29.2 us)
Async XLA Ops:
  7.2 7.9 %copy-start.2 = (bf16[2,4,64,128]{3,2,1,0:T(8,128)(2,1)S(1)}, bf16[2,4,64,128]{3,2,1,0:T(8,128)(2,1)}, u32[]{:S(2)}) copy-start(bf16[2,4,64,128]{3,2,1,0:T(8,128)(2,1)} %param.5) | copy-start | bytes 393220
  7.2 7.9 %copy-start.6 = (bf16[64,3,3,3,256]{4,0,3,2,1:T(8,128)(2,1)S(1)}, bf16[64,3,3,3,256]{4,0,3,2,1:T(8,128)(2,1)}, u32[]{:S(2)}) copy-start(bf16[64,3,3,3,256]{4,0,3,2,1:T(8,128)(2,1)} %param.7) | copy-start | bytes 2654212
  7.2 83.2 %all-reduce.17.cloned.1.call-start = ((), (), s32[]{:S(2)}) async-start(), calls=%async_computation.1 | async-start | bytes 2097152
  7.2 8.2 %collective-permute-start = (bf16[2,4,64,128]{3,2,1,0:T(8,128)(2,1)}, bf16[2,4,64,128]{3,2,1,0:T(8,128)(2,1)S(1)}, u32[]{:S(2)}, u32[]{:S(2)}) collective-permute-start(bf16[2,4,64,128]{3,2,1,0:T(8,128)(2,1)} %param.5), channel_id=1, source_target_pairs={{16,0},{32,16},{48,32},{64,48},{80,64},{96,80},{112,96},{128,112},... | collective-permute-start | bytes 393224 | tf_op jit(solution)/shard_map/ppermute | solution.py:10
  16.5 5.2 %collective-permute-start.2 = (bf16[4,1,64,128]{3,2,1,0:T(8,128)(2,1)S(1)}, bf16[4,1,64,128]{3,2,1,0:T(8,128)(2,1)S(1)}, u32[]{:S(2)}, u32[]{:S(2)}) collective-permute-start(bf16[4,1,64,128]{3,2,1,0:T(8,128)(2,1)S(1)} %get-tuple-element.20), channel_id=1, source_target_pairs={{0,4},{4,8},{8,12},{1,5},{5,9},{9,13},{2,6},{6,10},{10,14},{3,7},{... | collective-permute-start | bytes 196616 | tf_op jit(solution)/shard_map/ppermute | solution.py:21
  19.3 5.0 %collective-permute-start.1 = (bf16[4,1,64,128]{3,2,1,0:T(8,128)(2,1)S(1)}, bf16[4,1,64,128]{3,2,1,0:T(8,128)(2,1)S(1)}, u32[]{:S(2)}, u32[]{:S(2)}) collective-permute-start(bf16[4,1,64,128]{3,2,1,0:T(8,128)(2,1)S(1)} %get-tuple-element.19), channel_id=1, source_target_pairs={{4,0},{8,4},{12,8},{5,1},{9,5},{13,9},{6,2},{10,6},{14,10},{7,3},{... | collective-permute-start | bytes 196616 | tf_op jit(solution)/shard_map/ppermute | solution.py:23
  36.7 1.4 copy-start.8
  38.0 14.9 %copy-start.9 = (u32[256]{0:T(256)S(1)}, u32[256]{0:T(256)}, u32[]{:S(2)}) copy-start(u32[256]{0:T(256)} %constant.34) | copy-start | bytes 3076
  38.1 86.2 %all-gather.2.cloned.1.call-start = ((), (), s32[]{:S(2)}) async-start(), calls=%async_computation | async-start | bytes 1966080 | tf_op jit(solution)/shard_map/all_gather | solution.py:109
  38.1 5.6 %collective-permute-start.3 = (bf16[2,4,64,128]{3,2,1,0:T(8,128)(2,1)S(1)}, bf16[2,4,64,128]{3,2,1,0:T(8,128)(2,1)S(1)}, u32[]{:S(2)}, u32[]{:S(2)}) collective-permute-start(bf16[2,4,64,128]{3,2,1,0:T(8,128)(2,1)S(1)} %copy-done.8), channel_id=1, source_target_pairs={{0,16},{16,32},{32,48},{48,64},{64,80},{80,96},{96,112},{112,128},... | collective-permute-start | bytes 393224 | tf_op jit(solution)/shard_map/ppermute | solution.py:10
  43.7 4.4 %collective-permute-start.4 = (bf16[4,1,64,128]{3,2,1,0:T(8,128)(2,1)S(1)}, bf16[4,1,64,128]{3,2,1,0:T(8,128)(2,1)S(1)}, u32[]{:S(2)}, u32[]{:S(2)}) collective-permute-start(bf16[4,1,64,128]{3,2,1,0:T(8,128)(2,1)S(1)} %get-tuple-element.17), channel_id=1, source_target_pairs={{0,4},{4,8},{8,12},{1,5},{5,9},{9,13},{2,6},{6,10},{10,14},{3,7},{... | collective-permute-start | bytes 196616 | tf_op jit(solution)/shard_map/ppermute | solution.py:21
  46.9 5.0 %collective-permute-start.5 = (bf16[4,1,64,128]{3,2,1,0:T(8,128)(2,1)S(1)}, bf16[4,1,64,128]{3,2,1,0:T(8,128)(2,1)S(1)}, u32[]{:S(2)}, u32[]{:S(2)}) collective-permute-start(bf16[4,1,64,128]{3,2,1,0:T(8,128)(2,1)S(1)} %get-tuple-element.18), channel_id=1, source_target_pairs={{4,0},{8,4},{12,8},{5,1},{9,5},{13,9},{6,2},{10,6},{14,10},{7,3},{... | collective-permute-start | bytes 196616 | tf_op jit(solution)/shard_map/ppermute | solution.py:23
  52.7 175.7 %all-reduce.19.cloned.1.call-start = ((), (), s32[]{:S(2)}) async-start(), calls=%async_computation.2 | async-start | bytes 1048576
  124.3 2.8 copy-start
  125.7 3.3 copy-start.1
  133.3 1.0 copy-start.7
  134.7 29.9 %collective-permute-start.6 = (bf16[2,4,64,128]{3,2,1,0:T(8,128)(2,1)S(1)}, bf16[2,4,64,128]{3,2,1,0:T(8,128)(2,1)S(1)}, u32[]{:S(2)}, u32[]{:S(2)}) collective-permute-start(bf16[2,4,64,128]{3,2,1,0:T(8,128)(2,1)S(1)} %get-tuple-element.14), channel_id=1, source_target_pairs={{16,0},{32,16},{48,32},{64,48},{80,64},{96,80},{112,96},{128,112},... | collective-permute-start | bytes 393224 | tf_op jit(solution)/shard_map/ppermute | solution.py:10
  157.7 1.4 copy-start.3
  164.6 5.7 %copy-start.5 = (f32[64,27,256]{2,0,1:T(8,128)}, f32[64,27,256]{2,0,1:T(8,128)S(1)}, u32[]{:S(2)}) copy-start(f32[64,27,256]{2,0,1:T(8,128)S(1)} %fusion.73) | copy-start | bytes 5308420
  164.6 6.6 %collective-permute-start.8 = (bf16[4,1,64,128]{3,2,1,0:T(8,128)(2,1)S(1)}, bf16[4,1,64,128]{3,2,1,0:T(8,128)(2,1)S(1)}, u32[]{:S(2)}, u32[]{:S(2)}) collective-permute-start(bf16[4,1,64,128]{3,2,1,0:T(8,128)(2,1)S(1)} %get-tuple-element.15), channel_id=1, source_target_pairs={{0,4},{4,8},{8,12},{1,5},{5,9},{9,13},{2,6},{6,10},{10,14},{3,7},{... | collective-permute-start | bytes 196616 | tf_op jit(solution)/shard_map/ppermute | solution.py:21
  167.7 5.0 %collective-permute-start.7 = (bf16[4,1,64,128]{3,2,1,0:T(8,128)(2,1)S(1)}, bf16[4,1,64,128]{3,2,1,0:T(8,128)(2,1)S(1)}, u32[]{:S(2)}, u32[]{:S(2)}) collective-permute-start(bf16[4,1,64,128]{3,2,1,0:T(8,128)(2,1)S(1)} %get-tuple-element.16), channel_id=1, source_target_pairs={{4,0},{8,4},{12,8},{5,1},{9,5},{13,9},{6,2},{10,6},{14,10},{7,3},{... | collective-permute-start | bytes 196616 | tf_op jit(solution)/shard_map/ppermute | solution.py:23
  180.0 246.4 %all-reduce.21.cloned.1.call-start = ((), (), s32[]{:S(2)}) async-start(), calls=%async_computation.3 | async-start | bytes 7077888 | tf_op jit(solution)/shard_map/psum | solution.py:132
  426.4 3.0 copy-start.4
Sparse Core Ops, SparseCore 0:
  38.2 52.1 all-reduce.16
  92.9 31.3 all-gather.1
  180.2 48.1 all-reduce.18
  232.7 193.6 all-reduce.20
where the time goes:
time: 439 us; the launch traced here: 437 us
  waiting for transfers between devices  318 us (72%)
  matrix products  53.8 us (12%)
  starting transfers between devices  24.9 us (6%)
  between operations  15.3 us (3%)
  blocking collectives  11.6 us (3%)
  local copies, waits for them, and re-layouts  11.5 us (3%)
    psum x1, waiting for transfers between devices, on_device(): grad_one, grad_two = lax.psum((part_one, part_two), ('tm', 'height'))  196 us
    unnamed x6, waiting for transfers between devices  81.5 us
    dot_general x135, matrix products, product(): return jnp.einsum(form, left, right, preferred_element_type=jnp.float32)  53.8 us
    all_gather x1, waiting for transfers between devices, on_device(): frames_panel = lax.all_gather(frames_rows, 'chan', axis=2, tiled=True)  32.3 us
    all_gather x1, blocking collectives, on_device(): act_full = lax.all_gather(act, 'chan', axis=2, tiled=True)  11.6 us
    ppermute x3, starting transfers between devices, passed_along(): return lax.ppermute(block, axis, route)  11.5 us
    ppermute x3, starting transfers between devices, extended(): lax.ppermute(tail, axis, [(i, (i + 1) % count) for i in range(ends)])  8.99 us
  transfers between devices with their start and end apart: 13, of which 8 were waited for; matrix products, arithmetic and copies ran while one was open for 7% of the time, Pallas kernels for 0%

commit v1 on v0

v1 whole, which is shorter than its diff:
```python
import jax
import jax.numpy as jnp
from jax import lax
from jax.experimental import pallas as pl
from jax.experimental.pallas import tpu as pltpu
from jax.sharding import PartitionSpec as P


def passed_along(block, axis, distance):
    devices = range(lax.axis_size(axis))
    route = [(i - distance, i) for i in devices if i - distance in devices]
    return lax.ppermute(block, axis, route)


VMEM_LIMIT = 50 * 1024 * 1024
TAPS = [(a, b) for a in range(3) for b in range(3)]
SPOTS = [(t, i) for t in range(2) for i in range(4)]


def call(body, outs, scratch, place, *operands):
    vmem = pl.BlockSpec(memory_space=pltpu.VMEM)
    return pl.pallas_call(
        body,
        out_shape=outs,
        in_specs=[pl.BlockSpec(memory_space=pltpu.SMEM)] + [vmem] * len(operands),
        out_specs=[vmem] * len(outs),
        scratch_shapes=scratch,
        compiler_params=pltpu.CompilerParams(vmem_limit_bytes=VMEM_LIMIT),
    )(place, *operands)


def lanes_moved(cell):
    wide = cell.astype(jnp.float32)
    lane = lax.broadcasted_iota(jnp.int32, wide.shape, 1)
    ahead = jnp.where(lane == 127, 0.0, pltpu.roll(wide, 127, 1))
    behind = jnp.where(lane == 0, 0.0, pltpu.roll(wide, 1, 1))
    return ahead.astype(jnp.bfloat16), cell, behind.astype(jnp.bfloat16)


def forward_body(place, own, early, above, below, weight, panel, pre, act, wide):
    me = place[0]
    for f in range(4):
        for r in range(6):
            if r == 0:
                cell = above[f, 0]
            elif r == 5:
                cell = below[f, 0]
            else:
                cell = early[f, r - 1] if f < 2 else own[f - 2, r - 1]
            for k in range(4):
                at = pl.multiple_of(((me + 4 - k) % 4) * 64, 64)
                panel[f * 6 + r, pl.ds(at, 64), :] = cell[k * 64 : k * 64 + 64]
    for p, (t, i) in enumerate(SPOTS):
        for n, (a, b) in enumerate(TAPS):
            wide[n * 256 : n * 256 + 256, p * 128 : p * 128 + 128] = panel[(t + a) * 6 + i + b]
    for t in range(2):
        sums = jnp.dot(
            weight[...], wide[:, t * 512 : t * 512 + 512], preferred_element_type=jnp.float32
        )
        lane = lax.broadcasted_iota(jnp.int32, (64, 128), 1)
        for i in range(4):
            part = sums[:, i * 128 : i * 128 + 128]
            behind = jnp.where(lane == 0, 0.0, pltpu.roll(part[:64], 1, 1))
            ahead = jnp.where(lane == 127, 0.0, pltpu.roll(part[128:], 127, 1))
            value = behind + part[64:128] + ahead
            pre[t * 4 + i] = value
            act[t * 4 + i] = (value * jax.nn.sigmoid(value)).astype(jnp.bfloat16)


def spread(own, late, above, below, wide):
    for f in range(4):
        for r in range(6):
            if r == 0:
                cell = above[f, 0]
            elif r == 5:
                cell = below[f, 0]
            else:
                cell = own[f, r - 1] if f < 2 else late[f - 2, r - 1]
            moved = lanes_moved(cell)
            for n, (a, b) in enumerate(TAPS):
                t, i = f - 2 + a, r - 2 + b
                if (t, i) in SPOTS:
                    p = SPOTS.index((t, i))
                    for e in range(3):
                        row = (n * 3 + e) * 64
                        wide[row : row + 64, p * 128 : p * 128 + 128] = moved[e]


def transposed_body(place, own, late, above, below, weight, mine, one, two, three, wide, full):
    me = place[0]
    spread(own, late, above, below, wide)
    full[...] = jnp.dot(weight[...], wide[...], preferred_element_type=jnp.float32)
    for k, out in enumerate((mine, one, two, three)):
        at = pl.multiple_of(((me + k) % 4) * 64, 64)
        for p in range(8):
            out[p] = full[pl.ds(at, 64), p * 128 : p * 128 + 128].astype(out.dtype)


def against(left, right):
    return lax.dot_general(left, right, (((1,), (1,)), ((), ())), preferred_element_type=jnp.float32)


def store_filter(out, height, tap, rows):
    for q in range(4):
        out[(q + 4 - height) % 4, tap] = rows[q * 16 : q * 16 + 16].astype(jnp.bfloat16)


def first_filter_body(place, panel, gradient, out, moved):
    height = place[1]
    for p in range(8):
        for e, part in enumerate(lanes_moved(gradient[p])):
            moved[e * 64 : e * 64 + 64, p * 128 : p * 128 + 128] = part
    for n, (a, b) in enumerate(TAPS):
        window = jnp.concatenate([panel[(t + a) * 6 + i + b] for t, i in SPOTS], 1)
        sums = against(moved[...], window)
        for e in range(3):
            store_filter(out, height, n * 3 + e, sums[e * 64 : e * 64 + 64])


def second_filter_body(place, own, late, above, below, a0, a1, a2, a3, out, wide, acts):
    me, height = place[0], place[1]
    spread(own, late, above, below, wide)
    for k, part in enumerate((a0, a1, a2, a3)):
        at = pl.multiple_of(((me + 4 - k) % 4) * 64, 64)
        for p in range(8):
            acts[pl.ds(at, 64), p * 128 : p * 128 + 128] = part[p]
    for n in range(9):
        sums = against(wide[n * 192 : n * 192 + 192], acts[...])
        for e in range(3):
            store_filter(out, height, n * 3 + e, sums[e * 64 : e * 64 + 64])


def shaped(shape, dtype):
    return jax.ShapeDtypeStruct(shape, dtype)


def forward(place, own, early, above, below, weight):
    return call(
        forward_body,
        [shaped((24, 256, 128), jnp.bfloat16), shaped((8, 64, 128), jnp.float32), shaped((8, 64, 128), jnp.bfloat16)],
        [pltpu.VMEM((2304, 1024), jnp.bfloat16)],
        place, own, early, above, below, weight,
    )


def transposed(place, cells, weight):
    return call(
        transposed_body,
        [shaped((8, 64, 128), jnp.float32)] + [shaped((8, 64, 128), jnp.bfloat16)] * 3,
        [pltpu.VMEM((1728, 1024), jnp.bfloat16), pltpu.VMEM((256, 1024), jnp.float32)],
        place, *cells, weight,
    )


def first_filter(place, panel, gradient):
    return call(
        first_filter_body, [shaped((4, 27, 16, 256), jnp.bfloat16)],
        [pltpu.VMEM((192, 1024), jnp.bfloat16)], place, panel, gradient,
    )[0]


def second_filter(place, cells, acts):
    return call(
        second_filter_body, [shaped((4, 27, 16, 256), jnp.bfloat16)],
        [pltpu.VMEM((1728, 1024), jnp.bfloat16), pltpu.VMEM((256, 1024), jnp.bfloat16)],
        place, *cells, *acts,
    )[0]


def rotated(block, axis, distance):
    count = lax.axis_size(axis)
    return lax.ppermute(block, axis, [(i, (i + distance) % count) for i in range(count)])


def in_order(own, others, axis):
    me = lax.axis_index(axis)
    count = len(others) + 1
    pieces = [others[count - 2 - i] for i in range(count - 1)] + [own]
    ring = jnp.stack(pieces + pieces[:-1], 0)
    return lax.dynamic_slice_in_dim(ring, (count - 1 - me) % count, count, 0)


def all_rotated(block, axis):
    return [rotated(block, axis, k) for k in range(1, lax.axis_size(axis))]


def exchanged(pieces, axis):
    total = pieces[0].astype(jnp.float32)
    for k in range(1, len(pieces)):
        total = total + rotated(pieces[k], axis, k).astype(jnp.float32)
    return total


def swapped(block, distance):
    return lax.ppermute(block, "tm", [(i, i ^ distance) for i in range(lax.axis_size("tm"))])


def sum_of_halves(low, high, bit, distance):
    mine = jnp.where(bit == 1, high, low)
    theirs = jnp.where(bit == 1, low, high)
    other = swapped(theirs.astype(jnp.bfloat16), distance)
    return mine.astype(jnp.float32) + other.astype(jnp.float32)


def halves_joined(block, bit, distance, dim=0):
    other = swapped(block, distance)
    return jnp.concatenate([jnp.where(bit == 1, other, block), jnp.where(bit == 1, block, other)], dim)


def summed_filters(part_one, part_two):
    spot = lax.axis_index("tm")
    core, z_one, z_two = spot % 2, (spot // 2) % 2, (spot // 4) % 2
    total = sum_of_halves(part_one, part_two, core, 1)
    total = exchanged([total[0]] + [total[k].astype(jnp.bfloat16) for k in range(1, 4)], "height")
    total = sum_of_halves(total[:, :8], total[:, 8:], z_one, 2)
    total = sum_of_halves(total[..., :128], total[..., 128:], z_two, 4)
    total = total.astype(jnp.bfloat16)
    total = (total.astype(jnp.float32) + swapped(total, 8).astype(jnp.float32)).astype(jnp.bfloat16)
    total = halves_joined(total, z_two, 4, 2)
    total = halves_joined(total.transpose(1, 0, 2).reshape(432, 128), z_one, 2)
    total = in_order(total, all_rotated(total, "height"), "height").reshape(1728, 256)
    total = halves_joined(total, core, 1).reshape(2, 64, 3, 3, 3, 256).astype(jnp.float32)
    return total[0], total[1]


def edges(first, second):
    last = first.shape[1] - 1
    heads = jnp.concatenate([first[:, :1], second[:, :1]], 0)
    tails = jnp.concatenate([first[:, last:], second[:, last:]], 0)
    return passed_along(tails, "height", 1), passed_along(heads, "height", -1)


def with_later(cells):
    late = passed_along(cells, "tm", -1)
    return (cells, late) + edges(cells, late)


def on_device(frames, grad_out, weight_one, weight_two):
    place = jnp.stack([lax.axis_index("chan"), lax.axis_index("height")]).astype(jnp.int32)
    frames_all = jnp.concatenate([frames] + all_rotated(frames, "chan"), 2)
    early = passed_along(frames_all, "tm", 1)
    above, below = edges(early, frames_all)
    ahead = weight_one.transpose(3, 0, 1, 2, 4).reshape(192, 2304)
    back_one = weight_one.transpose(4, 1, 2, 3, 0).reshape(256, 1728)
    back_two = weight_two.transpose(4, 1, 2, 3, 0).reshape(256, 1728)
    panel, pre, act = forward(place, frames_all, early, above, below, ahead)
    grads = with_later(grad_out)
    grad_act = exchanged(transposed(place, grads, back_two), "chan")
    sigmoid_pre = jax.nn.sigmoid(pre)
    grad_pre = (grad_act * sigmoid_pre * (1.0 + pre * (1.0 - sigmoid_pre))).astype(jnp.bfloat16)
    part_one = first_filter(place, panel, grad_pre)
    part_two = second_filter(place, grads, [act] + all_rotated(act, "chan"))
    grad_one, grad_two = summed_filters(part_one, part_two)
    cells = with_later(grad_pre.reshape(2, 4, 64, 128))
    grad_frames = exchanged(transposed(place, cells, back_one), "chan")
    return (grad_frames.reshape(2, 4, 64, 128).astype(jnp.bfloat16), grad_one, grad_two)


def solution(mesh):
    in_specs = (
        P("tm", "height", "chan", None),
        P("tm", "height", "chan", None),
        P("chan", None, None, None, None),
        P("chan", None, None, None, None),
    )
    out_specs = (
        P("tm", "height", "chan", None),
        P("chan", None, None, None, None),
        P("chan", None, None, None, None),
    )
    return jax.shard_map(
        on_device, mesh=mesh, in_specs=in_specs, out_specs=out_specs, check_vma=False
    )
```

time: 439 us -> 162 us (0.37)
  waiting for transfers between devices: 318 us -> 48.6 us
  matrix products: 53.8 us -> 0 us
  starting transfers between devices: 24.9 us -> 71.8 us
  between operations: 15.3 us -> 1.19 us
  Pallas kernels: 0 us -> 11.8 us
  blocking collectives: 11.6 us -> 0 us
  local copies, waits for them, and re-layouts: 11.5 us -> 21.9 us
    psum x1 -> x0, waiting for transfers between devices: 196 us -> none  [on_device(): grad_one, grad_two = lax.psum((part_one, part_two), ('tm', 'height'))]
    unnamed x6 -> x0, waiting for transfers between devices: 81.5 us -> none
    dot_general x135 -> x0, matrix products: 53.8 us -> none  [product(): return jnp.einsum(form, left, right, preferred_element_type=jnp.float32)]
    ppermute x6 -> x25, starting transfers between devices: 13.1 us -> 45.6 us  [the longest x7 23.2 us: swapped(): lax.ppermute(block, 'tm', [(i, i ^ distance) for i in range(lax.axis_size...]
    all_gather x1 -> x0, waiting for transfers between devices: 32.3 us -> none  [on_device(): frames_panel = lax.all_gather(frames_rows, 'chan', axis=2, tiled=True)]
    ppermute x6 -> x25, waiting for transfers between devices: 5.82 us -> 36.1 us  [the longest x18 26 us: rotated(): lax.ppermute(block, axis, [(i, (i + distance) % count) for i in range(cou...]
    ppermute x3 -> x9, starting transfers between devices: 11.5 us -> 26.2 us  [passed_along(): return lax.ppermute(block, axis, route)]
    pallas_call x0 -> x5, Pallas kernels: none -> 11.8 us  [call(): pl.pallas_call(body, out_shape=outs, in_specs=[pl.BlockSpec(memory_space=...]
  transfers between devices with their start and end apart: 13 -> 34, of which waited for: 8 -> 15; matrix products, arithmetic and copies ran while one was open for 7% -> 8% of each run, Pallas kernels for 0% -> 6%
where the time goes in v1:
time: 162 us; the launch traced here: 161 us
  starting transfers between devices  71.8 us (44%)
  waiting for transfers between devices  48.6 us (30%)
  local copies, waits for them, and re-layouts  21.9 us (14%)
  Pallas kernels  11.8 us (7%)
  other arithmetic  5.93 us (4%)
    ppermute x9, starting transfers between devices, passed_along(): return lax.ppermute(block, axis, route)  26.2 us
    ppermute x18, waiting for transfers between devices, rotated(): lax.ppermute(block, axis, [(i, (i + distance) % count) for i in range(cou...  26 us
    ppermute x7, starting transfers between devices, swapped(): lax.ppermute(block, 'tm', [(i, i ^ distance) for i in range(lax.axis_size...  23.2 us
    ppermute x18, starting transfers between devices, rotated(): lax.ppermute(block, axis, [(i, (i + distance) % count) for i in range(cou...  22.4 us
    ppermute x9, waiting for transfers between devices, passed_along(): return lax.ppermute(block, axis, route)  12.5 us
    pallas_call x5, Pallas kernels, call(): pl.pallas_call(body, out_shape=outs, in_specs=[pl.BlockSpec(memory_space=...  11.8 us
    ppermute x7, waiting for transfers between devices, swapped(): lax.ppermute(block, 'tm', [(i, i ^ distance) for i in range(lax.axis_size...  10.1 us
    unnamed x16, local copies, waits for them, and re-layouts  5.54 us
  transfers between devices with their start and end apart: 34, of which 15 were waited for; matrix products, arithmetic and copies ran while one was open for 8% of the time, Pallas kernels for 6%

profile of v1, /device:TPU:1, one launch (start us, length us, event | category | flops | bytes accessed | tf_op | source)
XLA Modules:
  0.0 161.2 jit_solution(6470262035376815310)
XLA Ops:
  0.6 3.8 %collective-permute-start.7 = (bf16[2,4,64,128]{3,2,1,0:T(8,128)(2,1)}, bf16[2,4,64,128]{3,2,1,0:T(8,128)(2,1)S(1)}, u32[]{:S(2)}, u32[]{:S(2)}) collective-permute-start(bf16[2,4,64,128]{3,2,1,0:T(8,128)(2,1)} %param.4), channel_id=1, source_target_pairs={{0,2},{1,3},{2,0},{3,1},{4,6},{5,7},{6,4},{7,5},{8,10},{9,11},{10,... | collective-permute-start | bytes 393224 | tf_op jit(solution)/shard_map/ppermute | solution.py:172
  4.9 2.3 %collective-permute-start.8 = (bf16[2,4,64,128]{3,2,1,0:T(8,128)(2,1)}, bf16[2,4,64,128]{3,2,1,0:T(8,128)(2,1)S(1)}, u32[]{:S(2)}, u32[]{:S(2)}) collective-permute-start(bf16[2,4,64,128]{3,2,1,0:T(8,128)(2,1)} %param.4), channel_id=1, source_target_pairs={{0,3},{1,0},{2,1},{3,2},{4,7},{5,4},{6,5},{7,6},{8,11},{9,8},{10,9... | collective-permute-start | bytes 393224 | tf_op jit(solution)/shard_map/ppermute | solution.py:172
  7.1 3.4 %collective-permute-start = (bf16[2,4,64,128]{3,2,1,0:T(8,128)(2,1)}, bf16[2,4,64,128]{3,2,1,0:T(8,128)(2,1)S(1)}, u32[]{:S(2)}, u32[]{:S(2)}) collective-permute-start(bf16[2,4,64,128]{3,2,1,0:T(8,128)(2,1)} %own.3), channel_id=1, source_target_pairs={{16,0},{32,16},{48,32},{64,48},{80,64},{96,80},{112,96},{128,112},... | collective-permute-start | bytes 393224 | tf_op jit(solution)/shard_map/ppermute | solution.py:12
  10.6 0.8 fusion.9
  11.3 0.9 constant_dynamic-update-slice_fusion.3
  12.3 1.5 copy.10.weight
  13.9 3.5 %collective-permute-start.9 = (bf16[2,4,256,128]{3,2,1,0:T(8,128)(2,1)S(1)}, bf16[2,4,256,128]{3,2,1,0:T(8,128)(2,1)S(1)}, u32[]{:S(2)}, u32[]{:S(2)}) collective-permute-start(bf16[2,4,256,128]{3,2,1,0:T(8,128)(2,1)S(1)} %constant_dynamic-update-slice_fusion.own), channel_id=1, source_target_pairs={{0,16},{16,32},{32,48},{48,64},{64,80},{80,96},{96,112},{112,128},... | collective-permute-start | bytes 1572872 | tf_op jit(solution)/shard_map/ppermute | solution.py:12
  17.4 3.1 %collective-permute-start.1 = (bf16[4,1,64,128]{3,2,1,0:T(8,128)(2,1)S(1)}, bf16[4,1,64,128]{3,2,1,0:T(8,128)(2,1)S(1)}, u32[]{:S(2)}, u32[]{:S(2)}) collective-permute-start(bf16[4,1,64,128]{3,2,1,0:T(8,128)(2,1)S(1)} %pad_maximum_fusion.3), channel_id=1, source_target_pairs={{0,4},{4,8},{8,12},{1,5},{5,9},{9,13},{2,6},{6,10},{10,14},{3,7},{... | collective-permute-start | bytes 196616 | tf_op jit(solution)/shard_map/ppermute | solution.py:12
  20.5 2.9 %collective-permute-done.9.early = bf16[2,4,256,128]{3,2,1,0:T(8,128)(2,1)S(1)} collective-permute-done((bf16[2,4,256,128]{3,2,1,0:T(8,128)(2,1)S(1)}, bf16[2,4,256,128]{3,2,1,0:T(8,128)(2,1)S(1)}, u32[]{:S(2)}, u32[]{:S(2)}) %collective-permute-start.9) | collective-permute-done | bytes 524320 | tf_op jit(solution)/shard_map/ppermute | solution.py:12
  23.5 0.7 pad_maximum_fusion
  24.2 3.1 %collective-permute-start.10 = (bf16[4,1,256,128]{3,2,1,0:T(8,128)(2,1)}, bf16[4,1,256,128]{3,2,1,0:T(8,128)(2,1)S(1)}, u32[]{:S(2)}, u32[]{:S(2)}) collective-permute-start(bf16[4,1,256,128]{3,2,1,0:T(8,128)(2,1)} %pad_maximum_fusion), channel_id=1, source_target_pairs={{0,4},{4,8},{8,12},{1,5},{5,9},{9,13},{2,6},{6,10},{10,14},{3,7},{... | collective-permute-start | bytes 786440 | tf_op jit(solution)/shard_map/ppermute | solution.py:12
  27.3 0.7 pad_maximum_fusion.1
  28.0 1.3 collective-permute-start.11
  29.3 1.3 collective-permute-start.2
  30.7 5.9 %collective-permute-done.2.below = bf16[4,1,64,128]{3,2,1,0:T(8,128)(2,1)S(1)} collective-permute-done((bf16[4,1,64,128]{3,2,1,0:T(8,128)(2,1)S(1)}, bf16[4,1,64,128]{3,2,1,0:T(8,128)(2,1)S(1)}, u32[]{:S(2)}, u32[]{:S(2)}) %collective-permute-start.2) | collective-permute-done | bytes 65568 | tf_op jit(solution)/shard_map/ppermute | solution.py:12
  36.7 2.0 %shard_map.67 = (f32[8,64,128]{2,1,0:T(8,128)S(1)}, bf16[8,64,128]{2,1,0:T(8,128)(2,1)S(1)}, bf16[8,64,128]{2,1,0:T(8,128)(2,1)S(1)}, bf16[8,64,128]{2,1,0:T(8,128)(2,1)S(1)}) custom-call(s32[2]{0:T(128)S(1)} %pad_add_fusion.place, bf16[2,4,64,128]{3,2,1,0:T(8,128)(2,1)S(1)} %copy-done.1, bf16[2,4,64,128]{3,2,1,0:T(8,128)(2,1)S(1)} %collective-permute-done.late, ...), custom_call_target="tpu_custom_call" | custom-call | tf_op jit(solution)/shard_map/pallas_call | solution.py:22
  38.7 1.8 %collective-permute-start.4 = (bf16[8,64,128]{2,1,0:T(8,128)(2,1)S(1)}, bf16[8,64,128]{2,1,0:T(8,128)(2,1)}, u32[]{:S(2)}, u32[]{:S(2)}) collective-permute-start(bf16[8,64,128]{2,1,0:T(8,128)(2,1)S(1)} %get-tuple-element.16), channel_id=1, source_target_pairs={{0,2},{1,3},{2,0},{3,1},{4,6},{5,7},{6,4},{7,5},{8,10},{9,11},{10,... | collective-permute-start | bytes 393224 | tf_op jit(solution)/shard_map/ppermute | solution.py:172
  40.6 0.8 collective-permute-start.5
  41.4 2.9 %copy.11 = bf16[3,64,3,3,256]{4,3,2,1,0:T(4,128)(2,1)} copy(bf16[3,64,3,3,256]{4,1,0,3,2:T(8,128)(2,1)} %bitcast.41) | data formatting | bytes 1769472 | tf_op jit(solution)/shard_map/transpose | solution.py:243
  44.3 2.7 %reshape.36.weight = bf16[192,2304]{1,0:T(8,128)(2,1)S(1)} reshape(bf16[3,64,3,3,256]{4,3,2,1,0:T(4,128)(2,1)} %copy.11) | data formatting | bytes 1769472 | tf_op jit(solution)/shard_map/reshape | solution.py:243
  47.1 3.1 %shard_map.68 = (bf16[24,256,128]{2,1,0:T(8,128)(2,1)}, f32[8,64,128]{2,1,0:T(8,128)S(1)}, bf16[8,64,128]{2,1,0:T(8,128)(2,1)S(1)}) custom-call(s32[2]{0:T(128)S(1)} %pad_add_fusion.place, bf16[2,4,256,128]{3,2,1,0:T(8,128)(2,1)S(1)} %constant_dynamic-update-slice_fusion.own, bf16[2,4,256,128]{3,2,1,0:T(8,128)(2,1)S(1)} %collective-permute-done.9.early, ...), custom_call_target="tpu_custom_call" | custom-call | tf_op jit(solution)/shard_map/pallas_call | solution.py:22
  50.2 0.7 collective-permute-start.20
  50.9 1.8 %collective-permute-start.19 = (bf16[8,64,128]{2,1,0:T(8,128)(2,1)S(1)}, bf16[8,64,128]{2,1,0:T(8,128)(2,1)S(1)}, u32[]{:S(2)}, u32[]{:S(2)}) collective-permute-start(bf16[8,64,128]{2,1,0:T(8,128)(2,1)S(1)} %get-tuple-element.23.a0), channel_id=1, source_target_pairs={{0,2},{1,3},{2,0},{3,1},{4,6},{5,7},{6,4},{7,5},{8,10},{9,11},{10,... | collective-permute-start | bytes 393224 | tf_op jit(solution)/shard_map/ppermute | solution.py:172
  52.6 0.8 collective-permute-start.18
  53.4 1.2 multiply_convert_fusion.gradient
  54.6 1.4 copy-done
  56.0 2.3 %shard_map.71 = bf16[4,27,16,256]{3,2,1,0:T(8,128)(2,1)S(1)} custom-call(s32[2]{0:T(128)S(1)} %pad_add_fusion.place, bf16[24,256,128]{2,1,0:T(8,128)(2,1)S(1)} %copy-done, bf16[8,64,128]{2,1,0:T(8,128)(2,1)S(1)} %multiply_convert_fusion.gradient), custom_call_target="tpu_custom_call" | custom-call | tf_op jit(solution)/shard_map/pallas_call | solution.py:22
  58.3 1.1 collective-permute-done.18.a1
  59.4 2.5 %shard_map.70 = bf16[4,27,16,256]{3,2,1,0:T(8,128)(2,1)S(1)} custom-call(s32[2]{0:T(128)S(1)} %pad_add_fusion.place, bf16[2,4,64,128]{3,2,1,0:T(8,128)(2,1)S(1)} %copy-done.1, bf16[2,4,64,128]{3,2,1,0:T(8,128)(2,1)S(1)} %collective-permute-done.late, bf16[4,1,64,128]{3,2,1,0:T(8,128)(2,1)S(1)} %collective-permute-done.1.above, ...), custom_call_target="tpu_custom_call" | custom-call | tf_op jit(solution)/shard_map/pallas_call | solution.py:22
  62.5 2.1 %collective-permute-done.21 = bf16[4,27,16,256]{3,2,1,0:T(8,128)(2,1)S(1)} collective-permute-done((bf16[4,27,16,256]{3,2,1,0:T(8,128)(2,1)S(1)}, bf16[4,27,16,256]{3,2,1,0:T(8,128)(2,1)S(1)}, u32[]{:S(2)}, u32[]{:S(2)}) %collective-permute-start.21) | collective-permute-done | bytes 884768 | tf_op jit(solution)/shard_map/ppermute | solution.py:195
  65.0 0.7 collective-permute-start.22
  65.7 2.1 %collective-permute-start.24 = (bf16[27,16,256]{2,1,0:T(8,128)(2,1)S(1)}, bf16[27,16,256]{2,1,0:T(8,128)(2,1)S(1)}, u32[]{:S(2)}, u32[]{:S(2)}) collective-permute-start(bf16[27,16,256]{2,1,0:T(8,128)(2,1)S(1)} %get-tuple-element.35), channel_id=1, source_target_pairs={{0,12},{4,0},{8,4},{12,8},{1,13},{5,1},{9,5},{13,9},{2,14},{6,2},{... | collective-permute-start | bytes 663560 | tf_op jit(solution)/shard_map/ppermute | solution.py:172
  68.0 9.7 %collective-permute-done.22 = bf16[27,16,256]{2,1,0:T(8,128)(2,1)S(1)} collective-permute-done((bf16[27,16,256]{2,1,0:T(8,128)(2,1)S(1)}, bf16[27,16,256]{2,1,0:T(8,128)(2,1)S(1)}, u32[]{:S(2)}, u32[]{:S(2)}) %collective-permute-start.22) | collective-permute-done | bytes 221216 | tf_op jit(solution)/shard_map/ppermute | solution.py:172
  77.9 6.4 %collective-permute-start.25 = (bf16[27,8,256]{2,1,0:T(8,128)(2,1)S(1)}, bf16[27,8,256]{2,1,0:T(8,128)(2,1)S(1)}, u32[]{:S(2)}, u32[]{:S(2)}) collective-permute-start(bf16[27,8,256]{2,1,0:T(8,128)(2,1)S(1)} %select_convert_fusion), channel_id=1, source_target_pairs={{0,32},{16,48},{32,0},{48,16},{64,96},{80,112},{96,64},{112,80},{1... | collective-permute-start | bytes 331784 | tf_op jit(solution)/shard_map/ppermute | solution.py:195
  84.3 2.1 %collective-permute-done.25 = bf16[27,8,256]{2,1,0:T(8,128)(2,1)S(1)} collective-permute-done((bf16[27,8,256]{2,1,0:T(8,128)(2,1)S(1)}, bf16[27,8,256]{2,1,0:T(8,128)(2,1)S(1)}, u32[]{:S(2)}, u32[]{:S(2)}) %collective-permute-start.25) | collective-permute-done | bytes 110624 | tf_op jit(solution)/shard_map/ppermute | solution.py:195
  86.5 4.4 %collective-permute-start.26 = (bf16[27,8,128]{2,1,0:T(8,128)(2,1)S(1)}, bf16[27,8,128]{2,1,0:T(8,128)(2,1)S(1)}, u32[]{:S(2)}, u32[]{:S(2)}) collective-permute-start(bf16[27,8,128]{2,1,0:T(8,128)(2,1)S(1)} %select_convert_fusion.1), channel_id=1, source_target_pairs={{0,64},{16,80},{32,96},{48,112},{64,0},{80,16},{96,32},{112,48},{1... | collective-permute-start | bytes 165896 | tf_op jit(solution)/shard_map/ppermute | solution.py:195
  90.9 1.5 collective-permute-done.26
  92.5 4.8 %collective-permute-start.27 = (bf16[27,8,128]{2,1,0:T(8,128)(2,1)S(1)}, bf16[27,8,128]{2,1,0:T(8,128)(2,1)S(1)}, u32[]{:S(2)}, u32[]{:S(2)}) collective-permute-start(bf16[27,8,128]{2,1,0:T(8,128)(2,1)S(1)} %add_convert_fusion.2), channel_id=1, source_target_pairs={{0,128},{16,144},{32,160},{48,176},{64,192},{80,208},{96,224},{112... | collective-permute-start | bytes 165896 | tf_op jit(solution)/shard_map/ppermute | solution.py:195
  97.3 2.2 %collective-permute-done.27 = bf16[27,8,128]{2,1,0:T(8,128)(2,1)S(1)} collective-permute-done((bf16[27,8,128]{2,1,0:T(8,128)(2,1)S(1)}, bf16[27,8,128]{2,1,0:T(8,128)(2,1)S(1)}, u32[]{:S(2)}, u32[]{:S(2)}) %collective-permute-start.27) | collective-permute-done | bytes 55328 | tf_op jit(solution)/shard_map/ppermute | solution.py:195
  99.6 2.7 %collective-permute-start.28 = (bf16[27,8,128]{2,1,0:T(8,128)(2,1)S(1)}, bf16[27,8,128]{2,1,0:T(8,128)(2,1)S(1)}, u32[]{:S(2)}, u32[]{:S(2)}) collective-permute-start(bf16[27,8,128]{2,1,0:T(8,128)(2,1)S(1)} %add_convert_fusion.1), channel_id=1, source_target_pairs={{0,64},{16,80},{32,96},{48,112},{64,0},{80,16},{96,32},{112,48},{1... | collective-permute-start | bytes 165896 | tf_op jit(solution)/shard_map/ppermute | solution.py:195
  102.3 2.1 %collective-permute-done.28 = bf16[27,8,128]{2,1,0:T(8,128)(2,1)S(1)} collective-permute-done((bf16[27,8,128]{2,1,0:T(8,128)(2,1)S(1)}, bf16[27,8,128]{2,1,0:T(8,128)(2,1)S(1)}, u32[]{:S(2)}, u32[]{:S(2)}) %collective-permute-start.28) | collective-permute-done | bytes 55328 | tf_op jit(solution)/shard_map/ppermute | solution.py:195
  104.6 1.0 collective-permute-start.29
  105.6 7.9 %collective-permute-start.12 = (bf16[2,4,64,128]{3,2,1,0:T(8,128)(2,1)S(1)}, bf16[2,4,64,128]{3,2,1,0:T(8,128)(2,1)S(1)}, u32[]{:S(2)}, u32[]{:S(2)}) collective-permute-start(bf16[2,4,64,128]{3,2,1,0:T(8,128)(2,1)S(1)} %bitcast.38), channel_id=1, source_target_pairs={{16,0},{32,16},{48,32},{64,48},{80,64},{96,80},{112,96},{128,112},... | collective-permute-start | bytes 393224 | tf_op jit(solution)/shard_map/ppermute | solution.py:12
  113.5 2.6 %collective-permute-start.30 = (bf16[864,128]{1,0:T(8,128)(2,1)S(1)}, bf16[864,128]{1,0:T(8,128)(2,1)S(1)}, u32[]{:S(2)}, u32[]{:S(2)}) collective-permute-start(bf16[864,128]{1,0:T(8,128)(2,1)S(1)} %pad_maximum_fusion.2), channel_id=1, source_target_pairs={{0,12},{4,0},{8,4},{12,8},{1,13},{5,1},{9,5},{13,9},{2,14},{6,2},{... | collective-permute-start | bytes 663560 | tf_op jit(solution)/shard_map/ppermute | solution.py:172
  116.2 1.3 collective-permute-start.31
  117.4 2.5 %collective-permute-done.30 = bf16[864,128]{1,0:T(8,128)(2,1)S(1)} collective-permute-done((bf16[864,128]{1,0:T(8,128)(2,1)S(1)}, bf16[864,128]{1,0:T(8,128)(2,1)S(1)}, u32[]{:S(2)}, u32[]{:S(2)}) %collective-permute-start.30) | collective-permute-done | bytes 221216 | tf_op jit(solution)/shard_map/ppermute | solution.py:172
  120.0 6.9 %collective-permute-done.31 = bf16[864,128]{1,0:T(8,128)(2,1)S(1)} collective-permute-done((bf16[864,128]{1,0:T(8,128)(2,1)S(1)}, bf16[864,128]{1,0:T(8,128)(2,1)S(1)}, u32[]{:S(2)}, u32[]{:S(2)}) %collective-permute-start.31) | collective-permute-done | bytes 221216 | tf_op jit(solution)/shard_map/ppermute | solution.py:172
  127.5 3.3 %collective-permute-start.33 = (bf16[1728,256]{1,0:T(8,128)(2,1)S(1)}, bf16[1728,256]{1,0:T(8,128)(2,1)}, u32[]{:S(2)}, u32[]{:S(2)}) collective-permute-start(bf16[1728,256]{1,0:T(8,128)(2,1)S(1)} %reshape.40), channel_id=1, source_target_pairs={{0,16},{16,0},{32,48},{48,32},{64,80},{80,64},{96,112},{112,96},{1... | collective-permute-start | bytes 2654216 | tf_op jit(solution)/shard_map/ppermute | solution.py:195
  130.9 1.3 collective-permute-start.13
  132.2 1.3 collective-permute-start.14
  133.5 0.6 copy.12.weight
  134.1 3.7 %collective-permute-done.14.below = bf16[4,1,64,128]{3,2,1,0:T(8,128)(2,1)S(1)} collective-permute-done((bf16[4,1,64,128]{3,2,1,0:T(8,128)(2,1)S(1)}, bf16[4,1,64,128]{3,2,1,0:T(8,128)(2,1)S(1)}, u32[]{:S(2)}, u32[]{:S(2)}) %collective-permute-start.14) | collective-permute-done | bytes 65568 | tf_op jit(solution)/shard_map/ppermute | solution.py:12
  137.8 2.0 %shard_map.69 = (f32[8,64,128]{2,1,0:T(8,128)S(1)}, bf16[8,64,128]{2,1,0:T(8,128)(2,1)S(1)}, bf16[8,64,128]{2,1,0:T(8,128)(2,1)S(1)}, bf16[8,64,128]{2,1,0:T(8,128)(2,1)S(1)}) custom-call(s32[2]{0:T(128)S(1)} %pad_add_fusion.place, bf16[2,4,64,128]{3,2,1,0:T(8,128)(2,1)S(1)} %bitcast.40, bf16[2,4,64,128]{3,2,1,0:T(8,128)(2,1)S(1)} %collective-permute-done.12.late, ...), custom_call_target="tpu_custom_call" | custom-call | tf_op jit(solution)/shard_map/pallas_call | solution.py:22
  140.3 2.1 %collective-permute-start.16 = (bf16[8,64,128]{2,1,0:T(8,128)(2,1)S(1)}, bf16[8,64,128]{2,1,0:T(8,128)(2,1)S(1)}, u32[]{:S(2)}, u32[]{:S(2)}) collective-permute-start(bf16[8,64,128]{2,1,0:T(8,128)(2,1)S(1)} %get-tuple-element.21), channel_id=1, source_target_pairs={{0,2},{1,3},{2,0},{3,1},{4,6},{5,7},{6,4},{7,5},{8,10},{9,11},{10,... | collective-permute-start | bytes 393224 | tf_op jit(solution)/shard_map/ppermute | solution.py:172
  142.8 2.6 %collective-permute-done.15 = bf16[8,64,128]{2,1,0:T(8,128)(2,1)S(1)} collective-permute-done((bf16[8,64,128]{2,1,0:T(8,128)(2,1)S(1)}, bf16[8,64,128]{2,1,0:T(8,128)(2,1)S(1)}, u32[]{:S(2)}, u32[]{:S(2)}) %collective-permute-start.15) | collective-permute-done | bytes 131104 | tf_op jit(solution)/shard_map/ppermute | solution.py:172
  145.4 2.6 %collective-permute-done.16 = bf16[8,64,128]{2,1,0:T(8,128)(2,1)S(1)} collective-permute-done((bf16[8,64,128]{2,1,0:T(8,128)(2,1)S(1)}, bf16[8,64,128]{2,1,0:T(8,128)(2,1)S(1)}, u32[]{:S(2)}, u32[]{:S(2)}) %collective-permute-start.16) | collective-permute-done | bytes 131104 | tf_op jit(solution)/shard_map/ppermute | solution.py:172
  147.9 0.6 collective-permute-done.17
  148.5 0.7 add_convert_fusion
  149.2 1.3 broadcast_select_fusion.2
  150.8 2.0 %fusion.4 = (f32[1728,256]{1,0:T(8,128)}, f32[1728,256]{1,0:T(8,128)}) fusion(f32[3456,256]{1,0:T(8,128)S(1)} %maximum_convert_fusion), kind=kLoop, calls=%fused_computation.45 | loop fusion | bytes 7077888 | tf_op jit(solution)/shard_map/slice | solution.py:223
  152.8 2.6 %squeeze.14 = f32[64,3,3,3,256]{4,3,2,1,0:T(4,128)S(1)} reshape(f32[1728,256]{1,0:T(8,128)} %get-tuple-element.30) | data formatting | bytes 3538944 | tf_op jit(solution)/shard_map/squeeze | solution.py:223
  155.5 1.5 copy.15
  157.0 2.6 %squeeze.13 = f32[64,3,3,3,256]{4,3,2,1,0:T(4,128)S(1)} reshape(f32[1728,256]{1,0:T(8,128)} %get-tuple-element.31) | data formatting | bytes 3538944 | tf_op jit(solution)/shard_map/squeeze | solution.py:223
  159.7 1.5 copy.14
  (69 shorter events, 4.3 us)
Async XLA Ops:
  0.6 13.2 %collective-permute-start.7 = (bf16[2,4,64,128]{3,2,1,0:T(8,128)(2,1)}, bf16[2,4,64,128]{3,2,1,0:T(8,128)(2,1)S(1)}, u32[]{:S(2)}, u32[]{:S(2)}) collective-permute-start(bf16[2,4,64,128]{3,2,1,0:T(8,128)(2,1)} %param.4), channel_id=1, source_target_pairs={{0,2},{1,3},{2,0},{3,1},{4,6},{5,7},{6,4},{7,5},{8,10},{9,11},{10,... | collective-permute-start | bytes 393224 | tf_op jit(solution)/shard_map/ppermute | solution.py:172
  4.5 9.3 %collective-permute-start.6 = (bf16[2,4,64,128]{3,2,1,0:T(8,128)(2,1)}, bf16[2,4,64,128]{3,2,1,0:T(8,128)(2,1)S(1)}, u32[]{:S(2)}, u32[]{:S(2)}) collective-permute-start(bf16[2,4,64,128]{3,2,1,0:T(8,128)(2,1)} %param.4), channel_id=1, source_target_pairs={{0,1},{1,2},{2,3},{3,0},{4,5},{5,6},{6,7},{7,4},{8,9},{9,10},{10,1... | collective-permute-start | bytes 393224 | tf_op jit(solution)/shard_map/ppermute | solution.py:172
  4.9 9.0 %collective-permute-start.8 = (bf16[2,4,64,128]{3,2,1,0:T(8,128)(2,1)}, bf16[2,4,64,128]{3,2,1,0:T(8,128)(2,1)S(1)}, u32[]{:S(2)}, u32[]{:S(2)}) collective-permute-start(bf16[2,4,64,128]{3,2,1,0:T(8,128)(2,1)} %param.4), channel_id=1, source_target_pairs={{0,3},{1,0},{2,1},{3,2},{4,7},{5,4},{6,5},{7,6},{8,11},{9,8},{10,9... | collective-permute-start | bytes 393224 | tf_op jit(solution)/shard_map/ppermute | solution.py:172
  7.1 10.2 %collective-permute-start = (bf16[2,4,64,128]{3,2,1,0:T(8,128)(2,1)}, bf16[2,4,64,128]{3,2,1,0:T(8,128)(2,1)S(1)}, u32[]{:S(2)}, u32[]{:S(2)}) collective-permute-start(bf16[2,4,64,128]{3,2,1,0:T(8,128)(2,1)} %own.3), channel_id=1, source_target_pairs={{16,0},{32,16},{48,32},{64,48},{80,64},{96,80},{112,96},{128,112},... | collective-permute-start | bytes 393224 | tf_op jit(solution)/shard_map/ppermute | solution.py:12
  13.8 22.9 %copy-start.1 = (bf16[2,4,64,128]{3,2,1,0:T(8,128)(2,1)S(1)}, bf16[2,4,64,128]{3,2,1,0:T(8,128)(2,1)}, u32[]{:S(2)}) copy-start(bf16[2,4,64,128]{3,2,1,0:T(8,128)(2,1)} %own.3) | copy-start | bytes 393220
  13.9 9.6 %collective-permute-start.9 = (bf16[2,4,256,128]{3,2,1,0:T(8,128)(2,1)S(1)}, bf16[2,4,256,128]{3,2,1,0:T(8,128)(2,1)S(1)}, u32[]{:S(2)}, u32[]{:S(2)}) collective-permute-start(bf16[2,4,256,128]{3,2,1,0:T(8,128)(2,1)S(1)} %constant_dynamic-update-slice_fusion.own), channel_id=1, source_target_pairs={{0,16},{16,32},{32,48},{48,64},{64,80},{80,96},{96,112},{112,128},... | collective-permute-start | bytes 1572872 | tf_op jit(solution)/shard_map/ppermute | solution.py:12
  17.4 13.3 %collective-permute-start.1 = (bf16[4,1,64,128]{3,2,1,0:T(8,128)(2,1)S(1)}, bf16[4,1,64,128]{3,2,1,0:T(8,128)(2,1)S(1)}, u32[]{:S(2)}, u32[]{:S(2)}) collective-permute-start(bf16[4,1,64,128]{3,2,1,0:T(8,128)(2,1)S(1)} %pad_maximum_fusion.3), channel_id=1, source_target_pairs={{0,4},{4,8},{8,12},{1,5},{5,9},{9,13},{2,6},{6,10},{10,14},{3,7},{... | collective-permute-start | bytes 196616 | tf_op jit(solution)/shard_map/ppermute | solution.py:12
  24.2 22.8 %collective-permute-start.10 = (bf16[4,1,256,128]{3,2,1,0:T(8,128)(2,1)}, bf16[4,1,256,128]{3,2,1,0:T(8,128)(2,1)S(1)}, u32[]{:S(2)}, u32[]{:S(2)}) collective-permute-start(bf16[4,1,256,128]{3,2,1,0:T(8,128)(2,1)} %pad_maximum_fusion), channel_id=1, source_target_pairs={{0,4},{4,8},{8,12},{1,5},{5,9},{9,13},{2,6},{6,10},{10,14},{3,7},{... | collective-permute-start | bytes 786440 | tf_op jit(solution)/shard_map/ppermute | solution.py:12
  28.0 19.0 %collective-permute-start.11 = (bf16[4,1,256,128]{3,2,1,0:T(8,128)(2,1)}, bf16[4,1,256,128]{3,2,1,0:T(8,128)(2,1)S(1)}, u32[]{:S(2)}, u32[]{:S(2)}) collective-permute-start(bf16[4,1,256,128]{3,2,1,0:T(8,128)(2,1)} %pad_maximum_fusion.1), channel_id=1, source_target_pairs={{4,0},{8,4},{12,8},{5,1},{9,5},{13,9},{6,2},{10,6},{14,10},{7,3},{... | collective-permute-start | bytes 786440 | tf_op jit(solution)/shard_map/ppermute | solution.py:12
  29.3 7.3 %collective-permute-start.2 = (bf16[4,1,64,128]{3,2,1,0:T(8,128)(2,1)S(1)}, bf16[4,1,64,128]{3,2,1,0:T(8,128)(2,1)S(1)}, u32[]{:S(2)}, u32[]{:S(2)}) collective-permute-start(bf16[4,1,64,128]{3,2,1,0:T(8,128)(2,1)S(1)} %pad_maximum_fusion.4), channel_id=1, source_target_pairs={{4,0},{8,4},{12,8},{5,1},{9,5},{13,9},{6,2},{10,6},{14,10},{7,3},{... | collective-permute-start | bytes 196616 | tf_op jit(solution)/shard_map/ppermute | solution.py:12
  38.6 14.0 %collective-permute-start.3 = (bf16[8,64,128]{2,1,0:T(8,128)(2,1)S(1)}, bf16[8,64,128]{2,1,0:T(8,128)(2,1)}, u32[]{:S(2)}, u32[]{:S(2)}) collective-permute-start(bf16[8,64,128]{2,1,0:T(8,128)(2,1)S(1)} %get-tuple-element.15), channel_id=1, source_target_pairs={{0,1},{1,2},{2,3},{3,0},{4,5},{5,6},{6,7},{7,4},{8,9},{9,10},{10,1... | collective-permute-start | bytes 393224 | tf_op jit(solution)/shard_map/ppermute | solution.py:172
  38.7 14.7 %collective-permute-start.4 = (bf16[8,64,128]{2,1,0:T(8,128)(2,1)S(1)}, bf16[8,64,128]{2,1,0:T(8,128)(2,1)}, u32[]{:S(2)}, u32[]{:S(2)}) collective-permute-start(bf16[8,64,128]{2,1,0:T(8,128)(2,1)S(1)} %get-tuple-element.16), channel_id=1, source_target_pairs={{0,2},{1,3},{2,0},{3,1},{4,6},{5,7},{6,4},{7,5},{8,10},{9,11},{10,... | collective-permute-start | bytes 393224 | tf_op jit(solution)/shard_map/ppermute | solution.py:172
  40.6 12.8 %collective-permute-start.5 = (bf16[8,64,128]{2,1,0:T(8,128)(2,1)S(1)}, bf16[8,64,128]{2,1,0:T(8,128)(2,1)}, u32[]{:S(2)}, u32[]{:S(2)}) collective-permute-start(bf16[8,64,128]{2,1,0:T(8,128)(2,1)S(1)} %get-tuple-element.17), channel_id=1, source_target_pairs={{0,3},{1,0},{2,1},{3,2},{4,7},{5,4},{6,5},{7,6},{8,11},{9,8},{10,9... | collective-permute-start | bytes 393224 | tf_op jit(solution)/shard_map/ppermute | solution.py:172
  50.2 8.1 %collective-permute-start.20 = (bf16[8,64,128]{2,1,0:T(8,128)(2,1)S(1)}, bf16[8,64,128]{2,1,0:T(8,128)(2,1)S(1)}, u32[]{:S(2)}, u32[]{:S(2)}) collective-permute-start(bf16[8,64,128]{2,1,0:T(8,128)(2,1)S(1)} %get-tuple-element.23.a0), channel_id=1, source_target_pairs={{0,3},{1,0},{2,1},{3,2},{4,7},{5,4},{6,5},{7,6},{8,11},{9,8},{10,9... | collective-permute-start | bytes 393224 | tf_op jit(solution)/shard_map/ppermute | solution.py:172
  50.9 7.4 %collective-permute-start.19 = (bf16[8,64,128]{2,1,0:T(8,128)(2,1)S(1)}, bf16[8,64,128]{2,1,0:T(8,128)(2,1)S(1)}, u32[]{:S(2)}, u32[]{:S(2)}) collective-permute-start(bf16[8,64,128]{2,1,0:T(8,128)(2,1)S(1)} %get-tuple-element.23.a0), channel_id=1, source_target_pairs={{0,2},{1,3},{2,0},{3,1},{4,6},{5,7},{6,4},{7,5},{8,10},{9,11},{10,... | collective-permute-start | bytes 393224 | tf_op jit(solution)/shard_map/ppermute | solution.py:172
  52.6 6.8 %collective-permute-start.18 = (bf16[8,64,128]{2,1,0:T(8,128)(2,1)S(1)}, bf16[8,64,128]{2,1,0:T(8,128)(2,1)S(1)}, u32[]{:S(2)}, u32[]{:S(2)}) collective-permute-start(bf16[8,64,128]{2,1,0:T(8,128)(2,1)S(1)} %get-tuple-element.23.a0), channel_id=1, source_target_pairs={{0,1},{1,2},{2,3},{3,0},{4,5},{5,6},{6,7},{7,4},{8,9},{9,10},{10,1... | collective-permute-start | bytes 393224 | tf_op jit(solution)/shard_map/ppermute | solution.py:172
  54.6 1.4 copy-start
  62.0 2.5 %collective-permute-start.21 = (bf16[4,27,16,256]{3,2,1,0:T(8,128)(2,1)S(1)}, bf16[4,27,16,256]{3,2,1,0:T(8,128)(2,1)S(1)}, u32[]{:S(2)}, u32[]{:S(2)}) collective-permute-start(bf16[4,27,16,256]{3,2,1,0:T(8,128)(2,1)S(1)} %broadcast_select_fusion), channel_id=1, source_target_pairs={{0,16},{16,0},{32,48},{48,32},{64,80},{80,64},{96,112},{112,96},{1... | collective-permute-start | bytes 2654216 | tf_op jit(solution)/shard_map/ppermute | solution.py:195
  65.0 12.7 %collective-permute-start.22 = (bf16[27,16,256]{2,1,0:T(8,128)(2,1)S(1)}, bf16[27,16,256]{2,1,0:T(8,128)(2,1)S(1)}, u32[]{:S(2)}, u32[]{:S(2)}) collective-permute-start(bf16[27,16,256]{2,1,0:T(8,128)(2,1)S(1)} %get-tuple-element.34), channel_id=1, source_target_pairs={{0,4},{4,8},{8,12},{12,0},{1,5},{5,9},{9,13},{13,1},{2,6},{6,10},{... | collective-permute-start | bytes 663560 | tf_op jit(solution)/shard_map/ppermute | solution.py:172
  65.7 12.0 %collective-permute-start.24 = (bf16[27,16,256]{2,1,0:T(8,128)(2,1)S(1)}, bf16[27,16,256]{2,1,0:T(8,128)(2,1)S(1)}, u32[]{:S(2)}, u32[]{:S(2)}) collective-permute-start(bf16[27,16,256]{2,1,0:T(8,128)(2,1)S(1)} %get-tuple-element.35), channel_id=1, source_target_pairs={{0,12},{4,0},{8,4},{12,8},{1,13},{5,1},{9,5},{13,9},{2,14},{6,2},{... | collective-permute-start | bytes 663560 | tf_op jit(solution)/shard_map/ppermute | solution.py:172
  67.8 9.9 %collective-permute-start.23 = (bf16[27,16,256]{2,1,0:T(8,128)(2,1)S(1)}, bf16[27,16,256]{2,1,0:T(8,128)(2,1)S(1)}, u32[]{:S(2)}, u32[]{:S(2)}) collective-permute-start(bf16[27,16,256]{2,1,0:T(8,128)(2,1)S(1)} %get-tuple-element.36), channel_id=1, source_target_pairs={{0,8},{4,12},{8,0},{12,4},{1,9},{5,13},{9,1},{13,5},{2,10},{6,14},... | collective-permute-start | bytes 663560 | tf_op jit(solution)/shard_map/ppermute | solution.py:172
  77.9 8.6 %collective-permute-start.25 = (bf16[27,8,256]{2,1,0:T(8,128)(2,1)S(1)}, bf16[27,8,256]{2,1,0:T(8,128)(2,1)S(1)}, u32[]{:S(2)}, u32[]{:S(2)}) collective-permute-start(bf16[27,8,256]{2,1,0:T(8,128)(2,1)S(1)} %select_convert_fusion), channel_id=1, source_target_pairs={{0,32},{16,48},{32,0},{48,16},{64,96},{80,112},{96,64},{112,80},{1... | collective-permute-start | bytes 331784 | tf_op jit(solution)/shard_map/ppermute | solution.py:195
  86.5 6.0 %collective-permute-start.26 = (bf16[27,8,128]{2,1,0:T(8,128)(2,1)S(1)}, bf16[27,8,128]{2,1,0:T(8,128)(2,1)S(1)}, u32[]{:S(2)}, u32[]{:S(2)}) collective-permute-start(bf16[27,8,128]{2,1,0:T(8,128)(2,1)S(1)} %select_convert_fusion.1), channel_id=1, source_target_pairs={{0,64},{16,80},{32,96},{48,112},{64,0},{80,16},{96,32},{112,48},{1... | collective-permute-start | bytes 165896 | tf_op jit(solution)/shard_map/ppermute | solution.py:195
  92.5 7.0 %collective-permute-start.27 = (bf16[27,8,128]{2,1,0:T(8,128)(2,1)S(1)}, bf16[27,8,128]{2,1,0:T(8,128)(2,1)S(1)}, u32[]{:S(2)}, u32[]{:S(2)}) collective-permute-start(bf16[27,8,128]{2,1,0:T(8,128)(2,1)S(1)} %add_convert_fusion.2), channel_id=1, source_target_pairs={{0,128},{16,144},{32,160},{48,176},{64,192},{80,208},{96,224},{112... | collective-permute-start | bytes 165896 | tf_op jit(solution)/shard_map/ppermute | solution.py:195
  99.6 4.9 %collective-permute-start.28 = (bf16[27,8,128]{2,1,0:T(8,128)(2,1)S(1)}, bf16[27,8,128]{2,1,0:T(8,128)(2,1)S(1)}, u32[]{:S(2)}, u32[]{:S(2)}) collective-permute-start(bf16[27,8,128]{2,1,0:T(8,128)(2,1)S(1)} %add_convert_fusion.1), channel_id=1, source_target_pairs={{0,64},{16,80},{32,96},{48,112},{64,0},{80,16},{96,32},{112,48},{1... | collective-permute-start | bytes 165896 | tf_op jit(solution)/shard_map/ppermute | solution.py:195
  104.6 8.9 %collective-permute-start.29 = (bf16[432,128]{1,0:T(8,128)(2,1)S(1)}, bf16[432,128]{1,0:T(8,128)(2,1)S(1)}, u32[]{:S(2)}, u32[]{:S(2)}) collective-permute-start(bf16[432,128]{1,0:T(8,128)(2,1)S(1)} %reshape.39), channel_id=1, source_target_pairs={{0,32},{16,48},{32,0},{48,16},{64,96},{80,112},{96,64},{112,80},{1... | collective-permute-start | bytes 331784 | tf_op jit(solution)/shard_map/ppermute | solution.py:195
  105.6 25.3 %collective-permute-start.12 = (bf16[2,4,64,128]{3,2,1,0:T(8,128)(2,1)S(1)}, bf16[2,4,64,128]{3,2,1,0:T(8,128)(2,1)S(1)}, u32[]{:S(2)}, u32[]{:S(2)}) collective-permute-start(bf16[2,4,64,128]{3,2,1,0:T(8,128)(2,1)S(1)} %bitcast.38), channel_id=1, source_target_pairs={{16,0},{32,16},{48,32},{64,48},{80,64},{96,80},{112,96},{128,112},... | collective-permute-start | bytes 393224 | tf_op jit(solution)/shard_map/ppermute | solution.py:12
  113.5 6.5 %collective-permute-start.30 = (bf16[864,128]{1,0:T(8,128)(2,1)S(1)}, bf16[864,128]{1,0:T(8,128)(2,1)S(1)}, u32[]{:S(2)}, u32[]{:S(2)}) collective-permute-start(bf16[864,128]{1,0:T(8,128)(2,1)S(1)} %pad_maximum_fusion.2), channel_id=1, source_target_pairs={{0,12},{4,0},{8,4},{12,8},{1,13},{5,1},{9,5},{13,9},{2,14},{6,2},{... | collective-permute-start | bytes 663560 | tf_op jit(solution)/shard_map/ppermute | solution.py:172
  116.2 10.8 %collective-permute-start.32 = (bf16[864,128]{1,0:T(8,128)(2,1)S(1)}, bf16[864,128]{1,0:T(8,128)(2,1)S(1)}, u32[]{:S(2)}, u32[]{:S(2)}) collective-permute-start(bf16[864,128]{1,0:T(8,128)(2,1)S(1)} %pad_maximum_fusion.2), channel_id=1, source_target_pairs={{0,4},{4,8},{8,12},{12,0},{1,5},{5,9},{9,13},{13,1},{2,6},{6,10},{... | collective-permute-start | bytes 663560 | tf_op jit(solution)/shard_map/ppermute | solution.py:172
  116.2 10.7 %collective-permute-start.31 = (bf16[864,128]{1,0:T(8,128)(2,1)S(1)}, bf16[864,128]{1,0:T(8,128)(2,1)S(1)}, u32[]{:S(2)}, u32[]{:S(2)}) collective-permute-start(bf16[864,128]{1,0:T(8,128)(2,1)S(1)} %pad_maximum_fusion.2), channel_id=1, source_target_pairs={{0,8},{4,12},{8,0},{12,4},{1,9},{5,13},{9,1},{13,5},{2,10},{6,14},... | collective-permute-start | bytes 663560 | tf_op jit(solution)/shard_map/ppermute | solution.py:172
  127.1 6.3 %copy-start.2 = (bf16[64,3,3,3,256]{4,0,3,2,1:T(8,128)(2,1)S(1)}, bf16[64,3,3,3,256]{4,0,3,2,1:T(8,128)(2,1)}, u32[]{:S(2)}) copy-start(bf16[64,3,3,3,256]{4,0,3,2,1:T(8,128)(2,1)} %param.6) | copy-start | bytes 2654212
  127.5 21.7 %collective-permute-start.33 = (bf16[1728,256]{1,0:T(8,128)(2,1)S(1)}, bf16[1728,256]{1,0:T(8,128)(2,1)}, u32[]{:S(2)}, u32[]{:S(2)}) collective-permute-start(bf16[1728,256]{1,0:T(8,128)(2,1)S(1)} %reshape.40), channel_id=1, source_target_pairs={{0,16},{16,0},{32,48},{48,32},{64,80},{80,64},{96,112},{112,96},{1... | collective-permute-start | bytes 2654216 | tf_op jit(solution)/shard_map/ppermute | solution.py:195
  130.9 3.2 %collective-permute-start.13 = (bf16[4,1,64,128]{3,2,1,0:T(8,128)(2,1)S(1)}, bf16[4,1,64,128]{3,2,1,0:T(8,128)(2,1)S(1)}, u32[]{:S(2)}, u32[]{:S(2)}) collective-permute-start(bf16[4,1,64,128]{3,2,1,0:T(8,128)(2,1)S(1)} %pad_maximum_fusion.5), channel_id=1, source_target_pairs={{0,4},{4,8},{8,12},{1,5},{5,9},{9,13},{2,6},{6,10},{10,14},{3,7},{... | collective-permute-start | bytes 196616 | tf_op jit(solution)/shard_map/ppermute | solution.py:12
  132.2 5.6 %collective-permute-start.14 = (bf16[4,1,64,128]{3,2,1,0:T(8,128)(2,1)S(1)}, bf16[4,1,64,128]{3,2,1,0:T(8,128)(2,1)S(1)}, u32[]{:S(2)}, u32[]{:S(2)}) collective-permute-start(bf16[4,1,64,128]{3,2,1,0:T(8,128)(2,1)S(1)} %pad_maximum_fusion.6), channel_id=1, source_target_pairs={{4,0},{8,4},{12,8},{5,1},{9,5},{13,9},{6,2},{10,6},{14,10},{7,3},{... | collective-permute-start | bytes 196616 | tf_op jit(solution)/shard_map/ppermute | solution.py:12
  139.7 5.6 %collective-permute-start.15 = (bf16[8,64,128]{2,1,0:T(8,128)(2,1)S(1)}, bf16[8,64,128]{2,1,0:T(8,128)(2,1)S(1)}, u32[]{:S(2)}, u32[]{:S(2)}) collective-permute-start(bf16[8,64,128]{2,1,0:T(8,128)(2,1)S(1)} %get-tuple-element.20), channel_id=1, source_target_pairs={{0,1},{1,2},{2,3},{3,0},{4,5},{5,6},{6,7},{7,4},{8,9},{9,10},{10,1... | collective-permute-start | bytes 393224 | tf_op jit(solution)/shard_map/ppermute | solution.py:172
  140.3 7.6 %collective-permute-start.16 = (bf16[8,64,128]{2,1,0:T(8,128)(2,1)S(1)}, bf16[8,64,128]{2,1,0:T(8,128)(2,1)S(1)}, u32[]{:S(2)}, u32[]{:S(2)}) collective-permute-start(bf16[8,64,128]{2,1,0:T(8,128)(2,1)S(1)} %get-tuple-element.21), channel_id=1, source_target_pairs={{0,2},{1,3},{2,0},{3,1},{4,6},{5,7},{6,4},{7,5},{8,10},{9,11},{10,... | collective-permute-start | bytes 393224 | tf_op jit(solution)/shard_map/ppermute | solution.py:172
  142.4 6.1 %collective-permute-start.17 = (bf16[8,64,128]{2,1,0:T(8,128)(2,1)S(1)}, bf16[8,64,128]{2,1,0:T(8,128)(2,1)S(1)}, u32[]{:S(2)}, u32[]{:S(2)}) collective-permute-start(bf16[8,64,128]{2,1,0:T(8,128)(2,1)S(1)} %get-tuple-element.22), channel_id=1, source_target_pairs={{0,3},{1,0},{2,1},{3,2},{4,7},{5,4},{6,5},{7,6},{8,11},{9,8},{10,9... | collective-permute-start | bytes 393224 | tf_op jit(solution)/shard_map/ppermute | solution.py:172

commit v2 on v1

--- a/solution.py
+++ b/solution.py
@@ -17,16 +17,20 @@
 SPOTS = [(t, i) for t in range(2) for i in range(4)]
 
 
-def call(body, outs, scratch, place, *operands):
+def call(body, outs, scratch, place, *operands, after=()):
     vmem = pl.BlockSpec(memory_space=pltpu.VMEM)
+    used = 1 + len(operands)
+    rest = used + len(after)
     return pl.pallas_call(
-        body,
+        lambda *refs: body(*refs[:used], *refs[rest:]),
         out_shape=outs,
-        in_specs=[pl.BlockSpec(memory_space=pltpu.SMEM)] + [vmem] * len(operands),
+        in_specs=[pl.BlockSpec(memory_space=pltpu.SMEM)]
+        + [vmem] * len(operands)
+        + [pl.BlockSpec(memory_space=pl.ANY)] * len(after),
         out_specs=[vmem] * len(outs),
         scratch_shapes=scratch,
         compiler_params=pltpu.CompilerParams(vmem_limit_bytes=VMEM_LIMIT),
-    )(place, *operands)
+    )(place, *operands, *after)
 
 
 def lanes_moved(cell):
@@ -37,8 +41,10 @@
     return ahead.astype(jnp.bfloat16), cell, behind.astype(jnp.bfloat16)
 
 
-def forward_body(place, own, early, above, below, weight, panel, pre, act, wide):
+def forward_body(place, own, early, above, below, weight, panel, pre, act, wide, flat):
     me = place[0]
+    for n in range(9):
+        flat[:, n * 256 : n * 256 + 256] = weight[n]
     for f in range(4):
         for r in range(6):
             if r == 0:
@@ -55,7 +61,7 @@
             wide[n * 256 : n * 256 + 256, p * 128 : p * 128 + 128] = panel[(t + a) * 6 + i + b]
     for t in range(2):
         sums = jnp.dot(
-            weight[...], wide[:, t * 512 : t * 512 + 512], preferred_element_type=jnp.float32
+            flat[...], wide[:, t * 512 : t * 512 + 512], preferred_element_type=jnp.float32
         )
         lane = lax.broadcasted_iota(jnp.int32, (64, 128), 1)
         for i in range(4):
@@ -89,7 +95,9 @@
 def transposed_body(place, own, late, above, below, weight, mine, one, two, three, wide, full):
     me = place[0]
     spread(own, late, above, below, wide)
-    full[...] = jnp.dot(weight[...], wide[...], preferred_element_type=jnp.float32)
+    full[...] = lax.dot_general(
+        weight[...], wide[...], (((0,), (0,)), ((), ())), preferred_element_type=jnp.float32
+    )
     for k, out in enumerate((mine, one, two, three)):
         at = pl.multiple_of(((me + k) % 4) * 64, 64)
         for p in range(8):
@@ -134,12 +142,12 @@
     return jax.ShapeDtypeStruct(shape, dtype)
 
 
-def forward(place, own, early, above, below, weight):
+def forward(place, own, early, above, below, weight, after):
     return call(
         forward_body,
         [shaped((24, 256, 128), jnp.bfloat16), shaped((8, 64, 128), jnp.float32), shaped((8, 64, 128), jnp.bfloat16)],
-        [pltpu.VMEM((2304, 1024), jnp.bfloat16)],
-        place, own, early, above, below, weight,
+        [pltpu.VMEM((2304, 1024), jnp.bfloat16), pltpu.VMEM((192, 2304), jnp.bfloat16)],
+        place, own, early, above, below, weight, after=after,
     )
 
 
@@ -167,60 +175,104 @@
     )[0]
 
 
+def quarters_body(place, own, one, two, three, mine, first, second, third, sums):
+    z = place[2]
+    total = own[...].astype(jnp.float32)
+    for part in (one, two, three):
+        total = total + part[...].astype(jnp.float32)
+    for q in range(4):
+        o, c = (q // 2) * 8, (q % 2) * 128
+        sums[q] = total[:, o : o + 8, c : c + 128]
+    for k, out in enumerate((mine, first, second, third)):
+        out[...] = sums[(z + k) % 4].astype(out.dtype)
+
+
+def quarters(place, pieces, after):
+    small = [shaped((27, 8, 128), jnp.float32)] + [shaped((27, 8, 128), jnp.bfloat16)] * 3
+    return call(
+        quarters_body, small, [pltpu.VMEM((4, 27, 8, 128), jnp.float32)], place, *pieces, after=after
+    )
+
+
+def rejoined_body(place, own, one, two, three, out, parts):
+    z = place[2]
+    for k, part in enumerate((own, one, two, three)):
+        parts[(z + 4 - k) % 4] = part[...]
+    for q in range(4):
+        o, c = (q // 2) * 8, (q % 2) * 128
+        out[:, o : o + 8, c : c + 128] = parts[q]
+
+
+def rejoined(place, pieces, after):
+    return call(
+        rejoined_body, [shaped((27, 16, 256), jnp.bfloat16)],
+        [pltpu.VMEM((4, 27, 8, 128), jnp.bfloat16)], place, *pieces, after=after,
+    )[0]
+
+
+def stacked_body(place, own, one, two, three, out):
+    height = place[1]
+    for k, part in enumerate((own, one, two, three)):
+        at = pl.multiple_of(((height + 4 - k) % 4) * 16, 16)
+        out[:, pl.ds(at, 16), :] = part[...]
+
+
+def stacked(place, pieces):
+    return call(stacked_body, [shaped((27, 64, 256), jnp.bfloat16)], [], place, *pieces)[0]
+
+
 def rotated(block, axis, distance):
     count = lax.axis_size(axis)
     return lax.ppermute(block, axis, [(i, (i + distance) % count) for i in range(count)])
 
 
-def in_order(own, others, axis):
-    me = lax.axis_index(axis)
-    count = len(others) + 1
-    pieces = [others[count - 2 - i] for i in range(count - 1)] + [own]
-    ring = jnp.stack(pieces + pieces[:-1], 0)
-    return lax.dynamic_slice_in_dim(ring, (count - 1 - me) % count, count, 0)
-
-
 def all_rotated(block, axis):
     return [rotated(block, axis, k) for k in range(1, lax.axis_size(axis))]
 
 
+def sent_on(pieces, axis):
+    return [pieces[0]] + [rotated(pieces[k], axis, k) for k in range(1, len(pieces))]
+
+
 def exchanged(pieces, axis):
-    total = pieces[0].astype(jnp.float32)
-    for k in range(1, len(pieces)):
-        total = total + rotated(pieces[k], axis, k).astype(jnp.float32)
-    return total
+    return sum(part.astype(jnp.float32) for part in sent_on(pieces, axis))
 
 
 def swapped(block, distance):
     return lax.ppermute(block, "tm", [(i, i ^ distance) for i in range(lax.axis_size("tm"))])
 
 
-def sum_of_halves(low, high, bit, distance):
-    mine = jnp.where(bit == 1, high, low)
-    theirs = jnp.where(bit == 1, low, high)
-    other = swapped(theirs.astype(jnp.bfloat16), distance)
-    return mine.astype(jnp.float32) + other.astype(jnp.float32)
-
-
-def halves_joined(block, bit, distance, dim=0):
-    other = swapped(block, distance)
-    return jnp.concatenate([jnp.where(bit == 1, other, block), jnp.where(bit == 1, block, other)], dim)
-
-
-def summed_filters(part_one, part_two):
-    spot = lax.axis_index("tm")
-    core, z_one, z_two = spot % 2, (spot // 2) % 2, (spot // 4) % 2
-    total = sum_of_halves(part_one, part_two, core, 1)
-    total = exchanged([total[0]] + [total[k].astype(jnp.bfloat16) for k in range(1, 4)], "height")
-    total = sum_of_halves(total[:, :8], total[:, 8:], z_one, 2)
-    total = sum_of_halves(total[..., :128], total[..., 128:], z_two, 4)
+def quad_rotated(block, distance):
+    route = [(i, i - i % 8 + (i + 2 * distance) % 8) for i in range(lax.axis_size("tm"))]
+    return lax.ppermute(block, "tm", route)
+
+
+def summed_pair(part_one, part_two, core):
+    mine = jnp.where(core == 1, part_two, part_one)
+    theirs = jnp.where(core == 1, part_one, part_two)
+    total = mine.astype(jnp.float32) + swapped(theirs, 1).astype(jnp.float32)
+    return [total[0]] + [total[k].astype(jnp.bfloat16) for k in range(1, 4)]
+
+
+def rest_of_sum(place, pieces, gradient_pieces, core):
+    mine, *others = quarters(place, sent_on(pieces, "height"), [gradient_pieces[0]])
+    gradient = exchanged(gradient_pieces, "chan")
+    total = mine
+    for k, part in enumerate(others):
+        total = total + quad_rotated(part, k + 1).astype(jnp.float32)
     total = total.astype(jnp.bfloat16)
+    gradient = gradient.reshape(2, 4, 64, 128).astype(jnp.bfloat16)
     total = (total.astype(jnp.float32) + swapped(total, 8).astype(jnp.float32)).astype(jnp.bfloat16)
-    total = halves_joined(total, z_two, 4, 2)
-    total = halves_joined(total.transpose(1, 0, 2).reshape(432, 128), z_one, 2)
-    total = in_order(total, all_rotated(total, "height"), "height").reshape(1728, 256)
-    total = halves_joined(total, core, 1).reshape(2, 64, 3, 3, 3, 256).astype(jnp.float32)
-    return total[0], total[1]
+    total = rejoined(place, [total] + [quad_rotated(total, k) for k in range(1, 4)], [gradient])
+    total = stacked(place, [total] + all_rotated(total, "height"))
+    other = swapped(total, 1)
+    one = jnp.where(core == 1, other, total).astype(jnp.float32)
+    two = jnp.where(core == 1, total, other).astype(jnp.float32)
+    return gradient, one, two
+
+
+def filter_shape(flat):
+    return flat.reshape(3, 3, 3, 64, 256).transpose(3, 0, 1, 2, 4)
 
 
 def edges(first, second):
@@ -236,24 +288,29 @@
 
 
 def on_device(frames, grad_out, weight_one, weight_two):
-    place = jnp.stack([lax.axis_index("chan"), lax.axis_index("height")]).astype(jnp.int32)
+    spot = lax.axis_index("tm")
+    core = spot % 2
+    place = jnp.stack([lax.axis_index("chan"), lax.axis_index("height"), (spot // 2) % 4]).astype(jnp.int32)
+    taps_one = weight_one.transpose(1, 2, 3, 0, 4).reshape(1728, 256)
+    taps_two = weight_two.transpose(1, 2, 3, 0, 4).reshape(1728, 256)
     frames_all = jnp.concatenate([frames] + all_rotated(frames, "chan"), 2)
     early = passed_along(frames_all, "tm", 1)
     above, below = edges(early, frames_all)
-    ahead = weight_one.transpose(3, 0, 1, 2, 4).reshape(192, 2304)
-    back_one = weight_one.transpose(4, 1, 2, 3, 0).reshape(256, 1728)
-    back_two = weight_two.transpose(4, 1, 2, 3, 0).reshape(256, 1728)
-    panel, pre, act = forward(place, frames_all, early, above, below, ahead)
     grads = with_later(grad_out)
-    grad_act = exchanged(transposed(place, grads, back_two), "chan")
+    act_pieces = transposed(place, grads, taps_two)
+    panel, pre, act = forward(
+        place, frames_all, early, above, below, taps_one.reshape(9, 192, 256), [act_pieces[0]]
+    )
+    grad_act = exchanged(act_pieces, "chan")
     sigmoid_pre = jax.nn.sigmoid(pre)
     grad_pre = (grad_act * sigmoid_pre * (1.0 + pre * (1.0 - sigmoid_pre))).astype(jnp.bfloat16)
     part_one = first_filter(place, panel, grad_pre)
     part_two = second_filter(place, grads, [act] + all_rotated(act, "chan"))
-    grad_one, grad_two = summed_filters(part_one, part_two)
+    pieces = summed_pair(part_one, part_two, core)
     cells = with_later(grad_pre.reshape(2, 4, 64, 128))
-    grad_frames = exchanged(transposed(place, cells, back_one), "chan")
-    return (grad_frames.reshape(2, 4, 64, 128).astype(jnp.bfloat16), grad_one, grad_two)
+    gradient_pieces = transposed(place, cells, taps_one)
+    grad_frames, grad_one, grad_two = rest_of_sum(place, pieces, gradient_pieces, core)
+    return (grad_frames, filter_shape(grad_one), filter_shape(grad_two))
 
 
 def solution(mesh):

time: 162 us -> 141 us (0.87)
  local copies, waits for them, and re-layouts: 21.9 us -> 3.41 us
  starting transfers between devices: 71.8 us -> 62.5 us
  waiting for transfers between devices: 48.6 us -> 53.8 us
  Pallas kernels: 11.8 us -> 15.1 us
    ppermute x7 -> x3, starting transfers between devices: 23.2 us -> 5.92 us  [swapped(): lax.ppermute(block, 'tm', [(i, i ^ distance) for i in range(lax.axis_size...]
    ppermute x0 -> x6, starting transfers between devices: none -> 12.9 us  [quad_rotated(): return lax.ppermute(block, 'tm', route)]
    ppermute x9, waiting for transfers between devices: 12.5 us -> 23.3 us  [passed_along(): return lax.ppermute(block, axis, route)]
    ppermute x18, waiting for transfers between devices: 26 us -> 16.6 us  [rotated(): lax.ppermute(block, axis, [(i, (i + distance) % count) for i in range(cou...]
    ppermute x0 -> x6, waiting for transfers between devices: none -> 9.06 us  [quad_rotated(): return lax.ppermute(block, 'tm', route)]
    ppermute x7 -> x3, waiting for transfers between devices: 10.1 us -> 4.79 us  [swapped(): lax.ppermute(block, 'tm', [(i, i ^ distance) for i in range(lax.axis_size...]
    squeeze x2 -> x1, local copies, waits for them, and re-layouts: 5.29 us -> 0.03 us  [summed_pair(): return [total[0]] + [total[k].astype(jnp.bfloat16) for k in range(1, 4)]]
    reshape x5 -> x0, local copies, waits for them, and re-layouts: 5.1 us -> none  [the longest x1 2.68 us: on_device(): ahead = weight_one.transpose(3, 0, 1, 2, 4).reshape(192, 2304)]
  transfers between devices with their start and end apart: 34 -> 36, of which waited for: 15 -> 18; matrix products, arithmetic and copies ran while one was open for 8% -> 3% of each run, Pallas kernels for 6% -> 8%
where the time goes in v2:
time: 141 us
  starting transfers between devices  62.5 us (44%)
  waiting for transfers between devices  53.8 us (38%)
  Pallas kernels  15.1 us (11%)
  other arithmetic  4.77 us (3%)
  local copies, waits for them, and re-layouts  3.41 us (2%)
    ppermute x9, waiting for transfers between devices, passed_along(): return lax.ppermute(block, axis, route)  23.3 us
    ppermute x9, starting transfers between devices, passed_along(): return lax.ppermute(block, axis, route)  22.6 us
    ppermute x18, starting transfers between devices, rotated(): lax.ppermute(block, axis, [(i, (i + distance) % count) for i in range(cou...  21 us
    ppermute x18, waiting for transfers between devices, rotated(): lax.ppermute(block, axis, [(i, (i + distance) % count) for i in range(cou...  16.6 us
    pallas_call x8, Pallas kernels, call(): pl.pallas_call(lambda *refs: body(*refs[:used], *refs[rest:]), out_shape=...  15.1 us
    ppermute x6, starting transfers between devices, quad_rotated(): return lax.ppermute(block, 'tm', route)  12.9 us
    ppermute x6, waiting for transfers between devices, quad_rotated(): return lax.ppermute(block, 'tm', route)  9.06 us
    ppermute x3, starting transfers between devices, swapped(): lax.ppermute(block, 'tm', [(i, i ^ distance) for i in range(lax.axis_size...  5.92 us
  transfers between devices with their start and end apart: 36, of which 18 were waited for; matrix products, arithmetic and copies ran while one was open for 3% of the time, Pallas kernels for 8%

profile of v2, /device:TPU:1, one launch (start us, length us, event | category | flops | bytes accessed | tf_op | source)
XLA Modules:
  0.0 140.5 jit_solution(9268540158356610036)
XLA Ops:
  0.6 3.8 %collective-permute-start.7 = (bf16[2,4,64,128]{3,2,1,0:T(8,128)(2,1)}, bf16[2,4,64,128]{3,2,1,0:T(8,128)(2,1)S(1)}, u32[]{:S(2)}, u32[]{:S(2)}) collective-permute-start(bf16[2,4,64,128]{3,2,1,0:T(8,128)(2,1)} %param.4), channel_id=1, source_target_pairs={{0,2},{1,3},{2,0},{3,1},{4,6},{5,7},{6,4},{7,5},{8,10},{9,11},{10,... | collective-permute-start | bytes 393224 | tf_op jit(solution)/shard_map/ppermute | solution.py:226
  4.5 0.4 collective-permute-start.6
  4.9 2.3 %collective-permute-start.8 = (bf16[2,4,64,128]{3,2,1,0:T(8,128)(2,1)}, bf16[2,4,64,128]{3,2,1,0:T(8,128)(2,1)S(1)}, u32[]{:S(2)}, u32[]{:S(2)}) collective-permute-start(bf16[2,4,64,128]{3,2,1,0:T(8,128)(2,1)} %param.4), channel_id=1, source_target_pairs={{0,3},{1,0},{2,1},{3,2},{4,7},{5,4},{6,5},{7,6},{8,11},{9,8},{10,9... | collective-permute-start | bytes 393224 | tf_op jit(solution)/shard_map/ppermute | solution.py:226
  7.1 3.4 %collective-permute-start = (bf16[2,4,64,128]{3,2,1,0:T(8,128)(2,1)}, bf16[2,4,64,128]{3,2,1,0:T(8,128)(2,1)S(1)}, u32[]{:S(2)}, u32[]{:S(2)}) collective-permute-start(bf16[2,4,64,128]{3,2,1,0:T(8,128)(2,1)} %refs_1_.3), channel_id=1, source_target_pairs={{16,0},{32,16},{48,32},{64,48},{80,64},{96,80},{112,96},{128,112},... | collective-permute-start | bytes 393224 | tf_op jit(solution)/shard_map/ppermute | solution.py:12
  10.6 0.8 fusion.5
  11.4 1.0 constant_dynamic-update-slice_fusion.3
  12.5 3.5 %collective-permute-start.9 = (bf16[2,4,256,128]{3,2,1,0:T(8,128)(2,1)S(1)}, bf16[2,4,256,128]{3,2,1,0:T(8,128)(2,1)S(1)}, u32[]{:S(2)}, u32[]{:S(2)}) collective-permute-start(bf16[2,4,256,128]{3,2,1,0:T(8,128)(2,1)S(1)} %constant_dynamic-update-slice_fusion.refs_1_), channel_id=1, source_target_pairs={{0,16},{16,32},{32,48},{48,64},{64,80},{80,96},{96,112},{112,128},... | collective-permute-start | bytes 1572872 | tf_op jit(solution)/shard_map/ppermute | solution.py:12
  16.0 3.2 %collective-permute-start.1 = (bf16[4,1,64,128]{3,2,1,0:T(8,128)(2,1)S(1)}, bf16[4,1,64,128]{3,2,1,0:T(8,128)(2,1)S(1)}, u32[]{:S(2)}, u32[]{:S(2)}) collective-permute-start(bf16[4,1,64,128]{3,2,1,0:T(8,128)(2,1)S(1)} %pad_maximum_fusion.2), channel_id=1, source_target_pairs={{0,4},{4,8},{8,12},{1,5},{5,9},{9,13},{2,6},{6,10},{10,14},{3,7},{... | collective-permute-start | bytes 196616 | tf_op jit(solution)/shard_map/ppermute | solution.py:12
  19.3 2.8 %collective-permute-done.9.refs_2_ = bf16[2,4,256,128]{3,2,1,0:T(8,128)(2,1)S(1)} collective-permute-done((bf16[2,4,256,128]{3,2,1,0:T(8,128)(2,1)S(1)}, bf16[2,4,256,128]{3,2,1,0:T(8,128)(2,1)S(1)}, u32[]{:S(2)}, u32[]{:S(2)}) %collective-permute-start.9) | collective-permute-done | bytes 524320 | tf_op jit(solution)/shard_map/ppermute | solution.py:12
  22.1 0.7 pad_maximum_fusion
  22.8 3.8 %collective-permute-start.10 = (bf16[4,1,256,128]{3,2,1,0:T(8,128)(2,1)}, bf16[4,1,256,128]{3,2,1,0:T(8,128)(2,1)}, u32[]{:S(2)}, u32[]{:S(2)}) collective-permute-start(bf16[4,1,256,128]{3,2,1,0:T(8,128)(2,1)} %pad_maximum_fusion), channel_id=1, source_target_pairs={{0,4},{4,8},{8,12},{1,5},{5,9},{9,13},{2,6},{6,10},{10,14},{3,7},{... | collective-permute-start | bytes 786440 | tf_op jit(solution)/shard_map/ppermute | solution.py:12
  26.6 0.7 pad_maximum_fusion.1
  27.4 1.3 collective-permute-start.11
  28.7 1.3 collective-permute-start.2
  30.1 6.1 %collective-permute-done.2.refs_4_ = bf16[4,1,64,128]{3,2,1,0:T(8,128)(2,1)S(1)} collective-permute-done((bf16[4,1,64,128]{3,2,1,0:T(8,128)(2,1)S(1)}, bf16[4,1,64,128]{3,2,1,0:T(8,128)(2,1)S(1)}, u32[]{:S(2)}, u32[]{:S(2)}) %collective-permute-start.2) | collective-permute-done | bytes 65568 | tf_op jit(solution)/shard_map/ppermute | solution.py:12
  36.2 2.8 %shard_map.67 = (f32[8,64,128]{2,1,0:T(8,128)S(1)}, bf16[8,64,128]{2,1,0:T(8,128)(2,1)}, bf16[8,64,128]{2,1,0:T(8,128)(2,1)}, bf16[8,64,128]{2,1,0:T(8,128)(2,1)}) custom-call(s32[3]{0:T(128)S(1)} %pad_add_fusion.refs_0_, bf16[2,4,64,128]{3,2,1,0:T(8,128)(2,1)S(1)} %copy-done.3, bf16[2,4,64,128]{3,2,1,0:T(8,128)(2,1)S(1)} %collective-permute-done.refs_2_, ...), custom_call_target="tpu_custom_call" | custom-call | tf_op jit(solution)/shard_map/pallas_call | solution.py:24
  38.9 0.3 collective-permute-start.3
  39.2 2.8 %collective-permute-start.4 = (bf16[8,64,128]{2,1,0:T(8,128)(2,1)}, bf16[8,64,128]{2,1,0:T(8,128)(2,1)S(1)}, u32[]{:S(2)}, u32[]{:S(2)}) collective-permute-start(bf16[8,64,128]{2,1,0:T(8,128)(2,1)} %get-tuple-element.20), channel_id=1, source_target_pairs={{0,2},{1,3},{2,0},{3,1},{4,6},{5,7},{6,4},{7,5},{8,10},{9,11},{10,... | collective-permute-start | bytes 393224 | tf_op jit(solution)/shard_map/ppermute | solution.py:226
  42.0 3.6 %shard_map.68 = (bf16[24,256,128]{2,1,0:T(8,128)(2,1)}, f32[8,64,128]{2,1,0:T(8,128)S(1)}, bf16[8,64,128]{2,1,0:T(8,128)(2,1)S(1)}) custom-call(s32[3]{0:T(128)S(1)} %pad_add_fusion.refs_0_, bf16[2,4,256,128]{3,2,1,0:T(8,128)(2,1)S(1)} %constant_dynamic-update-slice_fusion.refs_1_, bf16[2,4,256,128]{3,2,1,0:T(8,128)(2,1)S(1)} %collective-permute-done.9.refs_2_, ...), custom_call_target="tpu_custom_call" | custom-call | tf_op jit(solution)/shard_map/pallas_call | solution.py:24
  45.6 0.5 collective-permute-start.20
  46.1 2.8 %collective-permute-start.19 = (bf16[8,64,128]{2,1,0:T(8,128)(2,1)S(1)}, bf16[8,64,128]{2,1,0:T(8,128)(2,1)S(1)}, u32[]{:S(2)}, u32[]{:S(2)}) collective-permute-start(bf16[8,64,128]{2,1,0:T(8,128)(2,1)S(1)} %get-tuple-element.27.refs_5_), channel_id=1, source_target_pairs={{0,2},{1,3},{2,0},{3,1},{4,6},{5,7},{6,4},{7,5},{8,10},{9,11},{10,... | collective-permute-start | bytes 393224 | tf_op jit(solution)/shard_map/ppermute | solution.py:226
  48.9 0.2 multiply_convert_fusion.refs_2_
  49.1 1.4 copy-done.1
  50.5 2.3 %shard_map.71 = bf16[4,27,16,256]{3,2,1,0:T(8,128)(2,1)S(1)} custom-call(s32[3]{0:T(128)S(1)} %pad_add_fusion.refs_0_, bf16[24,256,128]{2,1,0:T(8,128)(2,1)S(1)} %copy-done.1, bf16[8,64,128]{2,1,0:T(8,128)(2,1)S(1)} %multiply_convert_fusion.refs_2_), custom_call_target="tpu_custom_call" | custom-call | tf_op jit(solution)/shard_map/pallas_call | solution.py:24
  52.8 2.0 %collective-permute-done.18.refs_6_ = bf16[8,64,128]{2,1,0:T(8,128)(2,1)S(1)} collective-permute-done((bf16[8,64,128]{2,1,0:T(8,128)(2,1)S(1)}, bf16[8,64,128]{2,1,0:T(8,128)(2,1)S(1)}, u32[]{:S(2)}, u32[]{:S(2)}) %collective-permute-start.18) | collective-permute-done | bytes 131104 | tf_op jit(solution)/shard_map/ppermute | solution.py:226
  54.8 2.5 %shard_map.70 = bf16[4,27,16,256]{3,2,1,0:T(8,128)(2,1)S(1)} custom-call(s32[3]{0:T(128)S(1)} %pad_add_fusion.refs_0_, bf16[2,4,64,128]{3,2,1,0:T(8,128)(2,1)S(1)} %copy-done.3, bf16[2,4,64,128]{3,2,1,0:T(8,128)(2,1)S(1)} %collective-permute-done.refs_2_, bf16[4,1,64,128]{3,2,1,0:T(8,128)(2,1)S(1)} %collective-permute-done.1.refs_3_, ...), custom_call_target="tpu_custom_call" | custom-call | tf_op jit(solution)/shard_map/pallas_call | solution.py:24
  57.3 0.1 broadcast_select_fusion
  57.4 0.1 collective-permute-start.21
  57.5 2.4 %collective-permute-start.12 = (bf16[2,4,64,128]{3,2,1,0:T(8,128)(2,1)S(1)}, bf16[2,4,64,128]{3,2,1,0:T(8,128)(2,1)S(1)}, u32[]{:S(2)}, u32[]{:S(2)}) collective-permute-start(bf16[2,4,64,128]{3,2,1,0:T(8,128)(2,1)S(1)} %bitcast.31), channel_id=1, source_target_pairs={{16,0},{32,16},{48,32},{64,48},{80,64},{96,80},{112,96},{128,112},... | collective-permute-start | bytes 393224 | tf_op jit(solution)/shard_map/ppermute | solution.py:12
  59.9 9.8 %collective-permute-done.12.refs_2_ = bf16[2,4,64,128]{3,2,1,0:T(8,128)(2,1)S(1)} collective-permute-done((bf16[2,4,64,128]{3,2,1,0:T(8,128)(2,1)S(1)}, bf16[2,4,64,128]{3,2,1,0:T(8,128)(2,1)S(1)}, u32[]{:S(2)}, u32[]{:S(2)}) %collective-permute-start.12) | collective-permute-done | bytes 131104 | tf_op jit(solution)/shard_map/ppermute | solution.py:12
  69.7 2.4 %collective-permute-start.13 = (bf16[4,1,64,128]{3,2,1,0:T(8,128)(2,1)S(1)}, bf16[4,1,64,128]{3,2,1,0:T(8,128)(2,1)S(1)}, u32[]{:S(2)}, u32[]{:S(2)}) collective-permute-start(bf16[4,1,64,128]{3,2,1,0:T(8,128)(2,1)S(1)} %pad_maximum_fusion.4), channel_id=1, source_target_pairs={{0,4},{4,8},{8,12},{1,5},{5,9},{9,13},{2,6},{6,10},{10,14},{3,7},{... | collective-permute-start | bytes 196616 | tf_op jit(solution)/shard_map/ppermute | solution.py:12
  72.2 1.3 collective-permute-start.14
  73.5 4.6 %collective-permute-done.14.refs_4_ = bf16[4,1,64,128]{3,2,1,0:T(8,128)(2,1)S(1)} collective-permute-done((bf16[4,1,64,128]{3,2,1,0:T(8,128)(2,1)S(1)}, bf16[4,1,64,128]{3,2,1,0:T(8,128)(2,1)S(1)}, u32[]{:S(2)}, u32[]{:S(2)}) %collective-permute-start.14) | collective-permute-done | bytes 65568 | tf_op jit(solution)/shard_map/ppermute | solution.py:12
  78.1 2.0 %shard_map.69 = (f32[8,64,128]{2,1,0:T(8,128)S(1)}, bf16[8,64,128]{2,1,0:T(8,128)(2,1)S(1)}, bf16[8,64,128]{2,1,0:T(8,128)(2,1)S(1)}, bf16[8,64,128]{2,1,0:T(8,128)(2,1)S(1)}) custom-call(s32[3]{0:T(128)S(1)} %pad_add_fusion.refs_0_, bf16[2,4,64,128]{3,2,1,0:T(8,128)(2,1)S(1)} %bitcast.33, bf16[2,4,64,128]{3,2,1,0:T(8,128)(2,1)S(1)} %collective-permute-done.12.refs_2_, ...), custom_call_target="tpu_custom_call" | custom-call | tf_op jit(solution)/shard_map/pallas_call | solution.py:24
  80.2 0.5 fusion
  80.8 2.4 %collective-permute-start.23 = (bf16[27,16,256]{2,1,0:T(8,128)(2,1)S(1)}, bf16[27,16,256]{2,1,0:T(8,128)(2,1)S(1)}, u32[]{:S(2)}, u32[]{:S(2)}) collective-permute-start(bf16[27,16,256]{2,1,0:T(8,128)(2,1)S(1)} %get-tuple-element.38), channel_id=1, source_target_pairs={{0,8},{4,12},{8,0},{12,4},{1,9},{5,13},{9,1},{13,5},{2,10},{6,14},... | collective-permute-start | bytes 663560 | tf_op jit(solution)/shard_map/ppermute | solution.py:226
  83.2 2.3 %collective-permute-done.24.refs_4_ = bf16[27,16,256]{2,1,0:T(8,128)(2,1)S(1)} collective-permute-done((bf16[27,16,256]{2,1,0:T(8,128)(2,1)S(1)}, bf16[27,16,256]{2,1,0:T(8,128)(2,1)S(1)}, u32[]{:S(2)}, u32[]{:S(2)}) %collective-permute-start.24) | collective-permute-done | bytes 221216 | tf_op jit(solution)/shard_map/ppermute | solution.py:226
  85.6 1.6 %collective-permute-done.23.refs_3_ = bf16[27,16,256]{2,1,0:T(8,128)(2,1)S(1)} collective-permute-done((bf16[27,16,256]{2,1,0:T(8,128)(2,1)S(1)}, bf16[27,16,256]{2,1,0:T(8,128)(2,1)S(1)}, u32[]{:S(2)}, u32[]{:S(2)}) %collective-permute-start.23) | collective-permute-done | bytes 221216 | tf_op jit(solution)/shard_map/ppermute | solution.py:226
  87.2 2.3 %collective-permute-done.22.refs_2_ = bf16[27,16,256]{2,1,0:T(8,128)(2,1)S(1)} collective-permute-done((bf16[27,16,256]{2,1,0:T(8,128)(2,1)S(1)}, bf16[27,16,256]{2,1,0:T(8,128)(2,1)S(1)}, u32[]{:S(2)}, u32[]{:S(2)}) %collective-permute-start.22) | collective-permute-done | bytes 221216 | tf_op jit(solution)/shard_map/ppermute | solution.py:226
  89.5 0.7 shard_map.72
  90.2 5.6 %collective-permute-start.25 = (bf16[27,8,128]{2,1,0:T(8,128)(2,1)S(1)}, bf16[27,8,128]{2,1,0:T(8,128)(2,1)S(1)}, u32[]{:S(2)}, u32[]{:S(2)}) collective-permute-start(bf16[27,8,128]{2,1,0:T(8,128)(2,1)S(1)} %get-tuple-element.30), channel_id=1, source_target_pairs={{0,32},{16,48},{32,64},{48,80},{64,96},{80,112},{96,0},{112,16},{1... | collective-permute-start | bytes 165896 | tf_op jit(solution)/shard_map/ppermute | solution.py:247
  95.9 4.3 %collective-permute-start.26 = (bf16[27,8,128]{2,1,0:T(8,128)(2,1)S(1)}, bf16[27,8,128]{2,1,0:T(8,128)(2,1)S(1)}, u32[]{:S(2)}, u32[]{:S(2)}) collective-permute-start(bf16[27,8,128]{2,1,0:T(8,128)(2,1)S(1)} %get-tuple-element.31), channel_id=1, source_target_pairs={{0,64},{16,80},{32,96},{48,112},{64,0},{80,16},{96,32},{112,48},{1... | collective-permute-start | bytes 165896 | tf_op jit(solution)/shard_map/ppermute | solution.py:247
  100.2 1.6 %collective-permute-done.25 = bf16[27,8,128]{2,1,0:T(8,128)(2,1)S(1)} collective-permute-done((bf16[27,8,128]{2,1,0:T(8,128)(2,1)S(1)}, bf16[27,8,128]{2,1,0:T(8,128)(2,1)S(1)}, u32[]{:S(2)}, u32[]{:S(2)}) %collective-permute-start.25) | collective-permute-done | bytes 55328 | tf_op jit(solution)/shard_map/ppermute | solution.py:247
  101.8 2.8 %collective-permute-done.26 = bf16[27,8,128]{2,1,0:T(8,128)(2,1)S(1)} collective-permute-done((bf16[27,8,128]{2,1,0:T(8,128)(2,1)S(1)}, bf16[27,8,128]{2,1,0:T(8,128)(2,1)S(1)}, u32[]{:S(2)}, u32[]{:S(2)}) %collective-permute-start.26) | collective-permute-done | bytes 55328 | tf_op jit(solution)/shard_map/ppermute | solution.py:247
  104.7 1.7 %collective-permute-start.28 = (bf16[27,8,128]{2,1,0:T(8,128)(2,1)S(1)}, bf16[27,8,128]{2,1,0:T(8,128)(2,1)S(1)}, u32[]{:S(2)}, u32[]{:S(2)}) collective-permute-start(bf16[27,8,128]{2,1,0:T(8,128)(2,1)S(1)} %add_convert_fusion.2), channel_id=1, source_target_pairs={{0,128},{16,144},{32,160},{48,176},{64,192},{80,208},{96,224},{112... | collective-permute-start | bytes 165896 | tf_op jit(solution)/shard_map/ppermute | solution.py:242
  106.4 1.8 %collective-permute-start.16 = (bf16[8,64,128]{2,1,0:T(8,128)(2,1)S(1)}, bf16[8,64,128]{2,1,0:T(8,128)(2,1)S(1)}, u32[]{:S(2)}, u32[]{:S(2)}) collective-permute-start(bf16[8,64,128]{2,1,0:T(8,128)(2,1)S(1)} %get-tuple-element.25), channel_id=1, source_target_pairs={{0,2},{1,3},{2,0},{3,1},{4,6},{5,7},{6,4},{7,5},{8,10},{9,11},{10,... | collective-permute-start | bytes 393224 | tf_op jit(solution)/shard_map/ppermute | solution.py:226
  108.2 0.8 collective-permute-start.17
  109.0 2.7 %collective-permute-done.28 = bf16[27,8,128]{2,1,0:T(8,128)(2,1)S(1)} collective-permute-done((bf16[27,8,128]{2,1,0:T(8,128)(2,1)S(1)}, bf16[27,8,128]{2,1,0:T(8,128)(2,1)S(1)}, u32[]{:S(2)}, u32[]{:S(2)}) %collective-permute-start.28) | collective-permute-done | bytes 55328 | tf_op jit(solution)/shard_map/ppermute | solution.py:242
  111.8 1.1 collective-permute-start.31
  112.9 1.7 %collective-permute-start.30 = (bf16[27,8,128]{2,1,0:T(8,128)(2,1)S(1)}, bf16[27,8,128]{2,1,0:T(8,128)(2,1)S(1)}, u32[]{:S(2)}, u32[]{:S(2)}) collective-permute-start(bf16[27,8,128]{2,1,0:T(8,128)(2,1)S(1)} %add_convert_fusion.1.refs_1_), channel_id=1, source_target_pairs={{0,64},{16,80},{32,96},{48,112},{64,0},{80,16},{96,32},{112,48},{1... | collective-permute-start | bytes 165896 | tf_op jit(solution)/shard_map/ppermute | solution.py:247
  114.8 0.5 collective-permute-done.31.refs_4_
  115.3 2.1 %collective-permute-done.30.refs_3_ = bf16[27,8,128]{2,1,0:T(8,128)(2,1)S(1)} collective-permute-done((bf16[27,8,128]{2,1,0:T(8,128)(2,1)S(1)}, bf16[27,8,128]{2,1,0:T(8,128)(2,1)S(1)}, u32[]{:S(2)}, u32[]{:S(2)}) %collective-permute-start.30) | collective-permute-done | bytes 55328 | tf_op jit(solution)/shard_map/ppermute | solution.py:247
  117.4 2.1 %collective-permute-done.29.refs_2_ = bf16[27,8,128]{2,1,0:T(8,128)(2,1)S(1)} collective-permute-done((bf16[27,8,128]{2,1,0:T(8,128)(2,1)S(1)}, bf16[27,8,128]{2,1,0:T(8,128)(2,1)S(1)}, u32[]{:S(2)}, u32[]{:S(2)}) %collective-permute-start.29) | collective-permute-done | bytes 55328 | tf_op jit(solution)/shard_map/ppermute | solution.py:247
  119.5 0.6 shard_map.73.refs_1_
  120.1 1.2 collective-permute-start.34
  121.3 1.8 %collective-permute-start.33 = (bf16[27,16,256]{2,1,0:T(8,128)(2,1)S(1)}, bf16[27,16,256]{2,1,0:T(8,128)(2,1)S(1)}, u32[]{:S(2)}, u32[]{:S(2)}) collective-permute-start(bf16[27,16,256]{2,1,0:T(8,128)(2,1)S(1)} %shard_map.73.refs_1_), channel_id=1, source_target_pairs={{0,8},{4,12},{8,0},{12,4},{1,9},{5,13},{9,1},{13,5},{2,10},{6,14},... | collective-permute-start | bytes 663560 | tf_op jit(solution)/shard_map/ppermute | solution.py:226
  123.1 1.9 %collective-permute-done.34.refs_4_ = bf16[27,16,256]{2,1,0:T(8,128)(2,1)S(1)} collective-permute-done((bf16[27,16,256]{2,1,0:T(8,128)(2,1)S(1)}, bf16[27,16,256]{2,1,0:T(8,128)(2,1)S(1)}, u32[]{:S(2)}, u32[]{:S(2)}) %collective-permute-start.34) | collective-permute-done | bytes 221216 | tf_op jit(solution)/shard_map/ppermute | solution.py:226
  124.9 2.8 %collective-permute-done.33.refs_3_ = bf16[27,16,256]{2,1,0:T(8,128)(2,1)S(1)} collective-permute-done((bf16[27,16,256]{2,1,0:T(8,128)(2,1)S(1)}, bf16[27,16,256]{2,1,0:T(8,128)(2,1)S(1)}, u32[]{:S(2)}, u32[]{:S(2)}) %collective-permute-start.33) | collective-permute-done | bytes 221216 | tf_op jit(solution)/shard_map/ppermute | solution.py:226
  127.7 3.7 %collective-permute-done.32.refs_2_ = bf16[27,16,256]{2,1,0:T(8,128)(2,1)S(1)} collective-permute-done((bf16[27,16,256]{2,1,0:T(8,128)(2,1)S(1)}, bf16[27,16,256]{2,1,0:T(8,128)(2,1)S(1)}, u32[]{:S(2)}, u32[]{:S(2)}) %collective-permute-start.32) | collective-permute-done | bytes 221216 | tf_op jit(solution)/shard_map/ppermute | solution.py:226
  131.3 0.6 shard_map.74
  132.0 4.1 %collective-permute-start.35 = (bf16[27,64,256]{2,1,0:T(8,128)(2,1)S(1)}, bf16[27,64,256]{2,1,0:T(8,128)(2,1)S(1)}, u32[]{:S(2)}, u32[]{:S(2)}) collective-permute-start(bf16[27,64,256]{2,1,0:T(8,128)(2,1)S(1)} %shard_map.74), channel_id=1, source_target_pairs={{0,16},{16,0},{32,48},{48,32},{64,80},{80,64},{96,112},{112,96},{1... | collective-permute-start | bytes 2654216 | tf_op jit(solution)/shard_map/ppermute | solution.py:242
  136.1 2.1 %collective-permute-done.35 = bf16[27,64,256]{2,1,0:T(8,128)(2,1)S(1)} collective-permute-done((bf16[27,64,256]{2,1,0:T(8,128)(2,1)S(1)}, bf16[27,64,256]{2,1,0:T(8,128)(2,1)S(1)}, u32[]{:S(2)}, u32[]{:S(2)}) %collective-permute-start.35) | collective-permute-done | bytes 884768 | tf_op jit(solution)/shard_map/ppermute | solution.py:242
  138.2 0.1 broadcast_select_fusion.1
  138.3 2.2 %convert_bitcast_fusion = (f32[64,3,3,3,256]{4,0,3,2,1:T(8,128)}, f32[64,3,3,3,256]{4,0,3,2,1:T(8,128)}) fusion(bf16[3,3,3,64,256]{4,3,2,1,0:T(8,128)(2,1)S(1)} %bitcast.37, bf16[3,3,3,64,256]{4,3,2,1,0:T(8,128)(2,1)S(1)} %bitcast.38), kind=kLoop, calls=%fused_computation | loop fusion | flops 884736 | bytes 5308416 | tf_op jit(solution)/shard_map/transpose | solution.py:275
  (53 shorter events, 0.7 us)
Async XLA Ops:
  0.6 11.8 %collective-permute-start.7 = (bf16[2,4,64,128]{3,2,1,0:T(8,128)(2,1)}, bf16[2,4,64,128]{3,2,1,0:T(8,128)(2,1)S(1)}, u32[]{:S(2)}, u32[]{:S(2)}) collective-permute-start(bf16[2,4,64,128]{3,2,1,0:T(8,128)(2,1)} %param.4), channel_id=1, source_target_pairs={{0,2},{1,3},{2,0},{3,1},{4,6},{5,7},{6,4},{7,5},{8,10},{9,11},{10,... | collective-permute-start | bytes 393224 | tf_op jit(solution)/shard_map/ppermute | solution.py:226
  4.5 7.9 %collective-permute-start.6 = (bf16[2,4,64,128]{3,2,1,0:T(8,128)(2,1)}, bf16[2,4,64,128]{3,2,1,0:T(8,128)(2,1)S(1)}, u32[]{:S(2)}, u32[]{:S(2)}) collective-permute-start(bf16[2,4,64,128]{3,2,1,0:T(8,128)(2,1)} %param.4), channel_id=1, source_target_pairs={{0,1},{1,2},{2,3},{3,0},{4,5},{5,6},{6,7},{7,4},{8,9},{9,10},{10,1... | collective-permute-start | bytes 393224 | tf_op jit(solution)/shard_map/ppermute | solution.py:226
  4.9 7.6 %collective-permute-start.8 = (bf16[2,4,64,128]{3,2,1,0:T(8,128)(2,1)}, bf16[2,4,64,128]{3,2,1,0:T(8,128)(2,1)S(1)}, u32[]{:S(2)}, u32[]{:S(2)}) collective-permute-start(bf16[2,4,64,128]{3,2,1,0:T(8,128)(2,1)} %param.4), channel_id=1, source_target_pairs={{0,3},{1,0},{2,1},{3,2},{4,7},{5,4},{6,5},{7,6},{8,11},{9,8},{10,9... | collective-permute-start | bytes 393224 | tf_op jit(solution)/shard_map/ppermute | solution.py:226
  7.1 8.8 %collective-permute-start = (bf16[2,4,64,128]{3,2,1,0:T(8,128)(2,1)}, bf16[2,4,64,128]{3,2,1,0:T(8,128)(2,1)S(1)}, u32[]{:S(2)}, u32[]{:S(2)}) collective-permute-start(bf16[2,4,64,128]{3,2,1,0:T(8,128)(2,1)} %refs_1_.3), channel_id=1, source_target_pairs={{16,0},{32,16},{48,32},{64,48},{80,64},{96,80},{112,96},{128,112},... | collective-permute-start | bytes 393224 | tf_op jit(solution)/shard_map/ppermute | solution.py:12
  11.3 24.8 %copy-start.2 = (bf16[64,3,3,3,256]{4,0,3,2,1:T(8,128)(2,1)S(1)}, bf16[64,3,3,3,256]{4,0,3,2,1:T(8,128)(2,1)}, u32[]{:S(2)}) copy-start(bf16[64,3,3,3,256]{4,0,3,2,1:T(8,128)(2,1)} %param.7) | copy-start | bytes 2654212
  11.3 24.8 %copy-start.3 = (bf16[2,4,64,128]{3,2,1,0:T(8,128)(2,1)S(1)}, bf16[2,4,64,128]{3,2,1,0:T(8,128)(2,1)}, u32[]{:S(2)}) copy-start(bf16[2,4,64,128]{3,2,1,0:T(8,128)(2,1)} %refs_1_.3) | copy-start | bytes 393220
  12.5 9.6 %collective-permute-start.9 = (bf16[2,4,256,128]{3,2,1,0:T(8,128)(2,1)S(1)}, bf16[2,4,256,128]{3,2,1,0:T(8,128)(2,1)S(1)}, u32[]{:S(2)}, u32[]{:S(2)}) collective-permute-start(bf16[2,4,256,128]{3,2,1,0:T(8,128)(2,1)S(1)} %constant_dynamic-update-slice_fusion.refs_1_), channel_id=1, source_target_pairs={{0,16},{16,32},{32,48},{48,64},{64,80},{80,96},{96,112},{112,128},... | collective-permute-start | bytes 1572872 | tf_op jit(solution)/shard_map/ppermute | solution.py:12
  16.0 26.0 %copy-start = (bf16[64,3,3,3,256]{4,0,3,2,1:T(8,128)(2,1)S(1)}, bf16[64,3,3,3,256]{4,0,3,2,1:T(8,128)(2,1)}, u32[]{:S(2)}) copy-start(bf16[64,3,3,3,256]{4,0,3,2,1:T(8,128)(2,1)} %param.6) | copy-start | bytes 2654212
  16.0 14.0 %collective-permute-start.1 = (bf16[4,1,64,128]{3,2,1,0:T(8,128)(2,1)S(1)}, bf16[4,1,64,128]{3,2,1,0:T(8,128)(2,1)S(1)}, u32[]{:S(2)}, u32[]{:S(2)}) collective-permute-start(bf16[4,1,64,128]{3,2,1,0:T(8,128)(2,1)S(1)} %pad_maximum_fusion.2), channel_id=1, source_target_pairs={{0,4},{4,8},{8,12},{1,5},{5,9},{9,13},{2,6},{6,10},{10,14},{3,7},{... | collective-permute-start | bytes 196616 | tf_op jit(solution)/shard_map/ppermute | solution.py:12
  22.8 19.2 %collective-permute-start.10 = (bf16[4,1,256,128]{3,2,1,0:T(8,128)(2,1)}, bf16[4,1,256,128]{3,2,1,0:T(8,128)(2,1)}, u32[]{:S(2)}, u32[]{:S(2)}) collective-permute-start(bf16[4,1,256,128]{3,2,1,0:T(8,128)(2,1)} %pad_maximum_fusion), channel_id=1, source_target_pairs={{0,4},{4,8},{8,12},{1,5},{5,9},{9,13},{2,6},{6,10},{10,14},{3,7},{... | collective-permute-start | bytes 786440 | tf_op jit(solution)/shard_map/ppermute | solution.py:12
  27.4 14.6 %collective-permute-start.11 = (bf16[4,1,256,128]{3,2,1,0:T(8,128)(2,1)}, bf16[4,1,256,128]{3,2,1,0:T(8,128)(2,1)}, u32[]{:S(2)}, u32[]{:S(2)}) collective-permute-start(bf16[4,1,256,128]{3,2,1,0:T(8,128)(2,1)} %pad_maximum_fusion.1), channel_id=1, source_target_pairs={{4,0},{8,4},{12,8},{5,1},{9,5},{13,9},{6,2},{10,6},{14,10},{7,3},{... | collective-permute-start | bytes 786440 | tf_op jit(solution)/shard_map/ppermute | solution.py:12
  28.7 7.5 %collective-permute-start.2 = (bf16[4,1,64,128]{3,2,1,0:T(8,128)(2,1)S(1)}, bf16[4,1,64,128]{3,2,1,0:T(8,128)(2,1)S(1)}, u32[]{:S(2)}, u32[]{:S(2)}) collective-permute-start(bf16[4,1,64,128]{3,2,1,0:T(8,128)(2,1)S(1)} %pad_maximum_fusion.3), channel_id=1, source_target_pairs={{4,0},{8,4},{12,8},{5,1},{9,5},{13,9},{6,2},{10,6},{14,10},{7,3},{... | collective-permute-start | bytes 196616 | tf_op jit(solution)/shard_map/ppermute | solution.py:12
  38.9 10.0 %collective-permute-start.3 = (bf16[8,64,128]{2,1,0:T(8,128)(2,1)}, bf16[8,64,128]{2,1,0:T(8,128)(2,1)S(1)}, u32[]{:S(2)}, u32[]{:S(2)}) collective-permute-start(bf16[8,64,128]{2,1,0:T(8,128)(2,1)} %get-tuple-element.19), channel_id=1, source_target_pairs={{0,1},{1,2},{2,3},{3,0},{4,5},{5,6},{6,7},{7,4},{8,9},{9,10},{10,1... | collective-permute-start | bytes 393224 | tf_op jit(solution)/shard_map/ppermute | solution.py:226
  39.2 9.7 %collective-permute-start.4 = (bf16[8,64,128]{2,1,0:T(8,128)(2,1)}, bf16[8,64,128]{2,1,0:T(8,128)(2,1)S(1)}, u32[]{:S(2)}, u32[]{:S(2)}) collective-permute-start(bf16[8,64,128]{2,1,0:T(8,128)(2,1)} %get-tuple-element.20), channel_id=1, source_target_pairs={{0,2},{1,3},{2,0},{3,1},{4,6},{5,7},{6,4},{7,5},{8,10},{9,11},{10,... | collective-permute-start | bytes 393224 | tf_op jit(solution)/shard_map/ppermute | solution.py:226
  42.0 6.9 %collective-permute-start.5 = (bf16[8,64,128]{2,1,0:T(8,128)(2,1)}, bf16[8,64,128]{2,1,0:T(8,128)(2,1)S(1)}, u32[]{:S(2)}, u32[]{:S(2)}) collective-permute-start(bf16[8,64,128]{2,1,0:T(8,128)(2,1)} %get-tuple-element.21), channel_id=1, source_target_pairs={{0,3},{1,0},{2,1},{3,2},{4,7},{5,4},{6,5},{7,6},{8,11},{9,8},{10,9... | collective-permute-start | bytes 393224 | tf_op jit(solution)/shard_map/ppermute | solution.py:226
  45.6 7.1 %collective-permute-start.20 = (bf16[8,64,128]{2,1,0:T(8,128)(2,1)S(1)}, bf16[8,64,128]{2,1,0:T(8,128)(2,1)S(1)}, u32[]{:S(2)}, u32[]{:S(2)}) collective-permute-start(bf16[8,64,128]{2,1,0:T(8,128)(2,1)S(1)} %get-tuple-element.27.refs_5_), channel_id=1, source_target_pairs={{0,3},{1,0},{2,1},{3,2},{4,7},{5,4},{6,5},{7,6},{8,11},{9,8},{10,9... | collective-permute-start | bytes 393224 | tf_op jit(solution)/shard_map/ppermute | solution.py:226
  46.1 6.7 %collective-permute-start.19 = (bf16[8,64,128]{2,1,0:T(8,128)(2,1)S(1)}, bf16[8,64,128]{2,1,0:T(8,128)(2,1)S(1)}, u32[]{:S(2)}, u32[]{:S(2)}) collective-permute-start(bf16[8,64,128]{2,1,0:T(8,128)(2,1)S(1)} %get-tuple-element.27.refs_5_), channel_id=1, source_target_pairs={{0,2},{1,3},{2,0},{3,1},{4,6},{5,7},{6,4},{7,5},{8,10},{9,11},{10,... | collective-permute-start | bytes 393224 | tf_op jit(solution)/shard_map/ppermute | solution.py:226
  48.9 5.9 %collective-permute-start.18 = (bf16[8,64,128]{2,1,0:T(8,128)(2,1)S(1)}, bf16[8,64,128]{2,1,0:T(8,128)(2,1)S(1)}, u32[]{:S(2)}, u32[]{:S(2)}) collective-permute-start(bf16[8,64,128]{2,1,0:T(8,128)(2,1)S(1)} %get-tuple-element.27.refs_5_), channel_id=1, source_target_pairs={{0,1},{1,2},{2,3},{3,0},{4,5},{5,6},{6,7},{7,4},{8,9},{9,10},{10,1... | collective-permute-start | bytes 393224 | tf_op jit(solution)/shard_map/ppermute | solution.py:226
  49.1 1.4 %copy-start.1 = (bf16[24,256,128]{2,1,0:T(8,128)(2,1)S(1)}, bf16[24,256,128]{2,1,0:T(8,128)(2,1)}, u32[]{:S(2)}) copy-start(bf16[24,256,128]{2,1,0:T(8,128)(2,1)} %get-tuple-element.28.refs_1_) | copy-start | bytes 4718596
  57.4 22.8 %collective-permute-start.21 = (bf16[4,27,16,256]{3,2,1,0:T(8,128)(2,1)S(1)}, bf16[4,27,16,256]{3,2,1,0:T(8,128)(2,1)S(1)}, u32[]{:S(2)}, u32[]{:S(2)}) collective-permute-start(bf16[4,27,16,256]{3,2,1,0:T(8,128)(2,1)S(1)} %broadcast_select_fusion), channel_id=1, source_target_pairs={{0,16},{16,0},{32,48},{48,32},{64,80},{80,64},{96,112},{112,96},{1... | collective-permute-start | bytes 2654216 | tf_op jit(solution)/shard_map/ppermute | solution.py:242
  57.5 12.2 %collective-permute-start.12 = (bf16[2,4,64,128]{3,2,1,0:T(8,128)(2,1)S(1)}, bf16[2,4,64,128]{3,2,1,0:T(8,128)(2,1)S(1)}, u32[]{:S(2)}, u32[]{:S(2)}) collective-permute-start(bf16[2,4,64,128]{3,2,1,0:T(8,128)(2,1)S(1)} %bitcast.31), channel_id=1, source_target_pairs={{16,0},{32,16},{48,32},{64,48},{80,64},{96,80},{112,96},{128,112},... | collective-permute-start | bytes 393224 | tf_op jit(solution)/shard_map/ppermute | solution.py:12
  69.7 3.8 %collective-permute-start.13 = (bf16[4,1,64,128]{3,2,1,0:T(8,128)(2,1)S(1)}, bf16[4,1,64,128]{3,2,1,0:T(8,128)(2,1)S(1)}, u32[]{:S(2)}, u32[]{:S(2)}) collective-permute-start(bf16[4,1,64,128]{3,2,1,0:T(8,128)(2,1)S(1)} %pad_maximum_fusion.4), channel_id=1, source_target_pairs={{0,4},{4,8},{8,12},{1,5},{5,9},{9,13},{2,6},{6,10},{10,14},{3,7},{... | collective-permute-start | bytes 196616 | tf_op jit(solution)/shard_map/ppermute | solution.py:12
  72.2 6.0 %collective-permute-start.14 = (bf16[4,1,64,128]{3,2,1,0:T(8,128)(2,1)S(1)}, bf16[4,1,64,128]{3,2,1,0:T(8,128)(2,1)S(1)}, u32[]{:S(2)}, u32[]{:S(2)}) collective-permute-start(bf16[4,1,64,128]{3,2,1,0:T(8,128)(2,1)S(1)} %pad_maximum_fusion.5), channel_id=1, source_target_pairs={{4,0},{8,4},{12,8},{5,1},{9,5},{13,9},{6,2},{10,6},{14,10},{7,3},{... | collective-permute-start | bytes 196616 | tf_op jit(solution)/shard_map/ppermute | solution.py:12
  80.7 4.9 %collective-permute-start.24 = (bf16[27,16,256]{2,1,0:T(8,128)(2,1)S(1)}, bf16[27,16,256]{2,1,0:T(8,128)(2,1)S(1)}, u32[]{:S(2)}, u32[]{:S(2)}) collective-permute-start(bf16[27,16,256]{2,1,0:T(8,128)(2,1)S(1)} %get-tuple-element.37), channel_id=1, source_target_pairs={{0,12},{4,0},{8,4},{12,8},{1,13},{5,1},{9,5},{13,9},{2,14},{6,2},{... | collective-permute-start | bytes 663560 | tf_op jit(solution)/shard_map/ppermute | solution.py:226
  80.8 6.4 %collective-permute-start.23 = (bf16[27,16,256]{2,1,0:T(8,128)(2,1)S(1)}, bf16[27,16,256]{2,1,0:T(8,128)(2,1)S(1)}, u32[]{:S(2)}, u32[]{:S(2)}) collective-permute-start(bf16[27,16,256]{2,1,0:T(8,128)(2,1)S(1)} %get-tuple-element.38), channel_id=1, source_target_pairs={{0,8},{4,12},{8,0},{12,4},{1,9},{5,13},{9,1},{13,5},{2,10},{6,14},... | collective-permute-start | bytes 663560 | tf_op jit(solution)/shard_map/ppermute | solution.py:226
  83.2 6.3 %collective-permute-start.22 = (bf16[27,16,256]{2,1,0:T(8,128)(2,1)S(1)}, bf16[27,16,256]{2,1,0:T(8,128)(2,1)S(1)}, u32[]{:S(2)}, u32[]{:S(2)}) collective-permute-start(bf16[27,16,256]{2,1,0:T(8,128)(2,1)S(1)} %get-tuple-element.39), channel_id=1, source_target_pairs={{0,4},{4,8},{8,12},{12,0},{1,5},{5,9},{9,13},{13,1},{2,6},{6,10},{... | collective-permute-start | bytes 663560 | tf_op jit(solution)/shard_map/ppermute | solution.py:226
  90.2 11.6 %collective-permute-start.25 = (bf16[27,8,128]{2,1,0:T(8,128)(2,1)S(1)}, bf16[27,8,128]{2,1,0:T(8,128)(2,1)S(1)}, u32[]{:S(2)}, u32[]{:S(2)}) collective-permute-start(bf16[27,8,128]{2,1,0:T(8,128)(2,1)S(1)} %get-tuple-element.30), channel_id=1, source_target_pairs={{0,32},{16,48},{32,64},{48,80},{64,96},{80,112},{96,0},{112,16},{1... | collective-permute-start | bytes 165896 | tf_op jit(solution)/shard_map/ppermute | solution.py:247
  95.9 8.7 %collective-permute-start.26 = (bf16[27,8,128]{2,1,0:T(8,128)(2,1)S(1)}, bf16[27,8,128]{2,1,0:T(8,128)(2,1)S(1)}, u32[]{:S(2)}, u32[]{:S(2)}) collective-permute-start(bf16[27,8,128]{2,1,0:T(8,128)(2,1)S(1)} %get-tuple-element.31), channel_id=1, source_target_pairs={{0,64},{16,80},{32,96},{48,112},{64,0},{80,16},{96,32},{112,48},{1... | collective-permute-start | bytes 165896 | tf_op jit(solution)/shard_map/ppermute | solution.py:247
  100.2 4.4 %collective-permute-start.27 = (bf16[27,8,128]{2,1,0:T(8,128)(2,1)S(1)}, bf16[27,8,128]{2,1,0:T(8,128)(2,1)S(1)}, u32[]{:S(2)}, u32[]{:S(2)}) collective-permute-start(bf16[27,8,128]{2,1,0:T(8,128)(2,1)S(1)} %get-tuple-element.32), channel_id=1, source_target_pairs={{0,96},{16,112},{32,0},{48,16},{64,32},{80,48},{96,64},{112,80},{1... | collective-permute-start | bytes 165896 | tf_op jit(solution)/shard_map/ppermute | solution.py:247
  104.7 7.1 %collective-permute-start.28 = (bf16[27,8,128]{2,1,0:T(8,128)(2,1)S(1)}, bf16[27,8,128]{2,1,0:T(8,128)(2,1)S(1)}, u32[]{:S(2)}, u32[]{:S(2)}) collective-permute-start(bf16[27,8,128]{2,1,0:T(8,128)(2,1)S(1)} %add_convert_fusion.2), channel_id=1, source_target_pairs={{0,128},{16,144},{32,160},{48,176},{64,192},{80,208},{96,224},{112... | collective-permute-start | bytes 165896 | tf_op jit(solution)/shard_map/ppermute | solution.py:242
  106.3 8.3 %collective-permute-start.15 = (bf16[8,64,128]{2,1,0:T(8,128)(2,1)S(1)}, bf16[8,64,128]{2,1,0:T(8,128)(2,1)S(1)}, u32[]{:S(2)}, u32[]{:S(2)}) collective-permute-start(bf16[8,64,128]{2,1,0:T(8,128)(2,1)S(1)} %get-tuple-element.24), channel_id=1, source_target_pairs={{0,1},{1,2},{2,3},{3,0},{4,5},{5,6},{6,7},{7,4},{8,9},{9,10},{10,1... | collective-permute-start | bytes 393224 | tf_op jit(solution)/shard_map/ppermute | solution.py:226
  106.4 8.4 %collective-permute-start.16 = (bf16[8,64,128]{2,1,0:T(8,128)(2,1)S(1)}, bf16[8,64,128]{2,1,0:T(8,128)(2,1)S(1)}, u32[]{:S(2)}, u32[]{:S(2)}) collective-permute-start(bf16[8,64,128]{2,1,0:T(8,128)(2,1)S(1)} %get-tuple-element.25), channel_id=1, source_target_pairs={{0,2},{1,3},{2,0},{3,1},{4,6},{5,7},{6,4},{7,5},{8,10},{9,11},{10,... | collective-permute-start | bytes 393224 | tf_op jit(solution)/shard_map/ppermute | solution.py:226
  108.2 6.6 %collective-permute-start.17 = (bf16[8,64,128]{2,1,0:T(8,128)(2,1)S(1)}, bf16[8,64,128]{2,1,0:T(8,128)(2,1)S(1)}, u32[]{:S(2)}, u32[]{:S(2)}) collective-permute-start(bf16[8,64,128]{2,1,0:T(8,128)(2,1)S(1)} %get-tuple-element.26), channel_id=1, source_target_pairs={{0,3},{1,0},{2,1},{3,2},{4,7},{5,4},{6,5},{7,6},{8,11},{9,8},{10,9... | collective-permute-start | bytes 393224 | tf_op jit(solution)/shard_map/ppermute | solution.py:226
  111.8 3.5 %collective-permute-start.31 = (bf16[27,8,128]{2,1,0:T(8,128)(2,1)S(1)}, bf16[27,8,128]{2,1,0:T(8,128)(2,1)S(1)}, u32[]{:S(2)}, u32[]{:S(2)}) collective-permute-start(bf16[27,8,128]{2,1,0:T(8,128)(2,1)S(1)} %add_convert_fusion.1.refs_1_), channel_id=1, source_target_pairs={{0,96},{16,112},{32,0},{48,16},{64,32},{80,48},{96,64},{112,80},{1... | collective-permute-start | bytes 165896 | tf_op jit(solution)/shard_map/ppermute | solution.py:247
  112.9 4.5 %collective-permute-start.30 = (bf16[27,8,128]{2,1,0:T(8,128)(2,1)S(1)}, bf16[27,8,128]{2,1,0:T(8,128)(2,1)S(1)}, u32[]{:S(2)}, u32[]{:S(2)}) collective-permute-start(bf16[27,8,128]{2,1,0:T(8,128)(2,1)S(1)} %add_convert_fusion.1.refs_1_), channel_id=1, source_target_pairs={{0,64},{16,80},{32,96},{48,112},{64,0},{80,16},{96,32},{112,48},{1... | collective-permute-start | bytes 165896 | tf_op jit(solution)/shard_map/ppermute | solution.py:247
  114.7 4.8 %collective-permute-start.29 = (bf16[27,8,128]{2,1,0:T(8,128)(2,1)S(1)}, bf16[27,8,128]{2,1,0:T(8,128)(2,1)S(1)}, u32[]{:S(2)}, u32[]{:S(2)}) collective-permute-start(bf16[27,8,128]{2,1,0:T(8,128)(2,1)S(1)} %add_convert_fusion.1.refs_1_), channel_id=1, source_target_pairs={{0,32},{16,48},{32,64},{48,80},{64,96},{80,112},{96,0},{112,16},{1... | collective-permute-start | bytes 165896 | tf_op jit(solution)/shard_map/ppermute | solution.py:247
  114.8 23.4 %copy-start.4 = (bf16[8,64,128]{2,1,0:T(8,128)(2,1)}, bf16[8,64,128]{2,1,0:T(8,128)(2,1)S(1)}, u32[]{:S(2)}) copy-start(bf16[8,64,128]{2,1,0:T(8,128)(2,1)S(1)} %add_convert_fusion) | copy-start | bytes 393220
  120.1 4.9 %collective-permute-start.34 = (bf16[27,16,256]{2,1,0:T(8,128)(2,1)S(1)}, bf16[27,16,256]{2,1,0:T(8,128)(2,1)S(1)}, u32[]{:S(2)}, u32[]{:S(2)}) collective-permute-start(bf16[27,16,256]{2,1,0:T(8,128)(2,1)S(1)} %shard_map.73.refs_1_), channel_id=1, source_target_pairs={{0,12},{4,0},{8,4},{12,8},{1,13},{5,1},{9,5},{13,9},{2,14},{6,2},{... | collective-permute-start | bytes 663560 | tf_op jit(solution)/shard_map/ppermute | solution.py:226
  121.3 6.4 %collective-permute-start.33 = (bf16[27,16,256]{2,1,0:T(8,128)(2,1)S(1)}, bf16[27,16,256]{2,1,0:T(8,128)(2,1)S(1)}, u32[]{:S(2)}, u32[]{:S(2)}) collective-permute-start(bf16[27,16,256]{2,1,0:T(8,128)(2,1)S(1)} %shard_map.73.refs_1_), channel_id=1, source_target_pairs={{0,8},{4,12},{8,0},{12,4},{1,9},{5,13},{9,1},{13,5},{2,10},{6,14},... | collective-permute-start | bytes 663560 | tf_op jit(solution)/shard_map/ppermute | solution.py:226
  123.1 8.3 %collective-permute-start.32 = (bf16[27,16,256]{2,1,0:T(8,128)(2,1)S(1)}, bf16[27,16,256]{2,1,0:T(8,128)(2,1)S(1)}, u32[]{:S(2)}, u32[]{:S(2)}) collective-permute-start(bf16[27,16,256]{2,1,0:T(8,128)(2,1)S(1)} %shard_map.73.refs_1_), channel_id=1, source_target_pairs={{0,4},{4,8},{8,12},{12,0},{1,5},{5,9},{9,13},{13,1},{2,6},{6,10},{... | collective-permute-start | bytes 663560 | tf_op jit(solution)/shard_map/ppermute | solution.py:226
  132.0 6.2 %collective-permute-start.35 = (bf16[27,64,256]{2,1,0:T(8,128)(2,1)S(1)}, bf16[27,64,256]{2,1,0:T(8,128)(2,1)S(1)}, u32[]{:S(2)}, u32[]{:S(2)}) collective-permute-start(bf16[27,64,256]{2,1,0:T(8,128)(2,1)S(1)} %shard_map.74), channel_id=1, source_target_pairs={{0,16},{16,0},{32,48},{48,32},{64,80},{80,64},{96,112},{112,96},{1... | collective-permute-start | bytes 2654216 | tf_op jit(solution)/shard_map/ppermute | solution.py:242

commit v3 on v2

--- a/solution.py
+++ b/solution.py
@@ -41,16 +41,15 @@
     return ahead.astype(jnp.bfloat16), cell, behind.astype(jnp.bfloat16)
 
 
-def forward_body(place, own, early, above, below, weight, panel, pre, act, wide, flat):
-    me = place[0]
+def run_forward(me, own, early, above, below, weight, panel, pre, sent, wide, flat):
     for n in range(9):
         flat[:, n * 256 : n * 256 + 256] = weight[n]
     for f in range(4):
         for r in range(6):
             if r == 0:
-                cell = above[f, 0]
+                cell = above[f, :256]
             elif r == 5:
-                cell = below[f, 0]
+                cell = below[f, :256]
             else:
                 cell = early[f, r - 1] if f < 2 else own[f - 2, r - 1]
             for k in range(4):
@@ -70,16 +69,18 @@
             ahead = jnp.where(lane == 127, 0.0, pltpu.roll(part[128:], 127, 1))
             value = behind + part[64:128] + ahead
             pre[t * 4 + i] = value
-            act[t * 4 + i] = (value * jax.nn.sigmoid(value)).astype(jnp.bfloat16)
-
-
-def spread(own, late, above, below, wide):
+            act = (value * jax.nn.sigmoid(value)).astype(jnp.bfloat16)
+            for out in sent:
+                out[t * 4 + i] = act
+
+
+def spread(own, late, above, below, wide, skip=0):
     for f in range(4):
         for r in range(6):
             if r == 0:
-                cell = above[f, 0]
+                cell = above[f, skip:]
             elif r == 5:
-                cell = below[f, 0]
+                cell = below[f, skip:]
             else:
                 cell = own[f, r - 1] if f < 2 else late[f - 2, r - 1]
             moved = lanes_moved(cell)
@@ -92,62 +93,105 @@
                         wide[row : row + 64, p * 128 : p * 128 + 128] = moved[e]
 
 
-def transposed_body(place, own, late, above, below, weight, mine, one, two, three, wide, full):
-    me = place[0]
-    spread(own, late, above, below, wide)
+def run_transposed(me, weight, wide, full, outs, base):
     full[...] = lax.dot_general(
         weight[...], wide[...], (((0,), (0,)), ((), ())), preferred_element_type=jnp.float32
     )
-    for k, out in enumerate((mine, one, two, three)):
+    for k, out in enumerate(outs):
         at = pl.multiple_of(((me + k) % 4) * 64, 64)
         for p in range(8):
-            out[p] = full[pl.ds(at, 64), p * 128 : p * 128 + 128].astype(out.dtype)
+            block = full[pl.ds(at, 64), p * 128 : p * 128 + 128]
+            out[p + (base if k else 0)] = block.astype(out.dtype)
+
+
+def transposed_body(place, own, late, above, below, weight, mine, one, two, three, wide, full):
+    spread(own, late, above, below, wide)
+    run_transposed(place[0], weight, wide, full, (mine, one, two, three), 0)
+
+
+def opening_body(
+    place, own, early, late, grads, above, below, weight_one, weight_two,
+    panel, pre, mine, one, two, three, tall, flat, wide, full,
+):
+    me = place[0]
+    spread(grads, late, above, below, wide, 256)
+    run_transposed(me, weight_two, wide, full, (mine, one, two, three), 8)
+    run_forward(me, own, early, above, below, weight_one, panel, pre, (one, two, three), tall, flat)
+
+
+def frame_rows_body(place, early, own, grads, late, heads, tails):
+    for f in range(4):
+        cells = (early, f) if f < 2 else (own, f - 2)
+        others = (grads, f) if f < 2 else (late, f - 2)
+        for row, out in ((0, heads), (3, tails)):
+            out[f, :256] = cells[0][cells[1], row]
+            out[f, 256:] = others[0][others[1], row]
+
+
+def gradient_rows_body(place, own, late, heads, tails):
+    for f in range(4):
+        cells = (own, f) if f < 2 else (late, f - 2)
+        for row, out in ((0, heads), (3, tails)):
+            out[f] = cells[0][cells[1], row]
 
 
 def against(left, right):
     return lax.dot_general(left, right, (((1,), (1,)), ((), ())), preferred_element_type=jnp.float32)
 
 
-def store_filter(out, height, tap, rows):
+def store_filter(both, slot, height, tap, rows):
     for q in range(4):
-        out[(q + 4 - height) % 4, tap] = rows[q * 16 : q * 16 + 16].astype(jnp.bfloat16)
-
-
-def first_filter_body(place, panel, gradient, out, moved):
-    height = place[1]
+        both[slot, (q + 4 - height) % 4, tap] = rows[q * 16 : q * 16 + 16].astype(jnp.bfloat16)
+
+
+def filters_body(
+    place, panel, pre, mine, r1, r2, r3, sent, own, late, above, below,
+    gradient, keep, give, moved, wide, acts, both,
+):
+    me, height, core = place[0], place[1], place[3]
     for p in range(8):
-        for e, part in enumerate(lanes_moved(gradient[p])):
+        value = pre[p]
+        sig = jax.nn.sigmoid(value)
+        total = mine[p]
+        for part in (r1, r2, r3):
+            total = total + part[8 + p].astype(jnp.float32)
+        total = (total * sig * (1.0 + value * (1.0 - sig))).astype(jnp.bfloat16)
+        gradient[p // 4, p % 4] = total
+        for e, part in enumerate(lanes_moved(total)):
             moved[e * 64 : e * 64 + 64, p * 128 : p * 128 + 128] = part
     for n, (a, b) in enumerate(TAPS):
         window = jnp.concatenate([panel[(t + a) * 6 + i + b] for t, i in SPOTS], 1)
         sums = against(moved[...], window)
         for e in range(3):
-            store_filter(out, height, n * 3 + e, sums[e * 64 : e * 64 + 64])
-
-
-def second_filter_body(place, own, late, above, below, a0, a1, a2, a3, out, wide, acts):
-    me, height = place[0], place[1]
-    spread(own, late, above, below, wide)
-    for k, part in enumerate((a0, a1, a2, a3)):
+            store_filter(both, core, height, n * 3 + e, sums[e * 64 : e * 64 + 64])
+    spread(own, late, above, below, wide, 256)
+    for k, part in enumerate((sent, r1, r2, r3)):
         at = pl.multiple_of(((me + 4 - k) % 4) * 64, 64)
         for p in range(8):
             acts[pl.ds(at, 64), p * 128 : p * 128 + 128] = part[p]
     for n in range(9):
         sums = against(wide[n * 192 : n * 192 + 192], acts[...])
         for e in range(3):
-            store_filter(out, height, n * 3 + e, sums[e * 64 : e * 64 + 64])
+            store_filter(both, 1 - core, height, n * 3 + e, sums[e * 64 : e * 64 + 64])
+    keep[...] = both[0]
+    give[...] = both[1]
 
 
 def shaped(shape, dtype):
     return jax.ShapeDtypeStruct(shape, dtype)
 
 
-def forward(place, own, early, above, below, weight, after):
-    return call(
-        forward_body,
-        [shaped((24, 256, 128), jnp.bfloat16), shaped((8, 64, 128), jnp.float32), shaped((8, 64, 128), jnp.bfloat16)],
-        [pltpu.VMEM((2304, 1024), jnp.bfloat16), pltpu.VMEM((192, 2304), jnp.bfloat16)],
-        place, own, early, above, below, weight, after=after,
+def opening(place, *operands):
+    return call(
+        opening_body,
+        [shaped((24, 256, 128), jnp.bfloat16)]
+        + [shaped((8, 64, 128), jnp.float32)] * 2
+        + [shaped((16, 64, 128), jnp.bfloat16)] * 3,
+        [
+            pltpu.VMEM((2304, 1024), jnp.bfloat16), pltpu.VMEM((192, 2304), jnp.bfloat16),
+            pltpu.VMEM((1728, 1024), jnp.bfloat16), pltpu.VMEM((256, 1024), jnp.float32),
+        ],
+        place, *operands,
     )
 
 
@@ -160,19 +204,25 @@
     )
 
 
-def first_filter(place, panel, gradient):
-    return call(
-        first_filter_body, [shaped((4, 27, 16, 256), jnp.bfloat16)],
-        [pltpu.VMEM((192, 1024), jnp.bfloat16)], place, panel, gradient,
-    )[0]
-
-
-def second_filter(place, cells, acts):
-    return call(
-        second_filter_body, [shaped((4, 27, 16, 256), jnp.bfloat16)],
-        [pltpu.VMEM((1728, 1024), jnp.bfloat16), pltpu.VMEM((256, 1024), jnp.bfloat16)],
-        place, *cells, *acts,
-    )[0]
+def frame_rows(place, *operands):
+    return call(frame_rows_body, [shaped((4, 320, 128), jnp.bfloat16)] * 2, [], place, *operands)
+
+
+def gradient_rows(place, own, late, after):
+    rows = [shaped((4, 64, 128), jnp.bfloat16)] * 2
+    return call(gradient_rows_body, rows, [], place, own, late, after=after)
+
+
+def filters(place, *operands):
+    return call(
+        filters_body,
+        [shaped((2, 4, 64, 128), jnp.bfloat16)] + [shaped((4, 27, 16, 256), jnp.bfloat16)] * 2,
+        [
+            pltpu.VMEM((192, 1024), jnp.bfloat16), pltpu.VMEM((1728, 1024), jnp.bfloat16),
+            pltpu.VMEM((256, 1024), jnp.bfloat16), pltpu.VMEM((2, 4, 27, 16, 256), jnp.bfloat16),
+        ],
+        place, *operands,
+    )
 
 
 def quarters_body(place, own, one, two, three, mine, first, second, third, sums):
@@ -247,10 +297,8 @@
     return lax.ppermute(block, "tm", route)
 
 
-def summed_pair(part_one, part_two, core):
-    mine = jnp.where(core == 1, part_two, part_one)
-    theirs = jnp.where(core == 1, part_one, part_two)
-    total = mine.astype(jnp.float32) + swapped(theirs, 1).astype(jnp.float32)
+def summed_pair(keep, give):
+    total = keep.astype(jnp.float32) + swapped(give, 1).astype(jnp.float32)
     return [total[0]] + [total[k].astype(jnp.bfloat16) for k in range(1, 4)]
 
 
@@ -275,40 +323,32 @@
     return flat.reshape(3, 3, 3, 64, 256).transpose(3, 0, 1, 2, 4)
 
 
-def edges(first, second):
-    last = first.shape[1] - 1
-    heads = jnp.concatenate([first[:, :1], second[:, :1]], 0)
-    tails = jnp.concatenate([first[:, last:], second[:, last:]], 0)
+def traded(heads, tails):
     return passed_along(tails, "height", 1), passed_along(heads, "height", -1)
-
-
-def with_later(cells):
-    late = passed_along(cells, "tm", -1)
-    return (cells, late) + edges(cells, late)
 
 
 def on_device(frames, grad_out, weight_one, weight_two):
     spot = lax.axis_index("tm")
     core = spot % 2
-    place = jnp.stack([lax.axis_index("chan"), lax.axis_index("height"), (spot // 2) % 4]).astype(jnp.int32)
+    place = jnp.stack([lax.axis_index("chan"), lax.axis_index("height"), (spot // 2) % 4, core])
+    place = place.astype(jnp.int32)
     taps_one = weight_one.transpose(1, 2, 3, 0, 4).reshape(1728, 256)
     taps_two = weight_two.transpose(1, 2, 3, 0, 4).reshape(1728, 256)
     frames_all = jnp.concatenate([frames] + all_rotated(frames, "chan"), 2)
     early = passed_along(frames_all, "tm", 1)
-    above, below = edges(early, frames_all)
-    grads = with_later(grad_out)
-    act_pieces = transposed(place, grads, taps_two)
-    panel, pre, act = forward(
-        place, frames_all, early, above, below, taps_one.reshape(9, 192, 256), [act_pieces[0]]
-    )
-    grad_act = exchanged(act_pieces, "chan")
-    sigmoid_pre = jax.nn.sigmoid(pre)
-    grad_pre = (grad_act * sigmoid_pre * (1.0 + pre * (1.0 - sigmoid_pre))).astype(jnp.bfloat16)
-    part_one = first_filter(place, panel, grad_pre)
-    part_two = second_filter(place, grads, [act] + all_rotated(act, "chan"))
-    pieces = summed_pair(part_one, part_two, core)
-    cells = with_later(grad_pre.reshape(2, 4, 64, 128))
-    gradient_pieces = transposed(place, cells, taps_one)
+    late = passed_along(grad_out, "tm", -1)
+    above, below = traded(*frame_rows(place, early, frames_all, grad_out, late))
+    panel, pre, mine, *sent = opening(
+        place, frames_all, early, late, grad_out, above, below, taps_one.reshape(9, 192, 256), taps_two
+    )
+    received = [rotated(part, "chan", k + 1) for k, part in enumerate(sent)]
+    grad_pre, keep, give = filters(
+        place, panel, pre, mine, *received, sent[0], grad_out, late, above, below
+    )
+    pieces = summed_pair(keep, give)
+    later = passed_along(grad_pre, "tm", -1)
+    edges = traded(*gradient_rows(place, grad_pre, later, [pieces[1]]))
+    gradient_pieces = transposed(place, (grad_pre, later) + edges, taps_one)
     grad_frames, grad_one, grad_two = rest_of_sum(place, pieces, gradient_pieces, core)
     return (grad_frames, filter_shape(grad_one), filter_shape(grad_two))
 

time: 141 us -> 139 us (0.986)
  waiting for transfers between devices: 53.8 us -> 58.9 us
  starting transfers between devices: 62.5 us -> 57.6 us
  other arithmetic: 4.77 us -> 2.91 us
  local copies, waits for them, and re-layouts: 3.41 us -> 2 us
    ppermute x18 -> x15, waiting for transfers between devices: 16.6 us -> 26.9 us  [rotated(): lax.ppermute(block, axis, [(i, (i + distance) % count) for i in range(cou...]
    ppermute x9 -> x7, waiting for transfers between devices: 23.3 us -> 18.1 us  [passed_along(): return lax.ppermute(block, axis, route)]
    ppermute x9 -> x7, starting transfers between devices: 22.6 us -> 17.7 us  [passed_along(): return lax.ppermute(block, axis, route)]
    ppermute x18 -> x15, starting transfers between devices: 21 us -> 25.4 us  [rotated(): lax.ppermute(block, axis, [(i, (i + distance) % count) for i in range(cou...]
    ppermute x3, starting transfers between devices: 5.92 us -> 3.03 us  [swapped(): lax.ppermute(block, 'tm', [(i, i ^ distance) for i in range(lax.axis_size...]
    ppermute x6, starting transfers between devices: 12.9 us -> 11.4 us  [quad_rotated(): return lax.ppermute(block, 'tm', route)]
    concatenate x6 -> x0, other arithmetic: 1.49 us -> none  [the longest x3 0.75 us: edges(): heads = jnp.concatenate([first[:, :1], second[:, :1]], 0)]
  transfers between devices with their start and end apart: 36 -> 31, of which waited for: 18 -> 23; matrix products, arithmetic and copies ran while one was open for 3% -> 1% of each run, Pallas kernels for 8% -> 2%
where the time goes in v3:
time: 139 us
  waiting for transfers between devices  58.9 us (42%)
  starting transfers between devices  57.6 us (41%)
  Pallas kernels  16.4 us (12%)
  other arithmetic  2.91 us (2%)
  local copies, waits for them, and re-layouts  2 us (1%)
    ppermute x15, waiting for transfers between devices, rotated(): lax.ppermute(block, axis, [(i, (i + distance) % count) for i in range(cou...  26.9 us
    ppermute x15, starting transfers between devices, rotated(): lax.ppermute(block, axis, [(i, (i + distance) % count) for i in range(cou...  25.4 us
    ppermute x7, waiting for transfers between devices, passed_along(): return lax.ppermute(block, axis, route)  18.1 us
    ppermute x7, starting transfers between devices, passed_along(): return lax.ppermute(block, axis, route)  17.7 us
    pallas_call x8, Pallas kernels, call(): pl.pallas_call(lambda *refs: body(*refs[:used], *refs[rest:]), out_shape=...  16.4 us
    ppermute x6, starting transfers between devices, quad_rotated(): return lax.ppermute(block, 'tm', route)  11.4 us
    ppermute x6, waiting for transfers between devices, quad_rotated(): return lax.ppermute(block, 'tm', route)  9.15 us
    ppermute x3, waiting for transfers between devices, swapped(): lax.ppermute(block, 'tm', [(i, i ^ distance) for i in range(lax.axis_size...  4.79 us
  transfers between devices with their start and end apart: 31, of which 23 were waited for; matrix products, arithmetic and copies ran while one was open for 1% of the time, Pallas kernels for 2%

profile of v3, /device:TPU:1, one launch (start us, length us, event | category | flops | bytes accessed | tf_op | source)
XLA Modules:
  0.0 138.6 jit_solution(4333220529579489242)
XLA Ops:
  0.6 2.2 %collective-permute-start = (bf16[2,4,64,128]{3,2,1,0:T(8,128)(2,1)}, bf16[2,4,64,128]{3,2,1,0:T(8,128)(2,1)S(1)}, u32[]{:S(2)}, u32[]{:S(2)}) collective-permute-start(bf16[2,4,64,128]{3,2,1,0:T(8,128)(2,1)} %param.4), channel_id=1, source_target_pairs={{0,1},{1,2},{2,3},{3,0},{4,5},{5,6},{6,7},{7,4},{8,9},{9,10},{10,1... | collective-permute-start | bytes 393224 | tf_op jit(solution)/shard_map/ppermute | solution.py:276
  2.8 2.6 %collective-permute-start.1 = (bf16[2,4,64,128]{3,2,1,0:T(8,128)(2,1)}, bf16[2,4,64,128]{3,2,1,0:T(8,128)(2,1)S(1)}, u32[]{:S(2)}, u32[]{:S(2)}) collective-permute-start(bf16[2,4,64,128]{3,2,1,0:T(8,128)(2,1)} %param.4), channel_id=1, source_target_pairs={{0,2},{1,3},{2,0},{3,1},{4,6},{5,7},{6,4},{7,5},{8,10},{9,11},{10,... | collective-permute-start | bytes 393224 | tf_op jit(solution)/shard_map/ppermute | solution.py:276
  5.5 1.1 collective-permute-start.2
  6.5 0.9 constant_dynamic-update-slice_fusion.3
  7.5 3.9 %collective-permute-done.1 = bf16[2,4,64,128]{3,2,1,0:T(8,128)(2,1)S(1)} collective-permute-done((bf16[2,4,64,128]{3,2,1,0:T(8,128)(2,1)}, bf16[2,4,64,128]{3,2,1,0:T(8,128)(2,1)S(1)}, u32[]{:S(2)}, u32[]{:S(2)}) %collective-permute-start.1) | collective-permute-done | bytes 131104 | tf_op jit(solution)/shard_map/ppermute | solution.py:276
  11.4 5.0 %collective-permute-start.3 = (bf16[2,4,256,128]{3,2,1,0:T(8,128)(2,1)S(1)}, bf16[2,4,256,128]{3,2,1,0:T(8,128)(2,1)S(1)}, u32[]{:S(2)}, u32[]{:S(2)}) collective-permute-start(bf16[2,4,256,128]{3,2,1,0:T(8,128)(2,1)S(1)} %constant_dynamic-update-slice_fusion.refs_2_.refs_1_), channel_id=1, source_target_pairs={{0,16},{16,32},{32,48},{48,64},{64,80},{80,96},{96,112},{112,128},... | collective-permute-start | bytes 1572872 | tf_op jit(solution)/shard_map/ppermute | solution.py:12
  16.4 1.9 %collective-permute-start.4 = (bf16[2,4,64,128]{3,2,1,0:T(8,128)(2,1)}, bf16[2,4,64,128]{3,2,1,0:T(8,128)(2,1)S(1)}, u32[]{:S(2)}, u32[]{:S(2)}) collective-permute-start(bf16[2,4,64,128]{3,2,1,0:T(8,128)(2,1)} %refs_8_.1), channel_id=1, source_target_pairs={{16,0},{32,16},{48,32},{64,48},{80,64},{96,80},{112,96},{128,112},... | collective-permute-start | bytes 393224 | tf_op jit(solution)/shard_map/ppermute | solution.py:12
  18.5 4.5 %collective-permute-done.4.refs_4_.refs_3_.refs_9_ = bf16[2,4,64,128]{3,2,1,0:T(8,128)(2,1)S(1)} collective-permute-done((bf16[2,4,64,128]{3,2,1,0:T(8,128)(2,1)}, bf16[2,4,64,128]{3,2,1,0:T(8,128)(2,1)S(1)}, u32[]{:S(2)}, u32[]{:S(2)}) %collective-permute-start.4) | collective-permute-done | bytes 131104 | tf_op jit(solution)/shard_map/ppermute | solution.py:12
  22.9 0.9 copy-done.1
  23.8 0.6 shard_map.67
  24.4 3.1 %collective-permute-start.5 = (bf16[4,320,128]{2,1,0:T(8,128)(2,1)S(1)}, bf16[4,320,128]{2,1,0:T(8,128)(2,1)S(1)}, u32[]{:S(2)}, u32[]{:S(2)}) collective-permute-start(bf16[4,320,128]{2,1,0:T(8,128)(2,1)S(1)} %get-tuple-element.24), channel_id=1, source_target_pairs={{0,4},{4,8},{8,12},{1,5},{5,9},{9,13},{2,6},{6,10},{10,14},{3,7},{... | collective-permute-start | bytes 983048 | tf_op jit(solution)/shard_map/ppermute | solution.py:12
  27.6 1.3 collective-permute-start.6
  28.9 3.6 %collective-permute-done.5.refs_5_.refs_10_ = bf16[4,320,128]{2,1,0:T(8,128)(2,1)S(1)} collective-permute-done((bf16[4,320,128]{2,1,0:T(8,128)(2,1)S(1)}, bf16[4,320,128]{2,1,0:T(8,128)(2,1)S(1)}, u32[]{:S(2)}, u32[]{:S(2)}) %collective-permute-start.5) | collective-permute-done | bytes 327712 | tf_op jit(solution)/shard_map/ppermute | solution.py:12
  32.5 4.1 %collective-permute-done.6.refs_6_.refs_11_ = bf16[4,320,128]{2,1,0:T(8,128)(2,1)S(1)} collective-permute-done((bf16[4,320,128]{2,1,0:T(8,128)(2,1)S(1)}, bf16[4,320,128]{2,1,0:T(8,128)(2,1)S(1)}, u32[]{:S(2)}, u32[]{:S(2)}) %collective-permute-start.6) | collective-permute-done | bytes 327712 | tf_op jit(solution)/shard_map/ppermute | solution.py:12
  36.6 5.4 %shard_map.68 = (bf16[24,256,128]{2,1,0:T(8,128)(2,1)}, f32[8,64,128]{2,1,0:T(8,128)S(1)}, f32[8,64,128]{2,1,0:T(8,128)S(1)}, bf16[16,64,128]{2,1,0:T(8,128)(2,1...) custom-call(s32[4]{0:T(128)S(1)} %pad_add_fusion.refs_0_, ...), custom_call_target="tpu_custom_call" | custom-call | tf_op jit(solution)/shard_map/pallas_call | solution.py:24
  42.0 2.3 %collective-permute-start.8 = (bf16[16,64,128]{2,1,0:T(8,128)(2,1)S(1)}, bf16[16,64,128]{2,1,0:T(8,128)(2,1)S(1)}, u32[]{:S(2)}, u32[]{:S(2)}) collective-permute-start(bf16[16,64,128]{2,1,0:T(8,128)(2,1)S(1)} %get-tuple-element.30), channel_id=1, source_target_pairs={{0,2},{1,3},{2,0},{3,1},{4,6},{5,7},{6,4},{7,5},{8,10},{9,11},{10,... | collective-permute-start | bytes 786440 | tf_op jit(solution)/shard_map/ppermute | solution.py:276
  44.2 1.1 collective-permute-start.9
  45.3 0.4 collective-permute-start.7
  45.7 5.8 %collective-permute-done.8.refs_5_ = bf16[16,64,128]{2,1,0:T(8,128)(2,1)S(1)} collective-permute-done((bf16[16,64,128]{2,1,0:T(8,128)(2,1)S(1)}, bf16[16,64,128]{2,1,0:T(8,128)(2,1)S(1)}, u32[]{:S(2)}, u32[]{:S(2)}) %collective-permute-start.8) | collective-permute-done | bytes 262176 | tf_op jit(solution)/shard_map/ppermute | solution.py:276
  51.5 4.2 %collective-permute-done.9.refs_6_ = bf16[16,64,128]{2,1,0:T(8,128)(2,1)S(1)} collective-permute-done((bf16[16,64,128]{2,1,0:T(8,128)(2,1)S(1)}, bf16[16,64,128]{2,1,0:T(8,128)(2,1)S(1)}, u32[]{:S(2)}, u32[]{:S(2)}) %collective-permute-start.9) | collective-permute-done | bytes 262176 | tf_op jit(solution)/shard_map/ppermute | solution.py:276
  55.7 0.4 collective-permute-done.7.refs_4_
  56.2 5.9 %shard_map.69 = (bf16[2,4,64,128]{3,2,1,0:T(8,128)(2,1)S(1)}, bf16[4,27,16,256]{3,2,1,0:T(8,128)(2,1)S(1)}, bf16[4,27,16,256]{3,2,1,0:T(8,128)(2,1)}) custom-call(s32[4]{0:T(128)S(1)} %pad_add_fusion.refs_0_, bf16[24,256,128]{2,1,0:T(8,128)(2,1)} %get-tuple-element.26.refs_1_, f32[8,64,128]{2,1,0:T(8,128)S(1)} %get-tuple-element.27.refs_2_, ...), custom_call_target="tpu_custom_call" | custom-call | tf_op jit(solution)/shard_map/pallas_call | solution.py:24
  62.1 0.4 collective-permute-start.11
  62.5 2.0 %collective-permute-start.10 = (bf16[2,4,64,128]{3,2,1,0:T(8,128)(2,1)S(1)}, bf16[2,4,64,128]{3,2,1,0:T(8,128)(2,1)S(1)}, u32[]{:S(2)}, u32[]{:S(2)}) collective-permute-start(bf16[2,4,64,128]{3,2,1,0:T(8,128)(2,1)S(1)} %get-tuple-element.32.refs_1_), channel_id=1, source_target_pairs={{16,0},{32,16},{48,32},{64,48},{80,64},{96,80},{112,96},{128,112},... | collective-permute-start | bytes 393224 | tf_op jit(solution)/shard_map/ppermute | solution.py:12
  64.5 0.2 collective-permute-done.11
  64.7 0.3 convert_add_fusion
  65.1 1.3 collective-permute-start.17
  66.4 5.3 %collective-permute-done.10.refs_2_ = bf16[2,4,64,128]{3,2,1,0:T(8,128)(2,1)S(1)} collective-permute-done((bf16[2,4,64,128]{3,2,1,0:T(8,128)(2,1)S(1)}, bf16[2,4,64,128]{3,2,1,0:T(8,128)(2,1)S(1)}, u32[]{:S(2)}, u32[]{:S(2)}) %collective-permute-start.10) | collective-permute-done | bytes 131104 | tf_op jit(solution)/shard_map/ppermute | solution.py:12
  71.7 0.5 shard_map.70
  72.3 3.1 %collective-permute-start.12 = (bf16[4,64,128]{2,1,0:T(8,128)(2,1)S(1)}, bf16[4,64,128]{2,1,0:T(8,128)(2,1)S(1)}, u32[]{:S(2)}, u32[]{:S(2)}) collective-permute-start(bf16[4,64,128]{2,1,0:T(8,128)(2,1)S(1)} %get-tuple-element.35), channel_id=1, source_target_pairs={{0,4},{4,8},{8,12},{1,5},{5,9},{9,13},{2,6},{6,10},{10,14},{3,7},{... | collective-permute-start | bytes 196616 | tf_op jit(solution)/shard_map/ppermute | solution.py:12
  75.4 1.3 collective-permute-start.13
  76.7 2.4 %collective-permute-start.19 = (bf16[27,16,256]{2,1,0:T(8,128)(2,1)S(1)}, bf16[27,16,256]{2,1,0:T(8,128)(2,1)S(1)}, u32[]{:S(2)}, u32[]{:S(2)}) collective-permute-start(bf16[27,16,256]{2,1,0:T(8,128)(2,1)S(1)} %get-tuple-element.49), channel_id=1, source_target_pairs={{0,12},{4,0},{8,4},{12,8},{1,13},{5,1},{9,5},{13,9},{2,14},{6,2},{... | collective-permute-start | bytes 663560 | tf_op jit(solution)/shard_map/ppermute | solution.py:276
  79.1 1.7 %collective-permute-start.18 = (bf16[27,16,256]{2,1,0:T(8,128)(2,1)S(1)}, bf16[27,16,256]{2,1,0:T(8,128)(2,1)S(1)}, u32[]{:S(2)}, u32[]{:S(2)}) collective-permute-start(bf16[27,16,256]{2,1,0:T(8,128)(2,1)S(1)} %get-tuple-element.50), channel_id=1, source_target_pairs={{0,8},{4,12},{8,0},{12,4},{1,9},{5,13},{9,1},{13,5},{2,10},{6,14},... | collective-permute-start | bytes 663560 | tf_op jit(solution)/shard_map/ppermute | solution.py:276
  80.8 0.6 collective-permute-done.13.refs_4_
  81.4 2.0 %shard_map.71 = (f32[8,64,128]{2,1,0:T(8,128)S(1)}, bf16[8,64,128]{2,1,0:T(8,128)(2,1)S(1)}, bf16[8,64,128]{2,1,0:T(8,128)(2,1)S(1)}, bf16[8,64,128]{2,1,0:T(8,128)(2,1)S(1)}) custom-call(s32[4]{0:T(128)S(1)} %pad_add_fusion.refs_0_, bf16[2,4,64,128]{3,2,1,0:T(8,128)(2,1)S(1)} %get-tuple-element.32.refs_1_, ...), custom_call_target="tpu_custom_call" | custom-call | tf_op jit(solution)/shard_map/pallas_call | solution.py:24
  83.5 0.6 collective-permute-done.19.refs_4_
  84.1 1.3 collective-permute-done.18.refs_3_
  85.4 0.7 shard_map.72
  86.1 3.8 %collective-permute-start.20 = (bf16[27,8,128]{2,1,0:T(8,128)(2,1)S(1)}, bf16[27,8,128]{2,1,0:T(8,128)(2,1)S(1)}, u32[]{:S(2)}, u32[]{:S(2)}) collective-permute-start(bf16[27,8,128]{2,1,0:T(8,128)(2,1)S(1)} %get-tuple-element.42), channel_id=1, source_target_pairs={{0,32},{16,48},{32,64},{48,80},{64,96},{80,112},{96,0},{112,16},{1... | collective-permute-start | bytes 165896 | tf_op jit(solution)/shard_map/ppermute | solution.py:297
  89.9 5.0 %collective-permute-start.21 = (bf16[27,8,128]{2,1,0:T(8,128)(2,1)S(1)}, bf16[27,8,128]{2,1,0:T(8,128)(2,1)S(1)}, u32[]{:S(2)}, u32[]{:S(2)}) collective-permute-start(bf16[27,8,128]{2,1,0:T(8,128)(2,1)S(1)} %get-tuple-element.43), channel_id=1, source_target_pairs={{0,64},{16,80},{32,96},{48,112},{64,0},{80,16},{96,32},{112,48},{1... | collective-permute-start | bytes 165896 | tf_op jit(solution)/shard_map/ppermute | solution.py:297
  94.9 1.9 %collective-permute-done.20 = bf16[27,8,128]{2,1,0:T(8,128)(2,1)S(1)} collective-permute-done((bf16[27,8,128]{2,1,0:T(8,128)(2,1)S(1)}, bf16[27,8,128]{2,1,0:T(8,128)(2,1)S(1)}, u32[]{:S(2)}, u32[]{:S(2)}) %collective-permute-start.20) | collective-permute-done | bytes 55328 | tf_op jit(solution)/shard_map/ppermute | solution.py:297
  96.8 2.1 %collective-permute-done.21 = bf16[27,8,128]{2,1,0:T(8,128)(2,1)S(1)} collective-permute-done((bf16[27,8,128]{2,1,0:T(8,128)(2,1)S(1)}, bf16[27,8,128]{2,1,0:T(8,128)(2,1)S(1)}, u32[]{:S(2)}, u32[]{:S(2)}) %collective-permute-start.21) | collective-permute-done | bytes 55328 | tf_op jit(solution)/shard_map/ppermute | solution.py:297
  98.9 0.9 collective-permute-done.22
  99.8 0.1 collective-permute-start.23
  99.9 1.0 collective-permute-start.14
  100.9 2.1 %collective-permute-start.15 = (bf16[8,64,128]{2,1,0:T(8,128)(2,1)S(1)}, bf16[8,64,128]{2,1,0:T(8,128)(2,1)S(1)}, u32[]{:S(2)}, u32[]{:S(2)}) collective-permute-start(bf16[8,64,128]{2,1,0:T(8,128)(2,1)S(1)} %get-tuple-element.39), channel_id=1, source_target_pairs={{0,2},{1,3},{2,0},{3,1},{4,6},{5,7},{6,4},{7,5},{8,10},{9,11},{10,... | collective-permute-start | bytes 393224 | tf_op jit(solution)/shard_map/ppermute | solution.py:276
  103.0 1.3 collective-permute-start.16
  104.3 2.5 %collective-permute-done.23 = bf16[27,8,128]{2,1,0:T(8,128)(2,1)S(1)} collective-permute-done((bf16[27,8,128]{2,1,0:T(8,128)(2,1)S(1)}, bf16[27,8,128]{2,1,0:T(8,128)(2,1)S(1)}, u32[]{:S(2)}, u32[]{:S(2)}) %collective-permute-start.23) | collective-permute-done | bytes 55328 | tf_op jit(solution)/shard_map/ppermute | solution.py:292
  106.8 2.2 %collective-permute-start.26 = (bf16[27,8,128]{2,1,0:T(8,128)(2,1)S(1)}, bf16[27,8,128]{2,1,0:T(8,128)(2,1)S(1)}, u32[]{:S(2)}, u32[]{:S(2)}) collective-permute-start(bf16[27,8,128]{2,1,0:T(8,128)(2,1)S(1)} %add_convert_fusion.1.refs_1_), channel_id=1, source_target_pairs={{0,96},{16,112},{32,0},{48,16},{64,32},{80,48},{96,64},{112,80},{1... | collective-permute-start | bytes 165896 | tf_op jit(solution)/shard_map/ppermute | solution.py:297
  109.0 0.4 collective-permute-start.24
  109.4 0.8 collective-permute-done.26.refs_4_
  110.2 3.0 %collective-permute-done.25.refs_3_ = bf16[27,8,128]{2,1,0:T(8,128)(2,1)S(1)} collective-permute-done((bf16[27,8,128]{2,1,0:T(8,128)(2,1)S(1)}, bf16[27,8,128]{2,1,0:T(8,128)(2,1)S(1)}, u32[]{:S(2)}, u32[]{:S(2)}) %collective-permute-start.25) | collective-permute-done | bytes 55328 | tf_op jit(solution)/shard_map/ppermute | solution.py:297
  113.2 0.6 collective-permute-done.24.refs_2_
  113.8 0.6 shard_map.73.refs_1_
  114.4 5.0 %collective-permute-start.29 = (bf16[27,16,256]{2,1,0:T(8,128)(2,1)S(1)}, bf16[27,16,256]{2,1,0:T(8,128)(2,1)S(1)}, u32[]{:S(2)}, u32[]{:S(2)}) collective-permute-start(bf16[27,16,256]{2,1,0:T(8,128)(2,1)S(1)} %shard_map.73.refs_1_), channel_id=1, source_target_pairs={{0,12},{4,0},{8,4},{12,8},{1,13},{5,1},{9,5},{13,9},{2,14},{6,2},{... | collective-permute-start | bytes 663560 | tf_op jit(solution)/shard_map/ppermute | solution.py:276
  119.4 1.0 collective-permute-start.28
  120.4 4.7 %collective-permute-done.29.refs_4_ = bf16[27,16,256]{2,1,0:T(8,128)(2,1)S(1)} collective-permute-done((bf16[27,16,256]{2,1,0:T(8,128)(2,1)S(1)}, bf16[27,16,256]{2,1,0:T(8,128)(2,1)S(1)}, u32[]{:S(2)}, u32[]{:S(2)}) %collective-permute-start.29) | collective-permute-done | bytes 221216 | tf_op jit(solution)/shard_map/ppermute | solution.py:276
  125.1 0.7 collective-permute-done.28.refs_3_
  125.8 5.2 %collective-permute-done.27.refs_2_ = bf16[27,16,256]{2,1,0:T(8,128)(2,1)S(1)} collective-permute-done((bf16[27,16,256]{2,1,0:T(8,128)(2,1)S(1)}, bf16[27,16,256]{2,1,0:T(8,128)(2,1)S(1)}, u32[]{:S(2)}, u32[]{:S(2)}) %collective-permute-start.27) | collective-permute-done | bytes 221216 | tf_op jit(solution)/shard_map/ppermute | solution.py:276
  131.0 0.6 shard_map.74
  131.7 2.5 %collective-permute-start.30 = (bf16[27,64,256]{2,1,0:T(8,128)(2,1)S(1)}, bf16[27,64,256]{2,1,0:T(8,128)(2,1)S(1)}, u32[]{:S(2)}, u32[]{:S(2)}) collective-permute-start(bf16[27,64,256]{2,1,0:T(8,128)(2,1)S(1)} %shard_map.74), channel_id=1, source_target_pairs={{0,16},{16,0},{32,48},{48,32},{64,80},{80,64},{96,112},{112,96},{1... | collective-permute-start | bytes 2654216 | tf_op jit(solution)/shard_map/ppermute | solution.py:292
  134.2 2.1 %collective-permute-done.30 = bf16[27,64,256]{2,1,0:T(8,128)(2,1)S(1)} collective-permute-done((bf16[27,64,256]{2,1,0:T(8,128)(2,1)S(1)}, bf16[27,64,256]{2,1,0:T(8,128)(2,1)S(1)}, u32[]{:S(2)}, u32[]{:S(2)}) %collective-permute-start.30) | collective-permute-done | bytes 884768 | tf_op jit(solution)/shard_map/ppermute | solution.py:292
  136.3 0.1 broadcast_select_fusion
  136.4 2.2 %convert_bitcast_fusion = (f32[64,3,3,3,256]{4,0,3,2,1:T(8,128)}, f32[64,3,3,3,256]{4,0,3,2,1:T(8,128)}) fusion(bf16[3,3,3,64,256]{4,3,2,1,0:T(8,128)(2,1)S(1)} %bitcast.33, bf16[3,3,3,64,256]{4,3,2,1,0:T(8,128)(2,1)S(1)} %bitcast.34), kind=kLoop, calls=%fused_computation | loop fusion | flops 884736 | bytes 5308416 | tf_op jit(solution)/shard_map/transpose | solution.py:323
  (25 shorter events, 0.4 us)
Async XLA Ops:
  0.6 6.8 %collective-permute-start = (bf16[2,4,64,128]{3,2,1,0:T(8,128)(2,1)}, bf16[2,4,64,128]{3,2,1,0:T(8,128)(2,1)S(1)}, u32[]{:S(2)}, u32[]{:S(2)}) collective-permute-start(bf16[2,4,64,128]{3,2,1,0:T(8,128)(2,1)} %param.4), channel_id=1, source_target_pairs={{0,1},{1,2},{2,3},{3,0},{4,5},{5,6},{6,7},{7,4},{8,9},{9,10},{10,1... | collective-permute-start | bytes 393224 | tf_op jit(solution)/shard_map/ppermute | solution.py:276
  2.8 8.5 %collective-permute-start.1 = (bf16[2,4,64,128]{3,2,1,0:T(8,128)(2,1)}, bf16[2,4,64,128]{3,2,1,0:T(8,128)(2,1)S(1)}, u32[]{:S(2)}, u32[]{:S(2)}) collective-permute-start(bf16[2,4,64,128]{3,2,1,0:T(8,128)(2,1)} %param.4), channel_id=1, source_target_pairs={{0,2},{1,3},{2,0},{3,1},{4,6},{5,7},{6,4},{7,5},{8,10},{9,11},{10,... | collective-permute-start | bytes 393224 | tf_op jit(solution)/shard_map/ppermute | solution.py:276
  5.5 5.9 %collective-permute-start.2 = (bf16[2,4,64,128]{3,2,1,0:T(8,128)(2,1)}, bf16[2,4,64,128]{3,2,1,0:T(8,128)(2,1)S(1)}, u32[]{:S(2)}, u32[]{:S(2)}) collective-permute-start(bf16[2,4,64,128]{3,2,1,0:T(8,128)(2,1)} %param.4), channel_id=1, source_target_pairs={{0,3},{1,0},{2,1},{3,2},{4,7},{5,4},{6,5},{7,6},{8,11},{9,8},{10,9... | collective-permute-start | bytes 393224 | tf_op jit(solution)/shard_map/ppermute | solution.py:276
  11.4 11.5 %collective-permute-start.3 = (bf16[2,4,256,128]{3,2,1,0:T(8,128)(2,1)S(1)}, bf16[2,4,256,128]{3,2,1,0:T(8,128)(2,1)S(1)}, u32[]{:S(2)}, u32[]{:S(2)}) collective-permute-start(bf16[2,4,256,128]{3,2,1,0:T(8,128)(2,1)S(1)} %constant_dynamic-update-slice_fusion.refs_2_.refs_1_), channel_id=1, source_target_pairs={{0,16},{16,32},{32,48},{48,64},{64,80},{80,96},{96,112},{112,128},... | collective-permute-start | bytes 1572872 | tf_op jit(solution)/shard_map/ppermute | solution.py:12
  16.4 6.5 %collective-permute-start.4 = (bf16[2,4,64,128]{3,2,1,0:T(8,128)(2,1)}, bf16[2,4,64,128]{3,2,1,0:T(8,128)(2,1)S(1)}, u32[]{:S(2)}, u32[]{:S(2)}) collective-permute-start(bf16[2,4,64,128]{3,2,1,0:T(8,128)(2,1)} %refs_8_.1), channel_id=1, source_target_pairs={{16,0},{32,16},{48,32},{64,48},{80,64},{96,80},{112,96},{128,112},... | collective-permute-start | bytes 393224 | tf_op jit(solution)/shard_map/ppermute | solution.py:12
  22.9 0.9 copy-start.1
  24.4 8.1 %collective-permute-start.5 = (bf16[4,320,128]{2,1,0:T(8,128)(2,1)S(1)}, bf16[4,320,128]{2,1,0:T(8,128)(2,1)S(1)}, u32[]{:S(2)}, u32[]{:S(2)}) collective-permute-start(bf16[4,320,128]{2,1,0:T(8,128)(2,1)S(1)} %get-tuple-element.24), channel_id=1, source_target_pairs={{0,4},{4,8},{8,12},{1,5},{5,9},{9,13},{2,6},{6,10},{10,14},{3,7},{... | collective-permute-start | bytes 983048 | tf_op jit(solution)/shard_map/ppermute | solution.py:12
  27.6 9.0 %collective-permute-start.6 = (bf16[4,320,128]{2,1,0:T(8,128)(2,1)S(1)}, bf16[4,320,128]{2,1,0:T(8,128)(2,1)S(1)}, u32[]{:S(2)}, u32[]{:S(2)}) collective-permute-start(bf16[4,320,128]{2,1,0:T(8,128)(2,1)S(1)} %get-tuple-element.25), channel_id=1, source_target_pairs={{4,0},{8,4},{12,8},{5,1},{9,5},{13,9},{6,2},{10,6},{14,10},{7,3},{... | collective-permute-start | bytes 983048 | tf_op jit(solution)/shard_map/ppermute | solution.py:12
  42.0 9.6 %collective-permute-start.8 = (bf16[16,64,128]{2,1,0:T(8,128)(2,1)S(1)}, bf16[16,64,128]{2,1,0:T(8,128)(2,1)S(1)}, u32[]{:S(2)}, u32[]{:S(2)}) collective-permute-start(bf16[16,64,128]{2,1,0:T(8,128)(2,1)S(1)} %get-tuple-element.30), channel_id=1, source_target_pairs={{0,2},{1,3},{2,0},{3,1},{4,6},{5,7},{6,4},{7,5},{8,10},{9,11},{10,... | collective-permute-start | bytes 786440 | tf_op jit(solution)/shard_map/ppermute | solution.py:276
  44.2 11.5 %collective-permute-start.9 = (bf16[16,64,128]{2,1,0:T(8,128)(2,1)S(1)}, bf16[16,64,128]{2,1,0:T(8,128)(2,1)S(1)}, u32[]{:S(2)}, u32[]{:S(2)}) collective-permute-start(bf16[16,64,128]{2,1,0:T(8,128)(2,1)S(1)} %get-tuple-element.31), channel_id=1, source_target_pairs={{0,3},{1,0},{2,1},{3,2},{4,7},{5,4},{6,5},{7,6},{8,11},{9,8},{10,9... | collective-permute-start | bytes 786440 | tf_op jit(solution)/shard_map/ppermute | solution.py:276
  45.3 10.9 %collective-permute-start.7 = (bf16[16,64,128]{2,1,0:T(8,128)(2,1)S(1)}, bf16[16,64,128]{2,1,0:T(8,128)(2,1)S(1)}, u32[]{:S(2)}, u32[]{:S(2)}) collective-permute-start(bf16[16,64,128]{2,1,0:T(8,128)(2,1)S(1)} %get-tuple-element.29.refs_7_), channel_id=1, source_target_pairs={{0,1},{1,2},{2,3},{3,0},{4,5},{5,6},{6,7},{7,4},{8,9},{9,10},{10,1... | collective-permute-start | bytes 786440 | tf_op jit(solution)/shard_map/ppermute | solution.py:276
  62.1 2.7 %collective-permute-start.11 = (bf16[4,27,16,256]{3,2,1,0:T(8,128)(2,1)}, bf16[4,27,16,256]{3,2,1,0:T(8,128)(2,1)S(1)}, u32[]{:S(2)}, u32[]{:S(2)}) collective-permute-start(bf16[4,27,16,256]{3,2,1,0:T(8,128)(2,1)} %get-tuple-element.34), channel_id=1, source_target_pairs={{0,16},{16,0},{32,48},{48,32},{64,80},{80,64},{96,112},{112,96},{1... | collective-permute-start | bytes 2654216 | tf_op jit(solution)/shard_map/ppermute | solution.py:292
  62.5 9.2 %collective-permute-start.10 = (bf16[2,4,64,128]{3,2,1,0:T(8,128)(2,1)S(1)}, bf16[2,4,64,128]{3,2,1,0:T(8,128)(2,1)S(1)}, u32[]{:S(2)}, u32[]{:S(2)}) collective-permute-start(bf16[2,4,64,128]{3,2,1,0:T(8,128)(2,1)S(1)} %get-tuple-element.32.refs_1_), channel_id=1, source_target_pairs={{16,0},{32,16},{48,32},{64,48},{80,64},{96,80},{112,96},{128,112},... | collective-permute-start | bytes 393224 | tf_op jit(solution)/shard_map/ppermute | solution.py:12
  65.1 16.4 %copy-start = (bf16[64,3,3,3,256]{4,0,3,2,1:T(8,128)(2,1)S(1)}, bf16[64,3,3,3,256]{4,0,3,2,1:T(8,128)(2,1)}, u32[]{:S(2)}) copy-start(bf16[64,3,3,3,256]{4,0,3,2,1:T(8,128)(2,1)} %param.6) | copy-start | bytes 2654212
  65.1 20.2 %collective-permute-start.17 = (bf16[27,16,256]{2,1,0:T(8,128)(2,1)S(1)}, bf16[27,16,256]{2,1,0:T(8,128)(2,1)S(1)}, u32[]{:S(2)}, u32[]{:S(2)}) collective-permute-start(bf16[27,16,256]{2,1,0:T(8,128)(2,1)S(1)} %get-tuple-element.51.refs_3_), channel_id=1, source_target_pairs={{0,4},{4,8},{8,12},{12,0},{1,5},{5,9},{9,13},{13,1},{2,6},{6,10},{... | collective-permute-start | bytes 663560 | tf_op jit(solution)/shard_map/ppermute | solution.py:276
  72.3 8.6 %collective-permute-start.12 = (bf16[4,64,128]{2,1,0:T(8,128)(2,1)S(1)}, bf16[4,64,128]{2,1,0:T(8,128)(2,1)S(1)}, u32[]{:S(2)}, u32[]{:S(2)}) collective-permute-start(bf16[4,64,128]{2,1,0:T(8,128)(2,1)S(1)} %get-tuple-element.35), channel_id=1, source_target_pairs={{0,4},{4,8},{8,12},{1,5},{5,9},{9,13},{2,6},{6,10},{10,14},{3,7},{... | collective-permute-start | bytes 196616 | tf_op jit(solution)/shard_map/ppermute | solution.py:12
  75.4 6.1 %collective-permute-start.13 = (bf16[4,64,128]{2,1,0:T(8,128)(2,1)S(1)}, bf16[4,64,128]{2,1,0:T(8,128)(2,1)S(1)}, u32[]{:S(2)}, u32[]{:S(2)}) collective-permute-start(bf16[4,64,128]{2,1,0:T(8,128)(2,1)S(1)} %get-tuple-element.36), channel_id=1, source_target_pairs={{4,0},{8,4},{12,8},{5,1},{9,5},{13,9},{6,2},{10,6},{14,10},{7,3},{... | collective-permute-start | bytes 196616 | tf_op jit(solution)/shard_map/ppermute | solution.py:12
  76.7 7.4 %collective-permute-start.19 = (bf16[27,16,256]{2,1,0:T(8,128)(2,1)S(1)}, bf16[27,16,256]{2,1,0:T(8,128)(2,1)S(1)}, u32[]{:S(2)}, u32[]{:S(2)}) collective-permute-start(bf16[27,16,256]{2,1,0:T(8,128)(2,1)S(1)} %get-tuple-element.49), channel_id=1, source_target_pairs={{0,12},{4,0},{8,4},{12,8},{1,13},{5,1},{9,5},{13,9},{2,14},{6,2},{... | collective-permute-start | bytes 663560 | tf_op jit(solution)/shard_map/ppermute | solution.py:276
  79.1 6.3 %collective-permute-start.18 = (bf16[27,16,256]{2,1,0:T(8,128)(2,1)S(1)}, bf16[27,16,256]{2,1,0:T(8,128)(2,1)S(1)}, u32[]{:S(2)}, u32[]{:S(2)}) collective-permute-start(bf16[27,16,256]{2,1,0:T(8,128)(2,1)S(1)} %get-tuple-element.50), channel_id=1, source_target_pairs={{0,8},{4,12},{8,0},{12,4},{1,9},{5,13},{9,1},{13,5},{2,10},{6,14},... | collective-permute-start | bytes 663560 | tf_op jit(solution)/shard_map/ppermute | solution.py:276
  86.1 10.7 %collective-permute-start.20 = (bf16[27,8,128]{2,1,0:T(8,128)(2,1)S(1)}, bf16[27,8,128]{2,1,0:T(8,128)(2,1)S(1)}, u32[]{:S(2)}, u32[]{:S(2)}) collective-permute-start(bf16[27,8,128]{2,1,0:T(8,128)(2,1)S(1)} %get-tuple-element.42), channel_id=1, source_target_pairs={{0,32},{16,48},{32,64},{48,80},{64,96},{80,112},{96,0},{112,16},{1... | collective-permute-start | bytes 165896 | tf_op jit(solution)/shard_map/ppermute | solution.py:297
  89.9 8.9 %collective-permute-start.21 = (bf16[27,8,128]{2,1,0:T(8,128)(2,1)S(1)}, bf16[27,8,128]{2,1,0:T(8,128)(2,1)S(1)}, u32[]{:S(2)}, u32[]{:S(2)}) collective-permute-start(bf16[27,8,128]{2,1,0:T(8,128)(2,1)S(1)} %get-tuple-element.43), channel_id=1, source_target_pairs={{0,64},{16,80},{32,96},{48,112},{64,0},{80,16},{96,32},{112,48},{1... | collective-permute-start | bytes 165896 | tf_op jit(solution)/shard_map/ppermute | solution.py:297
  94.9 4.8 %collective-permute-start.22 = (bf16[27,8,128]{2,1,0:T(8,128)(2,1)S(1)}, bf16[27,8,128]{2,1,0:T(8,128)(2,1)S(1)}, u32[]{:S(2)}, u32[]{:S(2)}) collective-permute-start(bf16[27,8,128]{2,1,0:T(8,128)(2,1)S(1)} %get-tuple-element.44), channel_id=1, source_target_pairs={{0,96},{16,112},{32,0},{48,16},{64,32},{80,48},{96,64},{112,80},{1... | collective-permute-start | bytes 165896 | tf_op jit(solution)/shard_map/ppermute | solution.py:297
  99.8 7.0 %collective-permute-start.23 = (bf16[27,8,128]{2,1,0:T(8,128)(2,1)S(1)}, bf16[27,8,128]{2,1,0:T(8,128)(2,1)S(1)}, u32[]{:S(2)}, u32[]{:S(2)}) collective-permute-start(bf16[27,8,128]{2,1,0:T(8,128)(2,1)S(1)} %add_convert_fusion.2), channel_id=1, source_target_pairs={{0,128},{16,144},{32,160},{48,176},{64,192},{80,208},{96,224},{112... | collective-permute-start | bytes 165896 | tf_op jit(solution)/shard_map/ppermute | solution.py:292
  99.9 9.1 %collective-permute-start.14 = (bf16[8,64,128]{2,1,0:T(8,128)(2,1)S(1)}, bf16[8,64,128]{2,1,0:T(8,128)(2,1)S(1)}, u32[]{:S(2)}, u32[]{:S(2)}) collective-permute-start(bf16[8,64,128]{2,1,0:T(8,128)(2,1)S(1)} %get-tuple-element.38), channel_id=1, source_target_pairs={{0,1},{1,2},{2,3},{3,0},{4,5},{5,6},{6,7},{7,4},{8,9},{9,10},{10,1... | collective-permute-start | bytes 393224 | tf_op jit(solution)/shard_map/ppermute | solution.py:276
  100.9 8.5 %collective-permute-start.15 = (bf16[8,64,128]{2,1,0:T(8,128)(2,1)S(1)}, bf16[8,64,128]{2,1,0:T(8,128)(2,1)S(1)}, u32[]{:S(2)}, u32[]{:S(2)}) collective-permute-start(bf16[8,64,128]{2,1,0:T(8,128)(2,1)S(1)} %get-tuple-element.39), channel_id=1, source_target_pairs={{0,2},{1,3},{2,0},{3,1},{4,6},{5,7},{6,4},{7,5},{8,10},{9,11},{10,... | collective-permute-start | bytes 393224 | tf_op jit(solution)/shard_map/ppermute | solution.py:276
  103.0 6.4 %collective-permute-start.16 = (bf16[8,64,128]{2,1,0:T(8,128)(2,1)S(1)}, bf16[8,64,128]{2,1,0:T(8,128)(2,1)S(1)}, u32[]{:S(2)}, u32[]{:S(2)}) collective-permute-start(bf16[8,64,128]{2,1,0:T(8,128)(2,1)S(1)} %get-tuple-element.40), channel_id=1, source_target_pairs={{0,3},{1,0},{2,1},{3,2},{4,7},{5,4},{6,5},{7,6},{8,11},{9,8},{10,9... | collective-permute-start | bytes 393224 | tf_op jit(solution)/shard_map/ppermute | solution.py:276
  106.8 3.4 %collective-permute-start.26 = (bf16[27,8,128]{2,1,0:T(8,128)(2,1)S(1)}, bf16[27,8,128]{2,1,0:T(8,128)(2,1)S(1)}, u32[]{:S(2)}, u32[]{:S(2)}) collective-permute-start(bf16[27,8,128]{2,1,0:T(8,128)(2,1)S(1)} %add_convert_fusion.1.refs_1_), channel_id=1, source_target_pairs={{0,96},{16,112},{32,0},{48,16},{64,32},{80,48},{96,64},{112,80},{1... | collective-permute-start | bytes 165896 | tf_op jit(solution)/shard_map/ppermute | solution.py:297
  109.0 4.2 %collective-permute-start.25 = (bf16[27,8,128]{2,1,0:T(8,128)(2,1)S(1)}, bf16[27,8,128]{2,1,0:T(8,128)(2,1)S(1)}, u32[]{:S(2)}, u32[]{:S(2)}) collective-permute-start(bf16[27,8,128]{2,1,0:T(8,128)(2,1)S(1)} %add_convert_fusion.1.refs_1_), channel_id=1, source_target_pairs={{0,64},{16,80},{32,96},{48,112},{64,0},{80,16},{96,32},{112,48},{1... | collective-permute-start | bytes 165896 | tf_op jit(solution)/shard_map/ppermute | solution.py:297
  109.0 4.8 %collective-permute-start.24 = (bf16[27,8,128]{2,1,0:T(8,128)(2,1)S(1)}, bf16[27,8,128]{2,1,0:T(8,128)(2,1)S(1)}, u32[]{:S(2)}, u32[]{:S(2)}) collective-permute-start(bf16[27,8,128]{2,1,0:T(8,128)(2,1)S(1)} %add_convert_fusion.1.refs_1_), channel_id=1, source_target_pairs={{0,32},{16,48},{32,64},{48,80},{64,96},{80,112},{96,0},{112,16},{1... | collective-permute-start | bytes 165896 | tf_op jit(solution)/shard_map/ppermute | solution.py:297
  109.4 27.0 %copy-start.2 = (bf16[8,64,128]{2,1,0:T(8,128)(2,1)}, bf16[8,64,128]{2,1,0:T(8,128)(2,1)S(1)}, u32[]{:S(2)}) copy-start(bf16[8,64,128]{2,1,0:T(8,128)(2,1)S(1)} %add_convert_fusion) | copy-start | bytes 393220
  114.4 10.7 %collective-permute-start.29 = (bf16[27,16,256]{2,1,0:T(8,128)(2,1)S(1)}, bf16[27,16,256]{2,1,0:T(8,128)(2,1)S(1)}, u32[]{:S(2)}, u32[]{:S(2)}) collective-permute-start(bf16[27,16,256]{2,1,0:T(8,128)(2,1)S(1)} %shard_map.73.refs_1_), channel_id=1, source_target_pairs={{0,12},{4,0},{8,4},{12,8},{1,13},{5,1},{9,5},{13,9},{2,14},{6,2},{... | collective-permute-start | bytes 663560 | tf_op jit(solution)/shard_map/ppermute | solution.py:276
  119.4 6.4 %collective-permute-start.28 = (bf16[27,16,256]{2,1,0:T(8,128)(2,1)S(1)}, bf16[27,16,256]{2,1,0:T(8,128)(2,1)S(1)}, u32[]{:S(2)}, u32[]{:S(2)}) collective-permute-start(bf16[27,16,256]{2,1,0:T(8,128)(2,1)S(1)} %shard_map.73.refs_1_), channel_id=1, source_target_pairs={{0,8},{4,12},{8,0},{12,4},{1,9},{5,13},{9,1},{13,5},{2,10},{6,14},... | collective-permute-start | bytes 663560 | tf_op jit(solution)/shard_map/ppermute | solution.py:276
  120.4 10.7 %collective-permute-start.27 = (bf16[27,16,256]{2,1,0:T(8,128)(2,1)S(1)}, bf16[27,16,256]{2,1,0:T(8,128)(2,1)S(1)}, u32[]{:S(2)}, u32[]{:S(2)}) collective-permute-start(bf16[27,16,256]{2,1,0:T(8,128)(2,1)S(1)} %shard_map.73.refs_1_), channel_id=1, source_target_pairs={{0,4},{4,8},{8,12},{12,0},{1,5},{5,9},{9,13},{13,1},{2,6},{6,10},{... | collective-permute-start | bytes 663560 | tf_op jit(solution)/shard_map/ppermute | solution.py:276
  131.7 4.6 %collective-permute-start.30 = (bf16[27,64,256]{2,1,0:T(8,128)(2,1)S(1)}, bf16[27,64,256]{2,1,0:T(8,128)(2,1)S(1)}, u32[]{:S(2)}, u32[]{:S(2)}) collective-permute-start(bf16[27,64,256]{2,1,0:T(8,128)(2,1)S(1)} %shard_map.74), channel_id=1, source_target_pairs={{0,16},{16,0},{32,48},{48,32},{64,80},{80,64},{96,112},{112,96},{1... | collective-permute-start | bytes 2654216 | tf_op jit(solution)/shard_map/ppermute | solution.py:292

commit v4 on v3

--- a/solution.py
+++ b/solution.py
@@ -41,20 +41,15 @@
     return ahead.astype(jnp.bfloat16), cell, behind.astype(jnp.bfloat16)
 
 
-def run_forward(me, own, early, above, below, weight, panel, pre, sent, wide, flat):
+def run_forward(me, blocks, earlier, weight, panel, pre, sent, wide, flat):
     for n in range(9):
         flat[:, n * 256 : n * 256 + 256] = weight[n]
     for f in range(4):
         for r in range(6):
-            if r == 0:
-                cell = above[f, :256]
-            elif r == 5:
-                cell = below[f, :256]
-            else:
-                cell = early[f, r - 1] if f < 2 else own[f - 2, r - 1]
             for k in range(4):
                 at = pl.multiple_of(((me + 4 - k) % 4) * 64, 64)
-                panel[f * 6 + r, pl.ds(at, 64), :] = cell[k * 64 : k * 64 + 64]
+                cell = earlier[k][f, r] if f < 2 else blocks[k][f - 2, r]
+                panel[f * 6 + r, pl.ds(at, 64), :] = cell
     for p, (t, i) in enumerate(SPOTS):
         for n, (a, b) in enumerate(TAPS):
             wide[n * 256 : n * 256 + 256, p * 128 : p * 128 + 128] = panel[(t + a) * 6 + i + b]
@@ -74,15 +69,10 @@
                 out[t * 4 + i] = act
 
 
-def spread(own, late, above, below, wide, skip=0):
+def spread(own, late, wide):
     for f in range(4):
         for r in range(6):
-            if r == 0:
-                cell = above[f, skip:]
-            elif r == 5:
-                cell = below[f, skip:]
-            else:
-                cell = own[f, r - 1] if f < 2 else late[f - 2, r - 1]
+            cell = own[f, r] if f < 2 else late[f - 2, r]
             moved = lanes_moved(cell)
             for n, (a, b) in enumerate(TAPS):
                 t, i = f - 2 + a, r - 2 + b
@@ -104,35 +94,37 @@
             out[p + (base if k else 0)] = block.astype(out.dtype)
 
 
-def transposed_body(place, own, late, above, below, weight, mine, one, two, three, wide, full):
-    spread(own, late, above, below, wide)
+def transposed_body(place, own, late, weight, mine, one, two, three, wide, full):
+    spread(own, late, wide)
     run_transposed(place[0], weight, wide, full, (mine, one, two, three), 0)
 
 
 def opening_body(
-    place, own, early, late, grads, above, below, weight_one, weight_two,
+    place, b0, b1, b2, b3, e0, e1, e2, e3, grads, late, weight_one, weight_two,
     panel, pre, mine, one, two, three, tall, flat, wide, full,
 ):
     me = place[0]
-    spread(grads, late, above, below, wide, 256)
+    spread(grads, late, wide)
     run_transposed(me, weight_two, wide, full, (mine, one, two, three), 8)
-    run_forward(me, own, early, above, below, weight_one, panel, pre, (one, two, three), tall, flat)
-
-
-def frame_rows_body(place, early, own, grads, late, heads, tails):
-    for f in range(4):
-        cells = (early, f) if f < 2 else (own, f - 2)
-        others = (grads, f) if f < 2 else (late, f - 2)
+    blocks, earlier = (b0, b1, b2, b3), (e0, e1, e2, e3)
+    run_forward(me, blocks, earlier, weight_one, panel, pre, (one, two, three), tall, flat)
+
+
+def outer_rows_body(place, frames, grads, heads, tails):
+    for f in range(2):
         for row, out in ((0, heads), (3, tails)):
-            out[f, :256] = cells[0][cells[1], row]
-            out[f, 256:] = others[0][others[1], row]
-
-
-def gradient_rows_body(place, own, late, heads, tails):
-    for f in range(4):
-        cells = (own, f) if f < 2 else (late, f - 2)
-        for row, out in ((0, heads), (3, tails)):
-            out[f] = cells[0][cells[1], row]
+            out[f] = frames[f, row]
+            out[2 + f] = grads[f, row]
+
+
+def framed_body(place, above, below, *blocks):
+    half = len(blocks) // 2
+    for n in range(half):
+        for f in range(2):
+            blocks[half + n][f, 0] = above[2 * n + f]
+            blocks[half + n][f, 5] = below[2 * n + f]
+            for r in range(4):
+                blocks[half + n][f, r + 1] = blocks[n][f, r]
 
 
 def against(left, right):
@@ -145,8 +137,8 @@
 
 
 def filters_body(
-    place, panel, pre, mine, r1, r2, r3, sent, own, late, above, below,
-    gradient, keep, give, moved, wide, acts, both,
+    place, panel, pre, mine, r1, r2, r3, sent, own, late,
+    gradient, heads, tails, keep, give, moved, wide, acts, both,
 ):
     me, height, core = place[0], place[1], place[3]
     for p in range(8):
@@ -157,6 +149,10 @@
             total = total + part[8 + p].astype(jnp.float32)
         total = (total * sig * (1.0 + value * (1.0 - sig))).astype(jnp.bfloat16)
         gradient[p // 4, p % 4] = total
+        if p % 4 == 0:
+            heads[p // 4] = total
+        if p % 4 == 3:
+            tails[p // 4] = total
         for e, part in enumerate(lanes_moved(total)):
             moved[e * 64 : e * 64 + 64, p * 128 : p * 128 + 128] = part
     for n, (a, b) in enumerate(TAPS):
@@ -164,7 +160,7 @@
         sums = against(moved[...], window)
         for e in range(3):
             store_filter(both, core, height, n * 3 + e, sums[e * 64 : e * 64 + 64])
-    spread(own, late, above, below, wide, 256)
+    spread(own, late, wide)
     for k, part in enumerate((sent, r1, r2, r3)):
         at = pl.multiple_of(((me + 4 - k) % 4) * 64, 64)
         for p in range(8):
@@ -204,19 +200,21 @@
     )
 
 
-def frame_rows(place, *operands):
-    return call(frame_rows_body, [shaped((4, 320, 128), jnp.bfloat16)] * 2, [], place, *operands)
-
-
-def gradient_rows(place, own, late, after):
-    rows = [shaped((4, 64, 128), jnp.bfloat16)] * 2
-    return call(gradient_rows_body, rows, [], place, own, late, after=after)
+def outer_rows(place, frames, grads):
+    return call(outer_rows_body, [shaped((4, 64, 128), jnp.bfloat16)] * 2, [], place, frames, grads)
+
+
+def framed(place, above, below, *blocks, after=()):
+    outs = [shaped((2, 6, 64, 128), jnp.bfloat16)] * len(blocks)
+    return call(framed_body, outs, [], place, above, below, *blocks, after=after)
 
 
 def filters(place, *operands):
     return call(
         filters_body,
-        [shaped((2, 4, 64, 128), jnp.bfloat16)] + [shaped((4, 27, 16, 256), jnp.bfloat16)] * 2,
+        [shaped((2, 4, 64, 128), jnp.bfloat16)]
+        + [shaped((2, 64, 128), jnp.bfloat16)] * 2
+        + [shaped((4, 27, 16, 256), jnp.bfloat16)] * 2,
         [
             pltpu.VMEM((192, 1024), jnp.bfloat16), pltpu.VMEM((1728, 1024), jnp.bfloat16),
             pltpu.VMEM((256, 1024), jnp.bfloat16), pltpu.VMEM((2, 4, 27, 16, 256), jnp.bfloat16),
@@ -334,21 +332,24 @@
     place = place.astype(jnp.int32)
     taps_one = weight_one.transpose(1, 2, 3, 0, 4).reshape(1728, 256)
     taps_two = weight_two.transpose(1, 2, 3, 0, 4).reshape(1728, 256)
-    frames_all = jnp.concatenate([frames] + all_rotated(frames, "chan"), 2)
-    early = passed_along(frames_all, "tm", 1)
-    late = passed_along(grad_out, "tm", -1)
-    above, below = traded(*frame_rows(place, early, frames_all, grad_out, late))
+    above, below = traded(*outer_rows(place, frames, grad_out))
+    block, grads = framed(place, above, below, frames, grad_out)
+    early = passed_along(block, "tm", 1)
+    late = passed_along(grads, "tm", -1)
+    blocks = [block] + all_rotated(block, "chan")
+    earlier = [early] + all_rotated(early, "chan")
     panel, pre, mine, *sent = opening(
-        place, frames_all, early, late, grad_out, above, below, taps_one.reshape(9, 192, 256), taps_two
+        place, *blocks, *earlier, grads, late, taps_one.reshape(9, 192, 256), taps_two
     )
     received = [rotated(part, "chan", k + 1) for k, part in enumerate(sent)]
-    grad_pre, keep, give = filters(
-        place, panel, pre, mine, *received, sent[0], grad_out, late, above, below
+    grad_pre, heads, tails, keep, give = filters(
+        place, panel, pre, mine, *received, sent[0], grads, late
     )
     pieces = summed_pair(keep, give)
-    later = passed_along(grad_pre, "tm", -1)
-    edges = traded(*gradient_rows(place, grad_pre, later, [pieces[1]]))
-    gradient_pieces = transposed(place, (grad_pre, later) + edges, taps_one)
+    above, below = traded(heads, tails)
+    cells = framed(place, above, below, grad_pre, after=[pieces[1]])[0]
+    later = passed_along(cells, "tm", -1)
+    gradient_pieces = transposed(place, (cells, later), taps_one)
     grad_frames, grad_one, grad_two = rest_of_sum(place, pieces, gradient_pieces, core)
     return (grad_frames, filter_shape(grad_one), filter_shape(grad_two))
 

time: 139 us -> 143 us (1.029)
  starting transfers between devices: 57.6 us -> 63.2 us
    ppermute x7, waiting for transfers between devices: 18.1 us -> 8.85 us  [passed_along(): return lax.ppermute(block, axis, route)]
    ppermute x15 -> x18, waiting for transfers between devices: 26.9 us -> 35.7 us  [rotated(): lax.ppermute(block, axis, [(i, (i + distance) % count) for i in range(cou...]
    ppermute x3, starting transfers between devices: 3.03 us -> 6.76 us  [swapped(): lax.ppermute(block, 'tm', [(i, i ^ distance) for i in range(lax.axis_size...]
    ppermute x7, starting transfers between devices: 17.7 us -> 20.5 us  [passed_along(): return lax.ppermute(block, axis, route)]
    ppermute x6, waiting for transfers between devices: 9.15 us -> 7.47 us  [quad_rotated(): return lax.ppermute(block, 'tm', route)]
    ppermute x15 -> x18, starting transfers between devices: 25.4 us -> 24.3 us  [rotated(): lax.ppermute(block, axis, [(i, (i + distance) % count) for i in range(cou...]
    pallas_call x8 -> x9, Pallas kernels: 16.4 us -> 16 us  [call(): pl.pallas_call(lambda *refs: body(*refs[:used], *refs[rest:]), out_shape=...]
  transfers between devices with their start and end apart: 31 -> 34, of which waited for: 23 -> 20; matrix products, arithmetic and copies ran while one was open for 1% -> 0% of each run, Pallas kernels for 2% -> 2%
where the time goes in v4:
time: 143 us
  starting transfers between devices  63.2 us (44%)
  waiting for transfers between devices  57.6 us (40%)
  Pallas kernels  16 us (11%)
  other arithmetic  2.9 us (2%)
  local copies, waits for them, and re-layouts  1.91 us (1%)
    ppermute x18, waiting for transfers between devices, rotated(): lax.ppermute(block, axis, [(i, (i + distance) % count) for i in range(cou...  35.7 us
    ppermute x18, starting transfers between devices, rotated(): lax.ppermute(block, axis, [(i, (i + distance) % count) for i in range(cou...  24.3 us
    ppermute x7, starting transfers between devices, passed_along(): return lax.ppermute(block, axis, route)  20.5 us
    pallas_call x9, Pallas kernels, call(): pl.pallas_call(lambda *refs: body(*refs[:used], *refs[rest:]), out_shape=...  16 us
    ppermute x6, starting transfers between devices, quad_rotated(): return lax.ppermute(block, 'tm', route)  11.6 us
    ppermute x7, waiting for transfers between devices, passed_along(): return lax.ppermute(block, axis, route)  8.85 us
    ppermute x6, waiting for transfers between devices, quad_rotated(): return lax.ppermute(block, 'tm', route)  7.47 us
    ppermute x3, starting transfers between devices, swapped(): lax.ppermute(block, 'tm', [(i, i ^ distance) for i in range(lax.axis_size...  6.76 us
  transfers between devices with their start and end apart: 34, of which 20 were waited for; matrix products, arithmetic and copies ran while one was open for 0% of the time, Pallas kernels for 2%

profile of v4, /device:TPU:1, one launch (start us, length us, event | category | flops | bytes accessed | tf_op | source)
XLA Modules:
  0.0 142.6 jit_solution(9313923528508263977)
XLA Ops:
  0.7 0.9 copy-done.1
  1.7 0.9 copy-done.2
  2.6 0.5 shard_map.67
  3.1 3.9 %collective-permute-start = (bf16[4,64,128]{2,1,0:T(8,128)(2,1)S(1)}, bf16[4,64,128]{2,1,0:T(8,128)(2,1)S(1)}, u32[]{:S(2)}, u32[]{:S(2)}) collective-permute-start(bf16[4,64,128]{2,1,0:T(8,128)(2,1)S(1)} %get-tuple-element.26), channel_id=1, source_target_pairs={{0,4},{4,8},{8,12},{1,5},{5,9},{9,13},{2,6},{6,10},{10,14},{3,7},{... | collective-permute-start | bytes 196616 | tf_op jit(solution)/shard_map/ppermute | solution.py:12
  7.1 1.3 collective-permute-start.1
  8.4 3.7 %collective-permute-done.1.refs_2_ = bf16[4,64,128]{2,1,0:T(8,128)(2,1)S(1)} collective-permute-done((bf16[4,64,128]{2,1,0:T(8,128)(2,1)S(1)}, bf16[4,64,128]{2,1,0:T(8,128)(2,1)S(1)}, u32[]{:S(2)}, u32[]{:S(2)}) %collective-permute-start.1) | collective-permute-done | bytes 65568 | tf_op jit(solution)/shard_map/ppermute | solution.py:12
  12.1 0.6 shard_map.68
  12.7 5.5 %collective-permute-start.5 = (bf16[2,6,64,128]{3,2,1,0:T(8,128)(2,1)S(1)}, bf16[2,6,64,128]{3,2,1,0:T(8,128)(2,1)S(1)}, u32[]{:S(2)}, u32[]{:S(2)}) collective-permute-start(bf16[2,6,64,128]{3,2,1,0:T(8,128)(2,1)S(1)} %get-tuple-element.28.refs_1_), channel_id=1, source_target_pairs={{0,16},{16,32},{32,48},{48,64},{64,80},{80,96},{96,112},{112,128},... | collective-permute-start | bytes 589832 | tf_op jit(solution)/shard_map/ppermute | solution.py:12
  18.2 1.9 %collective-permute-start.9 = (bf16[2,6,64,128]{3,2,1,0:T(8,128)(2,1)S(1)}, bf16[2,6,64,128]{3,2,1,0:T(8,128)(2,1)S(1)}, u32[]{:S(2)}, u32[]{:S(2)}) collective-permute-start(bf16[2,6,64,128]{3,2,1,0:T(8,128)(2,1)S(1)} %get-tuple-element.29.refs_9_.refs_8_), channel_id=1, source_target_pairs={{16,0},{32,16},{48,32},{64,48},{80,64},{96,80},{112,96},{128,112},... | collective-permute-start | bytes 589832 | tf_op jit(solution)/shard_map/ppermute | solution.py:12
  20.1 2.8 %collective-permute-start.4 = (bf16[2,6,64,128]{3,2,1,0:T(8,128)(2,1)S(1)}, bf16[2,6,64,128]{3,2,1,0:T(8,128)(2,1)S(1)}, u32[]{:S(2)}, u32[]{:S(2)}) collective-permute-start(bf16[2,6,64,128]{3,2,1,0:T(8,128)(2,1)S(1)} %get-tuple-element.28.refs_1_), channel_id=1, source_target_pairs={{0,3},{1,0},{2,1},{3,2},{4,7},{5,4},{6,5},{7,6},{8,11},{9,8},{10,9... | collective-permute-start | bytes 589832 | tf_op jit(solution)/shard_map/ppermute | solution.py:274
  22.9 0.3 collective-permute-start.3
  23.3 0.7 collective-permute-start.2
  24.0 2.0 %collective-permute-start.8 = (bf16[2,6,64,128]{3,2,1,0:T(8,128)(2,1)S(1)}, bf16[2,6,64,128]{3,2,1,0:T(8,128)(2,1)S(1)}, u32[]{:S(2)}, u32[]{:S(2)}) collective-permute-start(bf16[2,6,64,128]{3,2,1,0:T(8,128)(2,1)S(1)} %collective-permute-done.5.refs_5_), channel_id=1, source_target_pairs={{0,3},{1,0},{2,1},{3,2},{4,7},{5,4},{6,5},{7,6},{8,11},{9,8},{10,9... | collective-permute-start | bytes 589832 | tf_op jit(solution)/shard_map/ppermute | solution.py:274
  26.0 2.4 %collective-permute-start.7 = (bf16[2,6,64,128]{3,2,1,0:T(8,128)(2,1)S(1)}, bf16[2,6,64,128]{3,2,1,0:T(8,128)(2,1)S(1)}, u32[]{:S(2)}, u32[]{:S(2)}) collective-permute-start(bf16[2,6,64,128]{3,2,1,0:T(8,128)(2,1)S(1)} %collective-permute-done.5.refs_5_), channel_id=1, source_target_pairs={{0,2},{1,3},{2,0},{3,1},{4,6},{5,7},{6,4},{7,5},{8,10},{9,11},{10,... | collective-permute-start | bytes 589832 | tf_op jit(solution)/shard_map/ppermute | solution.py:274
  28.4 3.1 %collective-permute-done.4.refs_4_ = bf16[2,6,64,128]{3,2,1,0:T(8,128)(2,1)S(1)} collective-permute-done((bf16[2,6,64,128]{3,2,1,0:T(8,128)(2,1)S(1)}, bf16[2,6,64,128]{3,2,1,0:T(8,128)(2,1)S(1)}, u32[]{:S(2)}, u32[]{:S(2)}) %collective-permute-start.4) | collective-permute-done | bytes 196640 | tf_op jit(solution)/shard_map/ppermute | solution.py:274
  31.5 4.4 %collective-permute-done.2.refs_2_ = bf16[2,6,64,128]{3,2,1,0:T(8,128)(2,1)S(1)} collective-permute-done((bf16[2,6,64,128]{3,2,1,0:T(8,128)(2,1)S(1)}, bf16[2,6,64,128]{3,2,1,0:T(8,128)(2,1)S(1)}, u32[]{:S(2)}, u32[]{:S(2)}) %collective-permute-start.2) | collective-permute-done | bytes 196640 | tf_op jit(solution)/shard_map/ppermute | solution.py:274
  35.9 2.1 %collective-permute-done.8.refs_8_ = bf16[2,6,64,128]{3,2,1,0:T(8,128)(2,1)S(1)} collective-permute-done((bf16[2,6,64,128]{3,2,1,0:T(8,128)(2,1)S(1)}, bf16[2,6,64,128]{3,2,1,0:T(8,128)(2,1)S(1)}, u32[]{:S(2)}, u32[]{:S(2)}) %collective-permute-start.8) | collective-permute-done | bytes 196640 | tf_op jit(solution)/shard_map/ppermute | solution.py:274
  38.0 1.6 %collective-permute-done.7.refs_7_ = bf16[2,6,64,128]{3,2,1,0:T(8,128)(2,1)S(1)} collective-permute-done((bf16[2,6,64,128]{3,2,1,0:T(8,128)(2,1)S(1)}, bf16[2,6,64,128]{3,2,1,0:T(8,128)(2,1)S(1)}, u32[]{:S(2)}, u32[]{:S(2)}) %collective-permute-start.7) | collective-permute-done | bytes 196640 | tf_op jit(solution)/shard_map/ppermute | solution.py:274
  39.6 2.1 %collective-permute-done.6.refs_6_ = bf16[2,6,64,128]{3,2,1,0:T(8,128)(2,1)S(1)} collective-permute-done((bf16[2,6,64,128]{3,2,1,0:T(8,128)(2,1)S(1)}, bf16[2,6,64,128]{3,2,1,0:T(8,128)(2,1)S(1)}, u32[]{:S(2)}, u32[]{:S(2)}) %collective-permute-start.6) | collective-permute-done | bytes 196640 | tf_op jit(solution)/shard_map/ppermute | solution.py:274
  41.7 5.4 %shard_map.69 = (bf16[24,256,128]{2,1,0:T(8,128)(2,1)}, f32[8,64,128]{2,1,0:T(8,128)S(1)}, f32[8,64,128]{2,1,0:T(8,128)S(1)}, bf16[16,64,128]{2,1,0:T(8,128)(2,1...) custom-call(s32[4]{0:T(128)S(1)} %pad_add_fusion.refs_0_, ...), custom_call_target="tpu_custom_call" | custom-call | tf_op jit(solution)/shard_map/pallas_call | solution.py:24
  47.1 0.4 collective-permute-start.11
  47.4 0.9 collective-permute-start.12
  48.3 0.6 collective-permute-start.10
  48.9 7.5 %collective-permute-done.11.refs_5_ = bf16[16,64,128]{2,1,0:T(8,128)(2,1)S(1)} collective-permute-done((bf16[16,64,128]{2,1,0:T(8,128)(2,1)S(1)}, bf16[16,64,128]{2,1,0:T(8,128)(2,1)S(1)}, u32[]{:S(2)}, u32[]{:S(2)}) %collective-permute-start.11) | collective-permute-done | bytes 262176 | tf_op jit(solution)/shard_map/ppermute | solution.py:274
  56.4 3.6 %collective-permute-done.12.refs_6_ = bf16[16,64,128]{2,1,0:T(8,128)(2,1)S(1)} collective-permute-done((bf16[16,64,128]{2,1,0:T(8,128)(2,1)S(1)}, bf16[16,64,128]{2,1,0:T(8,128)(2,1)S(1)}, u32[]{:S(2)}, u32[]{:S(2)}) %collective-permute-start.12) | collective-permute-done | bytes 262176 | tf_op jit(solution)/shard_map/ppermute | solution.py:274
  60.0 2.5 %collective-permute-done.10.refs_4_ = bf16[16,64,128]{2,1,0:T(8,128)(2,1)S(1)} collective-permute-done((bf16[16,64,128]{2,1,0:T(8,128)(2,1)S(1)}, bf16[16,64,128]{2,1,0:T(8,128)(2,1)S(1)}, u32[]{:S(2)}, u32[]{:S(2)}) %collective-permute-start.10) | collective-permute-done | bytes 262176 | tf_op jit(solution)/shard_map/ppermute | solution.py:274
  62.5 5.0 %shard_map.70 = (bf16[2,4,64,128]{3,2,1,0:T(8,128)(2,1)S(1)}, bf16[2,64,128]{2,1,0:T(8,128)(2,1)S(1)}, bf16[2,64,128]{2,1,0:T(8,128)(2,1)S(1)}, bf16[4,27,16,256...) custom-call(s32[4]{0:T(128)S(1)} %pad_add_fusion.refs_0_, bf16[24,256,128]{2,1,0:T(8,128)(2,1)} %get-tuple-element.30.refs_1_, ...), custom_call_target="tpu_custom_call" | custom-call | tf_op jit(solution)/shard_map/pallas_call | solution.py:24
  67.5 0.7 collective-permute-start.15
  68.2 3.1 %collective-permute-start.13 = (bf16[2,64,128]{2,1,0:T(8,128)(2,1)S(1)}, bf16[2,64,128]{2,1,0:T(8,128)(2,1)S(1)}, u32[]{:S(2)}, u32[]{:S(2)}) collective-permute-start(bf16[2,64,128]{2,1,0:T(8,128)(2,1)S(1)} %get-tuple-element.36), channel_id=1, source_target_pairs={{0,4},{4,8},{8,12},{1,5},{5,9},{9,13},{2,6},{6,10},{10,14},{3,7},{... | collective-permute-start | bytes 98312 | tf_op jit(solution)/shard_map/ppermute | solution.py:12
  71.3 1.3 collective-permute-start.14
  72.6 0.3 convert_add_fusion
  73.0 2.2 %collective-permute-start.20 = (bf16[27,16,256]{2,1,0:T(8,128)(2,1)S(1)}, bf16[27,16,256]{2,1,0:T(8,128)(2,1)S(1)}, u32[]{:S(2)}, u32[]{:S(2)}) collective-permute-start(bf16[27,16,256]{2,1,0:T(8,128)(2,1)S(1)} %get-tuple-element.55.refs_4_), channel_id=1, source_target_pairs={{0,4},{4,8},{8,12},{12,0},{1,5},{5,9},{9,13},{13,1},{2,6},{6,10},{... | collective-permute-start | bytes 663560 | tf_op jit(solution)/shard_map/ppermute | solution.py:274
  75.2 0.8 collective-permute-done.14.refs_2_
  76.0 0.6 shard_map.71.refs_1_
  76.5 3.4 %collective-permute-start.16 = (bf16[2,6,64,128]{3,2,1,0:T(8,128)(2,1)S(1)}, bf16[2,6,64,128]{3,2,1,0:T(8,128)(2,1)S(1)}, u32[]{:S(2)}, u32[]{:S(2)}) collective-permute-start(bf16[2,6,64,128]{3,2,1,0:T(8,128)(2,1)S(1)} %shard_map.71.refs_1_), channel_id=1, source_target_pairs={{16,0},{32,16},{48,32},{64,48},{80,64},{96,80},{112,96},{128,112},... | collective-permute-start | bytes 589832 | tf_op jit(solution)/shard_map/ppermute | solution.py:12
  80.0 2.7 %collective-permute-start.21 = (bf16[27,16,256]{2,1,0:T(8,128)(2,1)S(1)}, bf16[27,16,256]{2,1,0:T(8,128)(2,1)S(1)}, u32[]{:S(2)}, u32[]{:S(2)}) collective-permute-start(bf16[27,16,256]{2,1,0:T(8,128)(2,1)S(1)} %get-tuple-element.54), channel_id=1, source_target_pairs={{0,8},{4,12},{8,0},{12,4},{1,9},{5,13},{9,1},{13,5},{2,10},{6,14},... | collective-permute-start | bytes 663560 | tf_op jit(solution)/shard_map/ppermute | solution.py:274
  82.8 4.4 %collective-permute-done.16.refs_2_ = bf16[2,6,64,128]{3,2,1,0:T(8,128)(2,1)S(1)} collective-permute-done((bf16[2,6,64,128]{3,2,1,0:T(8,128)(2,1)S(1)}, bf16[2,6,64,128]{3,2,1,0:T(8,128)(2,1)S(1)}, u32[]{:S(2)}, u32[]{:S(2)}) %collective-permute-start.16) | collective-permute-done | bytes 196640 | tf_op jit(solution)/shard_map/ppermute | solution.py:12
  87.1 2.0 %shard_map.72 = (f32[8,64,128]{2,1,0:T(8,128)S(1)}, bf16[8,64,128]{2,1,0:T(8,128)(2,1)S(1)}, bf16[8,64,128]{2,1,0:T(8,128)(2,1)S(1)}, bf16[8,64,128]{2,1,0:T(8,128)(2,1)S(1)}) custom-call(s32[4]{0:T(128)S(1)} %pad_add_fusion.refs_0_, bf16[2,6,64,128]{3,2,1,0:T(8,128)(2,1)S(1)} %shard_map.71.refs_1_, ...), custom_call_target="tpu_custom_call" | custom-call | tf_op jit(solution)/shard_map/pallas_call | solution.py:24
  89.2 0.7 shard_map.73
  89.9 3.2 %collective-permute-start.23 = (bf16[27,8,128]{2,1,0:T(8,128)(2,1)S(1)}, bf16[27,8,128]{2,1,0:T(8,128)(2,1)S(1)}, u32[]{:S(2)}, u32[]{:S(2)}) collective-permute-start(bf16[27,8,128]{2,1,0:T(8,128)(2,1)S(1)} %get-tuple-element.46), channel_id=1, source_target_pairs={{0,32},{16,48},{32,64},{48,80},{64,96},{80,112},{96,0},{112,16},{1... | collective-permute-start | bytes 165896 | tf_op jit(solution)/shard_map/ppermute | solution.py:295
  93.1 4.2 %collective-permute-start.24 = (bf16[27,8,128]{2,1,0:T(8,128)(2,1)S(1)}, bf16[27,8,128]{2,1,0:T(8,128)(2,1)S(1)}, u32[]{:S(2)}, u32[]{:S(2)}) collective-permute-start(bf16[27,8,128]{2,1,0:T(8,128)(2,1)S(1)} %get-tuple-element.47), channel_id=1, source_target_pairs={{0,64},{16,80},{32,96},{48,112},{64,0},{80,16},{96,32},{112,48},{1... | collective-permute-start | bytes 165896 | tf_op jit(solution)/shard_map/ppermute | solution.py:295
  97.3 1.3 collective-permute-done.23
  98.6 3.1 %collective-permute-done.24 = bf16[27,8,128]{2,1,0:T(8,128)(2,1)S(1)} collective-permute-done((bf16[27,8,128]{2,1,0:T(8,128)(2,1)S(1)}, bf16[27,8,128]{2,1,0:T(8,128)(2,1)S(1)}, u32[]{:S(2)}, u32[]{:S(2)}) %collective-permute-start.24) | collective-permute-done | bytes 55328 | tf_op jit(solution)/shard_map/ppermute | solution.py:295
  101.8 1.4 collective-permute-start.26
  103.1 1.5 %collective-permute-start.18 = (bf16[8,64,128]{2,1,0:T(8,128)(2,1)S(1)}, bf16[8,64,128]{2,1,0:T(8,128)(2,1)S(1)}, u32[]{:S(2)}, u32[]{:S(2)}) collective-permute-start(bf16[8,64,128]{2,1,0:T(8,128)(2,1)S(1)} %get-tuple-element.43), channel_id=1, source_target_pairs={{0,2},{1,3},{2,0},{3,1},{4,6},{5,7},{6,4},{7,5},{8,10},{9,11},{10,... | collective-permute-start | bytes 393224 | tf_op jit(solution)/shard_map/ppermute | solution.py:274
  104.7 1.1 collective-permute-start.19
  105.8 3.6 %collective-permute-done.26 = bf16[27,8,128]{2,1,0:T(8,128)(2,1)S(1)} collective-permute-done((bf16[27,8,128]{2,1,0:T(8,128)(2,1)S(1)}, bf16[27,8,128]{2,1,0:T(8,128)(2,1)S(1)}, u32[]{:S(2)}, u32[]{:S(2)}) %collective-permute-start.26) | collective-permute-done | bytes 55328 | tf_op jit(solution)/shard_map/ppermute | solution.py:290
  109.4 0.6 collective-permute-start.29
  109.9 1.8 %collective-permute-start.28 = (bf16[27,8,128]{2,1,0:T(8,128)(2,1)S(1)}, bf16[27,8,128]{2,1,0:T(8,128)(2,1)S(1)}, u32[]{:S(2)}, u32[]{:S(2)}) collective-permute-start(bf16[27,8,128]{2,1,0:T(8,128)(2,1)S(1)} %add_convert_fusion.1.refs_1_), channel_id=1, source_target_pairs={{0,64},{16,80},{32,96},{48,112},{64,0},{80,16},{96,32},{112,48},{1... | collective-permute-start | bytes 165896 | tf_op jit(solution)/shard_map/ppermute | solution.py:295
  111.8 1.9 %collective-permute-start.27 = (bf16[27,8,128]{2,1,0:T(8,128)(2,1)S(1)}, bf16[27,8,128]{2,1,0:T(8,128)(2,1)S(1)}, u32[]{:S(2)}, u32[]{:S(2)}) collective-permute-start(bf16[27,8,128]{2,1,0:T(8,128)(2,1)S(1)} %add_convert_fusion.1.refs_1_), channel_id=1, source_target_pairs={{0,32},{16,48},{32,64},{48,80},{64,96},{80,112},{96,0},{112,16},{1... | collective-permute-start | bytes 165896 | tf_op jit(solution)/shard_map/ppermute | solution.py:295
  113.8 0.1 collective-permute-done.28.refs_3_
  113.9 2.9 %collective-permute-done.27.refs_2_ = bf16[27,8,128]{2,1,0:T(8,128)(2,1)S(1)} collective-permute-done((bf16[27,8,128]{2,1,0:T(8,128)(2,1)S(1)}, bf16[27,8,128]{2,1,0:T(8,128)(2,1)S(1)}, u32[]{:S(2)}, u32[]{:S(2)}) %collective-permute-start.27) | collective-permute-done | bytes 55328 | tf_op jit(solution)/shard_map/ppermute | solution.py:295
  116.8 0.6 shard_map.74.refs_1_
  117.4 5.9 %collective-permute-start.32 = (bf16[27,16,256]{2,1,0:T(8,128)(2,1)S(1)}, bf16[27,16,256]{2,1,0:T(8,128)(2,1)S(1)}, u32[]{:S(2)}, u32[]{:S(2)}) collective-permute-start(bf16[27,16,256]{2,1,0:T(8,128)(2,1)S(1)} %shard_map.74.refs_1_), channel_id=1, source_target_pairs={{0,12},{4,0},{8,4},{12,8},{1,13},{5,1},{9,5},{13,9},{2,14},{6,2},{... | collective-permute-start | bytes 663560 | tf_op jit(solution)/shard_map/ppermute | solution.py:274
  123.4 0.3 collective-permute-start.31
  123.7 0.4 collective-permute-start.30
  124.0 5.0 %collective-permute-done.32.refs_4_ = bf16[27,16,256]{2,1,0:T(8,128)(2,1)S(1)} collective-permute-done((bf16[27,16,256]{2,1,0:T(8,128)(2,1)S(1)}, bf16[27,16,256]{2,1,0:T(8,128)(2,1)S(1)}, u32[]{:S(2)}, u32[]{:S(2)}) %collective-permute-start.32) | collective-permute-done | bytes 221216 | tf_op jit(solution)/shard_map/ppermute | solution.py:274
  129.1 0.7 collective-permute-done.31.refs_3_
  129.8 3.1 %collective-permute-done.30.refs_2_ = bf16[27,16,256]{2,1,0:T(8,128)(2,1)S(1)} collective-permute-done((bf16[27,16,256]{2,1,0:T(8,128)(2,1)S(1)}, bf16[27,16,256]{2,1,0:T(8,128)(2,1)S(1)}, u32[]{:S(2)}, u32[]{:S(2)}) %collective-permute-start.30) | collective-permute-done | bytes 221216 | tf_op jit(solution)/shard_map/ppermute | solution.py:274
  132.8 0.6 shard_map.75
  133.4 4.7 %collective-permute-start.33 = (bf16[27,64,256]{2,1,0:T(8,128)(2,1)S(1)}, bf16[27,64,256]{2,1,0:T(8,128)(2,1)S(1)}, u32[]{:S(2)}, u32[]{:S(2)}) collective-permute-start(bf16[27,64,256]{2,1,0:T(8,128)(2,1)S(1)} %shard_map.75), channel_id=1, source_target_pairs={{0,16},{16,0},{32,48},{48,32},{64,80},{80,64},{96,112},{112,96},{1... | collective-permute-start | bytes 2654216 | tf_op jit(solution)/shard_map/ppermute | solution.py:290
  138.2 2.1 %collective-permute-done.33 = bf16[27,64,256]{2,1,0:T(8,128)(2,1)S(1)} collective-permute-done((bf16[27,64,256]{2,1,0:T(8,128)(2,1)S(1)}, bf16[27,64,256]{2,1,0:T(8,128)(2,1)S(1)}, u32[]{:S(2)}, u32[]{:S(2)}) %collective-permute-start.33) | collective-permute-done | bytes 884768 | tf_op jit(solution)/shard_map/ppermute | solution.py:290
  140.2 0.1 broadcast_select_fusion
  140.3 2.2 %convert_bitcast_fusion = (f32[64,3,3,3,256]{4,0,3,2,1:T(8,128)}, f32[64,3,3,3,256]{4,0,3,2,1:T(8,128)}) fusion(bf16[3,3,3,64,256]{4,3,2,1,0:T(8,128)(2,1)S(1)} %bitcast.33, bf16[3,3,3,64,256]{4,3,2,1,0:T(8,128)(2,1)S(1)} %bitcast.34), kind=kLoop, calls=%fused_computation | loop fusion | flops 884736 | bytes 5308416 | tf_op jit(solution)/shard_map/transpose | solution.py:321
  (30 shorter events, 0.4 us)
Async XLA Ops:
  0.7 0.9 copy-start.1
  1.6 0.9 copy-start.2
  3.1 5.3 %collective-permute-start = (bf16[4,64,128]{2,1,0:T(8,128)(2,1)S(1)}, bf16[4,64,128]{2,1,0:T(8,128)(2,1)S(1)}, u32[]{:S(2)}, u32[]{:S(2)}) collective-permute-start(bf16[4,64,128]{2,1,0:T(8,128)(2,1)S(1)} %get-tuple-element.26), channel_id=1, source_target_pairs={{0,4},{4,8},{8,12},{1,5},{5,9},{9,13},{2,6},{6,10},{10,14},{3,7},{... | collective-permute-start | bytes 196616 | tf_op jit(solution)/shard_map/ppermute | solution.py:12
  7.1 5.0 %collective-permute-start.1 = (bf16[4,64,128]{2,1,0:T(8,128)(2,1)S(1)}, bf16[4,64,128]{2,1,0:T(8,128)(2,1)S(1)}, u32[]{:S(2)}, u32[]{:S(2)}) collective-permute-start(bf16[4,64,128]{2,1,0:T(8,128)(2,1)S(1)} %get-tuple-element.27), channel_id=1, source_target_pairs={{4,0},{8,4},{12,8},{5,1},{9,5},{13,9},{6,2},{10,6},{14,10},{7,3},{... | collective-permute-start | bytes 196616 | tf_op jit(solution)/shard_map/ppermute | solution.py:12
  12.7 11.3 %collective-permute-start.5 = (bf16[2,6,64,128]{3,2,1,0:T(8,128)(2,1)S(1)}, bf16[2,6,64,128]{3,2,1,0:T(8,128)(2,1)S(1)}, u32[]{:S(2)}, u32[]{:S(2)}) collective-permute-start(bf16[2,6,64,128]{3,2,1,0:T(8,128)(2,1)S(1)} %get-tuple-element.28.refs_1_), channel_id=1, source_target_pairs={{0,16},{16,32},{32,48},{48,64},{64,80},{80,96},{96,112},{112,128},... | collective-permute-start | bytes 589832 | tf_op jit(solution)/shard_map/ppermute | solution.py:12
  18.2 7.8 %collective-permute-start.9 = (bf16[2,6,64,128]{3,2,1,0:T(8,128)(2,1)S(1)}, bf16[2,6,64,128]{3,2,1,0:T(8,128)(2,1)S(1)}, u32[]{:S(2)}, u32[]{:S(2)}) collective-permute-start(bf16[2,6,64,128]{3,2,1,0:T(8,128)(2,1)S(1)} %get-tuple-element.29.refs_9_.refs_8_), channel_id=1, source_target_pairs={{16,0},{32,16},{48,32},{64,48},{80,64},{96,80},{112,96},{128,112},... | collective-permute-start | bytes 589832 | tf_op jit(solution)/shard_map/ppermute | solution.py:12
  20.1 11.4 %collective-permute-start.4 = (bf16[2,6,64,128]{3,2,1,0:T(8,128)(2,1)S(1)}, bf16[2,6,64,128]{3,2,1,0:T(8,128)(2,1)S(1)}, u32[]{:S(2)}, u32[]{:S(2)}) collective-permute-start(bf16[2,6,64,128]{3,2,1,0:T(8,128)(2,1)S(1)} %get-tuple-element.28.refs_1_), channel_id=1, source_target_pairs={{0,3},{1,0},{2,1},{3,2},{4,7},{5,4},{6,5},{7,6},{8,11},{9,8},{10,9... | collective-permute-start | bytes 589832 | tf_op jit(solution)/shard_map/ppermute | solution.py:274
  22.9 8.6 %collective-permute-start.3 = (bf16[2,6,64,128]{3,2,1,0:T(8,128)(2,1)S(1)}, bf16[2,6,64,128]{3,2,1,0:T(8,128)(2,1)S(1)}, u32[]{:S(2)}, u32[]{:S(2)}) collective-permute-start(bf16[2,6,64,128]{3,2,1,0:T(8,128)(2,1)S(1)} %get-tuple-element.28.refs_1_), channel_id=1, source_target_pairs={{0,2},{1,3},{2,0},{3,1},{4,6},{5,7},{6,4},{7,5},{8,10},{9,11},{10,... | collective-permute-start | bytes 589832 | tf_op jit(solution)/shard_map/ppermute | solution.py:274
  23.3 12.6 %collective-permute-start.2 = (bf16[2,6,64,128]{3,2,1,0:T(8,128)(2,1)S(1)}, bf16[2,6,64,128]{3,2,1,0:T(8,128)(2,1)S(1)}, u32[]{:S(2)}, u32[]{:S(2)}) collective-permute-start(bf16[2,6,64,128]{3,2,1,0:T(8,128)(2,1)S(1)} %get-tuple-element.28.refs_1_), channel_id=1, source_target_pairs={{0,1},{1,2},{2,3},{3,0},{4,5},{5,6},{6,7},{7,4},{8,9},{9,10},{10,1... | collective-permute-start | bytes 589832 | tf_op jit(solution)/shard_map/ppermute | solution.py:274
  24.0 14.0 %collective-permute-start.8 = (bf16[2,6,64,128]{3,2,1,0:T(8,128)(2,1)S(1)}, bf16[2,6,64,128]{3,2,1,0:T(8,128)(2,1)S(1)}, u32[]{:S(2)}, u32[]{:S(2)}) collective-permute-start(bf16[2,6,64,128]{3,2,1,0:T(8,128)(2,1)S(1)} %collective-permute-done.5.refs_5_), channel_id=1, source_target_pairs={{0,3},{1,0},{2,1},{3,2},{4,7},{5,4},{6,5},{7,6},{8,11},{9,8},{10,9... | collective-permute-start | bytes 589832 | tf_op jit(solution)/shard_map/ppermute | solution.py:274
  26.0 13.6 %collective-permute-start.7 = (bf16[2,6,64,128]{3,2,1,0:T(8,128)(2,1)S(1)}, bf16[2,6,64,128]{3,2,1,0:T(8,128)(2,1)S(1)}, u32[]{:S(2)}, u32[]{:S(2)}) collective-permute-start(bf16[2,6,64,128]{3,2,1,0:T(8,128)(2,1)S(1)} %collective-permute-done.5.refs_5_), channel_id=1, source_target_pairs={{0,2},{1,3},{2,0},{3,1},{4,6},{5,7},{6,4},{7,5},{8,10},{9,11},{10,... | collective-permute-start | bytes 589832 | tf_op jit(solution)/shard_map/ppermute | solution.py:274
  31.5 10.2 %collective-permute-start.6 = (bf16[2,6,64,128]{3,2,1,0:T(8,128)(2,1)S(1)}, bf16[2,6,64,128]{3,2,1,0:T(8,128)(2,1)S(1)}, u32[]{:S(2)}, u32[]{:S(2)}) collective-permute-start(bf16[2,6,64,128]{3,2,1,0:T(8,128)(2,1)S(1)} %collective-permute-done.5.refs_5_), channel_id=1, source_target_pairs={{0,1},{1,2},{2,3},{3,0},{4,5},{5,6},{6,7},{7,4},{8,9},{9,10},{10,1... | collective-permute-start | bytes 589832 | tf_op jit(solution)/shard_map/ppermute | solution.py:274
  47.1 9.3 %collective-permute-start.11 = (bf16[16,64,128]{2,1,0:T(8,128)(2,1)S(1)}, bf16[16,64,128]{2,1,0:T(8,128)(2,1)S(1)}, u32[]{:S(2)}, u32[]{:S(2)}) collective-permute-start(bf16[16,64,128]{2,1,0:T(8,128)(2,1)S(1)} %get-tuple-element.34), channel_id=1, source_target_pairs={{0,2},{1,3},{2,0},{3,1},{4,6},{5,7},{6,4},{7,5},{8,10},{9,11},{10,... | collective-permute-start | bytes 786440 | tf_op jit(solution)/shard_map/ppermute | solution.py:274
  47.4 12.6 %collective-permute-start.12 = (bf16[16,64,128]{2,1,0:T(8,128)(2,1)S(1)}, bf16[16,64,128]{2,1,0:T(8,128)(2,1)S(1)}, u32[]{:S(2)}, u32[]{:S(2)}) collective-permute-start(bf16[16,64,128]{2,1,0:T(8,128)(2,1)S(1)} %get-tuple-element.35), channel_id=1, source_target_pairs={{0,3},{1,0},{2,1},{3,2},{4,7},{5,4},{6,5},{7,6},{8,11},{9,8},{10,9... | collective-permute-start | bytes 786440 | tf_op jit(solution)/shard_map/ppermute | solution.py:274
  48.3 14.2 %collective-permute-start.10 = (bf16[16,64,128]{2,1,0:T(8,128)(2,1)S(1)}, bf16[16,64,128]{2,1,0:T(8,128)(2,1)S(1)}, u32[]{:S(2)}, u32[]{:S(2)}) collective-permute-start(bf16[16,64,128]{2,1,0:T(8,128)(2,1)S(1)} %get-tuple-element.33.refs_7_), channel_id=1, source_target_pairs={{0,1},{1,2},{2,3},{3,0},{4,5},{5,6},{6,7},{7,4},{8,9},{9,10},{10,1... | collective-permute-start | bytes 786440 | tf_op jit(solution)/shard_map/ppermute | solution.py:274
  67.5 5.1 %collective-permute-start.15 = (bf16[4,27,16,256]{3,2,1,0:T(8,128)(2,1)S(1)}, bf16[4,27,16,256]{3,2,1,0:T(8,128)(2,1)S(1)}, u32[]{:S(2)}, u32[]{:S(2)}) collective-permute-start(bf16[4,27,16,256]{3,2,1,0:T(8,128)(2,1)S(1)} %get-tuple-element.40), channel_id=1, source_target_pairs={{0,16},{16,0},{32,48},{48,32},{64,80},{80,64},{96,112},{112,96},{1... | collective-permute-start | bytes 2654216 | tf_op jit(solution)/shard_map/ppermute | solution.py:290
  68.2 7.0 %collective-permute-start.13 = (bf16[2,64,128]{2,1,0:T(8,128)(2,1)S(1)}, bf16[2,64,128]{2,1,0:T(8,128)(2,1)S(1)}, u32[]{:S(2)}, u32[]{:S(2)}) collective-permute-start(bf16[2,64,128]{2,1,0:T(8,128)(2,1)S(1)} %get-tuple-element.36), channel_id=1, source_target_pairs={{0,4},{4,8},{8,12},{1,5},{5,9},{9,13},{2,6},{6,10},{10,14},{3,7},{... | collective-permute-start | bytes 98312 | tf_op jit(solution)/shard_map/ppermute | solution.py:12
  71.3 4.7 %collective-permute-start.14 = (bf16[2,64,128]{2,1,0:T(8,128)(2,1)S(1)}, bf16[2,64,128]{2,1,0:T(8,128)(2,1)S(1)}, u32[]{:S(2)}, u32[]{:S(2)}) collective-permute-start(bf16[2,64,128]{2,1,0:T(8,128)(2,1)S(1)} %get-tuple-element.37), channel_id=1, source_target_pairs={{4,0},{8,4},{12,8},{5,1},{9,5},{13,9},{6,2},{10,6},{14,10},{7,3},{... | collective-permute-start | bytes 98312 | tf_op jit(solution)/shard_map/ppermute | solution.py:12
  72.9 14.2 %copy-start = (bf16[64,3,3,3,256]{4,0,3,2,1:T(8,128)(2,1)S(1)}, bf16[64,3,3,3,256]{4,0,3,2,1:T(8,128)(2,1)}, u32[]{:S(2)}) copy-start(bf16[64,3,3,3,256]{4,0,3,2,1:T(8,128)(2,1)} %param.6) | copy-start | bytes 2654212
  73.0 16.2 %collective-permute-start.20 = (bf16[27,16,256]{2,1,0:T(8,128)(2,1)S(1)}, bf16[27,16,256]{2,1,0:T(8,128)(2,1)S(1)}, u32[]{:S(2)}, u32[]{:S(2)}) collective-permute-start(bf16[27,16,256]{2,1,0:T(8,128)(2,1)S(1)} %get-tuple-element.55.refs_4_), channel_id=1, source_target_pairs={{0,4},{4,8},{8,12},{12,0},{1,5},{5,9},{9,13},{13,1},{2,6},{6,10},{... | collective-permute-start | bytes 663560 | tf_op jit(solution)/shard_map/ppermute | solution.py:274
  76.5 10.6 %collective-permute-start.16 = (bf16[2,6,64,128]{3,2,1,0:T(8,128)(2,1)S(1)}, bf16[2,6,64,128]{3,2,1,0:T(8,128)(2,1)S(1)}, u32[]{:S(2)}, u32[]{:S(2)}) collective-permute-start(bf16[2,6,64,128]{3,2,1,0:T(8,128)(2,1)S(1)} %shard_map.71.refs_1_), channel_id=1, source_target_pairs={{16,0},{32,16},{48,32},{64,48},{80,64},{96,80},{112,96},{128,112},... | collective-permute-start | bytes 589832 | tf_op jit(solution)/shard_map/ppermute | solution.py:12
  79.9 9.3 %collective-permute-start.22 = (bf16[27,16,256]{2,1,0:T(8,128)(2,1)S(1)}, bf16[27,16,256]{2,1,0:T(8,128)(2,1)S(1)}, u32[]{:S(2)}, u32[]{:S(2)}) collective-permute-start(bf16[27,16,256]{2,1,0:T(8,128)(2,1)S(1)} %get-tuple-element.53), channel_id=1, source_target_pairs={{0,12},{4,0},{8,4},{12,8},{1,13},{5,1},{9,5},{13,9},{2,14},{6,2},{... | collective-permute-start | bytes 663560 | tf_op jit(solution)/shard_map/ppermute | solution.py:274
  80.0 9.2 %collective-permute-start.21 = (bf16[27,16,256]{2,1,0:T(8,128)(2,1)S(1)}, bf16[27,16,256]{2,1,0:T(8,128)(2,1)S(1)}, u32[]{:S(2)}, u32[]{:S(2)}) collective-permute-start(bf16[27,16,256]{2,1,0:T(8,128)(2,1)S(1)} %get-tuple-element.54), channel_id=1, source_target_pairs={{0,8},{4,12},{8,0},{12,4},{1,9},{5,13},{9,1},{13,5},{2,10},{6,14},... | collective-permute-start | bytes 663560 | tf_op jit(solution)/shard_map/ppermute | solution.py:274
  89.9 8.7 %collective-permute-start.23 = (bf16[27,8,128]{2,1,0:T(8,128)(2,1)S(1)}, bf16[27,8,128]{2,1,0:T(8,128)(2,1)S(1)}, u32[]{:S(2)}, u32[]{:S(2)}) collective-permute-start(bf16[27,8,128]{2,1,0:T(8,128)(2,1)S(1)} %get-tuple-element.46), channel_id=1, source_target_pairs={{0,32},{16,48},{32,64},{48,80},{64,96},{80,112},{96,0},{112,16},{1... | collective-permute-start | bytes 165896 | tf_op jit(solution)/shard_map/ppermute | solution.py:295
  93.1 8.6 %collective-permute-start.24 = (bf16[27,8,128]{2,1,0:T(8,128)(2,1)S(1)}, bf16[27,8,128]{2,1,0:T(8,128)(2,1)S(1)}, u32[]{:S(2)}, u32[]{:S(2)}) collective-permute-start(bf16[27,8,128]{2,1,0:T(8,128)(2,1)S(1)} %get-tuple-element.47), channel_id=1, source_target_pairs={{0,64},{16,80},{32,96},{48,112},{64,0},{80,16},{96,32},{112,48},{1... | collective-permute-start | bytes 165896 | tf_op jit(solution)/shard_map/ppermute | solution.py:295
  97.3 4.4 %collective-permute-start.25 = (bf16[27,8,128]{2,1,0:T(8,128)(2,1)S(1)}, bf16[27,8,128]{2,1,0:T(8,128)(2,1)S(1)}, u32[]{:S(2)}, u32[]{:S(2)}) collective-permute-start(bf16[27,8,128]{2,1,0:T(8,128)(2,1)S(1)} %get-tuple-element.48), channel_id=1, source_target_pairs={{0,96},{16,112},{32,0},{48,16},{64,32},{80,48},{96,64},{112,80},{1... | collective-permute-start | bytes 165896 | tf_op jit(solution)/shard_map/ppermute | solution.py:295
  101.8 7.6 %collective-permute-start.26 = (bf16[27,8,128]{2,1,0:T(8,128)(2,1)S(1)}, bf16[27,8,128]{2,1,0:T(8,128)(2,1)S(1)}, u32[]{:S(2)}, u32[]{:S(2)}) collective-permute-start(bf16[27,8,128]{2,1,0:T(8,128)(2,1)S(1)} %add_convert_fusion.2), channel_id=1, source_target_pairs={{0,128},{16,144},{32,160},{48,176},{64,192},{80,208},{96,224},{112... | collective-permute-start | bytes 165896 | tf_op jit(solution)/shard_map/ppermute | solution.py:290
  103.1 8.6 %collective-permute-start.17 = (bf16[8,64,128]{2,1,0:T(8,128)(2,1)S(1)}, bf16[8,64,128]{2,1,0:T(8,128)(2,1)S(1)}, u32[]{:S(2)}, u32[]{:S(2)}) collective-permute-start(bf16[8,64,128]{2,1,0:T(8,128)(2,1)S(1)} %get-tuple-element.42), channel_id=1, source_target_pairs={{0,1},{1,2},{2,3},{3,0},{4,5},{5,6},{6,7},{7,4},{8,9},{9,10},{10,1... | collective-permute-start | bytes 393224 | tf_op jit(solution)/shard_map/ppermute | solution.py:274
  103.1 10.5 %collective-permute-start.18 = (bf16[8,64,128]{2,1,0:T(8,128)(2,1)S(1)}, bf16[8,64,128]{2,1,0:T(8,128)(2,1)S(1)}, u32[]{:S(2)}, u32[]{:S(2)}) collective-permute-start(bf16[8,64,128]{2,1,0:T(8,128)(2,1)S(1)} %get-tuple-element.43), channel_id=1, source_target_pairs={{0,2},{1,3},{2,0},{3,1},{4,6},{5,7},{6,4},{7,5},{8,10},{9,11},{10,... | collective-permute-start | bytes 393224 | tf_op jit(solution)/shard_map/ppermute | solution.py:274
  104.7 9.0 %collective-permute-start.19 = (bf16[8,64,128]{2,1,0:T(8,128)(2,1)S(1)}, bf16[8,64,128]{2,1,0:T(8,128)(2,1)S(1)}, u32[]{:S(2)}, u32[]{:S(2)}) collective-permute-start(bf16[8,64,128]{2,1,0:T(8,128)(2,1)S(1)} %get-tuple-element.44), channel_id=1, source_target_pairs={{0,3},{1,0},{2,1},{3,2},{4,7},{5,4},{6,5},{7,6},{8,11},{9,8},{10,9... | collective-permute-start | bytes 393224 | tf_op jit(solution)/shard_map/ppermute | solution.py:274
  109.4 4.4 %collective-permute-start.29 = (bf16[27,8,128]{2,1,0:T(8,128)(2,1)S(1)}, bf16[27,8,128]{2,1,0:T(8,128)(2,1)S(1)}, u32[]{:S(2)}, u32[]{:S(2)}) collective-permute-start(bf16[27,8,128]{2,1,0:T(8,128)(2,1)S(1)} %add_convert_fusion.1.refs_1_), channel_id=1, source_target_pairs={{0,96},{16,112},{32,0},{48,16},{64,32},{80,48},{96,64},{112,80},{1... | collective-permute-start | bytes 165896 | tf_op jit(solution)/shard_map/ppermute | solution.py:295
  109.9 3.9 %collective-permute-start.28 = (bf16[27,8,128]{2,1,0:T(8,128)(2,1)S(1)}, bf16[27,8,128]{2,1,0:T(8,128)(2,1)S(1)}, u32[]{:S(2)}, u32[]{:S(2)}) collective-permute-start(bf16[27,8,128]{2,1,0:T(8,128)(2,1)S(1)} %add_convert_fusion.1.refs_1_), channel_id=1, source_target_pairs={{0,64},{16,80},{32,96},{48,112},{64,0},{80,16},{96,32},{112,48},{1... | collective-permute-start | bytes 165896 | tf_op jit(solution)/shard_map/ppermute | solution.py:295
  111.8 5.1 %collective-permute-start.27 = (bf16[27,8,128]{2,1,0:T(8,128)(2,1)S(1)}, bf16[27,8,128]{2,1,0:T(8,128)(2,1)S(1)}, u32[]{:S(2)}, u32[]{:S(2)}) collective-permute-start(bf16[27,8,128]{2,1,0:T(8,128)(2,1)S(1)} %add_convert_fusion.1.refs_1_), channel_id=1, source_target_pairs={{0,32},{16,48},{32,64},{48,80},{64,96},{80,112},{96,0},{112,16},{1... | collective-permute-start | bytes 165896 | tf_op jit(solution)/shard_map/ppermute | solution.py:295
  113.7 26.6 %copy-start.3 = (bf16[8,64,128]{2,1,0:T(8,128)(2,1)}, bf16[8,64,128]{2,1,0:T(8,128)(2,1)S(1)}, u32[]{:S(2)}) copy-start(bf16[8,64,128]{2,1,0:T(8,128)(2,1)S(1)} %add_convert_fusion) | copy-start | bytes 393220
  117.4 11.6 %collective-permute-start.32 = (bf16[27,16,256]{2,1,0:T(8,128)(2,1)S(1)}, bf16[27,16,256]{2,1,0:T(8,128)(2,1)S(1)}, u32[]{:S(2)}, u32[]{:S(2)}) collective-permute-start(bf16[27,16,256]{2,1,0:T(8,128)(2,1)S(1)} %shard_map.74.refs_1_), channel_id=1, source_target_pairs={{0,12},{4,0},{8,4},{12,8},{1,13},{5,1},{9,5},{13,9},{2,14},{6,2},{... | collective-permute-start | bytes 663560 | tf_op jit(solution)/shard_map/ppermute | solution.py:274
  123.4 6.4 %collective-permute-start.31 = (bf16[27,16,256]{2,1,0:T(8,128)(2,1)S(1)}, bf16[27,16,256]{2,1,0:T(8,128)(2,1)S(1)}, u32[]{:S(2)}, u32[]{:S(2)}) collective-permute-start(bf16[27,16,256]{2,1,0:T(8,128)(2,1)S(1)} %shard_map.74.refs_1_), channel_id=1, source_target_pairs={{0,8},{4,12},{8,0},{12,4},{1,9},{5,13},{9,1},{13,5},{2,10},{6,14},... | collective-permute-start | bytes 663560 | tf_op jit(solution)/shard_map/ppermute | solution.py:274
  123.7 9.1 %collective-permute-start.30 = (bf16[27,16,256]{2,1,0:T(8,128)(2,1)S(1)}, bf16[27,16,256]{2,1,0:T(8,128)(2,1)S(1)}, u32[]{:S(2)}, u32[]{:S(2)}) collective-permute-start(bf16[27,16,256]{2,1,0:T(8,128)(2,1)S(1)} %shard_map.74.refs_1_), channel_id=1, source_target_pairs={{0,4},{4,8},{8,12},{12,0},{1,5},{5,9},{9,13},{13,1},{2,6},{6,10},{... | collective-permute-start | bytes 663560 | tf_op jit(solution)/shard_map/ppermute | solution.py:274
  133.4 6.8 %collective-permute-start.33 = (bf16[27,64,256]{2,1,0:T(8,128)(2,1)S(1)}, bf16[27,64,256]{2,1,0:T(8,128)(2,1)S(1)}, u32[]{:S(2)}, u32[]{:S(2)}) collective-permute-start(bf16[27,64,256]{2,1,0:T(8,128)(2,1)S(1)} %shard_map.75), channel_id=1, source_target_pairs={{0,16},{16,0},{32,48},{48,32},{64,80},{80,64},{96,112},{112,96},{1... | collective-permute-start | bytes 2654216 | tf_op jit(solution)/shard_map/ppermute | solution.py:290

commit v5 on v2

--- a/solution.py
+++ b/solution.py
@@ -48,9 +48,9 @@
     for f in range(4):
         for r in range(6):
             if r == 0:
-                cell = above[f, 0]
+                cell = above[f]
             elif r == 5:
-                cell = below[f, 0]
+                cell = below[f]
             else:
                 cell = early[f, r - 1] if f < 2 else own[f - 2, r - 1]
             for k in range(4):
@@ -73,15 +73,10 @@
             act[t * 4 + i] = (value * jax.nn.sigmoid(value)).astype(jnp.bfloat16)
 
 
-def spread(own, late, above, below, wide):
+def spread(own, late, wide):
     for f in range(4):
         for r in range(6):
-            if r == 0:
-                cell = above[f, 0]
-            elif r == 5:
-                cell = below[f, 0]
-            else:
-                cell = own[f, r - 1] if f < 2 else late[f - 2, r - 1]
+            cell = own[f, r] if f < 2 else late[f - 2, r]
             moved = lanes_moved(cell)
             for n, (a, b) in enumerate(TAPS):
                 t, i = f - 2 + a, r - 2 + b
@@ -92,9 +87,9 @@
                         wide[row : row + 64, p * 128 : p * 128 + 128] = moved[e]
 
 
-def transposed_body(place, own, late, above, below, weight, mine, one, two, three, wide, full):
+def transposed_body(place, own, late, weight, mine, one, two, three, wide, full):
     me = place[0]
-    spread(own, late, above, below, wide)
+    spread(own, late, wide)
     full[...] = lax.dot_general(
         weight[...], wide[...], (((0,), (0,)), ((), ())), preferred_element_type=jnp.float32
     )
@@ -104,6 +99,28 @@
             out[p] = full[pl.ds(at, 64), p * 128 : p * 128 + 128].astype(out.dtype)
 
 
+def frame_rows_body(place, early, own, heads, tails):
+    for f in range(4):
+        for row, out in ((0, heads), (3, tails)):
+            out[f] = early[f, row] if f < 2 else own[f - 2, row]
+
+
+def edge_rows_body(place, cells, heads, tails):
+    for f in range(2):
+        heads[f] = cells[f, 0]
+        tails[f] = cells[f, 3]
+
+
+def framed_body(place, above, below, *blocks):
+    half = len(blocks) // 2
+    for n in range(half):
+        for f in range(2):
+            blocks[half + n][f, 0] = above[2 * n + f]
+            blocks[half + n][f, 5] = below[2 * n + f]
+            for r in range(4):
+                blocks[half + n][f, r + 1] = blocks[n][f, r]
+
+
 def against(left, right):
     return lax.dot_general(left, right, (((1,), (1,)), ((), ())), preferred_element_type=jnp.float32)
 
@@ -113,21 +130,36 @@
         out[(q + 4 - height) % 4, tap] = rows[q * 16 : q * 16 + 16].astype(jnp.bfloat16)
 
 
-def first_filter_body(place, panel, gradient, out, moved):
+def first_filter_body(
+    place, panel, pre, mine, r1, r2, r3, gradient, heads, tails, result, moved
+):
     height = place[1]
     for p in range(8):
-        for e, part in enumerate(lanes_moved(gradient[p])):
+        value = pre[p]
+        sig = jax.nn.sigmoid(value)
+        total = mine[p]
+        for part in (r1, r2, r3):
+            total = total + part[p].astype(jnp.float32)
+        total = (total * sig * (1.0 + value * (1.0 - sig))).astype(jnp.bfloat16)
+        gradient[p // 4, p % 4] = total
+        if p % 4 == 0:
+            heads[p // 4] = total
+        if p % 4 == 3:
+            tails[p // 4] = total
+        for e, part in enumerate(lanes_moved(total)):
             moved[e * 64 : e * 64 + 64, p * 128 : p * 128 + 128] = part
     for n, (a, b) in enumerate(TAPS):
         window = jnp.concatenate([panel[(t + a) * 6 + i + b] for t, i in SPOTS], 1)
         sums = against(moved[...], window)
         for e in range(3):
-            store_filter(out, height, n * 3 + e, sums[e * 64 : e * 64 + 64])
-
-
-def second_filter_body(place, own, late, above, below, a0, a1, a2, a3, out, wide, acts):
-    me, height = place[0], place[1]
-    spread(own, late, above, below, wide)
+            store_filter(result, height, n * 3 + e, sums[e * 64 : e * 64 + 64])
+
+
+def second_filter_body(
+    place, first, a0, a1, a2, a3, own, late, keep, give, wide, acts, result
+):
+    me, height, core = place[0], place[1], place[3]
+    spread(own, late, wide)
     for k, part in enumerate((a0, a1, a2, a3)):
         at = pl.multiple_of(((me + 4 - k) % 4) * 64, 64)
         for p in range(8):
@@ -135,44 +167,74 @@
     for n in range(9):
         sums = against(wide[n * 192 : n * 192 + 192], acts[...])
         for e in range(3):
-            store_filter(out, height, n * 3 + e, sums[e * 64 : e * 64 + 64])
+            store_filter(result, height, n * 3 + e, sums[e * 64 : e * 64 + 64])
+
+    @pl.when(core == 0)
+    def _():
+        keep[...] = first[...]
+        give[...] = result[...]
+
+    @pl.when(core == 1)
+    def _():
+        keep[...] = result[...]
+        give[...] = first[...]
 
 
 def shaped(shape, dtype):
     return jax.ShapeDtypeStruct(shape, dtype)
 
 
-def forward(place, own, early, above, below, weight, after):
+def forward(place, *operands, after):
     return call(
         forward_body,
         [shaped((24, 256, 128), jnp.bfloat16), shaped((8, 64, 128), jnp.float32), shaped((8, 64, 128), jnp.bfloat16)],
         [pltpu.VMEM((2304, 1024), jnp.bfloat16), pltpu.VMEM((192, 2304), jnp.bfloat16)],
-        place, own, early, above, below, weight, after=after,
-    )
-
-
-def transposed(place, cells, weight):
+        place, *operands, after=after,
+    )
+
+
+def transposed(place, own, late, weight, after=()):
     return call(
         transposed_body,
         [shaped((8, 64, 128), jnp.float32)] + [shaped((8, 64, 128), jnp.bfloat16)] * 3,
         [pltpu.VMEM((1728, 1024), jnp.bfloat16), pltpu.VMEM((256, 1024), jnp.float32)],
-        place, *cells, weight,
-    )
-
-
-def first_filter(place, panel, gradient):
-    return call(
-        first_filter_body, [shaped((4, 27, 16, 256), jnp.bfloat16)],
-        [pltpu.VMEM((192, 1024), jnp.bfloat16)], place, panel, gradient,
-    )[0]
-
-
-def second_filter(place, cells, acts):
-    return call(
-        second_filter_body, [shaped((4, 27, 16, 256), jnp.bfloat16)],
-        [pltpu.VMEM((1728, 1024), jnp.bfloat16), pltpu.VMEM((256, 1024), jnp.bfloat16)],
-        place, *cells, *acts,
-    )[0]
+        place, own, late, weight, after=after,
+    )
+
+
+def frame_rows(place, early, own):
+    return call(frame_rows_body, [shaped((4, 256, 128), jnp.bfloat16)] * 2, [], place, early, own)
+
+
+def edge_rows(place, cells):
+    return call(edge_rows_body, [shaped((2, 64, 128), jnp.bfloat16)] * 2, [], place, cells)
+
+
+def framed(place, above, below, block):
+    out = [shaped((2, 6, 64, 128), jnp.bfloat16)]
+    return call(framed_body, out, [], place, above, below, block)[0]
+
+
+def first_filter(place, *operands):
+    return call(
+        first_filter_body,
+        [shaped((2, 4, 64, 128), jnp.bfloat16)]
+        + [shaped((2, 64, 128), jnp.bfloat16)] * 2
+        + [shaped((4, 27, 16, 256), jnp.bfloat16)],
+        [pltpu.VMEM((192, 1024), jnp.bfloat16)], place, *operands,
+    )
+
+
+def second_filter(place, *operands, after):
+    return call(
+        second_filter_body,
+        [shaped((4, 27, 16, 256), jnp.bfloat16)] * 2,
+        [
+            pltpu.VMEM((1728, 1024), jnp.bfloat16), pltpu.VMEM((256, 1024), jnp.bfloat16),
+            pltpu.VMEM((4, 27, 16, 256), jnp.bfloat16),
+        ],
+        place, *operands, after=after,
+    )
 
 
 def quarters_body(place, own, one, two, three, mine, first, second, third, sums):
@@ -247,10 +309,8 @@
     return lax.ppermute(block, "tm", route)
 
 
-def summed_pair(part_one, part_two, core):
-    mine = jnp.where(core == 1, part_two, part_one)
-    theirs = jnp.where(core == 1, part_one, part_two)
-    total = mine.astype(jnp.float32) + swapped(theirs, 1).astype(jnp.float32)
+def summed_pair(keep, give):
+    total = keep.astype(jnp.float32) + swapped(give, 1).astype(jnp.float32)
     return [total[0]] + [total[k].astype(jnp.bfloat16) for k in range(1, 4)]
 
 
@@ -275,40 +335,33 @@
     return flat.reshape(3, 3, 3, 64, 256).transpose(3, 0, 1, 2, 4)
 
 
-def edges(first, second):
-    last = first.shape[1] - 1
-    heads = jnp.concatenate([first[:, :1], second[:, :1]], 0)
-    tails = jnp.concatenate([first[:, last:], second[:, last:]], 0)
+def traded(heads, tails):
     return passed_along(tails, "height", 1), passed_along(heads, "height", -1)
-
-
-def with_later(cells):
-    late = passed_along(cells, "tm", -1)
-    return (cells, late) + edges(cells, late)
 
 
 def on_device(frames, grad_out, weight_one, weight_two):
     spot = lax.axis_index("tm")
     core = spot % 2
-    place = jnp.stack([lax.axis_index("chan"), lax.axis_index("height"), (spot // 2) % 4]).astype(jnp.int32)
+    place = jnp.stack([lax.axis_index("chan"), lax.axis_index("height"), (spot // 2) % 4, core])
+    place = place.astype(jnp.int32)
     taps_one = weight_one.transpose(1, 2, 3, 0, 4).reshape(1728, 256)
     taps_two = weight_two.transpose(1, 2, 3, 0, 4).reshape(1728, 256)
     frames_all = jnp.concatenate([frames] + all_rotated(frames, "chan"), 2)
+    grads = framed(place, *traded(*edge_rows(place, grad_out)), grad_out)
+    late = passed_along(grads, "tm", -1)
     early = passed_along(frames_all, "tm", 1)
-    above, below = edges(early, frames_all)
-    grads = with_later(grad_out)
-    act_pieces = transposed(place, grads, taps_two)
+    above, below = traded(*frame_rows(place, early, frames_all))
+    act_pieces = transposed(place, grads, late, taps_two)
     panel, pre, act = forward(
-        place, frames_all, early, above, below, taps_one.reshape(9, 192, 256), [act_pieces[0]]
-    )
-    grad_act = exchanged(act_pieces, "chan")
-    sigmoid_pre = jax.nn.sigmoid(pre)
-    grad_pre = (grad_act * sigmoid_pre * (1.0 + pre * (1.0 - sigmoid_pre))).astype(jnp.bfloat16)
-    part_one = first_filter(place, panel, grad_pre)
-    part_two = second_filter(place, grads, [act] + all_rotated(act, "chan"))
-    pieces = summed_pair(part_one, part_two, core)
-    cells = with_later(grad_pre.reshape(2, 4, 64, 128))
-    gradient_pieces = transposed(place, cells, taps_one)
+        place, frames_all, early, above, below, taps_one.reshape(9, 192, 256), after=[act_pieces[0]]
+    )
+    grad_pre, heads, tails, first = first_filter(place, panel, pre, *sent_on(act_pieces, "chan"))
+    cells = framed(place, *traded(heads, tails), grad_pre)
+    later = passed_along(cells, "tm", -1)
+    acts = [act] + all_rotated(act, "chan")
+    keep, give = second_filter(place, first, *acts, grads, late, after=[cells])
+    pieces = summed_pair(keep, give)
+    gradient_pieces = transposed(place, cells, later, taps_one, after=[pieces[1]])
     grad_frames, grad_one, grad_two = rest_of_sum(place, pieces, gradient_pieces, core)
     return (grad_frames, filter_shape(grad_one), filter_shape(grad_two))
 

time: 141 us -> 130 us (0.922)
  waiting for transfers between devices: 53.8 us -> 40.7 us
  starting transfers between devices: 62.5 us -> 65.1 us
  other arithmetic: 4.77 us -> 2.92 us
    ppermute x9, waiting for transfers between devices: 23.3 us -> 12.5 us  [passed_along(): return lax.ppermute(block, axis, route)]
    ppermute x3, starting transfers between devices: 5.92 us -> 10.8 us  [swapped(): lax.ppermute(block, 'tm', [(i, i ^ distance) for i in range(lax.axis_size...]
    ppermute x6, starting transfers between devices: 12.9 us -> 9.87 us  [quad_rotated(): return lax.ppermute(block, 'tm', route)]
    ppermute x3, waiting for transfers between devices: 4.79 us -> 2.18 us  [swapped(): lax.ppermute(block, 'tm', [(i, i ^ distance) for i in range(lax.axis_size...]
    ppermute x18, starting transfers between devices: 21 us -> 22.5 us  [rotated(): lax.ppermute(block, axis, [(i, (i + distance) % count) for i in range(cou...]
    concatenate x6 -> x0, other arithmetic: 1.49 us -> none  [the longest x3 0.75 us: edges(): heads = jnp.concatenate([first[:, :1], second[:, :1]], 0)]
    pallas_call x8 -> x12, Pallas kernels: 15.1 us -> 16.3 us  [call(): pl.pallas_call(lambda *refs: body(*refs[:used], *refs[rest:]), out_shape=...]
  transfers between devices with their start and end apart: 36 -> 36, of which waited for: 18 -> 17; matrix products, arithmetic and copies ran while one was open for 3% -> 1% of each run, Pallas kernels for 8% -> 9%
where the time goes in v5:
time: 130 us; the launch traced here: 129 us
  starting transfers between devices  65.1 us (50%)
  waiting for transfers between devices  40.7 us (31%)
  Pallas kernels  16.3 us (13%)
  local copies, waits for them, and re-layouts  3.41 us (3%)
  other arithmetic  2.92 us (2%)
    ppermute x18, starting transfers between devices, rotated(): lax.ppermute(block, axis, [(i, (i + distance) % count) for i in range(cou...  22.5 us
    ppermute x9, starting transfers between devices, passed_along(): return lax.ppermute(block, axis, route)  21.9 us
    ppermute x18, waiting for transfers between devices, rotated(): lax.ppermute(block, axis, [(i, (i + distance) % count) for i in range(cou...  16.9 us
    pallas_call x12, Pallas kernels, call(): pl.pallas_call(lambda *refs: body(*refs[:used], *refs[rest:]), out_shape=...  16.3 us
    ppermute x9, waiting for transfers between devices, passed_along(): return lax.ppermute(block, axis, route)  12.5 us
    ppermute x3, starting transfers between devices, swapped(): lax.ppermute(block, 'tm', [(i, i ^ distance) for i in range(lax.axis_size...  10.8 us
    ppermute x6, starting transfers between devices, quad_rotated(): return lax.ppermute(block, 'tm', route)  9.87 us
    ppermute x6, waiting for transfers between devices, quad_rotated(): return lax.ppermute(block, 'tm', route)  9.07 us
  transfers between devices with their start and end apart: 36, of which 17 were waited for; matrix products, arithmetic and copies ran while one was open for 1% of the time, Pallas kernels for 9%

profile of v5, /device:TPU:1, one launch (start us, length us, event | category | flops | bytes accessed | tf_op | source)
XLA Modules:
  0.0 129.4 jit_solution(1390792305100253024)
XLA Ops:
  0.6 2.2 %collective-permute-start = (bf16[2,4,64,128]{3,2,1,0:T(8,128)(2,1)}, bf16[2,4,64,128]{3,2,1,0:T(8,128)(2,1)S(1)}, u32[]{:S(2)}, u32[]{:S(2)}) collective-permute-start(bf16[2,4,64,128]{3,2,1,0:T(8,128)(2,1)} %param.4), channel_id=1, source_target_pairs={{0,1},{1,2},{2,3},{3,0},{4,5},{5,6},{6,7},{7,4},{8,9},{9,10},{10,1... | collective-permute-start | bytes 393224 | tf_op jit(solution)/shard_map/ppermute | solution.py:288
  2.8 2.6 %collective-permute-start.1 = (bf16[2,4,64,128]{3,2,1,0:T(8,128)(2,1)}, bf16[2,4,64,128]{3,2,1,0:T(8,128)(2,1)S(1)}, u32[]{:S(2)}, u32[]{:S(2)}) collective-permute-start(bf16[2,4,64,128]{3,2,1,0:T(8,128)(2,1)} %param.4), channel_id=1, source_target_pairs={{0,2},{1,3},{2,0},{3,1},{4,6},{5,7},{6,4},{7,5},{8,10},{9,11},{10,... | collective-permute-start | bytes 393224 | tf_op jit(solution)/shard_map/ppermute | solution.py:288
  5.5 1.1 collective-permute-start.2
  6.5 0.9 constant_dynamic-update-slice_fusion.3
  7.5 3.8 %collective-permute-done.1 = bf16[2,4,64,128]{3,2,1,0:T(8,128)(2,1)S(1)} collective-permute-done((bf16[2,4,64,128]{3,2,1,0:T(8,128)(2,1)}, bf16[2,4,64,128]{3,2,1,0:T(8,128)(2,1)S(1)}, u32[]{:S(2)}, u32[]{:S(2)}) %collective-permute-start.1) | collective-permute-done | bytes 131104 | tf_op jit(solution)/shard_map/ppermute | solution.py:288
  11.4 5.0 %collective-permute-start.3 = (bf16[2,4,256,128]{3,2,1,0:T(8,128)(2,1)S(1)}, bf16[2,4,256,128]{3,2,1,0:T(8,128)(2,1)S(1)}, u32[]{:S(2)}, u32[]{:S(2)}) collective-permute-start(bf16[2,4,256,128]{3,2,1,0:T(8,128)(2,1)S(1)} %constant_dynamic-update-slice_fusion.refs_2_.refs_1_), channel_id=1, source_target_pairs={{0,16},{16,32},{32,48},{48,64},{64,80},{80,96},{96,112},{112,128},... | collective-permute-start | bytes 1572872 | tf_op jit(solution)/shard_map/ppermute | solution.py:12
  16.5 0.9 copy-done.3
  17.4 0.5 shard_map.68
  18.0 3.1 %collective-permute-start.6 = (bf16[2,64,128]{2,1,0:T(8,128)(2,1)S(1)}, bf16[2,64,128]{2,1,0:T(8,128)(2,1)S(1)}, u32[]{:S(2)}, u32[]{:S(2)}) collective-permute-start(bf16[2,64,128]{2,1,0:T(8,128)(2,1)S(1)} %get-tuple-element.30), channel_id=1, source_target_pairs={{0,4},{4,8},{8,12},{1,5},{5,9},{9,13},{2,6},{6,10},{10,14},{3,7},{... | collective-permute-start | bytes 98312 | tf_op jit(solution)/shard_map/ppermute | solution.py:12
  21.1 1.3 collective-permute-start.7
  22.4 3.3 %collective-permute-done.7.refs_2_ = bf16[2,64,128]{2,1,0:T(8,128)(2,1)S(1)} collective-permute-done((bf16[2,64,128]{2,1,0:T(8,128)(2,1)S(1)}, bf16[2,64,128]{2,1,0:T(8,128)(2,1)S(1)}, u32[]{:S(2)}, u32[]{:S(2)}) %collective-permute-start.7) | collective-permute-done | bytes 32800 | tf_op jit(solution)/shard_map/ppermute | solution.py:12
  25.8 0.6 shard_map.69.refs_1_.refs_6_
  26.3 1.9 %collective-permute-start.8 = (bf16[2,6,64,128]{3,2,1,0:T(8,128)(2,1)S(1)}, bf16[2,6,64,128]{3,2,1,0:T(8,128)(2,1)S(1)}, u32[]{:S(2)}, u32[]{:S(2)}) collective-permute-start(bf16[2,6,64,128]{3,2,1,0:T(8,128)(2,1)S(1)} %shard_map.69.refs_1_.refs_6_), channel_id=1, source_target_pairs={{16,0},{32,16},{48,32},{64,48},{80,64},{96,80},{112,96},{128,112},... | collective-permute-start | bytes 589832 | tf_op jit(solution)/shard_map/ppermute | solution.py:12
  28.3 0.6 shard_map.67
  28.9 3.1 %collective-permute-start.4 = (bf16[4,256,128]{2,1,0:T(8,128)(2,1)S(1)}, bf16[4,256,128]{2,1,0:T(8,128)(2,1)S(1)}, u32[]{:S(2)}, u32[]{:S(2)}) collective-permute-start(bf16[4,256,128]{2,1,0:T(8,128)(2,1)S(1)} %get-tuple-element.28), channel_id=1, source_target_pairs={{0,4},{4,8},{8,12},{1,5},{5,9},{9,13},{2,6},{6,10},{10,14},{3,7},{... | collective-permute-start | bytes 786440 | tf_op jit(solution)/shard_map/ppermute | solution.py:12
  32.0 1.3 collective-permute-start.5
  33.3 2.0 %shard_map.70 = (f32[8,64,128]{2,1,0:T(8,128)S(1)}, bf16[8,64,128]{2,1,0:T(8,128)(2,1)S(1)}, bf16[8,64,128]{2,1,0:T(8,128)(2,1)S(1)}, bf16[8,64,128]{2,1,0:T(8,128)(2,1)S(1)}) custom-call(s32[4]{0:T(128)S(1)} %pad_add_fusion.refs_0_, bf16[2,6,64,128]{3,2,1,0:T(8,128)(2,1)S(1)} %shard_map.69.refs_1_.refs_6_, ...), custom_call_target="tpu_custom_call" | custom-call | tf_op jit(solution)/shard_map/pallas_call | solution.py:24
  35.4 1.0 collective-permute-start.9
  36.4 2.1 %collective-permute-start.10 = (bf16[8,64,128]{2,1,0:T(8,128)(2,1)S(1)}, bf16[8,64,128]{2,1,0:T(8,128)(2,1)S(1)}, u32[]{:S(2)}, u32[]{:S(2)}) collective-permute-start(bf16[8,64,128]{2,1,0:T(8,128)(2,1)S(1)} %get-tuple-element.36), channel_id=1, source_target_pairs={{0,2},{1,3},{2,0},{3,1},{4,6},{5,7},{6,4},{7,5},{8,10},{9,11},{10,... | collective-permute-start | bytes 393224 | tf_op jit(solution)/shard_map/ppermute | solution.py:288
  38.5 1.3 %collective-permute-start.11 = (bf16[8,64,128]{2,1,0:T(8,128)(2,1)S(1)}, bf16[8,64,128]{2,1,0:T(8,128)(2,1)S(1)}, u32[]{:S(2)}, u32[]{:S(2)}) collective-permute-start(bf16[8,64,128]{2,1,0:T(8,128)(2,1)S(1)} %get-tuple-element.37), channel_id=1, source_target_pairs={{0,3},{1,0},{2,1},{3,2},{4,7},{5,4},{6,5},{7,6},{8,11},{9,8},{10,9... | collective-permute-start | bytes 393224 | tf_op jit(solution)/shard_map/ppermute | solution.py:288
  39.8 1.9 %collective-permute-done.5.refs_4_ = bf16[4,256,128]{2,1,0:T(8,128)(2,1)S(1)} collective-permute-done((bf16[4,256,128]{2,1,0:T(8,128)(2,1)S(1)}, bf16[4,256,128]{2,1,0:T(8,128)(2,1)S(1)}, u32[]{:S(2)}, u32[]{:S(2)}) %collective-permute-start.5) | collective-permute-done | bytes 262176 | tf_op jit(solution)/shard_map/ppermute | solution.py:12
  41.7 3.2 %shard_map.71 = (bf16[24,256,128]{2,1,0:T(8,128)(2,1)}, f32[8,64,128]{2,1,0:T(8,128)S(1)}, bf16[8,64,128]{2,1,0:T(8,128)(2,1)S(1)}) custom-call(s32[4]{0:T(128)S(1)} %pad_add_fusion.refs_0_, bf16[2,4,256,128]{3,2,1,0:T(8,128)(2,1)S(1)} %constant_dynamic-update-slice_fusion.refs_2_.refs_1_, ...), custom_call_target="tpu_custom_call" | custom-call | tf_op jit(solution)/shard_map/pallas_call | solution.py:24
  44.8 1.9 %collective-permute-start.17 = (bf16[8,64,128]{2,1,0:T(8,128)(2,1)S(1)}, bf16[8,64,128]{2,1,0:T(8,128)(2,1)S(1)}, u32[]{:S(2)}, u32[]{:S(2)}) collective-permute-start(bf16[8,64,128]{2,1,0:T(8,128)(2,1)S(1)} %get-tuple-element.42.refs_2_), channel_id=1, source_target_pairs={{0,3},{1,0},{2,1},{3,2},{4,7},{5,4},{6,5},{7,6},{8,11},{9,8},{10,9... | collective-permute-start | bytes 393224 | tf_op jit(solution)/shard_map/ppermute | solution.py:288
  46.7 0.9 collective-permute-start.16
  47.5 0.4 collective-permute-start.15
  48.0 1.4 %copy-done.1 = bf16[24,256,128]{2,1,0:T(8,128)(2,1)S(1)} copy-done((bf16[24,256,128]{2,1,0:T(8,128)(2,1)S(1)}, bf16[24,256,128]{2,1,0:T(8,128)(2,1)}, u32[]{:S(2)}) %copy-start.1) | copy-done | bytes 1572888
  49.4 2.3 %shard_map.72 = (bf16[2,4,64,128]{3,2,1,0:T(8,128)(2,1)S(1)}, bf16[2,64,128]{2,1,0:T(8,128)(2,1)S(1)}, bf16[2,64,128]{2,1,0:T(8,128)(2,1)S(1)}, bf16[4,27,16,256]{3,2,1,0:T(8,128)(2,1)S(1)}) custom-call(s32[4]{0:T(128)S(1)} %pad_add_fusion.refs_0_, bf16[24,256,128]{2,1,0:T(8,128)(2,1)S(1)} %copy-done.1, f32[8,64,128]{2,1,0:T(8,128)S(1)} %get-tuple-element.34.refs_2_, ...), custom_call_target="tpu_custom_call" | custom-call | tf_op jit(solution)/shard_map/pallas_call | solution.py:24
  51.7 2.7 %collective-permute-start.12 = (bf16[2,64,128]{2,1,0:T(8,128)(2,1)S(1)}, bf16[2,64,128]{2,1,0:T(8,128)(2,1)S(1)}, u32[]{:S(2)}, u32[]{:S(2)}) collective-permute-start(bf16[2,64,128]{2,1,0:T(8,128)(2,1)S(1)} %get-tuple-element.38), channel_id=1, source_target_pairs={{0,4},{4,8},{8,12},{1,5},{5,9},{9,13},{2,6},{6,10},{10,14},{3,7},{... | collective-permute-start | bytes 98312 | tf_op jit(solution)/shard_map/ppermute | solution.py:12
  54.4 1.5 %collective-permute-start.13 = (bf16[2,64,128]{2,1,0:T(8,128)(2,1)S(1)}, bf16[2,64,128]{2,1,0:T(8,128)(2,1)S(1)}, u32[]{:S(2)}, u32[]{:S(2)}) collective-permute-start(bf16[2,64,128]{2,1,0:T(8,128)(2,1)S(1)} %get-tuple-element.39), channel_id=1, source_target_pairs={{4,0},{8,4},{12,8},{5,1},{9,5},{13,9},{6,2},{10,6},{14,10},{7,3},{... | collective-permute-start | bytes 98312 | tf_op jit(solution)/shard_map/ppermute | solution.py:12
  55.9 3.2 %collective-permute-done.13.refs_2_ = bf16[2,64,128]{2,1,0:T(8,128)(2,1)S(1)} collective-permute-done((bf16[2,64,128]{2,1,0:T(8,128)(2,1)S(1)}, bf16[2,64,128]{2,1,0:T(8,128)(2,1)S(1)}, u32[]{:S(2)}, u32[]{:S(2)}) %collective-permute-start.13) | collective-permute-done | bytes 32800 | tf_op jit(solution)/shard_map/ppermute | solution.py:12
  59.1 0.6 shard_map.73.refs_8_.refs_1_
  59.7 2.6 %shard_map.74 = (bf16[4,27,16,256]{3,2,1,0:T(8,128)(2,1)S(1)}, bf16[4,27,16,256]{3,2,1,0:T(8,128)(2,1)S(1)}) custom-call(s32[4]{0:T(128)S(1)} %pad_add_fusion.refs_0_, bf16[4,27,16,256]{3,2,1,0:T(8,128)(2,1)S(1)} %get-tuple-element.41.refs_1_, bf16[8,64,128]{2,1,0:T(8,128)(2,1)S(1)} %get-tuple-element.42.refs_2_, ...), custom_call_target="tpu_custom_call" | custom-call | tf_op jit(solution)/shard_map/pallas_call | solution.py:24
  62.2 2.3 %collective-permute-start.18 = (bf16[4,27,16,256]{3,2,1,0:T(8,128)(2,1)S(1)}, bf16[4,27,16,256]{3,2,1,0:T(8,128)(2,1)S(1)}, u32[]{:S(2)}, u32[]{:S(2)}) collective-permute-start(bf16[4,27,16,256]{3,2,1,0:T(8,128)(2,1)S(1)} %get-tuple-element.44), channel_id=1, source_target_pairs={{0,16},{16,0},{32,48},{48,32},{64,80},{80,64},{96,112},{112,96},{1... | collective-permute-start | bytes 2654216 | tf_op jit(solution)/shard_map/ppermute | solution.py:304
  64.5 1.9 %collective-permute-start.14 = (bf16[2,6,64,128]{3,2,1,0:T(8,128)(2,1)S(1)}, bf16[2,6,64,128]{3,2,1,0:T(8,128)(2,1)S(1)}, u32[]{:S(2)}, u32[]{:S(2)}) collective-permute-start(bf16[2,6,64,128]{3,2,1,0:T(8,128)(2,1)S(1)} %shard_map.73.refs_8_.refs_1_), channel_id=1, source_target_pairs={{16,0},{32,16},{48,32},{64,48},{80,64},{96,80},{112,96},{128,112},... | collective-permute-start | bytes 589832 | tf_op jit(solution)/shard_map/ppermute | solution.py:12
  66.5 0.1 collective-permute-done.18
  66.6 0.4 convert_add_fusion
  67.1 1.5 %collective-permute-start.23 = (bf16[27,16,256]{2,1,0:T(8,128)(2,1)S(1)}, bf16[27,16,256]{2,1,0:T(8,128)(2,1)S(1)}, u32[]{:S(2)}, u32[]{:S(2)}) collective-permute-start(bf16[27,16,256]{2,1,0:T(8,128)(2,1)S(1)} %get-tuple-element.58), channel_id=1, source_target_pairs={{0,8},{4,12},{8,0},{12,4},{1,9},{5,13},{9,1},{13,5},{2,10},{6,14},... | collective-permute-start | bytes 663560 | tf_op jit(solution)/shard_map/ppermute | solution.py:288
  68.6 4.1 %collective-permute-done.14.refs_2_ = bf16[2,6,64,128]{3,2,1,0:T(8,128)(2,1)S(1)} collective-permute-done((bf16[2,6,64,128]{3,2,1,0:T(8,128)(2,1)S(1)}, bf16[2,6,64,128]{3,2,1,0:T(8,128)(2,1)S(1)}, u32[]{:S(2)}, u32[]{:S(2)}) %collective-permute-start.14) | collective-permute-done | bytes 196640 | tf_op jit(solution)/shard_map/ppermute | solution.py:12
  72.7 2.0 %shard_map.75 = (f32[8,64,128]{2,1,0:T(8,128)S(1)}, bf16[8,64,128]{2,1,0:T(8,128)(2,1)S(1)}, bf16[8,64,128]{2,1,0:T(8,128)(2,1)S(1)}, bf16[8,64,128]{2,1,0:T(8,128)(2,1)S(1)}) custom-call(s32[4]{0:T(128)S(1)} %pad_add_fusion.refs_0_, bf16[2,6,64,128]{3,2,1,0:T(8,128)(2,1)S(1)} %shard_map.73.refs_8_.refs_1_, ...), custom_call_target="tpu_custom_call" | custom-call | tf_op jit(solution)/shard_map/pallas_call | solution.py:24
  74.8 0.6 collective-permute-done.23.refs_3_
  75.4 5.4 %collective-permute-done.22.refs_2_ = bf16[27,16,256]{2,1,0:T(8,128)(2,1)S(1)} collective-permute-done((bf16[27,16,256]{2,1,0:T(8,128)(2,1)S(1)}, bf16[27,16,256]{2,1,0:T(8,128)(2,1)S(1)}, u32[]{:S(2)}, u32[]{:S(2)}) %collective-permute-start.22) | collective-permute-done | bytes 221216 | tf_op jit(solution)/shard_map/ppermute | solution.py:288
  80.8 0.7 shard_map.76
  81.5 2.8 %collective-permute-start.25 = (bf16[27,8,128]{2,1,0:T(8,128)(2,1)S(1)}, bf16[27,8,128]{2,1,0:T(8,128)(2,1)S(1)}, u32[]{:S(2)}, u32[]{:S(2)}) collective-permute-start(bf16[27,8,128]{2,1,0:T(8,128)(2,1)S(1)} %get-tuple-element.50), channel_id=1, source_target_pairs={{0,32},{16,48},{32,64},{48,80},{64,96},{80,112},{96,0},{112,16},{1... | collective-permute-start | bytes 165896 | tf_op jit(solution)/shard_map/ppermute | solution.py:309
  84.3 3.7 %collective-permute-start.26 = (bf16[27,8,128]{2,1,0:T(8,128)(2,1)S(1)}, bf16[27,8,128]{2,1,0:T(8,128)(2,1)S(1)}, u32[]{:S(2)}, u32[]{:S(2)}) collective-permute-start(bf16[27,8,128]{2,1,0:T(8,128)(2,1)S(1)} %get-tuple-element.51), channel_id=1, source_target_pairs={{0,64},{16,80},{32,96},{48,112},{64,0},{80,16},{96,32},{112,48},{1... | collective-permute-start | bytes 165896 | tf_op jit(solution)/shard_map/ppermute | solution.py:309
  88.0 1.3 collective-permute-done.25
  89.3 3.1 %collective-permute-done.26 = bf16[27,8,128]{2,1,0:T(8,128)(2,1)S(1)} collective-permute-done((bf16[27,8,128]{2,1,0:T(8,128)(2,1)S(1)}, bf16[27,8,128]{2,1,0:T(8,128)(2,1)S(1)}, u32[]{:S(2)}, u32[]{:S(2)}) %collective-permute-start.26) | collective-permute-done | bytes 55328 | tf_op jit(solution)/shard_map/ppermute | solution.py:309
  92.4 3.4 %collective-permute-start.28 = (bf16[27,8,128]{2,1,0:T(8,128)(2,1)S(1)}, bf16[27,8,128]{2,1,0:T(8,128)(2,1)S(1)}, u32[]{:S(2)}, u32[]{:S(2)}) collective-permute-start(bf16[27,8,128]{2,1,0:T(8,128)(2,1)S(1)} %add_convert_fusion.2), channel_id=1, source_target_pairs={{0,128},{16,144},{32,160},{48,176},{64,192},{80,208},{96,224},{112... | collective-permute-start | bytes 165896 | tf_op jit(solution)/shard_map/ppermute | solution.py:304
  95.8 2.9 %collective-permute-start.19 = (bf16[8,64,128]{2,1,0:T(8,128)(2,1)S(1)}, bf16[8,64,128]{2,1,0:T(8,128)(2,1)S(1)}, u32[]{:S(2)}, u32[]{:S(2)}) collective-permute-start(bf16[8,64,128]{2,1,0:T(8,128)(2,1)S(1)} %get-tuple-element.46), channel_id=1, source_target_pairs={{0,1},{1,2},{2,3},{3,0},{4,5},{5,6},{6,7},{7,4},{8,9},{9,10},{10,1... | collective-permute-start | bytes 393224 | tf_op jit(solution)/shard_map/ppermute | solution.py:288
  98.8 0.8 collective-permute-start.20
  99.5 1.6 %collective-permute-start.21 = (bf16[8,64,128]{2,1,0:T(8,128)(2,1)S(1)}, bf16[8,64,128]{2,1,0:T(8,128)(2,1)S(1)}, u32[]{:S(2)}, u32[]{:S(2)}) collective-permute-start(bf16[8,64,128]{2,1,0:T(8,128)(2,1)S(1)} %get-tuple-element.48), channel_id=1, source_target_pairs={{0,3},{1,0},{2,1},{3,2},{4,7},{5,4},{6,5},{7,6},{8,11},{9,8},{10,9... | collective-permute-start | bytes 393224 | tf_op jit(solution)/shard_map/ppermute | solution.py:288
  101.2 2.7 %collective-permute-start.31 = (bf16[27,8,128]{2,1,0:T(8,128)(2,1)S(1)}, bf16[27,8,128]{2,1,0:T(8,128)(2,1)S(1)}, u32[]{:S(2)}, u32[]{:S(2)}) collective-permute-start(bf16[27,8,128]{2,1,0:T(8,128)(2,1)S(1)} %add_convert_fusion.1.refs_1_), channel_id=1, source_target_pairs={{0,96},{16,112},{32,0},{48,16},{64,32},{80,48},{96,64},{112,80},{1... | collective-permute-start | bytes 165896 | tf_op jit(solution)/shard_map/ppermute | solution.py:309
  103.9 0.7 collective-permute-start.30
  104.7 0.5 collective-permute-done.31.refs_4_
  105.2 2.8 %collective-permute-done.30.refs_3_ = bf16[27,8,128]{2,1,0:T(8,128)(2,1)S(1)} collective-permute-done((bf16[27,8,128]{2,1,0:T(8,128)(2,1)S(1)}, bf16[27,8,128]{2,1,0:T(8,128)(2,1)S(1)}, u32[]{:S(2)}, u32[]{:S(2)}) %collective-permute-start.30) | collective-permute-done | bytes 55328 | tf_op jit(solution)/shard_map/ppermute | solution.py:309
  108.0 1.3 %collective-permute-done.29.refs_2_ = bf16[27,8,128]{2,1,0:T(8,128)(2,1)S(1)} collective-permute-done((bf16[27,8,128]{2,1,0:T(8,128)(2,1)S(1)}, bf16[27,8,128]{2,1,0:T(8,128)(2,1)S(1)}, u32[]{:S(2)}, u32[]{:S(2)}) %collective-permute-start.29) | collective-permute-done | bytes 55328 | tf_op jit(solution)/shard_map/ppermute | solution.py:309
  109.4 0.6 shard_map.77.refs_1_
  110.1 2.1 %collective-permute-start.33 = (bf16[27,16,256]{2,1,0:T(8,128)(2,1)S(1)}, bf16[27,16,256]{2,1,0:T(8,128)(2,1)S(1)}, u32[]{:S(2)}, u32[]{:S(2)}) collective-permute-start(bf16[27,16,256]{2,1,0:T(8,128)(2,1)S(1)} %shard_map.77.refs_1_), channel_id=1, source_target_pairs={{0,8},{4,12},{8,0},{12,4},{1,9},{5,13},{9,1},{13,5},{2,10},{6,14},... | collective-permute-start | bytes 663560 | tf_op jit(solution)/shard_map/ppermute | solution.py:288
  112.2 2.7 %collective-permute-done.34.refs_4_ = bf16[27,16,256]{2,1,0:T(8,128)(2,1)S(1)} collective-permute-done((bf16[27,16,256]{2,1,0:T(8,128)(2,1)S(1)}, bf16[27,16,256]{2,1,0:T(8,128)(2,1)S(1)}, u32[]{:S(2)}, u32[]{:S(2)}) %collective-permute-start.34) | collective-permute-done | bytes 221216 | tf_op jit(solution)/shard_map/ppermute | solution.py:288
  114.8 1.7 %collective-permute-done.33.refs_3_ = bf16[27,16,256]{2,1,0:T(8,128)(2,1)S(1)} collective-permute-done((bf16[27,16,256]{2,1,0:T(8,128)(2,1)S(1)}, bf16[27,16,256]{2,1,0:T(8,128)(2,1)S(1)}, u32[]{:S(2)}, u32[]{:S(2)}) %collective-permute-start.33) | collective-permute-done | bytes 221216 | tf_op jit(solution)/shard_map/ppermute | solution.py:288
  116.5 2.7 %collective-permute-done.32.refs_2_ = bf16[27,16,256]{2,1,0:T(8,128)(2,1)S(1)} collective-permute-done((bf16[27,16,256]{2,1,0:T(8,128)(2,1)S(1)}, bf16[27,16,256]{2,1,0:T(8,128)(2,1)S(1)}, u32[]{:S(2)}, u32[]{:S(2)}) %collective-permute-start.32) | collective-permute-done | bytes 221216 | tf_op jit(solution)/shard_map/ppermute | solution.py:288
  119.2 0.6 shard_map.78
  119.8 5.1 %collective-permute-start.35 = (bf16[27,64,256]{2,1,0:T(8,128)(2,1)S(1)}, bf16[27,64,256]{2,1,0:T(8,128)(2,1)S(1)}, u32[]{:S(2)}, u32[]{:S(2)}) collective-permute-start(bf16[27,64,256]{2,1,0:T(8,128)(2,1)S(1)} %shard_map.78), channel_id=1, source_target_pairs={{0,16},{16,0},{32,48},{48,32},{64,80},{80,64},{96,112},{112,96},{1... | collective-permute-start | bytes 2654216 | tf_op jit(solution)/shard_map/ppermute | solution.py:304
  125.0 2.1 %collective-permute-done.35 = bf16[27,64,256]{2,1,0:T(8,128)(2,1)S(1)} collective-permute-done((bf16[27,64,256]{2,1,0:T(8,128)(2,1)S(1)}, bf16[27,64,256]{2,1,0:T(8,128)(2,1)S(1)}, u32[]{:S(2)}, u32[]{:S(2)}) %collective-permute-start.35) | collective-permute-done | bytes 884768 | tf_op jit(solution)/shard_map/ppermute | solution.py:304
  127.1 2.2 %convert_bitcast_fusion = (f32[64,3,3,3,256]{4,0,3,2,1:T(8,128)}, f32[64,3,3,3,256]{4,0,3,2,1:T(8,128)}) fusion(bf16[3,3,3,64,256]{4,3,2,1,0:T(8,128)(2,1)S(1)} %bitcast.34, bf16[3,3,3,64,256]{4,3,2,1,0:T(8,128)(2,1)S(1)} %bitcast.35), kind=kLoop, calls=%fused_computation | loop fusion | flops 884736 | bytes 5308416 | tf_op jit(solution)/shard_map/transpose | solution.py:335
  (43 shorter events, 0.8 us)
Async XLA Ops:
  0.6 32.7 %copy-start.2 = (bf16[64,3,3,3,256]{4,0,3,2,1:T(8,128)(2,1)S(1)}, bf16[64,3,3,3,256]{4,0,3,2,1:T(8,128)(2,1)}, u32[]{:S(2)}) copy-start(bf16[64,3,3,3,256]{4,0,3,2,1:T(8,128)(2,1)} %param.7) | copy-start | bytes 2654212
  0.6 6.8 %collective-permute-start = (bf16[2,4,64,128]{3,2,1,0:T(8,128)(2,1)}, bf16[2,4,64,128]{3,2,1,0:T(8,128)(2,1)S(1)}, u32[]{:S(2)}, u32[]{:S(2)}) collective-permute-start(bf16[2,4,64,128]{3,2,1,0:T(8,128)(2,1)} %param.4), channel_id=1, source_target_pairs={{0,1},{1,2},{2,3},{3,0},{4,5},{5,6},{6,7},{7,4},{8,9},{9,10},{10,1... | collective-permute-start | bytes 393224 | tf_op jit(solution)/shard_map/ppermute | solution.py:288
  2.8 8.5 %collective-permute-start.1 = (bf16[2,4,64,128]{3,2,1,0:T(8,128)(2,1)}, bf16[2,4,64,128]{3,2,1,0:T(8,128)(2,1)S(1)}, u32[]{:S(2)}, u32[]{:S(2)}) collective-permute-start(bf16[2,4,64,128]{3,2,1,0:T(8,128)(2,1)} %param.4), channel_id=1, source_target_pairs={{0,2},{1,3},{2,0},{3,1},{4,6},{5,7},{6,4},{7,5},{8,10},{9,11},{10,... | collective-permute-start | bytes 393224 | tf_op jit(solution)/shard_map/ppermute | solution.py:288
  5.5 5.9 %collective-permute-start.2 = (bf16[2,4,64,128]{3,2,1,0:T(8,128)(2,1)}, bf16[2,4,64,128]{3,2,1,0:T(8,128)(2,1)S(1)}, u32[]{:S(2)}, u32[]{:S(2)}) collective-permute-start(bf16[2,4,64,128]{3,2,1,0:T(8,128)(2,1)} %param.4), channel_id=1, source_target_pairs={{0,3},{1,0},{2,1},{3,2},{4,7},{5,4},{6,5},{7,6},{8,11},{9,8},{10,9... | collective-permute-start | bytes 393224 | tf_op jit(solution)/shard_map/ppermute | solution.py:288
  7.5 34.1 %copy-start = (bf16[64,3,3,3,256]{4,0,3,2,1:T(8,128)(2,1)S(1)}, bf16[64,3,3,3,256]{4,0,3,2,1:T(8,128)(2,1)}, u32[]{:S(2)}) copy-start(bf16[64,3,3,3,256]{4,0,3,2,1:T(8,128)(2,1)} %param.6) | copy-start | bytes 2654212
  11.4 16.8 %collective-permute-start.3 = (bf16[2,4,256,128]{3,2,1,0:T(8,128)(2,1)S(1)}, bf16[2,4,256,128]{3,2,1,0:T(8,128)(2,1)S(1)}, u32[]{:S(2)}, u32[]{:S(2)}) collective-permute-start(bf16[2,4,256,128]{3,2,1,0:T(8,128)(2,1)S(1)} %constant_dynamic-update-slice_fusion.refs_2_.refs_1_), channel_id=1, source_target_pairs={{0,16},{16,32},{32,48},{48,64},{64,80},{80,96},{96,112},{112,128},... | collective-permute-start | bytes 1572872 | tf_op jit(solution)/shard_map/ppermute | solution.py:12
  16.5 0.9 copy-start.3
  18.0 4.4 %collective-permute-start.6 = (bf16[2,64,128]{2,1,0:T(8,128)(2,1)S(1)}, bf16[2,64,128]{2,1,0:T(8,128)(2,1)S(1)}, u32[]{:S(2)}, u32[]{:S(2)}) collective-permute-start(bf16[2,64,128]{2,1,0:T(8,128)(2,1)S(1)} %get-tuple-element.30), channel_id=1, source_target_pairs={{0,4},{4,8},{8,12},{1,5},{5,9},{9,13},{2,6},{6,10},{10,14},{3,7},{... | collective-permute-start | bytes 98312 | tf_op jit(solution)/shard_map/ppermute | solution.py:12
  21.1 4.7 %collective-permute-start.7 = (bf16[2,64,128]{2,1,0:T(8,128)(2,1)S(1)}, bf16[2,64,128]{2,1,0:T(8,128)(2,1)S(1)}, u32[]{:S(2)}, u32[]{:S(2)}) collective-permute-start(bf16[2,64,128]{2,1,0:T(8,128)(2,1)S(1)} %get-tuple-element.31), channel_id=1, source_target_pairs={{4,0},{8,4},{12,8},{5,1},{9,5},{13,9},{6,2},{10,6},{14,10},{7,3},{... | collective-permute-start | bytes 98312 | tf_op jit(solution)/shard_map/ppermute | solution.py:12
  26.3 7.0 %collective-permute-start.8 = (bf16[2,6,64,128]{3,2,1,0:T(8,128)(2,1)S(1)}, bf16[2,6,64,128]{3,2,1,0:T(8,128)(2,1)S(1)}, u32[]{:S(2)}, u32[]{:S(2)}) collective-permute-start(bf16[2,6,64,128]{3,2,1,0:T(8,128)(2,1)S(1)} %shard_map.69.refs_1_.refs_6_), channel_id=1, source_target_pairs={{16,0},{32,16},{48,32},{64,48},{80,64},{96,80},{112,96},{128,112},... | collective-permute-start | bytes 589832 | tf_op jit(solution)/shard_map/ppermute | solution.py:12
  28.9 10.9 %collective-permute-start.4 = (bf16[4,256,128]{2,1,0:T(8,128)(2,1)S(1)}, bf16[4,256,128]{2,1,0:T(8,128)(2,1)S(1)}, u32[]{:S(2)}, u32[]{:S(2)}) collective-permute-start(bf16[4,256,128]{2,1,0:T(8,128)(2,1)S(1)} %get-tuple-element.28), channel_id=1, source_target_pairs={{0,4},{4,8},{8,12},{1,5},{5,9},{9,13},{2,6},{6,10},{10,14},{3,7},{... | collective-permute-start | bytes 786440 | tf_op jit(solution)/shard_map/ppermute | solution.py:12
  32.0 9.7 %collective-permute-start.5 = (bf16[4,256,128]{2,1,0:T(8,128)(2,1)S(1)}, bf16[4,256,128]{2,1,0:T(8,128)(2,1)S(1)}, u32[]{:S(2)}, u32[]{:S(2)}) collective-permute-start(bf16[4,256,128]{2,1,0:T(8,128)(2,1)S(1)} %get-tuple-element.29), channel_id=1, source_target_pairs={{4,0},{8,4},{12,8},{5,1},{9,5},{13,9},{6,2},{10,6},{14,10},{7,3},{... | collective-permute-start | bytes 786440 | tf_op jit(solution)/shard_map/ppermute | solution.py:12
  35.4 12.2 %collective-permute-start.9 = (bf16[8,64,128]{2,1,0:T(8,128)(2,1)S(1)}, bf16[8,64,128]{2,1,0:T(8,128)(2,1)S(1)}, u32[]{:S(2)}, u32[]{:S(2)}) collective-permute-start(bf16[8,64,128]{2,1,0:T(8,128)(2,1)S(1)} %get-tuple-element.35), channel_id=1, source_target_pairs={{0,1},{1,2},{2,3},{3,0},{4,5},{5,6},{6,7},{7,4},{8,9},{9,10},{10,1... | collective-permute-start | bytes 393224 | tf_op jit(solution)/shard_map/ppermute | solution.py:288
  36.4 11.6 %collective-permute-start.10 = (bf16[8,64,128]{2,1,0:T(8,128)(2,1)S(1)}, bf16[8,64,128]{2,1,0:T(8,128)(2,1)S(1)}, u32[]{:S(2)}, u32[]{:S(2)}) collective-permute-start(bf16[8,64,128]{2,1,0:T(8,128)(2,1)S(1)} %get-tuple-element.36), channel_id=1, source_target_pairs={{0,2},{1,3},{2,0},{3,1},{4,6},{5,7},{6,4},{7,5},{8,10},{9,11},{10,... | collective-permute-start | bytes 393224 | tf_op jit(solution)/shard_map/ppermute | solution.py:288
  38.5 9.5 %collective-permute-start.11 = (bf16[8,64,128]{2,1,0:T(8,128)(2,1)S(1)}, bf16[8,64,128]{2,1,0:T(8,128)(2,1)S(1)}, u32[]{:S(2)}, u32[]{:S(2)}) collective-permute-start(bf16[8,64,128]{2,1,0:T(8,128)(2,1)S(1)} %get-tuple-element.37), channel_id=1, source_target_pairs={{0,3},{1,0},{2,1},{3,2},{4,7},{5,4},{6,5},{7,6},{8,11},{9,8},{10,9... | collective-permute-start | bytes 393224 | tf_op jit(solution)/shard_map/ppermute | solution.py:288
  44.8 14.8 %collective-permute-start.17 = (bf16[8,64,128]{2,1,0:T(8,128)(2,1)S(1)}, bf16[8,64,128]{2,1,0:T(8,128)(2,1)S(1)}, u32[]{:S(2)}, u32[]{:S(2)}) collective-permute-start(bf16[8,64,128]{2,1,0:T(8,128)(2,1)S(1)} %get-tuple-element.42.refs_2_), channel_id=1, source_target_pairs={{0,3},{1,0},{2,1},{3,2},{4,7},{5,4},{6,5},{7,6},{8,11},{9,8},{10,9... | collective-permute-start | bytes 393224 | tf_op jit(solution)/shard_map/ppermute | solution.py:288
  46.7 13.0 %collective-permute-start.16 = (bf16[8,64,128]{2,1,0:T(8,128)(2,1)S(1)}, bf16[8,64,128]{2,1,0:T(8,128)(2,1)S(1)}, u32[]{:S(2)}, u32[]{:S(2)}) collective-permute-start(bf16[8,64,128]{2,1,0:T(8,128)(2,1)S(1)} %get-tuple-element.42.refs_2_), channel_id=1, source_target_pairs={{0,2},{1,3},{2,0},{3,1},{4,6},{5,7},{6,4},{7,5},{8,10},{9,11},{10,... | collective-permute-start | bytes 393224 | tf_op jit(solution)/shard_map/ppermute | solution.py:288
  47.5 12.1 %collective-permute-start.15 = (bf16[8,64,128]{2,1,0:T(8,128)(2,1)S(1)}, bf16[8,64,128]{2,1,0:T(8,128)(2,1)S(1)}, u32[]{:S(2)}, u32[]{:S(2)}) collective-permute-start(bf16[8,64,128]{2,1,0:T(8,128)(2,1)S(1)} %get-tuple-element.42.refs_2_), channel_id=1, source_target_pairs={{0,1},{1,2},{2,3},{3,0},{4,5},{5,6},{6,7},{7,4},{8,9},{9,10},{10,1... | collective-permute-start | bytes 393224 | tf_op jit(solution)/shard_map/ppermute | solution.py:288
  48.0 1.4 %copy-start.1 = (bf16[24,256,128]{2,1,0:T(8,128)(2,1)S(1)}, bf16[24,256,128]{2,1,0:T(8,128)(2,1)}, u32[]{:S(2)}) copy-start(bf16[24,256,128]{2,1,0:T(8,128)(2,1)} %get-tuple-element.33.refs_1_) | copy-start | bytes 4718596
  51.7 4.2 %collective-permute-start.12 = (bf16[2,64,128]{2,1,0:T(8,128)(2,1)S(1)}, bf16[2,64,128]{2,1,0:T(8,128)(2,1)S(1)}, u32[]{:S(2)}, u32[]{:S(2)}) collective-permute-start(bf16[2,64,128]{2,1,0:T(8,128)(2,1)S(1)} %get-tuple-element.38), channel_id=1, source_target_pairs={{0,4},{4,8},{8,12},{1,5},{5,9},{9,13},{2,6},{6,10},{10,14},{3,7},{... | collective-permute-start | bytes 98312 | tf_op jit(solution)/shard_map/ppermute | solution.py:12
  54.4 4.7 %collective-permute-start.13 = (bf16[2,64,128]{2,1,0:T(8,128)(2,1)S(1)}, bf16[2,64,128]{2,1,0:T(8,128)(2,1)S(1)}, u32[]{:S(2)}, u32[]{:S(2)}) collective-permute-start(bf16[2,64,128]{2,1,0:T(8,128)(2,1)S(1)} %get-tuple-element.39), channel_id=1, source_target_pairs={{4,0},{8,4},{12,8},{5,1},{9,5},{13,9},{6,2},{10,6},{14,10},{7,3},{... | collective-permute-start | bytes 98312 | tf_op jit(solution)/shard_map/ppermute | solution.py:12
  62.2 4.3 %collective-permute-start.18 = (bf16[4,27,16,256]{3,2,1,0:T(8,128)(2,1)S(1)}, bf16[4,27,16,256]{3,2,1,0:T(8,128)(2,1)S(1)}, u32[]{:S(2)}, u32[]{:S(2)}) collective-permute-start(bf16[4,27,16,256]{3,2,1,0:T(8,128)(2,1)S(1)} %get-tuple-element.44), channel_id=1, source_target_pairs={{0,16},{16,0},{32,48},{48,32},{64,80},{80,64},{96,112},{112,96},{1... | collective-permute-start | bytes 2654216 | tf_op jit(solution)/shard_map/ppermute | solution.py:304
  64.5 8.2 %collective-permute-start.14 = (bf16[2,6,64,128]{3,2,1,0:T(8,128)(2,1)S(1)}, bf16[2,6,64,128]{3,2,1,0:T(8,128)(2,1)S(1)}, u32[]{:S(2)}, u32[]{:S(2)}) collective-permute-start(bf16[2,6,64,128]{3,2,1,0:T(8,128)(2,1)S(1)} %shard_map.73.refs_8_.refs_1_), channel_id=1, source_target_pairs={{16,0},{32,16},{48,32},{64,48},{80,64},{96,80},{112,96},{128,112},... | collective-permute-start | bytes 589832 | tf_op jit(solution)/shard_map/ppermute | solution.py:12
  67.0 7.8 %collective-permute-start.24 = (bf16[27,16,256]{2,1,0:T(8,128)(2,1)S(1)}, bf16[27,16,256]{2,1,0:T(8,128)(2,1)S(1)}, u32[]{:S(2)}, u32[]{:S(2)}) collective-permute-start(bf16[27,16,256]{2,1,0:T(8,128)(2,1)S(1)} %get-tuple-element.57), channel_id=1, source_target_pairs={{0,12},{4,0},{8,4},{12,8},{1,13},{5,1},{9,5},{13,9},{2,14},{6,2},{... | collective-permute-start | bytes 663560 | tf_op jit(solution)/shard_map/ppermute | solution.py:288
  67.1 8.3 %collective-permute-start.23 = (bf16[27,16,256]{2,1,0:T(8,128)(2,1)S(1)}, bf16[27,16,256]{2,1,0:T(8,128)(2,1)S(1)}, u32[]{:S(2)}, u32[]{:S(2)}) collective-permute-start(bf16[27,16,256]{2,1,0:T(8,128)(2,1)S(1)} %get-tuple-element.58), channel_id=1, source_target_pairs={{0,8},{4,12},{8,0},{12,4},{1,9},{5,13},{9,1},{13,5},{2,10},{6,14},... | collective-permute-start | bytes 663560 | tf_op jit(solution)/shard_map/ppermute | solution.py:288
  68.6 12.2 %collective-permute-start.22 = (bf16[27,16,256]{2,1,0:T(8,128)(2,1)S(1)}, bf16[27,16,256]{2,1,0:T(8,128)(2,1)S(1)}, u32[]{:S(2)}, u32[]{:S(2)}) collective-permute-start(bf16[27,16,256]{2,1,0:T(8,128)(2,1)S(1)} %get-tuple-element.59.refs_4_), channel_id=1, source_target_pairs={{0,4},{4,8},{8,12},{12,0},{1,5},{5,9},{9,13},{13,1},{2,6},{6,10},{... | collective-permute-start | bytes 663560 | tf_op jit(solution)/shard_map/ppermute | solution.py:288
  81.5 7.8 %collective-permute-start.25 = (bf16[27,8,128]{2,1,0:T(8,128)(2,1)S(1)}, bf16[27,8,128]{2,1,0:T(8,128)(2,1)S(1)}, u32[]{:S(2)}, u32[]{:S(2)}) collective-permute-start(bf16[27,8,128]{2,1,0:T(8,128)(2,1)S(1)} %get-tuple-element.50), channel_id=1, source_target_pairs={{0,32},{16,48},{32,64},{48,80},{64,96},{80,112},{96,0},{112,16},{1... | collective-permute-start | bytes 165896 | tf_op jit(solution)/shard_map/ppermute | solution.py:309
  84.3 8.1 %collective-permute-start.26 = (bf16[27,8,128]{2,1,0:T(8,128)(2,1)S(1)}, bf16[27,8,128]{2,1,0:T(8,128)(2,1)S(1)}, u32[]{:S(2)}, u32[]{:S(2)}) collective-permute-start(bf16[27,8,128]{2,1,0:T(8,128)(2,1)S(1)} %get-tuple-element.51), channel_id=1, source_target_pairs={{0,64},{16,80},{32,96},{48,112},{64,0},{80,16},{96,32},{112,48},{1... | collective-permute-start | bytes 165896 | tf_op jit(solution)/shard_map/ppermute | solution.py:309
  88.0 4.4 %collective-permute-start.27 = (bf16[27,8,128]{2,1,0:T(8,128)(2,1)S(1)}, bf16[27,8,128]{2,1,0:T(8,128)(2,1)S(1)}, u32[]{:S(2)}, u32[]{:S(2)}) collective-permute-start(bf16[27,8,128]{2,1,0:T(8,128)(2,1)S(1)} %get-tuple-element.52), channel_id=1, source_target_pairs={{0,96},{16,112},{32,0},{48,16},{64,32},{80,48},{96,64},{112,80},{1... | collective-permute-start | bytes 165896 | tf_op jit(solution)/shard_map/ppermute | solution.py:309
  92.4 8.8 %collective-permute-start.28 = (bf16[27,8,128]{2,1,0:T(8,128)(2,1)S(1)}, bf16[27,8,128]{2,1,0:T(8,128)(2,1)S(1)}, u32[]{:S(2)}, u32[]{:S(2)}) collective-permute-start(bf16[27,8,128]{2,1,0:T(8,128)(2,1)S(1)} %add_convert_fusion.2), channel_id=1, source_target_pairs={{0,128},{16,144},{32,160},{48,176},{64,192},{80,208},{96,224},{112... | collective-permute-start | bytes 165896 | tf_op jit(solution)/shard_map/ppermute | solution.py:304
  95.8 8.7 %collective-permute-start.19 = (bf16[8,64,128]{2,1,0:T(8,128)(2,1)S(1)}, bf16[8,64,128]{2,1,0:T(8,128)(2,1)S(1)}, u32[]{:S(2)}, u32[]{:S(2)}) collective-permute-start(bf16[8,64,128]{2,1,0:T(8,128)(2,1)S(1)} %get-tuple-element.46), channel_id=1, source_target_pairs={{0,1},{1,2},{2,3},{3,0},{4,5},{5,6},{6,7},{7,4},{8,9},{9,10},{10,1... | collective-permute-start | bytes 393224 | tf_op jit(solution)/shard_map/ppermute | solution.py:288
  98.8 5.8 %collective-permute-start.20 = (bf16[8,64,128]{2,1,0:T(8,128)(2,1)S(1)}, bf16[8,64,128]{2,1,0:T(8,128)(2,1)S(1)}, u32[]{:S(2)}, u32[]{:S(2)}) collective-permute-start(bf16[8,64,128]{2,1,0:T(8,128)(2,1)S(1)} %get-tuple-element.47), channel_id=1, source_target_pairs={{0,2},{1,3},{2,0},{3,1},{4,6},{5,7},{6,4},{7,5},{8,10},{9,11},{10,... | collective-permute-start | bytes 393224 | tf_op jit(solution)/shard_map/ppermute | solution.py:288
  99.5 5.1 %collective-permute-start.21 = (bf16[8,64,128]{2,1,0:T(8,128)(2,1)S(1)}, bf16[8,64,128]{2,1,0:T(8,128)(2,1)S(1)}, u32[]{:S(2)}, u32[]{:S(2)}) collective-permute-start(bf16[8,64,128]{2,1,0:T(8,128)(2,1)S(1)} %get-tuple-element.48), channel_id=1, source_target_pairs={{0,3},{1,0},{2,1},{3,2},{4,7},{5,4},{6,5},{7,6},{8,11},{9,8},{10,9... | collective-permute-start | bytes 393224 | tf_op jit(solution)/shard_map/ppermute | solution.py:288
  101.2 4.0 %collective-permute-start.31 = (bf16[27,8,128]{2,1,0:T(8,128)(2,1)S(1)}, bf16[27,8,128]{2,1,0:T(8,128)(2,1)S(1)}, u32[]{:S(2)}, u32[]{:S(2)}) collective-permute-start(bf16[27,8,128]{2,1,0:T(8,128)(2,1)S(1)} %add_convert_fusion.1.refs_1_), channel_id=1, source_target_pairs={{0,96},{16,112},{32,0},{48,16},{64,32},{80,48},{96,64},{112,80},{1... | collective-permute-start | bytes 165896 | tf_op jit(solution)/shard_map/ppermute | solution.py:309
  103.9 4.1 %collective-permute-start.30 = (bf16[27,8,128]{2,1,0:T(8,128)(2,1)S(1)}, bf16[27,8,128]{2,1,0:T(8,128)(2,1)S(1)}, u32[]{:S(2)}, u32[]{:S(2)}) collective-permute-start(bf16[27,8,128]{2,1,0:T(8,128)(2,1)S(1)} %add_convert_fusion.1.refs_1_), channel_id=1, source_target_pairs={{0,64},{16,80},{32,96},{48,112},{64,0},{80,16},{96,32},{112,48},{1... | collective-permute-start | bytes 165896 | tf_op jit(solution)/shard_map/ppermute | solution.py:309
  104.6 4.8 %collective-permute-start.29 = (bf16[27,8,128]{2,1,0:T(8,128)(2,1)S(1)}, bf16[27,8,128]{2,1,0:T(8,128)(2,1)S(1)}, u32[]{:S(2)}, u32[]{:S(2)}) collective-permute-start(bf16[27,8,128]{2,1,0:T(8,128)(2,1)S(1)} %add_convert_fusion.1.refs_1_), channel_id=1, source_target_pairs={{0,32},{16,48},{32,64},{48,80},{64,96},{80,112},{96,0},{112,16},{1... | collective-permute-start | bytes 165896 | tf_op jit(solution)/shard_map/ppermute | solution.py:309
  104.7 22.4 %copy-start.4 = (bf16[8,64,128]{2,1,0:T(8,128)(2,1)}, bf16[8,64,128]{2,1,0:T(8,128)(2,1)S(1)}, u32[]{:S(2)}) copy-start(bf16[8,64,128]{2,1,0:T(8,128)(2,1)S(1)} %add_convert_fusion) | copy-start | bytes 393220
  110.0 4.9 %collective-permute-start.34 = (bf16[27,16,256]{2,1,0:T(8,128)(2,1)S(1)}, bf16[27,16,256]{2,1,0:T(8,128)(2,1)S(1)}, u32[]{:S(2)}, u32[]{:S(2)}) collective-permute-start(bf16[27,16,256]{2,1,0:T(8,128)(2,1)S(1)} %shard_map.77.refs_1_), channel_id=1, source_target_pairs={{0,12},{4,0},{8,4},{12,8},{1,13},{5,1},{9,5},{13,9},{2,14},{6,2},{... | collective-permute-start | bytes 663560 | tf_op jit(solution)/shard_map/ppermute | solution.py:288
  110.1 6.4 %collective-permute-start.33 = (bf16[27,16,256]{2,1,0:T(8,128)(2,1)S(1)}, bf16[27,16,256]{2,1,0:T(8,128)(2,1)S(1)}, u32[]{:S(2)}, u32[]{:S(2)}) collective-permute-start(bf16[27,16,256]{2,1,0:T(8,128)(2,1)S(1)} %shard_map.77.refs_1_), channel_id=1, source_target_pairs={{0,8},{4,12},{8,0},{12,4},{1,9},{5,13},{9,1},{13,5},{2,10},{6,14},... | collective-permute-start | bytes 663560 | tf_op jit(solution)/shard_map/ppermute | solution.py:288
  112.2 7.1 %collective-permute-start.32 = (bf16[27,16,256]{2,1,0:T(8,128)(2,1)S(1)}, bf16[27,16,256]{2,1,0:T(8,128)(2,1)S(1)}, u32[]{:S(2)}, u32[]{:S(2)}) collective-permute-start(bf16[27,16,256]{2,1,0:T(8,128)(2,1)S(1)} %shard_map.77.refs_1_), channel_id=1, source_target_pairs={{0,4},{4,8},{8,12},{12,0},{1,5},{5,9},{9,13},{13,1},{2,6},{6,10},{... | collective-permute-start | bytes 663560 | tf_op jit(solution)/shard_map/ppermute | solution.py:288
  119.8 7.2 %collective-permute-start.35 = (bf16[27,64,256]{2,1,0:T(8,128)(2,1)S(1)}, bf16[27,64,256]{2,1,0:T(8,128)(2,1)S(1)}, u32[]{:S(2)}, u32[]{:S(2)}) collective-permute-start(bf16[27,64,256]{2,1,0:T(8,128)(2,1)S(1)} %shard_map.78), channel_id=1, source_target_pairs={{0,16},{16,0},{32,48},{48,32},{64,80},{80,64},{96,112},{112,96},{1... | collective-permute-start | bytes 2654216 | tf_op jit(solution)/shard_map/ppermute | solution.py:304

commit v6 on v5

--- a/solution.py
+++ b/solution.py
@@ -12,7 +12,7 @@
     return lax.ppermute(block, axis, route)
 
 
-VMEM_LIMIT = 50 * 1024 * 1024
+VMEM_LIMIT = 24 * 1024 * 1024
 TAPS = [(a, b) for a in range(3) for b in range(3)]
 SPOTS = [(t, i) for t in range(2) for i in range(4)]
 

time: 130 us -> 127 us (0.977)
  local copies, waits for them, and re-layouts: 3.41 us -> 2.01 us
    unnamed x13 -> x11, local copies, waits for them, and re-layouts: 3.32 us -> 1.91 us
  transfers between devices with their start and end apart: 36 -> 36, of which waited for: 17 -> 17; matrix products, arithmetic and copies ran while one was open for 1% -> 1% of each run, Pallas kernels for 9% -> 8%
where the time goes in v6:
time: 127 us
  starting transfers between devices  65.7 us (52%)
  waiting for transfers between devices  40.2 us (32%)
  Pallas kernels  15.3 us (12%)
  other arithmetic  2.89 us (2%)
  local copies, waits for them, and re-layouts  2.01 us (2%)
    ppermute x18, starting transfers between devices, rotated(): lax.ppermute(block, axis, [(i, (i + distance) % count) for i in range(cou...  22.8 us
    ppermute x9, starting transfers between devices, passed_along(): return lax.ppermute(block, axis, route)  21.9 us
    ppermute x18, waiting for transfers between devices, rotated(): lax.ppermute(block, axis, [(i, (i + distance) % count) for i in range(cou...  16.9 us
    pallas_call x12, Pallas kernels, call(): pl.pallas_call(lambda *refs: body(*refs[:used], *refs[rest:]), out_shape=...  15.3 us
    ppermute x9, waiting for transfers between devices, passed_along(): return lax.ppermute(block, axis, route)  12 us
    ppermute x3, starting transfers between devices, swapped(): lax.ppermute(block, 'tm', [(i, i ^ distance) for i in range(lax.axis_size...  10.8 us
    ppermute x6, starting transfers between devices, quad_rotated(): return lax.ppermute(block, 'tm', route)  10.2 us
    ppermute x6, waiting for transfers between devices, quad_rotated(): return lax.ppermute(block, 'tm', route)  9.09 us
  transfers between devices with their start and end apart: 36, of which 17 were waited for; matrix products, arithmetic and copies ran while one was open for 1% of the time, Pallas kernels for 8%

profile of v6, /device:TPU:1, one launch (start us, length us, event | category | flops | bytes accessed | tf_op | source)
XLA Modules:
  0.0 127.1 jit_solution(4486202913260575301)
XLA Ops:
  0.6 2.2 %collective-permute-start = (bf16[2,4,64,128]{3,2,1,0:T(8,128)(2,1)}, bf16[2,4,64,128]{3,2,1,0:T(8,128)(2,1)S(1)}, u32[]{:S(2)}, u32[]{:S(2)}) collective-permute-start(bf16[2,4,64,128]{3,2,1,0:T(8,128)(2,1)} %param.4), channel_id=1, source_target_pairs={{0,1},{1,2},{2,3},{3,0},{4,5},{5,6},{6,7},{7,4},{8,9},{9,10},{10,1... | collective-permute-start | bytes 393224 | tf_op jit(solution)/shard_map/ppermute | solution.py:288
  2.8 2.6 %collective-permute-start.1 = (bf16[2,4,64,128]{3,2,1,0:T(8,128)(2,1)}, bf16[2,4,64,128]{3,2,1,0:T(8,128)(2,1)S(1)}, u32[]{:S(2)}, u32[]{:S(2)}) collective-permute-start(bf16[2,4,64,128]{3,2,1,0:T(8,128)(2,1)} %param.4), channel_id=1, source_target_pairs={{0,2},{1,3},{2,0},{3,1},{4,6},{5,7},{6,4},{7,5},{8,10},{9,11},{10,... | collective-permute-start | bytes 393224 | tf_op jit(solution)/shard_map/ppermute | solution.py:288
  5.5 1.1 collective-permute-start.2
  6.5 0.9 constant_dynamic-update-slice_fusion.3
  7.5 3.8 %collective-permute-done.1 = bf16[2,4,64,128]{3,2,1,0:T(8,128)(2,1)S(1)} collective-permute-done((bf16[2,4,64,128]{3,2,1,0:T(8,128)(2,1)}, bf16[2,4,64,128]{3,2,1,0:T(8,128)(2,1)S(1)}, u32[]{:S(2)}, u32[]{:S(2)}) %collective-permute-start.1) | collective-permute-done | bytes 131104 | tf_op jit(solution)/shard_map/ppermute | solution.py:288
  11.4 5.0 %collective-permute-start.3 = (bf16[2,4,256,128]{3,2,1,0:T(8,128)(2,1)S(1)}, bf16[2,4,256,128]{3,2,1,0:T(8,128)(2,1)S(1)}, u32[]{:S(2)}, u32[]{:S(2)}) collective-permute-start(bf16[2,4,256,128]{3,2,1,0:T(8,128)(2,1)S(1)} %constant_dynamic-update-slice_fusion.refs_2_.refs_1_), channel_id=1, source_target_pairs={{0,16},{16,32},{32,48},{48,64},{64,80},{80,96},{96,112},{112,128},... | collective-permute-start | bytes 1572872 | tf_op jit(solution)/shard_map/ppermute | solution.py:12
  16.5 0.9 copy-done.2
  17.4 0.5 shard_map.68
  18.0 3.1 %collective-permute-start.6 = (bf16[2,64,128]{2,1,0:T(8,128)(2,1)S(1)}, bf16[2,64,128]{2,1,0:T(8,128)(2,1)S(1)}, u32[]{:S(2)}, u32[]{:S(2)}) collective-permute-start(bf16[2,64,128]{2,1,0:T(8,128)(2,1)S(1)} %get-tuple-element.30), channel_id=1, source_target_pairs={{0,4},{4,8},{8,12},{1,5},{5,9},{9,13},{2,6},{6,10},{10,14},{3,7},{... | collective-permute-start | bytes 98312 | tf_op jit(solution)/shard_map/ppermute | solution.py:12
  21.1 1.3 %collective-permute-start.7 = (bf16[2,64,128]{2,1,0:T(8,128)(2,1)S(1)}, bf16[2,64,128]{2,1,0:T(8,128)(2,1)S(1)}, u32[]{:S(2)}, u32[]{:S(2)}) collective-permute-start(bf16[2,64,128]{2,1,0:T(8,128)(2,1)S(1)} %get-tuple-element.31), channel_id=1, source_target_pairs={{4,0},{8,4},{12,8},{5,1},{9,5},{13,9},{6,2},{10,6},{14,10},{7,3},{... | collective-permute-start | bytes 98312 | tf_op jit(solution)/shard_map/ppermute | solution.py:12
  22.4 3.3 %collective-permute-done.7.refs_2_ = bf16[2,64,128]{2,1,0:T(8,128)(2,1)S(1)} collective-permute-done((bf16[2,64,128]{2,1,0:T(8,128)(2,1)S(1)}, bf16[2,64,128]{2,1,0:T(8,128)(2,1)S(1)}, u32[]{:S(2)}, u32[]{:S(2)}) %collective-permute-start.7) | collective-permute-done | bytes 32800 | tf_op jit(solution)/shard_map/ppermute | solution.py:12
  25.8 0.6 shard_map.69.refs_1_.refs_6_
  26.3 1.9 %collective-permute-start.8 = (bf16[2,6,64,128]{3,2,1,0:T(8,128)(2,1)S(1)}, bf16[2,6,64,128]{3,2,1,0:T(8,128)(2,1)S(1)}, u32[]{:S(2)}, u32[]{:S(2)}) collective-permute-start(bf16[2,6,64,128]{3,2,1,0:T(8,128)(2,1)S(1)} %shard_map.69.refs_1_.refs_6_), channel_id=1, source_target_pairs={{16,0},{32,16},{48,32},{64,48},{80,64},{96,80},{112,96},{128,112},... | collective-permute-start | bytes 589832 | tf_op jit(solution)/shard_map/ppermute | solution.py:12
  28.3 0.6 shard_map.67
  28.9 3.1 %collective-permute-start.4 = (bf16[4,256,128]{2,1,0:T(8,128)(2,1)S(1)}, bf16[4,256,128]{2,1,0:T(8,128)(2,1)S(1)}, u32[]{:S(2)}, u32[]{:S(2)}) collective-permute-start(bf16[4,256,128]{2,1,0:T(8,128)(2,1)S(1)} %get-tuple-element.28), channel_id=1, source_target_pairs={{0,4},{4,8},{8,12},{1,5},{5,9},{9,13},{2,6},{6,10},{10,14},{3,7},{... | collective-permute-start | bytes 786440 | tf_op jit(solution)/shard_map/ppermute | solution.py:12
  32.0 1.3 %collective-permute-start.5 = (bf16[4,256,128]{2,1,0:T(8,128)(2,1)S(1)}, bf16[4,256,128]{2,1,0:T(8,128)(2,1)S(1)}, u32[]{:S(2)}, u32[]{:S(2)}) collective-permute-start(bf16[4,256,128]{2,1,0:T(8,128)(2,1)S(1)} %get-tuple-element.29), channel_id=1, source_target_pairs={{4,0},{8,4},{12,8},{5,1},{9,5},{13,9},{6,2},{10,6},{14,10},{7,3},{... | collective-permute-start | bytes 786440 | tf_op jit(solution)/shard_map/ppermute | solution.py:12
  33.3 2.0 %shard_map.70 = (f32[8,64,128]{2,1,0:T(8,128)S(1)}, bf16[8,64,128]{2,1,0:T(8,128)(2,1)S(1)}, bf16[8,64,128]{2,1,0:T(8,128)(2,1)S(1)}, bf16[8,64,128]{2,1,0:T(8,128)(2,1)S(1)}) custom-call(s32[4]{0:T(128)S(1)} %pad_add_fusion.refs_0_, bf16[2,6,64,128]{3,2,1,0:T(8,128)(2,1)S(1)} %shard_map.69.refs_1_.refs_6_, ...), custom_call_target="tpu_custom_call" | custom-call | tf_op jit(solution)/shard_map/pallas_call | solution.py:24
  35.4 1.0 collective-permute-start.9
  36.4 2.1 %collective-permute-start.10 = (bf16[8,64,128]{2,1,0:T(8,128)(2,1)S(1)}, bf16[8,64,128]{2,1,0:T(8,128)(2,1)S(1)}, u32[]{:S(2)}, u32[]{:S(2)}) collective-permute-start(bf16[8,64,128]{2,1,0:T(8,128)(2,1)S(1)} %get-tuple-element.36), channel_id=1, source_target_pairs={{0,2},{1,3},{2,0},{3,1},{4,6},{5,7},{6,4},{7,5},{8,10},{9,11},{10,... | collective-permute-start | bytes 393224 | tf_op jit(solution)/shard_map/ppermute | solution.py:288
  38.5 1.3 %collective-permute-start.11 = (bf16[8,64,128]{2,1,0:T(8,128)(2,1)S(1)}, bf16[8,64,128]{2,1,0:T(8,128)(2,1)S(1)}, u32[]{:S(2)}, u32[]{:S(2)}) collective-permute-start(bf16[8,64,128]{2,1,0:T(8,128)(2,1)S(1)} %get-tuple-element.37), channel_id=1, source_target_pairs={{0,3},{1,0},{2,1},{3,2},{4,7},{5,4},{6,5},{7,6},{8,11},{9,8},{10,9... | collective-permute-start | bytes 393224 | tf_op jit(solution)/shard_map/ppermute | solution.py:288
  39.8 1.9 %collective-permute-done.5.refs_4_ = bf16[4,256,128]{2,1,0:T(8,128)(2,1)S(1)} collective-permute-done((bf16[4,256,128]{2,1,0:T(8,128)(2,1)S(1)}, bf16[4,256,128]{2,1,0:T(8,128)(2,1)S(1)}, u32[]{:S(2)}, u32[]{:S(2)}) %collective-permute-start.5) | collective-permute-done | bytes 262176 | tf_op jit(solution)/shard_map/ppermute | solution.py:12
  41.7 2.2 %shard_map.71 = (bf16[24,256,128]{2,1,0:T(8,128)(2,1)S(1)}, f32[8,64,128]{2,1,0:T(8,128)S(1)}, bf16[8,64,128]{2,1,0:T(8,128)(2,1)S(1)}) custom-call(s32[4]{0:T(128)S(1)} %pad_add_fusion.refs_0_, bf16[2,4,256,128]{3,2,1,0:T(8,128)(2,1)S(1)} %constant_dynamic-update-slice_fusion.refs_2_.refs_1_, ...), custom_call_target="tpu_custom_call" | custom-call | tf_op jit(solution)/shard_map/pallas_call | solution.py:24
  43.9 1.9 %collective-permute-start.17 = (bf16[8,64,128]{2,1,0:T(8,128)(2,1)S(1)}, bf16[8,64,128]{2,1,0:T(8,128)(2,1)S(1)}, u32[]{:S(2)}, u32[]{:S(2)}) collective-permute-start(bf16[8,64,128]{2,1,0:T(8,128)(2,1)S(1)} %get-tuple-element.42.refs_2_), channel_id=1, source_target_pairs={{0,3},{1,0},{2,1},{3,2},{4,7},{5,4},{6,5},{7,6},{8,11},{9,8},{10,9... | collective-permute-start | bytes 393224 | tf_op jit(solution)/shard_map/ppermute | solution.py:288
  45.8 0.9 collective-permute-start.16
  46.6 0.4 collective-permute-start.15
  47.1 2.3 %shard_map.72 = (bf16[2,4,64,128]{3,2,1,0:T(8,128)(2,1)S(1)}, bf16[2,64,128]{2,1,0:T(8,128)(2,1)S(1)}, bf16[2,64,128]{2,1,0:T(8,128)(2,1)S(1)}, bf16[4,27,16,256]{3,2,1,0:T(8,128)(2,1)S(1)}) custom-call(s32[4]{0:T(128)S(1)} %pad_add_fusion.refs_0_, bf16[24,256,128]{2,1,0:T(8,128)(2,1)S(1)} %get-tuple-element.33.refs_1_, ...), custom_call_target="tpu_custom_call" | custom-call | tf_op jit(solution)/shard_map/pallas_call | solution.py:24
  49.4 2.7 %collective-permute-start.12 = (bf16[2,64,128]{2,1,0:T(8,128)(2,1)S(1)}, bf16[2,64,128]{2,1,0:T(8,128)(2,1)S(1)}, u32[]{:S(2)}, u32[]{:S(2)}) collective-permute-start(bf16[2,64,128]{2,1,0:T(8,128)(2,1)S(1)} %get-tuple-element.38), channel_id=1, source_target_pairs={{0,4},{4,8},{8,12},{1,5},{5,9},{9,13},{2,6},{6,10},{10,14},{3,7},{... | collective-permute-start | bytes 98312 | tf_op jit(solution)/shard_map/ppermute | solution.py:12
  52.1 1.5 %collective-permute-start.13 = (bf16[2,64,128]{2,1,0:T(8,128)(2,1)S(1)}, bf16[2,64,128]{2,1,0:T(8,128)(2,1)S(1)}, u32[]{:S(2)}, u32[]{:S(2)}) collective-permute-start(bf16[2,64,128]{2,1,0:T(8,128)(2,1)S(1)} %get-tuple-element.39), channel_id=1, source_target_pairs={{4,0},{8,4},{12,8},{5,1},{9,5},{13,9},{6,2},{10,6},{14,10},{7,3},{... | collective-permute-start | bytes 98312 | tf_op jit(solution)/shard_map/ppermute | solution.py:12
  53.6 3.2 %collective-permute-done.13.refs_2_ = bf16[2,64,128]{2,1,0:T(8,128)(2,1)S(1)} collective-permute-done((bf16[2,64,128]{2,1,0:T(8,128)(2,1)S(1)}, bf16[2,64,128]{2,1,0:T(8,128)(2,1)S(1)}, u32[]{:S(2)}, u32[]{:S(2)}) %collective-permute-start.13) | collective-permute-done | bytes 32800 | tf_op jit(solution)/shard_map/ppermute | solution.py:12
  56.8 0.6 shard_map.73.refs_8_.refs_1_
  57.3 2.6 %shard_map.74 = (bf16[4,27,16,256]{3,2,1,0:T(8,128)(2,1)S(1)}, bf16[4,27,16,256]{3,2,1,0:T(8,128)(2,1)S(1)}) custom-call(s32[4]{0:T(128)S(1)} %pad_add_fusion.refs_0_, bf16[4,27,16,256]{3,2,1,0:T(8,128)(2,1)S(1)} %get-tuple-element.41.refs_1_, bf16[8,64,128]{2,1,0:T(8,128)(2,1)S(1)} %get-tuple-element.42.refs_2_, ...), custom_call_target="tpu_custom_call" | custom-call | tf_op jit(solution)/shard_map/pallas_call | solution.py:24
  59.9 2.3 %collective-permute-start.18 = (bf16[4,27,16,256]{3,2,1,0:T(8,128)(2,1)S(1)}, bf16[4,27,16,256]{3,2,1,0:T(8,128)(2,1)S(1)}, u32[]{:S(2)}, u32[]{:S(2)}) collective-permute-start(bf16[4,27,16,256]{3,2,1,0:T(8,128)(2,1)S(1)} %get-tuple-element.44), channel_id=1, source_target_pairs={{0,16},{16,0},{32,48},{48,32},{64,80},{80,64},{96,112},{112,96},{1... | collective-permute-start | bytes 2654216 | tf_op jit(solution)/shard_map/ppermute | solution.py:304
  62.2 1.9 %collective-permute-start.14 = (bf16[2,6,64,128]{3,2,1,0:T(8,128)(2,1)S(1)}, bf16[2,6,64,128]{3,2,1,0:T(8,128)(2,1)S(1)}, u32[]{:S(2)}, u32[]{:S(2)}) collective-permute-start(bf16[2,6,64,128]{3,2,1,0:T(8,128)(2,1)S(1)} %shard_map.73.refs_8_.refs_1_), channel_id=1, source_target_pairs={{16,0},{32,16},{48,32},{64,48},{80,64},{96,80},{112,96},{128,112},... | collective-permute-start | bytes 589832 | tf_op jit(solution)/shard_map/ppermute | solution.py:12
  64.2 0.1 collective-permute-done.18
  64.3 0.3 convert_add_fusion
  64.8 2.0 %collective-permute-start.23 = (bf16[27,16,256]{2,1,0:T(8,128)(2,1)S(1)}, bf16[27,16,256]{2,1,0:T(8,128)(2,1)S(1)}, u32[]{:S(2)}, u32[]{:S(2)}) collective-permute-start(bf16[27,16,256]{2,1,0:T(8,128)(2,1)S(1)} %get-tuple-element.58), channel_id=1, source_target_pairs={{0,8},{4,12},{8,0},{12,4},{1,9},{5,13},{9,1},{13,5},{2,10},{6,14},... | collective-permute-start | bytes 663560 | tf_op jit(solution)/shard_map/ppermute | solution.py:288
  66.8 3.6 %collective-permute-done.14.refs_2_ = bf16[2,6,64,128]{3,2,1,0:T(8,128)(2,1)S(1)} collective-permute-done((bf16[2,6,64,128]{3,2,1,0:T(8,128)(2,1)S(1)}, bf16[2,6,64,128]{3,2,1,0:T(8,128)(2,1)S(1)}, u32[]{:S(2)}, u32[]{:S(2)}) %collective-permute-start.14) | collective-permute-done | bytes 196640 | tf_op jit(solution)/shard_map/ppermute | solution.py:12
  70.4 2.0 %shard_map.75 = (f32[8,64,128]{2,1,0:T(8,128)S(1)}, bf16[8,64,128]{2,1,0:T(8,128)(2,1)S(1)}, bf16[8,64,128]{2,1,0:T(8,128)(2,1)S(1)}, bf16[8,64,128]{2,1,0:T(8,128)(2,1)S(1)}) custom-call(s32[4]{0:T(128)S(1)} %pad_add_fusion.refs_0_, bf16[2,6,64,128]{3,2,1,0:T(8,128)(2,1)S(1)} %shard_map.73.refs_8_.refs_1_, ...), custom_call_target="tpu_custom_call" | custom-call | tf_op jit(solution)/shard_map/pallas_call | solution.py:24
  72.5 0.6 collective-permute-done.23.refs_3_
  73.0 5.4 %collective-permute-done.22.refs_2_ = bf16[27,16,256]{2,1,0:T(8,128)(2,1)S(1)} collective-permute-done((bf16[27,16,256]{2,1,0:T(8,128)(2,1)S(1)}, bf16[27,16,256]{2,1,0:T(8,128)(2,1)S(1)}, u32[]{:S(2)}, u32[]{:S(2)}) %collective-permute-start.22) | collective-permute-done | bytes 221216 | tf_op jit(solution)/shard_map/ppermute | solution.py:288
  78.5 0.7 shard_map.76
  79.2 2.8 %collective-permute-start.25 = (bf16[27,8,128]{2,1,0:T(8,128)(2,1)S(1)}, bf16[27,8,128]{2,1,0:T(8,128)(2,1)S(1)}, u32[]{:S(2)}, u32[]{:S(2)}) collective-permute-start(bf16[27,8,128]{2,1,0:T(8,128)(2,1)S(1)} %get-tuple-element.50), channel_id=1, source_target_pairs={{0,32},{16,48},{32,64},{48,80},{64,96},{80,112},{96,0},{112,16},{1... | collective-permute-start | bytes 165896 | tf_op jit(solution)/shard_map/ppermute | solution.py:309
  81.9 3.7 %collective-permute-start.26 = (bf16[27,8,128]{2,1,0:T(8,128)(2,1)S(1)}, bf16[27,8,128]{2,1,0:T(8,128)(2,1)S(1)}, u32[]{:S(2)}, u32[]{:S(2)}) collective-permute-start(bf16[27,8,128]{2,1,0:T(8,128)(2,1)S(1)} %get-tuple-element.51), channel_id=1, source_target_pairs={{0,64},{16,80},{32,96},{48,112},{64,0},{80,16},{96,32},{112,48},{1... | collective-permute-start | bytes 165896 | tf_op jit(solution)/shard_map/ppermute | solution.py:309
  85.7 1.3 collective-permute-done.25
  86.9 3.1 %collective-permute-done.26 = bf16[27,8,128]{2,1,0:T(8,128)(2,1)S(1)} collective-permute-done((bf16[27,8,128]{2,1,0:T(8,128)(2,1)S(1)}, bf16[27,8,128]{2,1,0:T(8,128)(2,1)S(1)}, u32[]{:S(2)}, u32[]{:S(2)}) %collective-permute-start.26) | collective-permute-done | bytes 55328 | tf_op jit(solution)/shard_map/ppermute | solution.py:309
  90.1 3.4 %collective-permute-start.28 = (bf16[27,8,128]{2,1,0:T(8,128)(2,1)S(1)}, bf16[27,8,128]{2,1,0:T(8,128)(2,1)S(1)}, u32[]{:S(2)}, u32[]{:S(2)}) collective-permute-start(bf16[27,8,128]{2,1,0:T(8,128)(2,1)S(1)} %add_convert_fusion.2), channel_id=1, source_target_pairs={{0,128},{16,144},{32,160},{48,176},{64,192},{80,208},{96,224},{112... | collective-permute-start | bytes 165896 | tf_op jit(solution)/shard_map/ppermute | solution.py:304
  93.5 1.3 %collective-permute-start.19 = (bf16[8,64,128]{2,1,0:T(8,128)(2,1)S(1)}, bf16[8,64,128]{2,1,0:T(8,128)(2,1)S(1)}, u32[]{:S(2)}, u32[]{:S(2)}) collective-permute-start(bf16[8,64,128]{2,1,0:T(8,128)(2,1)S(1)} %get-tuple-element.46), channel_id=1, source_target_pairs={{0,1},{1,2},{2,3},{3,0},{4,5},{5,6},{6,7},{7,4},{8,9},{9,10},{10,1... | collective-permute-start | bytes 393224 | tf_op jit(solution)/shard_map/ppermute | solution.py:288
  94.8 2.4 %collective-permute-start.20 = (bf16[8,64,128]{2,1,0:T(8,128)(2,1)S(1)}, bf16[8,64,128]{2,1,0:T(8,128)(2,1)S(1)}, u32[]{:S(2)}, u32[]{:S(2)}) collective-permute-start(bf16[8,64,128]{2,1,0:T(8,128)(2,1)S(1)} %get-tuple-element.47), channel_id=1, source_target_pairs={{0,2},{1,3},{2,0},{3,1},{4,6},{5,7},{6,4},{7,5},{8,10},{9,11},{10,... | collective-permute-start | bytes 393224 | tf_op jit(solution)/shard_map/ppermute | solution.py:288
  97.2 1.3 %collective-permute-start.21 = (bf16[8,64,128]{2,1,0:T(8,128)(2,1)S(1)}, bf16[8,64,128]{2,1,0:T(8,128)(2,1)S(1)}, u32[]{:S(2)}, u32[]{:S(2)}) collective-permute-start(bf16[8,64,128]{2,1,0:T(8,128)(2,1)S(1)} %get-tuple-element.48), channel_id=1, source_target_pairs={{0,3},{1,0},{2,1},{3,2},{4,7},{5,4},{6,5},{7,6},{8,11},{9,8},{10,9... | collective-permute-start | bytes 393224 | tf_op jit(solution)/shard_map/ppermute | solution.py:288
  98.6 3.0 %collective-permute-start.31 = (bf16[27,8,128]{2,1,0:T(8,128)(2,1)S(1)}, bf16[27,8,128]{2,1,0:T(8,128)(2,1)S(1)}, u32[]{:S(2)}, u32[]{:S(2)}) collective-permute-start(bf16[27,8,128]{2,1,0:T(8,128)(2,1)S(1)} %add_convert_fusion.1.refs_1_), channel_id=1, source_target_pairs={{0,96},{16,112},{32,0},{48,16},{64,32},{80,48},{96,64},{112,80},{1... | collective-permute-start | bytes 165896 | tf_op jit(solution)/shard_map/ppermute | solution.py:309
  101.6 0.7 collective-permute-start.30
  102.4 0.4 collective-permute-done.31.refs_4_
  102.8 2.9 %collective-permute-done.30.refs_3_ = bf16[27,8,128]{2,1,0:T(8,128)(2,1)S(1)} collective-permute-done((bf16[27,8,128]{2,1,0:T(8,128)(2,1)S(1)}, bf16[27,8,128]{2,1,0:T(8,128)(2,1)S(1)}, u32[]{:S(2)}, u32[]{:S(2)}) %collective-permute-start.30) | collective-permute-done | bytes 55328 | tf_op jit(solution)/shard_map/ppermute | solution.py:309
  105.7 1.3 %collective-permute-done.29.refs_2_ = bf16[27,8,128]{2,1,0:T(8,128)(2,1)S(1)} collective-permute-done((bf16[27,8,128]{2,1,0:T(8,128)(2,1)S(1)}, bf16[27,8,128]{2,1,0:T(8,128)(2,1)S(1)}, u32[]{:S(2)}, u32[]{:S(2)}) %collective-permute-start.29) | collective-permute-done | bytes 55328 | tf_op jit(solution)/shard_map/ppermute | solution.py:309
  107.0 0.6 shard_map.77.refs_1_
  107.8 2.1 %collective-permute-start.33 = (bf16[27,16,256]{2,1,0:T(8,128)(2,1)S(1)}, bf16[27,16,256]{2,1,0:T(8,128)(2,1)S(1)}, u32[]{:S(2)}, u32[]{:S(2)}) collective-permute-start(bf16[27,16,256]{2,1,0:T(8,128)(2,1)S(1)} %shard_map.77.refs_1_), channel_id=1, source_target_pairs={{0,8},{4,12},{8,0},{12,4},{1,9},{5,13},{9,1},{13,5},{2,10},{6,14},... | collective-permute-start | bytes 663560 | tf_op jit(solution)/shard_map/ppermute | solution.py:288
  109.8 2.7 %collective-permute-done.34.refs_4_ = bf16[27,16,256]{2,1,0:T(8,128)(2,1)S(1)} collective-permute-done((bf16[27,16,256]{2,1,0:T(8,128)(2,1)S(1)}, bf16[27,16,256]{2,1,0:T(8,128)(2,1)S(1)}, u32[]{:S(2)}, u32[]{:S(2)}) %collective-permute-start.34) | collective-permute-done | bytes 221216 | tf_op jit(solution)/shard_map/ppermute | solution.py:288
  112.5 1.7 %collective-permute-done.33.refs_3_ = bf16[27,16,256]{2,1,0:T(8,128)(2,1)S(1)} collective-permute-done((bf16[27,16,256]{2,1,0:T(8,128)(2,1)S(1)}, bf16[27,16,256]{2,1,0:T(8,128)(2,1)S(1)}, u32[]{:S(2)}, u32[]{:S(2)}) %collective-permute-start.33) | collective-permute-done | bytes 221216 | tf_op jit(solution)/shard_map/ppermute | solution.py:288
  114.2 2.7 %collective-permute-done.32.refs_2_ = bf16[27,16,256]{2,1,0:T(8,128)(2,1)S(1)} collective-permute-done((bf16[27,16,256]{2,1,0:T(8,128)(2,1)S(1)}, bf16[27,16,256]{2,1,0:T(8,128)(2,1)S(1)}, u32[]{:S(2)}, u32[]{:S(2)}) %collective-permute-start.32) | collective-permute-done | bytes 221216 | tf_op jit(solution)/shard_map/ppermute | solution.py:288
  116.9 0.6 shard_map.78
  117.5 5.1 %collective-permute-start.35 = (bf16[27,64,256]{2,1,0:T(8,128)(2,1)S(1)}, bf16[27,64,256]{2,1,0:T(8,128)(2,1)S(1)}, u32[]{:S(2)}, u32[]{:S(2)}) collective-permute-start(bf16[27,64,256]{2,1,0:T(8,128)(2,1)S(1)} %shard_map.78), channel_id=1, source_target_pairs={{0,16},{16,0},{32,48},{48,32},{64,80},{80,64},{96,112},{112,96},{1... | collective-permute-start | bytes 2654216 | tf_op jit(solution)/shard_map/ppermute | solution.py:304
  122.6 2.1 %collective-permute-done.35 = bf16[27,64,256]{2,1,0:T(8,128)(2,1)S(1)} collective-permute-done((bf16[27,64,256]{2,1,0:T(8,128)(2,1)S(1)}, bf16[27,64,256]{2,1,0:T(8,128)(2,1)S(1)}, u32[]{:S(2)}, u32[]{:S(2)}) %collective-permute-start.35) | collective-permute-done | bytes 884768 | tf_op jit(solution)/shard_map/ppermute | solution.py:304
  124.7 0.1 broadcast_select_fusion
  124.8 2.2 %convert_bitcast_fusion = (f32[64,3,3,3,256]{4,0,3,2,1:T(8,128)}, f32[64,3,3,3,256]{4,0,3,2,1:T(8,128)}) fusion(bf16[3,3,3,64,256]{4,3,2,1,0:T(8,128)(2,1)S(1)} %bitcast.34, bf16[3,3,3,64,256]{4,3,2,1,0:T(8,128)(2,1)S(1)} %bitcast.35), kind=kLoop, calls=%fused_computation | loop fusion | flops 884736 | bytes 5308416 | tf_op jit(solution)/shard_map/transpose | solution.py:335
  (41 shorter events, 0.6 us)
Async XLA Ops:
  0.6 32.7 %copy-start.1 = (bf16[64,3,3,3,256]{4,0,3,2,1:T(8,128)(2,1)S(1)}, bf16[64,3,3,3,256]{4,0,3,2,1:T(8,128)(2,1)}, u32[]{:S(2)}) copy-start(bf16[64,3,3,3,256]{4,0,3,2,1:T(8,128)(2,1)} %param.7) | copy-start | bytes 2654212
  0.6 6.8 %collective-permute-start = (bf16[2,4,64,128]{3,2,1,0:T(8,128)(2,1)}, bf16[2,4,64,128]{3,2,1,0:T(8,128)(2,1)S(1)}, u32[]{:S(2)}, u32[]{:S(2)}) collective-permute-start(bf16[2,4,64,128]{3,2,1,0:T(8,128)(2,1)} %param.4), channel_id=1, source_target_pairs={{0,1},{1,2},{2,3},{3,0},{4,5},{5,6},{6,7},{7,4},{8,9},{9,10},{10,1... | collective-permute-start | bytes 393224 | tf_op jit(solution)/shard_map/ppermute | solution.py:288
  2.8 8.5 %collective-permute-start.1 = (bf16[2,4,64,128]{3,2,1,0:T(8,128)(2,1)}, bf16[2,4,64,128]{3,2,1,0:T(8,128)(2,1)S(1)}, u32[]{:S(2)}, u32[]{:S(2)}) collective-permute-start(bf16[2,4,64,128]{3,2,1,0:T(8,128)(2,1)} %param.4), channel_id=1, source_target_pairs={{0,2},{1,3},{2,0},{3,1},{4,6},{5,7},{6,4},{7,5},{8,10},{9,11},{10,... | collective-permute-start | bytes 393224 | tf_op jit(solution)/shard_map/ppermute | solution.py:288
  5.5 5.9 %collective-permute-start.2 = (bf16[2,4,64,128]{3,2,1,0:T(8,128)(2,1)}, bf16[2,4,64,128]{3,2,1,0:T(8,128)(2,1)S(1)}, u32[]{:S(2)}, u32[]{:S(2)}) collective-permute-start(bf16[2,4,64,128]{3,2,1,0:T(8,128)(2,1)} %param.4), channel_id=1, source_target_pairs={{0,3},{1,0},{2,1},{3,2},{4,7},{5,4},{6,5},{7,6},{8,11},{9,8},{10,9... | collective-permute-start | bytes 393224 | tf_op jit(solution)/shard_map/ppermute | solution.py:288
  7.5 34.1 %copy-start = (bf16[64,3,3,3,256]{4,0,3,2,1:T(8,128)(2,1)S(1)}, bf16[64,3,3,3,256]{4,0,3,2,1:T(8,128)(2,1)}, u32[]{:S(2)}) copy-start(bf16[64,3,3,3,256]{4,0,3,2,1:T(8,128)(2,1)} %param.6) | copy-start | bytes 2654212
  11.4 16.8 %collective-permute-start.3 = (bf16[2,4,256,128]{3,2,1,0:T(8,128)(2,1)S(1)}, bf16[2,4,256,128]{3,2,1,0:T(8,128)(2,1)S(1)}, u32[]{:S(2)}, u32[]{:S(2)}) collective-permute-start(bf16[2,4,256,128]{3,2,1,0:T(8,128)(2,1)S(1)} %constant_dynamic-update-slice_fusion.refs_2_.refs_1_), channel_id=1, source_target_pairs={{0,16},{16,32},{32,48},{48,64},{64,80},{80,96},{96,112},{112,128},... | collective-permute-start | bytes 1572872 | tf_op jit(solution)/shard_map/ppermute | solution.py:12
  16.5 0.9 copy-start.2
  18.0 4.4 %collective-permute-start.6 = (bf16[2,64,128]{2,1,0:T(8,128)(2,1)S(1)}, bf16[2,64,128]{2,1,0:T(8,128)(2,1)S(1)}, u32[]{:S(2)}, u32[]{:S(2)}) collective-permute-start(bf16[2,64,128]{2,1,0:T(8,128)(2,1)S(1)} %get-tuple-element.30), channel_id=1, source_target_pairs={{0,4},{4,8},{8,12},{1,5},{5,9},{9,13},{2,6},{6,10},{10,14},{3,7},{... | collective-permute-start | bytes 98312 | tf_op jit(solution)/shard_map/ppermute | solution.py:12
  21.1 4.7 %collective-permute-start.7 = (bf16[2,64,128]{2,1,0:T(8,128)(2,1)S(1)}, bf16[2,64,128]{2,1,0:T(8,128)(2,1)S(1)}, u32[]{:S(2)}, u32[]{:S(2)}) collective-permute-start(bf16[2,64,128]{2,1,0:T(8,128)(2,1)S(1)} %get-tuple-element.31), channel_id=1, source_target_pairs={{4,0},{8,4},{12,8},{5,1},{9,5},{13,9},{6,2},{10,6},{14,10},{7,3},{... | collective-permute-start | bytes 98312 | tf_op jit(solution)/shard_map/ppermute | solution.py:12
  26.3 7.0 %collective-permute-start.8 = (bf16[2,6,64,128]{3,2,1,0:T(8,128)(2,1)S(1)}, bf16[2,6,64,128]{3,2,1,0:T(8,128)(2,1)S(1)}, u32[]{:S(2)}, u32[]{:S(2)}) collective-permute-start(bf16[2,6,64,128]{3,2,1,0:T(8,128)(2,1)S(1)} %shard_map.69.refs_1_.refs_6_), channel_id=1, source_target_pairs={{16,0},{32,16},{48,32},{64,48},{80,64},{96,80},{112,96},{128,112},... | collective-permute-start | bytes 589832 | tf_op jit(solution)/shard_map/ppermute | solution.py:12
  28.9 10.9 %collective-permute-start.4 = (bf16[4,256,128]{2,1,0:T(8,128)(2,1)S(1)}, bf16[4,256,128]{2,1,0:T(8,128)(2,1)S(1)}, u32[]{:S(2)}, u32[]{:S(2)}) collective-permute-start(bf16[4,256,128]{2,1,0:T(8,128)(2,1)S(1)} %get-tuple-element.28), channel_id=1, source_target_pairs={{0,4},{4,8},{8,12},{1,5},{5,9},{9,13},{2,6},{6,10},{10,14},{3,7},{... | collective-permute-start | bytes 786440 | tf_op jit(solution)/shard_map/ppermute | solution.py:12
  32.0 9.7 %collective-permute-start.5 = (bf16[4,256,128]{2,1,0:T(8,128)(2,1)S(1)}, bf16[4,256,128]{2,1,0:T(8,128)(2,1)S(1)}, u32[]{:S(2)}, u32[]{:S(2)}) collective-permute-start(bf16[4,256,128]{2,1,0:T(8,128)(2,1)S(1)} %get-tuple-element.29), channel_id=1, source_target_pairs={{4,0},{8,4},{12,8},{5,1},{9,5},{13,9},{6,2},{10,6},{14,10},{7,3},{... | collective-permute-start | bytes 786440 | tf_op jit(solution)/shard_map/ppermute | solution.py:12
  35.4 11.3 %collective-permute-start.9 = (bf16[8,64,128]{2,1,0:T(8,128)(2,1)S(1)}, bf16[8,64,128]{2,1,0:T(8,128)(2,1)S(1)}, u32[]{:S(2)}, u32[]{:S(2)}) collective-permute-start(bf16[8,64,128]{2,1,0:T(8,128)(2,1)S(1)} %get-tuple-element.35), channel_id=1, source_target_pairs={{0,1},{1,2},{2,3},{3,0},{4,5},{5,6},{6,7},{7,4},{8,9},{9,10},{10,1... | collective-permute-start | bytes 393224 | tf_op jit(solution)/shard_map/ppermute | solution.py:288
  36.4 10.7 %collective-permute-start.10 = (bf16[8,64,128]{2,1,0:T(8,128)(2,1)S(1)}, bf16[8,64,128]{2,1,0:T(8,128)(2,1)S(1)}, u32[]{:S(2)}, u32[]{:S(2)}) collective-permute-start(bf16[8,64,128]{2,1,0:T(8,128)(2,1)S(1)} %get-tuple-element.36), channel_id=1, source_target_pairs={{0,2},{1,3},{2,0},{3,1},{4,6},{5,7},{6,4},{7,5},{8,10},{9,11},{10,... | collective-permute-start | bytes 393224 | tf_op jit(solution)/shard_map/ppermute | solution.py:288
  38.5 8.6 %collective-permute-start.11 = (bf16[8,64,128]{2,1,0:T(8,128)(2,1)S(1)}, bf16[8,64,128]{2,1,0:T(8,128)(2,1)S(1)}, u32[]{:S(2)}, u32[]{:S(2)}) collective-permute-start(bf16[8,64,128]{2,1,0:T(8,128)(2,1)S(1)} %get-tuple-element.37), channel_id=1, source_target_pairs={{0,3},{1,0},{2,1},{3,2},{4,7},{5,4},{6,5},{7,6},{8,11},{9,8},{10,9... | collective-permute-start | bytes 393224 | tf_op jit(solution)/shard_map/ppermute | solution.py:288
  43.9 13.5 %collective-permute-start.17 = (bf16[8,64,128]{2,1,0:T(8,128)(2,1)S(1)}, bf16[8,64,128]{2,1,0:T(8,128)(2,1)S(1)}, u32[]{:S(2)}, u32[]{:S(2)}) collective-permute-start(bf16[8,64,128]{2,1,0:T(8,128)(2,1)S(1)} %get-tuple-element.42.refs_2_), channel_id=1, source_target_pairs={{0,3},{1,0},{2,1},{3,2},{4,7},{5,4},{6,5},{7,6},{8,11},{9,8},{10,9... | collective-permute-start | bytes 393224 | tf_op jit(solution)/shard_map/ppermute | solution.py:288
  45.8 11.6 %collective-permute-start.16 = (bf16[8,64,128]{2,1,0:T(8,128)(2,1)S(1)}, bf16[8,64,128]{2,1,0:T(8,128)(2,1)S(1)}, u32[]{:S(2)}, u32[]{:S(2)}) collective-permute-start(bf16[8,64,128]{2,1,0:T(8,128)(2,1)S(1)} %get-tuple-element.42.refs_2_), channel_id=1, source_target_pairs={{0,2},{1,3},{2,0},{3,1},{4,6},{5,7},{6,4},{7,5},{8,10},{9,11},{10,... | collective-permute-start | bytes 393224 | tf_op jit(solution)/shard_map/ppermute | solution.py:288
  46.6 10.7 %collective-permute-start.15 = (bf16[8,64,128]{2,1,0:T(8,128)(2,1)S(1)}, bf16[8,64,128]{2,1,0:T(8,128)(2,1)S(1)}, u32[]{:S(2)}, u32[]{:S(2)}) collective-permute-start(bf16[8,64,128]{2,1,0:T(8,128)(2,1)S(1)} %get-tuple-element.42.refs_2_), channel_id=1, source_target_pairs={{0,1},{1,2},{2,3},{3,0},{4,5},{5,6},{6,7},{7,4},{8,9},{9,10},{10,1... | collective-permute-start | bytes 393224 | tf_op jit(solution)/shard_map/ppermute | solution.py:288
  49.4 4.2 %collective-permute-start.12 = (bf16[2,64,128]{2,1,0:T(8,128)(2,1)S(1)}, bf16[2,64,128]{2,1,0:T(8,128)(2,1)S(1)}, u32[]{:S(2)}, u32[]{:S(2)}) collective-permute-start(bf16[2,64,128]{2,1,0:T(8,128)(2,1)S(1)} %get-tuple-element.38), channel_id=1, source_target_pairs={{0,4},{4,8},{8,12},{1,5},{5,9},{9,13},{2,6},{6,10},{10,14},{3,7},{... | collective-permute-start | bytes 98312 | tf_op jit(solution)/shard_map/ppermute | solution.py:12
  52.1 4.7 %collective-permute-start.13 = (bf16[2,64,128]{2,1,0:T(8,128)(2,1)S(1)}, bf16[2,64,128]{2,1,0:T(8,128)(2,1)S(1)}, u32[]{:S(2)}, u32[]{:S(2)}) collective-permute-start(bf16[2,64,128]{2,1,0:T(8,128)(2,1)S(1)} %get-tuple-element.39), channel_id=1, source_target_pairs={{4,0},{8,4},{12,8},{5,1},{9,5},{13,9},{6,2},{10,6},{14,10},{7,3},{... | collective-permute-start | bytes 98312 | tf_op jit(solution)/shard_map/ppermute | solution.py:12
  59.9 4.3 %collective-permute-start.18 = (bf16[4,27,16,256]{3,2,1,0:T(8,128)(2,1)S(1)}, bf16[4,27,16,256]{3,2,1,0:T(8,128)(2,1)S(1)}, u32[]{:S(2)}, u32[]{:S(2)}) collective-permute-start(bf16[4,27,16,256]{3,2,1,0:T(8,128)(2,1)S(1)} %get-tuple-element.44), channel_id=1, source_target_pairs={{0,16},{16,0},{32,48},{48,32},{64,80},{80,64},{96,112},{112,96},{1... | collective-permute-start | bytes 2654216 | tf_op jit(solution)/shard_map/ppermute | solution.py:304
  62.2 8.2 %collective-permute-start.14 = (bf16[2,6,64,128]{3,2,1,0:T(8,128)(2,1)S(1)}, bf16[2,6,64,128]{3,2,1,0:T(8,128)(2,1)S(1)}, u32[]{:S(2)}, u32[]{:S(2)}) collective-permute-start(bf16[2,6,64,128]{3,2,1,0:T(8,128)(2,1)S(1)} %shard_map.73.refs_8_.refs_1_), channel_id=1, source_target_pairs={{16,0},{32,16},{48,32},{64,48},{80,64},{96,80},{112,96},{128,112},... | collective-permute-start | bytes 589832 | tf_op jit(solution)/shard_map/ppermute | solution.py:12
  64.7 7.8 %collective-permute-start.24 = (bf16[27,16,256]{2,1,0:T(8,128)(2,1)S(1)}, bf16[27,16,256]{2,1,0:T(8,128)(2,1)S(1)}, u32[]{:S(2)}, u32[]{:S(2)}) collective-permute-start(bf16[27,16,256]{2,1,0:T(8,128)(2,1)S(1)} %get-tuple-element.57), channel_id=1, source_target_pairs={{0,12},{4,0},{8,4},{12,8},{1,13},{5,1},{9,5},{13,9},{2,14},{6,2},{... | collective-permute-start | bytes 663560 | tf_op jit(solution)/shard_map/ppermute | solution.py:288
  64.8 8.3 %collective-permute-start.23 = (bf16[27,16,256]{2,1,0:T(8,128)(2,1)S(1)}, bf16[27,16,256]{2,1,0:T(8,128)(2,1)S(1)}, u32[]{:S(2)}, u32[]{:S(2)}) collective-permute-start(bf16[27,16,256]{2,1,0:T(8,128)(2,1)S(1)} %get-tuple-element.58), channel_id=1, source_target_pairs={{0,8},{4,12},{8,0},{12,4},{1,9},{5,13},{9,1},{13,5},{2,10},{6,14},... | collective-permute-start | bytes 663560 | tf_op jit(solution)/shard_map/ppermute | solution.py:288
  66.8 11.7 %collective-permute-start.22 = (bf16[27,16,256]{2,1,0:T(8,128)(2,1)S(1)}, bf16[27,16,256]{2,1,0:T(8,128)(2,1)S(1)}, u32[]{:S(2)}, u32[]{:S(2)}) collective-permute-start(bf16[27,16,256]{2,1,0:T(8,128)(2,1)S(1)} %get-tuple-element.59.refs_4_), channel_id=1, source_target_pairs={{0,4},{4,8},{8,12},{12,0},{1,5},{5,9},{9,13},{13,1},{2,6},{6,10},{... | collective-permute-start | bytes 663560 | tf_op jit(solution)/shard_map/ppermute | solution.py:288
  79.2 7.8 %collective-permute-start.25 = (bf16[27,8,128]{2,1,0:T(8,128)(2,1)S(1)}, bf16[27,8,128]{2,1,0:T(8,128)(2,1)S(1)}, u32[]{:S(2)}, u32[]{:S(2)}) collective-permute-start(bf16[27,8,128]{2,1,0:T(8,128)(2,1)S(1)} %get-tuple-element.50), channel_id=1, source_target_pairs={{0,32},{16,48},{32,64},{48,80},{64,96},{80,112},{96,0},{112,16},{1... | collective-permute-start | bytes 165896 | tf_op jit(solution)/shard_map/ppermute | solution.py:309
  81.9 8.1 %collective-permute-start.26 = (bf16[27,8,128]{2,1,0:T(8,128)(2,1)S(1)}, bf16[27,8,128]{2,1,0:T(8,128)(2,1)S(1)}, u32[]{:S(2)}, u32[]{:S(2)}) collective-permute-start(bf16[27,8,128]{2,1,0:T(8,128)(2,1)S(1)} %get-tuple-element.51), channel_id=1, source_target_pairs={{0,64},{16,80},{32,96},{48,112},{64,0},{80,16},{96,32},{112,48},{1... | collective-permute-start | bytes 165896 | tf_op jit(solution)/shard_map/ppermute | solution.py:309
  85.6 4.4 %collective-permute-start.27 = (bf16[27,8,128]{2,1,0:T(8,128)(2,1)S(1)}, bf16[27,8,128]{2,1,0:T(8,128)(2,1)S(1)}, u32[]{:S(2)}, u32[]{:S(2)}) collective-permute-start(bf16[27,8,128]{2,1,0:T(8,128)(2,1)S(1)} %get-tuple-element.52), channel_id=1, source_target_pairs={{0,96},{16,112},{32,0},{48,16},{64,32},{80,48},{96,64},{112,80},{1... | collective-permute-start | bytes 165896 | tf_op jit(solution)/shard_map/ppermute | solution.py:309
  90.1 8.4 %collective-permute-start.28 = (bf16[27,8,128]{2,1,0:T(8,128)(2,1)S(1)}, bf16[27,8,128]{2,1,0:T(8,128)(2,1)S(1)}, u32[]{:S(2)}, u32[]{:S(2)}) collective-permute-start(bf16[27,8,128]{2,1,0:T(8,128)(2,1)S(1)} %add_convert_fusion.2), channel_id=1, source_target_pairs={{0,128},{16,144},{32,160},{48,176},{64,192},{80,208},{96,224},{112... | collective-permute-start | bytes 165896 | tf_op jit(solution)/shard_map/ppermute | solution.py:304
  93.5 8.7 %collective-permute-start.19 = (bf16[8,64,128]{2,1,0:T(8,128)(2,1)S(1)}, bf16[8,64,128]{2,1,0:T(8,128)(2,1)S(1)}, u32[]{:S(2)}, u32[]{:S(2)}) collective-permute-start(bf16[8,64,128]{2,1,0:T(8,128)(2,1)S(1)} %get-tuple-element.46), channel_id=1, source_target_pairs={{0,1},{1,2},{2,3},{3,0},{4,5},{5,6},{6,7},{7,4},{8,9},{9,10},{10,1... | collective-permute-start | bytes 393224 | tf_op jit(solution)/shard_map/ppermute | solution.py:288
  94.8 7.4 %collective-permute-start.20 = (bf16[8,64,128]{2,1,0:T(8,128)(2,1)S(1)}, bf16[8,64,128]{2,1,0:T(8,128)(2,1)S(1)}, u32[]{:S(2)}, u32[]{:S(2)}) collective-permute-start(bf16[8,64,128]{2,1,0:T(8,128)(2,1)S(1)} %get-tuple-element.47), channel_id=1, source_target_pairs={{0,2},{1,3},{2,0},{3,1},{4,6},{5,7},{6,4},{7,5},{8,10},{9,11},{10,... | collective-permute-start | bytes 393224 | tf_op jit(solution)/shard_map/ppermute | solution.py:288
  97.2 5.0 %collective-permute-start.21 = (bf16[8,64,128]{2,1,0:T(8,128)(2,1)S(1)}, bf16[8,64,128]{2,1,0:T(8,128)(2,1)S(1)}, u32[]{:S(2)}, u32[]{:S(2)}) collective-permute-start(bf16[8,64,128]{2,1,0:T(8,128)(2,1)S(1)} %get-tuple-element.48), channel_id=1, source_target_pairs={{0,3},{1,0},{2,1},{3,2},{4,7},{5,4},{6,5},{7,6},{8,11},{9,8},{10,9... | collective-permute-start | bytes 393224 | tf_op jit(solution)/shard_map/ppermute | solution.py:288
  98.6 4.2 %collective-permute-start.31 = (bf16[27,8,128]{2,1,0:T(8,128)(2,1)S(1)}, bf16[27,8,128]{2,1,0:T(8,128)(2,1)S(1)}, u32[]{:S(2)}, u32[]{:S(2)}) collective-permute-start(bf16[27,8,128]{2,1,0:T(8,128)(2,1)S(1)} %add_convert_fusion.1.refs_1_), channel_id=1, source_target_pairs={{0,96},{16,112},{32,0},{48,16},{64,32},{80,48},{96,64},{112,80},{1... | collective-permute-start | bytes 165896 | tf_op jit(solution)/shard_map/ppermute | solution.py:309
  101.6 4.1 %collective-permute-start.30 = (bf16[27,8,128]{2,1,0:T(8,128)(2,1)S(1)}, bf16[27,8,128]{2,1,0:T(8,128)(2,1)S(1)}, u32[]{:S(2)}, u32[]{:S(2)}) collective-permute-start(bf16[27,8,128]{2,1,0:T(8,128)(2,1)S(1)} %add_convert_fusion.1.refs_1_), channel_id=1, source_target_pairs={{0,64},{16,80},{32,96},{48,112},{64,0},{80,16},{96,32},{112,48},{1... | collective-permute-start | bytes 165896 | tf_op jit(solution)/shard_map/ppermute | solution.py:309
  102.2 4.8 %collective-permute-start.29 = (bf16[27,8,128]{2,1,0:T(8,128)(2,1)S(1)}, bf16[27,8,128]{2,1,0:T(8,128)(2,1)S(1)}, u32[]{:S(2)}, u32[]{:S(2)}) collective-permute-start(bf16[27,8,128]{2,1,0:T(8,128)(2,1)S(1)} %add_convert_fusion.1.refs_1_), channel_id=1, source_target_pairs={{0,32},{16,48},{32,64},{48,80},{64,96},{80,112},{96,0},{112,16},{1... | collective-permute-start | bytes 165896 | tf_op jit(solution)/shard_map/ppermute | solution.py:309
  102.3 22.5 %copy-start.3 = (bf16[8,64,128]{2,1,0:T(8,128)(2,1)}, bf16[8,64,128]{2,1,0:T(8,128)(2,1)S(1)}, u32[]{:S(2)}) copy-start(bf16[8,64,128]{2,1,0:T(8,128)(2,1)S(1)} %add_convert_fusion) | copy-start | bytes 393220
  107.7 4.9 %collective-permute-start.34 = (bf16[27,16,256]{2,1,0:T(8,128)(2,1)S(1)}, bf16[27,16,256]{2,1,0:T(8,128)(2,1)S(1)}, u32[]{:S(2)}, u32[]{:S(2)}) collective-permute-start(bf16[27,16,256]{2,1,0:T(8,128)(2,1)S(1)} %shard_map.77.refs_1_), channel_id=1, source_target_pairs={{0,12},{4,0},{8,4},{12,8},{1,13},{5,1},{9,5},{13,9},{2,14},{6,2},{... | collective-permute-start | bytes 663560 | tf_op jit(solution)/shard_map/ppermute | solution.py:288
  107.8 6.4 %collective-permute-start.33 = (bf16[27,16,256]{2,1,0:T(8,128)(2,1)S(1)}, bf16[27,16,256]{2,1,0:T(8,128)(2,1)S(1)}, u32[]{:S(2)}, u32[]{:S(2)}) collective-permute-start(bf16[27,16,256]{2,1,0:T(8,128)(2,1)S(1)} %shard_map.77.refs_1_), channel_id=1, source_target_pairs={{0,8},{4,12},{8,0},{12,4},{1,9},{5,13},{9,1},{13,5},{2,10},{6,14},... | collective-permute-start | bytes 663560 | tf_op jit(solution)/shard_map/ppermute | solution.py:288
  109.8 7.1 %collective-permute-start.32 = (bf16[27,16,256]{2,1,0:T(8,128)(2,1)S(1)}, bf16[27,16,256]{2,1,0:T(8,128)(2,1)S(1)}, u32[]{:S(2)}, u32[]{:S(2)}) collective-permute-start(bf16[27,16,256]{2,1,0:T(8,128)(2,1)S(1)} %shard_map.77.refs_1_), channel_id=1, source_target_pairs={{0,4},{4,8},{8,12},{12,0},{1,5},{5,9},{9,13},{13,1},{2,6},{6,10},{... | collective-permute-start | bytes 663560 | tf_op jit(solution)/shard_map/ppermute | solution.py:288
  117.5 7.2 %collective-permute-start.35 = (bf16[27,64,256]{2,1,0:T(8,128)(2,1)S(1)}, bf16[27,64,256]{2,1,0:T(8,128)(2,1)S(1)}, u32[]{:S(2)}, u32[]{:S(2)}) collective-permute-start(bf16[27,64,256]{2,1,0:T(8,128)(2,1)S(1)} %shard_map.78), channel_id=1, source_target_pairs={{0,16},{16,0},{32,48},{48,32},{64,80},{80,64},{96,112},{112,96},{1... | collective-permute-start | bytes 2654216 | tf_op jit(solution)/shard_map/ppermute | solution.py:304

commit v7 on v6

--- a/solution.py
+++ b/solution.py
@@ -279,8 +279,8 @@
         out[:, pl.ds(at, 16), :] = part[...]
 
 
-def stacked(place, pieces):
-    return call(stacked_body, [shaped((27, 64, 256), jnp.bfloat16)], [], place, *pieces)[0]
+def stacked(place, pieces, after):
+    return call(stacked_body, [shaped((27, 64, 256), jnp.bfloat16)], [], place, *pieces, after=after)[0]
 
 
 def rotated(block, axis, distance):
@@ -323,8 +323,8 @@
     total = total.astype(jnp.bfloat16)
     gradient = gradient.reshape(2, 4, 64, 128).astype(jnp.bfloat16)
     total = (total.astype(jnp.float32) + swapped(total, 8).astype(jnp.float32)).astype(jnp.bfloat16)
-    total = rejoined(place, [total] + [quad_rotated(total, k) for k in range(1, 4)], [gradient])
-    total = stacked(place, [total] + all_rotated(total, "height"))
+    total = rejoined(place, [total] + [quad_rotated(total, k) for k in range(1, 4)], [])
+    total = stacked(place, [total] + all_rotated(total, "height"), [gradient])
     other = swapped(total, 1)
     one = jnp.where(core == 1, other, total).astype(jnp.float32)
     two = jnp.where(core == 1, total, other).astype(jnp.float32)

time: 127 us -> 129 us (1.016)
  starting transfers between devices: 65.7 us -> 67.1 us
  transfers between devices with their start and end apart: 36 -> 36, of which waited for: 17 -> 17; matrix products, arithmetic and copies ran while one was open for 1% -> 1% of each run, Pallas kernels for 8% -> 9%
where the time goes in v7:
time: 129 us
  starting transfers between devices  67.1 us (52%)
  waiting for transfers between devices  40.7 us (32%)
  Pallas kernels  15.3 us (12%)
  other arithmetic  2.89 us (2%)
  local copies, waits for them, and re-layouts  2.01 us (2%)
    ppermute x18, starting transfers between devices, rotated(): lax.ppermute(block, axis, [(i, (i + distance) % count) for i in range(cou...  22.2 us
    ppermute x9, starting transfers between devices, passed_along(): return lax.ppermute(block, axis, route)  21.9 us
    ppermute x18, waiting for transfers between devices, rotated(): lax.ppermute(block, axis, [(i, (i + distance) % count) for i in range(cou...  17 us
    pallas_call x12, Pallas kernels, call(): pl.pallas_call(lambda *refs: body(*refs[:used], *refs[rest:]), out_shape=...  15.3 us
    ppermute x9, waiting for transfers between devices, passed_along(): return lax.ppermute(block, axis, route)  12 us
    ppermute x3, starting transfers between devices, swapped(): lax.ppermute(block, 'tm', [(i, i ^ distance) for i in range(lax.axis_size...  11.6 us
    ppermute x6, starting transfers between devices, quad_rotated(): return lax.ppermute(block, 'tm', route)  11.5 us
    ppermute x6, waiting for transfers between devices, quad_rotated(): return lax.ppermute(block, 'tm', route)  9.45 us
  transfers between devices with their start and end apart: 36, of which 17 were waited for; matrix products, arithmetic and copies ran while one was open for 1% of the time, Pallas kernels for 9%

profile of v7, /device:TPU:1, one launch (start us, length us, event | category | flops | bytes accessed | tf_op | source)
XLA Modules:
  0.0 129.0 jit_solution(17183775573040948813)
XLA Ops:
  0.6 2.2 %collective-permute-start = (bf16[2,4,64,128]{3,2,1,0:T(8,128)(2,1)}, bf16[2,4,64,128]{3,2,1,0:T(8,128)(2,1)S(1)}, u32[]{:S(2)}, u32[]{:S(2)}) collective-permute-start(bf16[2,4,64,128]{3,2,1,0:T(8,128)(2,1)} %param.4), channel_id=1, source_target_pairs={{0,1},{1,2},{2,3},{3,0},{4,5},{5,6},{6,7},{7,4},{8,9},{9,10},{10,1... | collective-permute-start | bytes 393224 | tf_op jit(solution)/shard_map/ppermute | solution.py:288
  2.8 2.6 %collective-permute-start.1 = (bf16[2,4,64,128]{3,2,1,0:T(8,128)(2,1)}, bf16[2,4,64,128]{3,2,1,0:T(8,128)(2,1)S(1)}, u32[]{:S(2)}, u32[]{:S(2)}) collective-permute-start(bf16[2,4,64,128]{3,2,1,0:T(8,128)(2,1)} %param.4), channel_id=1, source_target_pairs={{0,2},{1,3},{2,0},{3,1},{4,6},{5,7},{6,4},{7,5},{8,10},{9,11},{10,... | collective-permute-start | bytes 393224 | tf_op jit(solution)/shard_map/ppermute | solution.py:288
  5.5 1.1 collective-permute-start.2
  6.5 0.9 constant_dynamic-update-slice_fusion.3
  7.5 3.8 %collective-permute-done.1 = bf16[2,4,64,128]{3,2,1,0:T(8,128)(2,1)S(1)} collective-permute-done((bf16[2,4,64,128]{3,2,1,0:T(8,128)(2,1)}, bf16[2,4,64,128]{3,2,1,0:T(8,128)(2,1)S(1)}, u32[]{:S(2)}, u32[]{:S(2)}) %collective-permute-start.1) | collective-permute-done | bytes 131104 | tf_op jit(solution)/shard_map/ppermute | solution.py:288
  11.4 5.0 %collective-permute-start.3 = (bf16[2,4,256,128]{3,2,1,0:T(8,128)(2,1)S(1)}, bf16[2,4,256,128]{3,2,1,0:T(8,128)(2,1)S(1)}, u32[]{:S(2)}, u32[]{:S(2)}) collective-permute-start(bf16[2,4,256,128]{3,2,1,0:T(8,128)(2,1)S(1)} %constant_dynamic-update-slice_fusion.refs_2_.refs_1_), channel_id=1, source_target_pairs={{0,16},{16,32},{32,48},{48,64},{64,80},{80,96},{96,112},{112,128},... | collective-permute-start | bytes 1572872 | tf_op jit(solution)/shard_map/ppermute | solution.py:12
  16.5 0.9 copy-done.2
  17.4 0.5 shard_map.68
  18.0 3.1 %collective-permute-start.6 = (bf16[2,64,128]{2,1,0:T(8,128)(2,1)S(1)}, bf16[2,64,128]{2,1,0:T(8,128)(2,1)S(1)}, u32[]{:S(2)}, u32[]{:S(2)}) collective-permute-start(bf16[2,64,128]{2,1,0:T(8,128)(2,1)S(1)} %get-tuple-element.30), channel_id=1, source_target_pairs={{0,4},{4,8},{8,12},{1,5},{5,9},{9,13},{2,6},{6,10},{10,14},{3,7},{... | collective-permute-start | bytes 98312 | tf_op jit(solution)/shard_map/ppermute | solution.py:12
  21.1 1.3 %collective-permute-start.7 = (bf16[2,64,128]{2,1,0:T(8,128)(2,1)S(1)}, bf16[2,64,128]{2,1,0:T(8,128)(2,1)S(1)}, u32[]{:S(2)}, u32[]{:S(2)}) collective-permute-start(bf16[2,64,128]{2,1,0:T(8,128)(2,1)S(1)} %get-tuple-element.31), channel_id=1, source_target_pairs={{4,0},{8,4},{12,8},{5,1},{9,5},{13,9},{6,2},{10,6},{14,10},{7,3},{... | collective-permute-start | bytes 98312 | tf_op jit(solution)/shard_map/ppermute | solution.py:12
  22.4 3.3 %collective-permute-done.7.refs_2_ = bf16[2,64,128]{2,1,0:T(8,128)(2,1)S(1)} collective-permute-done((bf16[2,64,128]{2,1,0:T(8,128)(2,1)S(1)}, bf16[2,64,128]{2,1,0:T(8,128)(2,1)S(1)}, u32[]{:S(2)}, u32[]{:S(2)}) %collective-permute-start.7) | collective-permute-done | bytes 32800 | tf_op jit(solution)/shard_map/ppermute | solution.py:12
  25.8 0.6 shard_map.69.refs_1_.refs_6_
  26.3 1.9 %collective-permute-start.8 = (bf16[2,6,64,128]{3,2,1,0:T(8,128)(2,1)S(1)}, bf16[2,6,64,128]{3,2,1,0:T(8,128)(2,1)S(1)}, u32[]{:S(2)}, u32[]{:S(2)}) collective-permute-start(bf16[2,6,64,128]{3,2,1,0:T(8,128)(2,1)S(1)} %shard_map.69.refs_1_.refs_6_), channel_id=1, source_target_pairs={{16,0},{32,16},{48,32},{64,48},{80,64},{96,80},{112,96},{128,112},... | collective-permute-start | bytes 589832 | tf_op jit(solution)/shard_map/ppermute | solution.py:12
  28.3 0.6 shard_map.67
  28.9 3.1 %collective-permute-start.4 = (bf16[4,256,128]{2,1,0:T(8,128)(2,1)S(1)}, bf16[4,256,128]{2,1,0:T(8,128)(2,1)S(1)}, u32[]{:S(2)}, u32[]{:S(2)}) collective-permute-start(bf16[4,256,128]{2,1,0:T(8,128)(2,1)S(1)} %get-tuple-element.28), channel_id=1, source_target_pairs={{0,4},{4,8},{8,12},{1,5},{5,9},{9,13},{2,6},{6,10},{10,14},{3,7},{... | collective-permute-start | bytes 786440 | tf_op jit(solution)/shard_map/ppermute | solution.py:12
  32.0 1.3 %collective-permute-start.5 = (bf16[4,256,128]{2,1,0:T(8,128)(2,1)S(1)}, bf16[4,256,128]{2,1,0:T(8,128)(2,1)S(1)}, u32[]{:S(2)}, u32[]{:S(2)}) collective-permute-start(bf16[4,256,128]{2,1,0:T(8,128)(2,1)S(1)} %get-tuple-element.29), channel_id=1, source_target_pairs={{4,0},{8,4},{12,8},{5,1},{9,5},{13,9},{6,2},{10,6},{14,10},{7,3},{... | collective-permute-start | bytes 786440 | tf_op jit(solution)/shard_map/ppermute | solution.py:12
  33.3 2.0 %shard_map.70 = (f32[8,64,128]{2,1,0:T(8,128)S(1)}, bf16[8,64,128]{2,1,0:T(8,128)(2,1)S(1)}, bf16[8,64,128]{2,1,0:T(8,128)(2,1)S(1)}, bf16[8,64,128]{2,1,0:T(8,128)(2,1)S(1)}) custom-call(s32[4]{0:T(128)S(1)} %pad_add_fusion.refs_0_, bf16[2,6,64,128]{3,2,1,0:T(8,128)(2,1)S(1)} %shard_map.69.refs_1_.refs_6_, ...), custom_call_target="tpu_custom_call" | custom-call | tf_op jit(solution)/shard_map/pallas_call | solution.py:24
  35.4 1.0 collective-permute-start.9
  36.4 2.1 %collective-permute-start.10 = (bf16[8,64,128]{2,1,0:T(8,128)(2,1)S(1)}, bf16[8,64,128]{2,1,0:T(8,128)(2,1)S(1)}, u32[]{:S(2)}, u32[]{:S(2)}) collective-permute-start(bf16[8,64,128]{2,1,0:T(8,128)(2,1)S(1)} %get-tuple-element.36), channel_id=1, source_target_pairs={{0,2},{1,3},{2,0},{3,1},{4,6},{5,7},{6,4},{7,5},{8,10},{9,11},{10,... | collective-permute-start | bytes 393224 | tf_op jit(solution)/shard_map/ppermute | solution.py:288
  38.5 1.3 %collective-permute-start.11 = (bf16[8,64,128]{2,1,0:T(8,128)(2,1)S(1)}, bf16[8,64,128]{2,1,0:T(8,128)(2,1)S(1)}, u32[]{:S(2)}, u32[]{:S(2)}) collective-permute-start(bf16[8,64,128]{2,1,0:T(8,128)(2,1)S(1)} %get-tuple-element.37), channel_id=1, source_target_pairs={{0,3},{1,0},{2,1},{3,2},{4,7},{5,4},{6,5},{7,6},{8,11},{9,8},{10,9... | collective-permute-start | bytes 393224 | tf_op jit(solution)/shard_map/ppermute | solution.py:288
  39.8 1.9 %collective-permute-done.5.refs_4_ = bf16[4,256,128]{2,1,0:T(8,128)(2,1)S(1)} collective-permute-done((bf16[4,256,128]{2,1,0:T(8,128)(2,1)S(1)}, bf16[4,256,128]{2,1,0:T(8,128)(2,1)S(1)}, u32[]{:S(2)}, u32[]{:S(2)}) %collective-permute-start.5) | collective-permute-done | bytes 262176 | tf_op jit(solution)/shard_map/ppermute | solution.py:12
  41.7 2.2 %shard_map.71 = (bf16[24,256,128]{2,1,0:T(8,128)(2,1)S(1)}, f32[8,64,128]{2,1,0:T(8,128)S(1)}, bf16[8,64,128]{2,1,0:T(8,128)(2,1)S(1)}) custom-call(s32[4]{0:T(128)S(1)} %pad_add_fusion.refs_0_, bf16[2,4,256,128]{3,2,1,0:T(8,128)(2,1)S(1)} %constant_dynamic-update-slice_fusion.refs_2_.refs_1_, ...), custom_call_target="tpu_custom_call" | custom-call | tf_op jit(solution)/shard_map/pallas_call | solution.py:24
  43.9 1.9 %collective-permute-start.17 = (bf16[8,64,128]{2,1,0:T(8,128)(2,1)S(1)}, bf16[8,64,128]{2,1,0:T(8,128)(2,1)S(1)}, u32[]{:S(2)}, u32[]{:S(2)}) collective-permute-start(bf16[8,64,128]{2,1,0:T(8,128)(2,1)S(1)} %get-tuple-element.42.refs_2_), channel_id=1, source_target_pairs={{0,3},{1,0},{2,1},{3,2},{4,7},{5,4},{6,5},{7,6},{8,11},{9,8},{10,9... | collective-permute-start | bytes 393224 | tf_op jit(solution)/shard_map/ppermute | solution.py:288
  45.8 0.9 collective-permute-start.16
  46.6 0.4 collective-permute-start.15
  47.1 2.3 %shard_map.72 = (bf16[2,4,64,128]{3,2,1,0:T(8,128)(2,1)S(1)}, bf16[2,64,128]{2,1,0:T(8,128)(2,1)S(1)}, bf16[2,64,128]{2,1,0:T(8,128)(2,1)S(1)}, bf16[4,27,16,256]{3,2,1,0:T(8,128)(2,1)S(1)}) custom-call(s32[4]{0:T(128)S(1)} %pad_add_fusion.refs_0_, bf16[24,256,128]{2,1,0:T(8,128)(2,1)S(1)} %get-tuple-element.33.refs_1_, ...), custom_call_target="tpu_custom_call" | custom-call | tf_op jit(solution)/shard_map/pallas_call | solution.py:24
  49.4 2.7 %collective-permute-start.12 = (bf16[2,64,128]{2,1,0:T(8,128)(2,1)S(1)}, bf16[2,64,128]{2,1,0:T(8,128)(2,1)S(1)}, u32[]{:S(2)}, u32[]{:S(2)}) collective-permute-start(bf16[2,64,128]{2,1,0:T(8,128)(2,1)S(1)} %get-tuple-element.38), channel_id=1, source_target_pairs={{0,4},{4,8},{8,12},{1,5},{5,9},{9,13},{2,6},{6,10},{10,14},{3,7},{... | collective-permute-start | bytes 98312 | tf_op jit(solution)/shard_map/ppermute | solution.py:12
  52.1 1.5 %collective-permute-start.13 = (bf16[2,64,128]{2,1,0:T(8,128)(2,1)S(1)}, bf16[2,64,128]{2,1,0:T(8,128)(2,1)S(1)}, u32[]{:S(2)}, u32[]{:S(2)}) collective-permute-start(bf16[2,64,128]{2,1,0:T(8,128)(2,1)S(1)} %get-tuple-element.39), channel_id=1, source_target_pairs={{4,0},{8,4},{12,8},{5,1},{9,5},{13,9},{6,2},{10,6},{14,10},{7,3},{... | collective-permute-start | bytes 98312 | tf_op jit(solution)/shard_map/ppermute | solution.py:12
  53.6 3.2 %collective-permute-done.13.refs_2_ = bf16[2,64,128]{2,1,0:T(8,128)(2,1)S(1)} collective-permute-done((bf16[2,64,128]{2,1,0:T(8,128)(2,1)S(1)}, bf16[2,64,128]{2,1,0:T(8,128)(2,1)S(1)}, u32[]{:S(2)}, u32[]{:S(2)}) %collective-permute-start.13) | collective-permute-done | bytes 32800 | tf_op jit(solution)/shard_map/ppermute | solution.py:12
  56.8 0.6 shard_map.73.refs_8_.refs_1_
  57.3 2.6 %shard_map.74 = (bf16[4,27,16,256]{3,2,1,0:T(8,128)(2,1)S(1)}, bf16[4,27,16,256]{3,2,1,0:T(8,128)(2,1)S(1)}) custom-call(s32[4]{0:T(128)S(1)} %pad_add_fusion.refs_0_, bf16[4,27,16,256]{3,2,1,0:T(8,128)(2,1)S(1)} %get-tuple-element.41.refs_1_, bf16[8,64,128]{2,1,0:T(8,128)(2,1)S(1)} %get-tuple-element.42.refs_2_, ...), custom_call_target="tpu_custom_call" | custom-call | tf_op jit(solution)/shard_map/pallas_call | solution.py:24
  59.9 2.3 %collective-permute-start.18 = (bf16[4,27,16,256]{3,2,1,0:T(8,128)(2,1)S(1)}, bf16[4,27,16,256]{3,2,1,0:T(8,128)(2,1)S(1)}, u32[]{:S(2)}, u32[]{:S(2)}) collective-permute-start(bf16[4,27,16,256]{3,2,1,0:T(8,128)(2,1)S(1)} %get-tuple-element.44), channel_id=1, source_target_pairs={{0,16},{16,0},{32,48},{48,32},{64,80},{80,64},{96,112},{112,96},{1... | collective-permute-start | bytes 2654216 | tf_op jit(solution)/shard_map/ppermute | solution.py:304
  62.2 1.9 %collective-permute-start.14 = (bf16[2,6,64,128]{3,2,1,0:T(8,128)(2,1)S(1)}, bf16[2,6,64,128]{3,2,1,0:T(8,128)(2,1)S(1)}, u32[]{:S(2)}, u32[]{:S(2)}) collective-permute-start(bf16[2,6,64,128]{3,2,1,0:T(8,128)(2,1)S(1)} %shard_map.73.refs_8_.refs_1_), channel_id=1, source_target_pairs={{16,0},{32,16},{48,32},{64,48},{80,64},{96,80},{112,96},{128,112},... | collective-permute-start | bytes 589832 | tf_op jit(solution)/shard_map/ppermute | solution.py:12
  64.2 0.1 collective-permute-done.18
  64.3 0.3 convert_add_fusion
  64.8 2.0 %collective-permute-start.23 = (bf16[27,16,256]{2,1,0:T(8,128)(2,1)S(1)}, bf16[27,16,256]{2,1,0:T(8,128)(2,1)S(1)}, u32[]{:S(2)}, u32[]{:S(2)}) collective-permute-start(bf16[27,16,256]{2,1,0:T(8,128)(2,1)S(1)} %get-tuple-element.58), channel_id=1, source_target_pairs={{0,8},{4,12},{8,0},{12,4},{1,9},{5,13},{9,1},{13,5},{2,10},{6,14},... | collective-permute-start | bytes 663560 | tf_op jit(solution)/shard_map/ppermute | solution.py:288
  66.8 3.6 %collective-permute-done.14.refs_2_ = bf16[2,6,64,128]{3,2,1,0:T(8,128)(2,1)S(1)} collective-permute-done((bf16[2,6,64,128]{3,2,1,0:T(8,128)(2,1)S(1)}, bf16[2,6,64,128]{3,2,1,0:T(8,128)(2,1)S(1)}, u32[]{:S(2)}, u32[]{:S(2)}) %collective-permute-start.14) | collective-permute-done | bytes 196640 | tf_op jit(solution)/shard_map/ppermute | solution.py:12
  70.4 2.0 %shard_map.75 = (f32[8,64,128]{2,1,0:T(8,128)S(1)}, bf16[8,64,128]{2,1,0:T(8,128)(2,1)S(1)}, bf16[8,64,128]{2,1,0:T(8,128)(2,1)S(1)}, bf16[8,64,128]{2,1,0:T(8,128)(2,1)S(1)}) custom-call(s32[4]{0:T(128)S(1)} %pad_add_fusion.refs_0_, bf16[2,6,64,128]{3,2,1,0:T(8,128)(2,1)S(1)} %shard_map.73.refs_8_.refs_1_, ...), custom_call_target="tpu_custom_call" | custom-call | tf_op jit(solution)/shard_map/pallas_call | solution.py:24
  72.5 0.6 collective-permute-done.23.refs_3_
  73.1 5.4 %collective-permute-done.22.refs_2_ = bf16[27,16,256]{2,1,0:T(8,128)(2,1)S(1)} collective-permute-done((bf16[27,16,256]{2,1,0:T(8,128)(2,1)S(1)}, bf16[27,16,256]{2,1,0:T(8,128)(2,1)S(1)}, u32[]{:S(2)}, u32[]{:S(2)}) %collective-permute-start.22) | collective-permute-done | bytes 221216 | tf_op jit(solution)/shard_map/ppermute | solution.py:288
  78.5 0.7 shard_map.76
  79.2 2.8 %collective-permute-start.25 = (bf16[27,8,128]{2,1,0:T(8,128)(2,1)S(1)}, bf16[27,8,128]{2,1,0:T(8,128)(2,1)S(1)}, u32[]{:S(2)}, u32[]{:S(2)}) collective-permute-start(bf16[27,8,128]{2,1,0:T(8,128)(2,1)S(1)} %get-tuple-element.50), channel_id=1, source_target_pairs={{0,32},{16,48},{32,64},{48,80},{64,96},{80,112},{96,0},{112,16},{1... | collective-permute-start | bytes 165896 | tf_op jit(solution)/shard_map/ppermute | solution.py:309
  82.0 3.7 %collective-permute-start.26 = (bf16[27,8,128]{2,1,0:T(8,128)(2,1)S(1)}, bf16[27,8,128]{2,1,0:T(8,128)(2,1)S(1)}, u32[]{:S(2)}, u32[]{:S(2)}) collective-permute-start(bf16[27,8,128]{2,1,0:T(8,128)(2,1)S(1)} %get-tuple-element.51), channel_id=1, source_target_pairs={{0,64},{16,80},{32,96},{48,112},{64,0},{80,16},{96,32},{112,48},{1... | collective-permute-start | bytes 165896 | tf_op jit(solution)/shard_map/ppermute | solution.py:309
  85.7 1.3 collective-permute-done.25
  86.9 3.1 %collective-permute-done.26 = bf16[27,8,128]{2,1,0:T(8,128)(2,1)S(1)} collective-permute-done((bf16[27,8,128]{2,1,0:T(8,128)(2,1)S(1)}, bf16[27,8,128]{2,1,0:T(8,128)(2,1)S(1)}, u32[]{:S(2)}, u32[]{:S(2)}) %collective-permute-start.26) | collective-permute-done | bytes 55328 | tf_op jit(solution)/shard_map/ppermute | solution.py:309
  90.1 3.4 %collective-permute-start.28 = (bf16[27,8,128]{2,1,0:T(8,128)(2,1)S(1)}, bf16[27,8,128]{2,1,0:T(8,128)(2,1)S(1)}, u32[]{:S(2)}, u32[]{:S(2)}) collective-permute-start(bf16[27,8,128]{2,1,0:T(8,128)(2,1)S(1)} %add_convert_fusion.2), channel_id=1, source_target_pairs={{0,128},{16,144},{32,160},{48,176},{64,192},{80,208},{96,224},{112... | collective-permute-start | bytes 165896 | tf_op jit(solution)/shard_map/ppermute | solution.py:304
  93.5 1.3 %collective-permute-start.19 = (bf16[8,64,128]{2,1,0:T(8,128)(2,1)S(1)}, bf16[8,64,128]{2,1,0:T(8,128)(2,1)S(1)}, u32[]{:S(2)}, u32[]{:S(2)}) collective-permute-start(bf16[8,64,128]{2,1,0:T(8,128)(2,1)S(1)} %get-tuple-element.46), channel_id=1, source_target_pairs={{0,1},{1,2},{2,3},{3,0},{4,5},{5,6},{6,7},{7,4},{8,9},{9,10},{10,1... | collective-permute-start | bytes 393224 | tf_op jit(solution)/shard_map/ppermute | solution.py:288
  94.8 2.4 %collective-permute-start.20 = (bf16[8,64,128]{2,1,0:T(8,128)(2,1)S(1)}, bf16[8,64,128]{2,1,0:T(8,128)(2,1)S(1)}, u32[]{:S(2)}, u32[]{:S(2)}) collective-permute-start(bf16[8,64,128]{2,1,0:T(8,128)(2,1)S(1)} %get-tuple-element.47), channel_id=1, source_target_pairs={{0,2},{1,3},{2,0},{3,1},{4,6},{5,7},{6,4},{7,5},{8,10},{9,11},{10,... | collective-permute-start | bytes 393224 | tf_op jit(solution)/shard_map/ppermute | solution.py:288
  97.2 1.3 %collective-permute-start.21 = (bf16[8,64,128]{2,1,0:T(8,128)(2,1)S(1)}, bf16[8,64,128]{2,1,0:T(8,128)(2,1)S(1)}, u32[]{:S(2)}, u32[]{:S(2)}) collective-permute-start(bf16[8,64,128]{2,1,0:T(8,128)(2,1)S(1)} %get-tuple-element.48), channel_id=1, source_target_pairs={{0,3},{1,0},{2,1},{3,2},{4,7},{5,4},{6,5},{7,6},{8,11},{9,8},{10,9... | collective-permute-start | bytes 393224 | tf_op jit(solution)/shard_map/ppermute | solution.py:288
  98.6 3.0 %collective-permute-start.31 = (bf16[27,8,128]{2,1,0:T(8,128)(2,1)S(1)}, bf16[27,8,128]{2,1,0:T(8,128)(2,1)S(1)}, u32[]{:S(2)}, u32[]{:S(2)}) collective-permute-start(bf16[27,8,128]{2,1,0:T(8,128)(2,1)S(1)} %add_convert_fusion.1.refs_1_), channel_id=1, source_target_pairs={{0,96},{16,112},{32,0},{48,16},{64,32},{80,48},{96,64},{112,80},{1... | collective-permute-start | bytes 165896 | tf_op jit(solution)/shard_map/ppermute | solution.py:309
  101.6 0.7 collective-permute-start.30
  102.2 0.5 collective-permute-done.31.refs_4_
  102.8 1.3 collective-permute-start.29
  104.1 1.6 %collective-permute-done.30.refs_3_ = bf16[27,8,128]{2,1,0:T(8,128)(2,1)S(1)} collective-permute-done((bf16[27,8,128]{2,1,0:T(8,128)(2,1)S(1)}, bf16[27,8,128]{2,1,0:T(8,128)(2,1)S(1)}, u32[]{:S(2)}, u32[]{:S(2)}) %collective-permute-start.30) | collective-permute-done | bytes 55328 | tf_op jit(solution)/shard_map/ppermute | solution.py:309
  105.7 2.9 %collective-permute-done.29.refs_2_ = bf16[27,8,128]{2,1,0:T(8,128)(2,1)S(1)} collective-permute-done((bf16[27,8,128]{2,1,0:T(8,128)(2,1)S(1)}, bf16[27,8,128]{2,1,0:T(8,128)(2,1)S(1)}, u32[]{:S(2)}, u32[]{:S(2)}) %collective-permute-start.29) | collective-permute-done | bytes 55328 | tf_op jit(solution)/shard_map/ppermute | solution.py:309
  108.6 0.6 shard_map.77.refs_1_
  109.3 1.4 %collective-permute-start.33 = (bf16[27,16,256]{2,1,0:T(8,128)(2,1)S(1)}, bf16[27,16,256]{2,1,0:T(8,128)(2,1)S(1)}, u32[]{:S(2)}, u32[]{:S(2)}) collective-permute-start(bf16[27,16,256]{2,1,0:T(8,128)(2,1)S(1)} %shard_map.77.refs_1_), channel_id=1, source_target_pairs={{0,8},{4,12},{8,0},{12,4},{1,9},{5,13},{9,1},{13,5},{2,10},{6,14},... | collective-permute-start | bytes 663560 | tf_op jit(solution)/shard_map/ppermute | solution.py:288
  110.8 3.2 %collective-permute-done.34.refs_4_ = bf16[27,16,256]{2,1,0:T(8,128)(2,1)S(1)} collective-permute-done((bf16[27,16,256]{2,1,0:T(8,128)(2,1)S(1)}, bf16[27,16,256]{2,1,0:T(8,128)(2,1)S(1)}, u32[]{:S(2)}, u32[]{:S(2)}) %collective-permute-start.34) | collective-permute-done | bytes 221216 | tf_op jit(solution)/shard_map/ppermute | solution.py:288
  114.1 1.7 %collective-permute-done.33.refs_3_ = bf16[27,16,256]{2,1,0:T(8,128)(2,1)S(1)} collective-permute-done((bf16[27,16,256]{2,1,0:T(8,128)(2,1)S(1)}, bf16[27,16,256]{2,1,0:T(8,128)(2,1)S(1)}, u32[]{:S(2)}, u32[]{:S(2)}) %collective-permute-start.33) | collective-permute-done | bytes 221216 | tf_op jit(solution)/shard_map/ppermute | solution.py:288
  115.8 2.3 %collective-permute-done.32.refs_2_ = bf16[27,16,256]{2,1,0:T(8,128)(2,1)S(1)} collective-permute-done((bf16[27,16,256]{2,1,0:T(8,128)(2,1)S(1)}, bf16[27,16,256]{2,1,0:T(8,128)(2,1)S(1)}, u32[]{:S(2)}, u32[]{:S(2)}) %collective-permute-start.32) | collective-permute-done | bytes 221216 | tf_op jit(solution)/shard_map/ppermute | solution.py:288
  118.0 0.6 shard_map.78
  118.6 5.9 %collective-permute-start.35 = (bf16[27,64,256]{2,1,0:T(8,128)(2,1)S(1)}, bf16[27,64,256]{2,1,0:T(8,128)(2,1)S(1)}, u32[]{:S(2)}, u32[]{:S(2)}) collective-permute-start(bf16[27,64,256]{2,1,0:T(8,128)(2,1)S(1)} %shard_map.78), channel_id=1, source_target_pairs={{0,16},{16,0},{32,48},{48,32},{64,80},{80,64},{96,112},{112,96},{1... | collective-permute-start | bytes 2654216 | tf_op jit(solution)/shard_map/ppermute | solution.py:304
  124.5 2.1 %collective-permute-done.35 = bf16[27,64,256]{2,1,0:T(8,128)(2,1)S(1)} collective-permute-done((bf16[27,64,256]{2,1,0:T(8,128)(2,1)S(1)}, bf16[27,64,256]{2,1,0:T(8,128)(2,1)S(1)}, u32[]{:S(2)}, u32[]{:S(2)}) %collective-permute-start.35) | collective-permute-done | bytes 884768 | tf_op jit(solution)/shard_map/ppermute | solution.py:304
  126.7 2.2 %convert_bitcast_fusion = (f32[64,3,3,3,256]{4,0,3,2,1:T(8,128)}, f32[64,3,3,3,256]{4,0,3,2,1:T(8,128)}) fusion(bf16[3,3,3,64,256]{4,3,2,1,0:T(8,128)(2,1)S(1)} %bitcast.34, bf16[3,3,3,64,256]{4,3,2,1,0:T(8,128)(2,1)S(1)} %bitcast.35), kind=kLoop, calls=%fused_computation | loop fusion | flops 884736 | bytes 5308416 | tf_op jit(solution)/shard_map/transpose | solution.py:335
  (41 shorter events, 0.8 us)
Async XLA Ops:
  0.6 32.7 %copy-start.1 = (bf16[64,3,3,3,256]{4,0,3,2,1:T(8,128)(2,1)S(1)}, bf16[64,3,3,3,256]{4,0,3,2,1:T(8,128)(2,1)}, u32[]{:S(2)}) copy-start(bf16[64,3,3,3,256]{4,0,3,2,1:T(8,128)(2,1)} %param.7) | copy-start | bytes 2654212
  0.6 6.8 %collective-permute-start = (bf16[2,4,64,128]{3,2,1,0:T(8,128)(2,1)}, bf16[2,4,64,128]{3,2,1,0:T(8,128)(2,1)S(1)}, u32[]{:S(2)}, u32[]{:S(2)}) collective-permute-start(bf16[2,4,64,128]{3,2,1,0:T(8,128)(2,1)} %param.4), channel_id=1, source_target_pairs={{0,1},{1,2},{2,3},{3,0},{4,5},{5,6},{6,7},{7,4},{8,9},{9,10},{10,1... | collective-permute-start | bytes 393224 | tf_op jit(solution)/shard_map/ppermute | solution.py:288
  2.8 8.5 %collective-permute-start.1 = (bf16[2,4,64,128]{3,2,1,0:T(8,128)(2,1)}, bf16[2,4,64,128]{3,2,1,0:T(8,128)(2,1)S(1)}, u32[]{:S(2)}, u32[]{:S(2)}) collective-permute-start(bf16[2,4,64,128]{3,2,1,0:T(8,128)(2,1)} %param.4), channel_id=1, source_target_pairs={{0,2},{1,3},{2,0},{3,1},{4,6},{5,7},{6,4},{7,5},{8,10},{9,11},{10,... | collective-permute-start | bytes 393224 | tf_op jit(solution)/shard_map/ppermute | solution.py:288
  5.5 5.9 %collective-permute-start.2 = (bf16[2,4,64,128]{3,2,1,0:T(8,128)(2,1)}, bf16[2,4,64,128]{3,2,1,0:T(8,128)(2,1)S(1)}, u32[]{:S(2)}, u32[]{:S(2)}) collective-permute-start(bf16[2,4,64,128]{3,2,1,0:T(8,128)(2,1)} %param.4), channel_id=1, source_target_pairs={{0,3},{1,0},{2,1},{3,2},{4,7},{5,4},{6,5},{7,6},{8,11},{9,8},{10,9... | collective-permute-start | bytes 393224 | tf_op jit(solution)/shard_map/ppermute | solution.py:288
  7.5 34.1 %copy-start = (bf16[64,3,3,3,256]{4,0,3,2,1:T(8,128)(2,1)S(1)}, bf16[64,3,3,3,256]{4,0,3,2,1:T(8,128)(2,1)}, u32[]{:S(2)}) copy-start(bf16[64,3,3,3,256]{4,0,3,2,1:T(8,128)(2,1)} %param.6) | copy-start | bytes 2654212
  11.4 16.8 %collective-permute-start.3 = (bf16[2,4,256,128]{3,2,1,0:T(8,128)(2,1)S(1)}, bf16[2,4,256,128]{3,2,1,0:T(8,128)(2,1)S(1)}, u32[]{:S(2)}, u32[]{:S(2)}) collective-permute-start(bf16[2,4,256,128]{3,2,1,0:T(8,128)(2,1)S(1)} %constant_dynamic-update-slice_fusion.refs_2_.refs_1_), channel_id=1, source_target_pairs={{0,16},{16,32},{32,48},{48,64},{64,80},{80,96},{96,112},{112,128},... | collective-permute-start | bytes 1572872 | tf_op jit(solution)/shard_map/ppermute | solution.py:12
  16.5 0.9 copy-start.2
  18.0 4.4 %collective-permute-start.6 = (bf16[2,64,128]{2,1,0:T(8,128)(2,1)S(1)}, bf16[2,64,128]{2,1,0:T(8,128)(2,1)S(1)}, u32[]{:S(2)}, u32[]{:S(2)}) collective-permute-start(bf16[2,64,128]{2,1,0:T(8,128)(2,1)S(1)} %get-tuple-element.30), channel_id=1, source_target_pairs={{0,4},{4,8},{8,12},{1,5},{5,9},{9,13},{2,6},{6,10},{10,14},{3,7},{... | collective-permute-start | bytes 98312 | tf_op jit(solution)/shard_map/ppermute | solution.py:12
  21.1 4.7 %collective-permute-start.7 = (bf16[2,64,128]{2,1,0:T(8,128)(2,1)S(1)}, bf16[2,64,128]{2,1,0:T(8,128)(2,1)S(1)}, u32[]{:S(2)}, u32[]{:S(2)}) collective-permute-start(bf16[2,64,128]{2,1,0:T(8,128)(2,1)S(1)} %get-tuple-element.31), channel_id=1, source_target_pairs={{4,0},{8,4},{12,8},{5,1},{9,5},{13,9},{6,2},{10,6},{14,10},{7,3},{... | collective-permute-start | bytes 98312 | tf_op jit(solution)/shard_map/ppermute | solution.py:12
  26.3 7.0 %collective-permute-start.8 = (bf16[2,6,64,128]{3,2,1,0:T(8,128)(2,1)S(1)}, bf16[2,6,64,128]{3,2,1,0:T(8,128)(2,1)S(1)}, u32[]{:S(2)}, u32[]{:S(2)}) collective-permute-start(bf16[2,6,64,128]{3,2,1,0:T(8,128)(2,1)S(1)} %shard_map.69.refs_1_.refs_6_), channel_id=1, source_target_pairs={{16,0},{32,16},{48,32},{64,48},{80,64},{96,80},{112,96},{128,112},... | collective-permute-start | bytes 589832 | tf_op jit(solution)/shard_map/ppermute | solution.py:12
  28.9 10.9 %collective-permute-start.4 = (bf16[4,256,128]{2,1,0:T(8,128)(2,1)S(1)}, bf16[4,256,128]{2,1,0:T(8,128)(2,1)S(1)}, u32[]{:S(2)}, u32[]{:S(2)}) collective-permute-start(bf16[4,256,128]{2,1,0:T(8,128)(2,1)S(1)} %get-tuple-element.28), channel_id=1, source_target_pairs={{0,4},{4,8},{8,12},{1,5},{5,9},{9,13},{2,6},{6,10},{10,14},{3,7},{... | collective-permute-start | bytes 786440 | tf_op jit(solution)/shard_map/ppermute | solution.py:12
  32.0 9.7 %collective-permute-start.5 = (bf16[4,256,128]{2,1,0:T(8,128)(2,1)S(1)}, bf16[4,256,128]{2,1,0:T(8,128)(2,1)S(1)}, u32[]{:S(2)}, u32[]{:S(2)}) collective-permute-start(bf16[4,256,128]{2,1,0:T(8,128)(2,1)S(1)} %get-tuple-element.29), channel_id=1, source_target_pairs={{4,0},{8,4},{12,8},{5,1},{9,5},{13,9},{6,2},{10,6},{14,10},{7,3},{... | collective-permute-start | bytes 786440 | tf_op jit(solution)/shard_map/ppermute | solution.py:12
  35.4 11.3 %collective-permute-start.9 = (bf16[8,64,128]{2,1,0:T(8,128)(2,1)S(1)}, bf16[8,64,128]{2,1,0:T(8,128)(2,1)S(1)}, u32[]{:S(2)}, u32[]{:S(2)}) collective-permute-start(bf16[8,64,128]{2,1,0:T(8,128)(2,1)S(1)} %get-tuple-element.35), channel_id=1, source_target_pairs={{0,1},{1,2},{2,3},{3,0},{4,5},{5,6},{6,7},{7,4},{8,9},{9,10},{10,1... | collective-permute-start | bytes 393224 | tf_op jit(solution)/shard_map/ppermute | solution.py:288
  36.4 10.7 %collective-permute-start.10 = (bf16[8,64,128]{2,1,0:T(8,128)(2,1)S(1)}, bf16[8,64,128]{2,1,0:T(8,128)(2,1)S(1)}, u32[]{:S(2)}, u32[]{:S(2)}) collective-permute-start(bf16[8,64,128]{2,1,0:T(8,128)(2,1)S(1)} %get-tuple-element.36), channel_id=1, source_target_pairs={{0,2},{1,3},{2,0},{3,1},{4,6},{5,7},{6,4},{7,5},{8,10},{9,11},{10,... | collective-permute-start | bytes 393224 | tf_op jit(solution)/shard_map/ppermute | solution.py:288
  38.5 8.6 %collective-permute-start.11 = (bf16[8,64,128]{2,1,0:T(8,128)(2,1)S(1)}, bf16[8,64,128]{2,1,0:T(8,128)(2,1)S(1)}, u32[]{:S(2)}, u32[]{:S(2)}) collective-permute-start(bf16[8,64,128]{2,1,0:T(8,128)(2,1)S(1)} %get-tuple-element.37), channel_id=1, source_target_pairs={{0,3},{1,0},{2,1},{3,2},{4,7},{5,4},{6,5},{7,6},{8,11},{9,8},{10,9... | collective-permute-start | bytes 393224 | tf_op jit(solution)/shard_map/ppermute | solution.py:288
  43.9 13.5 %collective-permute-start.17 = (bf16[8,64,128]{2,1,0:T(8,128)(2,1)S(1)}, bf16[8,64,128]{2,1,0:T(8,128)(2,1)S(1)}, u32[]{:S(2)}, u32[]{:S(2)}) collective-permute-start(bf16[8,64,128]{2,1,0:T(8,128)(2,1)S(1)} %get-tuple-element.42.refs_2_), channel_id=1, source_target_pairs={{0,3},{1,0},{2,1},{3,2},{4,7},{5,4},{6,5},{7,6},{8,11},{9,8},{10,9... | collective-permute-start | bytes 393224 | tf_op jit(solution)/shard_map/ppermute | solution.py:288
  45.8 11.6 %collective-permute-start.16 = (bf16[8,64,128]{2,1,0:T(8,128)(2,1)S(1)}, bf16[8,64,128]{2,1,0:T(8,128)(2,1)S(1)}, u32[]{:S(2)}, u32[]{:S(2)}) collective-permute-start(bf16[8,64,128]{2,1,0:T(8,128)(2,1)S(1)} %get-tuple-element.42.refs_2_), channel_id=1, source_target_pairs={{0,2},{1,3},{2,0},{3,1},{4,6},{5,7},{6,4},{7,5},{8,10},{9,11},{10,... | collective-permute-start | bytes 393224 | tf_op jit(solution)/shard_map/ppermute | solution.py:288
  46.6 10.7 %collective-permute-start.15 = (bf16[8,64,128]{2,1,0:T(8,128)(2,1)S(1)}, bf16[8,64,128]{2,1,0:T(8,128)(2,1)S(1)}, u32[]{:S(2)}, u32[]{:S(2)}) collective-permute-start(bf16[8,64,128]{2,1,0:T(8,128)(2,1)S(1)} %get-tuple-element.42.refs_2_), channel_id=1, source_target_pairs={{0,1},{1,2},{2,3},{3,0},{4,5},{5,6},{6,7},{7,4},{8,9},{9,10},{10,1... | collective-permute-start | bytes 393224 | tf_op jit(solution)/shard_map/ppermute | solution.py:288
  49.4 4.2 %collective-permute-start.12 = (bf16[2,64,128]{2,1,0:T(8,128)(2,1)S(1)}, bf16[2,64,128]{2,1,0:T(8,128)(2,1)S(1)}, u32[]{:S(2)}, u32[]{:S(2)}) collective-permute-start(bf16[2,64,128]{2,1,0:T(8,128)(2,1)S(1)} %get-tuple-element.38), channel_id=1, source_target_pairs={{0,4},{4,8},{8,12},{1,5},{5,9},{9,13},{2,6},{6,10},{10,14},{3,7},{... | collective-permute-start | bytes 98312 | tf_op jit(solution)/shard_map/ppermute | solution.py:12
  52.1 4.7 %collective-permute-start.13 = (bf16[2,64,128]{2,1,0:T(8,128)(2,1)S(1)}, bf16[2,64,128]{2,1,0:T(8,128)(2,1)S(1)}, u32[]{:S(2)}, u32[]{:S(2)}) collective-permute-start(bf16[2,64,128]{2,1,0:T(8,128)(2,1)S(1)} %get-tuple-element.39), channel_id=1, source_target_pairs={{4,0},{8,4},{12,8},{5,1},{9,5},{13,9},{6,2},{10,6},{14,10},{7,3},{... | collective-permute-start | bytes 98312 | tf_op jit(solution)/shard_map/ppermute | solution.py:12
  59.9 4.3 %collective-permute-start.18 = (bf16[4,27,16,256]{3,2,1,0:T(8,128)(2,1)S(1)}, bf16[4,27,16,256]{3,2,1,0:T(8,128)(2,1)S(1)}, u32[]{:S(2)}, u32[]{:S(2)}) collective-permute-start(bf16[4,27,16,256]{3,2,1,0:T(8,128)(2,1)S(1)} %get-tuple-element.44), channel_id=1, source_target_pairs={{0,16},{16,0},{32,48},{48,32},{64,80},{80,64},{96,112},{112,96},{1... | collective-permute-start | bytes 2654216 | tf_op jit(solution)/shard_map/ppermute | solution.py:304
  62.2 8.2 %collective-permute-start.14 = (bf16[2,6,64,128]{3,2,1,0:T(8,128)(2,1)S(1)}, bf16[2,6,64,128]{3,2,1,0:T(8,128)(2,1)S(1)}, u32[]{:S(2)}, u32[]{:S(2)}) collective-permute-start(bf16[2,6,64,128]{3,2,1,0:T(8,128)(2,1)S(1)} %shard_map.73.refs_8_.refs_1_), channel_id=1, source_target_pairs={{16,0},{32,16},{48,32},{64,48},{80,64},{96,80},{112,96},{128,112},... | collective-permute-start | bytes 589832 | tf_op jit(solution)/shard_map/ppermute | solution.py:12
  64.7 7.8 %collective-permute-start.24 = (bf16[27,16,256]{2,1,0:T(8,128)(2,1)S(1)}, bf16[27,16,256]{2,1,0:T(8,128)(2,1)S(1)}, u32[]{:S(2)}, u32[]{:S(2)}) collective-permute-start(bf16[27,16,256]{2,1,0:T(8,128)(2,1)S(1)} %get-tuple-element.57), channel_id=1, source_target_pairs={{0,12},{4,0},{8,4},{12,8},{1,13},{5,1},{9,5},{13,9},{2,14},{6,2},{... | collective-permute-start | bytes 663560 | tf_op jit(solution)/shard_map/ppermute | solution.py:288
  64.8 8.3 %collective-permute-start.23 = (bf16[27,16,256]{2,1,0:T(8,128)(2,1)S(1)}, bf16[27,16,256]{2,1,0:T(8,128)(2,1)S(1)}, u32[]{:S(2)}, u32[]{:S(2)}) collective-permute-start(bf16[27,16,256]{2,1,0:T(8,128)(2,1)S(1)} %get-tuple-element.58), channel_id=1, source_target_pairs={{0,8},{4,12},{8,0},{12,4},{1,9},{5,13},{9,1},{13,5},{2,10},{6,14},... | collective-permute-start | bytes 663560 | tf_op jit(solution)/shard_map/ppermute | solution.py:288
  66.8 11.7 %collective-permute-start.22 = (bf16[27,16,256]{2,1,0:T(8,128)(2,1)S(1)}, bf16[27,16,256]{2,1,0:T(8,128)(2,1)S(1)}, u32[]{:S(2)}, u32[]{:S(2)}) collective-permute-start(bf16[27,16,256]{2,1,0:T(8,128)(2,1)S(1)} %get-tuple-element.59.refs_4_), channel_id=1, source_target_pairs={{0,4},{4,8},{8,12},{12,0},{1,5},{5,9},{9,13},{13,1},{2,6},{6,10},{... | collective-permute-start | bytes 663560 | tf_op jit(solution)/shard_map/ppermute | solution.py:288
  79.2 7.8 %collective-permute-start.25 = (bf16[27,8,128]{2,1,0:T(8,128)(2,1)S(1)}, bf16[27,8,128]{2,1,0:T(8,128)(2,1)S(1)}, u32[]{:S(2)}, u32[]{:S(2)}) collective-permute-start(bf16[27,8,128]{2,1,0:T(8,128)(2,1)S(1)} %get-tuple-element.50), channel_id=1, source_target_pairs={{0,32},{16,48},{32,64},{48,80},{64,96},{80,112},{96,0},{112,16},{1... | collective-permute-start | bytes 165896 | tf_op jit(solution)/shard_map/ppermute | solution.py:309
  82.0 8.1 %collective-permute-start.26 = (bf16[27,8,128]{2,1,0:T(8,128)(2,1)S(1)}, bf16[27,8,128]{2,1,0:T(8,128)(2,1)S(1)}, u32[]{:S(2)}, u32[]{:S(2)}) collective-permute-start(bf16[27,8,128]{2,1,0:T(8,128)(2,1)S(1)} %get-tuple-element.51), channel_id=1, source_target_pairs={{0,64},{16,80},{32,96},{48,112},{64,0},{80,16},{96,32},{112,48},{1... | collective-permute-start | bytes 165896 | tf_op jit(solution)/shard_map/ppermute | solution.py:309
  85.7 4.4 %collective-permute-start.27 = (bf16[27,8,128]{2,1,0:T(8,128)(2,1)S(1)}, bf16[27,8,128]{2,1,0:T(8,128)(2,1)S(1)}, u32[]{:S(2)}, u32[]{:S(2)}) collective-permute-start(bf16[27,8,128]{2,1,0:T(8,128)(2,1)S(1)} %get-tuple-element.52), channel_id=1, source_target_pairs={{0,96},{16,112},{32,0},{48,16},{64,32},{80,48},{96,64},{112,80},{1... | collective-permute-start | bytes 165896 | tf_op jit(solution)/shard_map/ppermute | solution.py:309
  90.1 8.4 %collective-permute-start.28 = (bf16[27,8,128]{2,1,0:T(8,128)(2,1)S(1)}, bf16[27,8,128]{2,1,0:T(8,128)(2,1)S(1)}, u32[]{:S(2)}, u32[]{:S(2)}) collective-permute-start(bf16[27,8,128]{2,1,0:T(8,128)(2,1)S(1)} %add_convert_fusion.2), channel_id=1, source_target_pairs={{0,128},{16,144},{32,160},{48,176},{64,192},{80,208},{96,224},{112... | collective-permute-start | bytes 165896 | tf_op jit(solution)/shard_map/ppermute | solution.py:304
  93.5 17.2 %collective-permute-start.19 = (bf16[8,64,128]{2,1,0:T(8,128)(2,1)S(1)}, bf16[8,64,128]{2,1,0:T(8,128)(2,1)S(1)}, u32[]{:S(2)}, u32[]{:S(2)}) collective-permute-start(bf16[8,64,128]{2,1,0:T(8,128)(2,1)S(1)} %get-tuple-element.46), channel_id=1, source_target_pairs={{0,1},{1,2},{2,3},{3,0},{4,5},{5,6},{6,7},{7,4},{8,9},{9,10},{10,1... | collective-permute-start | bytes 393224 | tf_op jit(solution)/shard_map/ppermute | solution.py:288
  94.8 15.9 %collective-permute-start.20 = (bf16[8,64,128]{2,1,0:T(8,128)(2,1)S(1)}, bf16[8,64,128]{2,1,0:T(8,128)(2,1)S(1)}, u32[]{:S(2)}, u32[]{:S(2)}) collective-permute-start(bf16[8,64,128]{2,1,0:T(8,128)(2,1)S(1)} %get-tuple-element.47), channel_id=1, source_target_pairs={{0,2},{1,3},{2,0},{3,1},{4,6},{5,7},{6,4},{7,5},{8,10},{9,11},{10,... | collective-permute-start | bytes 393224 | tf_op jit(solution)/shard_map/ppermute | solution.py:288
  97.2 13.5 %collective-permute-start.21 = (bf16[8,64,128]{2,1,0:T(8,128)(2,1)S(1)}, bf16[8,64,128]{2,1,0:T(8,128)(2,1)S(1)}, u32[]{:S(2)}, u32[]{:S(2)}) collective-permute-start(bf16[8,64,128]{2,1,0:T(8,128)(2,1)S(1)} %get-tuple-element.48), channel_id=1, source_target_pairs={{0,3},{1,0},{2,1},{3,2},{4,7},{5,4},{6,5},{7,6},{8,11},{9,8},{10,9... | collective-permute-start | bytes 393224 | tf_op jit(solution)/shard_map/ppermute | solution.py:288
  98.6 4.2 %collective-permute-start.31 = (bf16[27,8,128]{2,1,0:T(8,128)(2,1)S(1)}, bf16[27,8,128]{2,1,0:T(8,128)(2,1)S(1)}, u32[]{:S(2)}, u32[]{:S(2)}) collective-permute-start(bf16[27,8,128]{2,1,0:T(8,128)(2,1)S(1)} %add_convert_fusion.1.refs_1_), channel_id=1, source_target_pairs={{0,96},{16,112},{32,0},{48,16},{64,32},{80,48},{96,64},{112,80},{1... | collective-permute-start | bytes 165896 | tf_op jit(solution)/shard_map/ppermute | solution.py:309
  101.6 4.1 %collective-permute-start.30 = (bf16[27,8,128]{2,1,0:T(8,128)(2,1)S(1)}, bf16[27,8,128]{2,1,0:T(8,128)(2,1)S(1)}, u32[]{:S(2)}, u32[]{:S(2)}) collective-permute-start(bf16[27,8,128]{2,1,0:T(8,128)(2,1)S(1)} %add_convert_fusion.1.refs_1_), channel_id=1, source_target_pairs={{0,64},{16,80},{32,96},{48,112},{64,0},{80,16},{96,32},{112,48},{1... | collective-permute-start | bytes 165896 | tf_op jit(solution)/shard_map/ppermute | solution.py:309
  102.8 5.8 %collective-permute-start.29 = (bf16[27,8,128]{2,1,0:T(8,128)(2,1)S(1)}, bf16[27,8,128]{2,1,0:T(8,128)(2,1)S(1)}, u32[]{:S(2)}, u32[]{:S(2)}) collective-permute-start(bf16[27,8,128]{2,1,0:T(8,128)(2,1)S(1)} %add_convert_fusion.1.refs_1_), channel_id=1, source_target_pairs={{0,32},{16,48},{32,64},{48,80},{64,96},{80,112},{96,0},{112,16},{1... | collective-permute-start | bytes 165896 | tf_op jit(solution)/shard_map/ppermute | solution.py:309
  109.2 4.9 %collective-permute-start.34 = (bf16[27,16,256]{2,1,0:T(8,128)(2,1)S(1)}, bf16[27,16,256]{2,1,0:T(8,128)(2,1)S(1)}, u32[]{:S(2)}, u32[]{:S(2)}) collective-permute-start(bf16[27,16,256]{2,1,0:T(8,128)(2,1)S(1)} %shard_map.77.refs_1_), channel_id=1, source_target_pairs={{0,12},{4,0},{8,4},{12,8},{1,13},{5,1},{9,5},{13,9},{2,14},{6,2},{... | collective-permute-start | bytes 663560 | tf_op jit(solution)/shard_map/ppermute | solution.py:288
  109.3 6.5 %collective-permute-start.33 = (bf16[27,16,256]{2,1,0:T(8,128)(2,1)S(1)}, bf16[27,16,256]{2,1,0:T(8,128)(2,1)S(1)}, u32[]{:S(2)}, u32[]{:S(2)}) collective-permute-start(bf16[27,16,256]{2,1,0:T(8,128)(2,1)S(1)} %shard_map.77.refs_1_), channel_id=1, source_target_pairs={{0,8},{4,12},{8,0},{12,4},{1,9},{5,13},{9,1},{13,5},{2,10},{6,14},... | collective-permute-start | bytes 663560 | tf_op jit(solution)/shard_map/ppermute | solution.py:288
  110.7 7.3 %collective-permute-start.32 = (bf16[27,16,256]{2,1,0:T(8,128)(2,1)S(1)}, bf16[27,16,256]{2,1,0:T(8,128)(2,1)S(1)}, u32[]{:S(2)}, u32[]{:S(2)}) collective-permute-start(bf16[27,16,256]{2,1,0:T(8,128)(2,1)S(1)} %shard_map.77.refs_1_), channel_id=1, source_target_pairs={{0,4},{4,8},{8,12},{12,0},{1,5},{5,9},{9,13},{13,1},{2,6},{6,10},{... | collective-permute-start | bytes 663560 | tf_op jit(solution)/shard_map/ppermute | solution.py:288
  110.8 15.9 %copy-start.3 = (bf16[8,64,128]{2,1,0:T(8,128)(2,1)}, bf16[8,64,128]{2,1,0:T(8,128)(2,1)S(1)}, u32[]{:S(2)}) copy-start(bf16[8,64,128]{2,1,0:T(8,128)(2,1)S(1)} %add_convert_fusion) | copy-start | bytes 393220
  118.6 8.0 %collective-permute-start.35 = (bf16[27,64,256]{2,1,0:T(8,128)(2,1)S(1)}, bf16[27,64,256]{2,1,0:T(8,128)(2,1)S(1)}, u32[]{:S(2)}, u32[]{:S(2)}) collective-permute-start(bf16[27,64,256]{2,1,0:T(8,128)(2,1)S(1)} %shard_map.78), channel_id=1, source_target_pairs={{0,16},{16,0},{32,48},{48,32},{64,80},{80,64},{96,112},{112,96},{1... | collective-permute-start | bytes 2654216 | tf_op jit(solution)/shard_map/ppermute | solution.py:304
